TPU v7x, 128 devices: a whole 4x4x4 slice. The times are simulated.
128 devices in a mesh: chan: 32 (over x, y, z_lo), tm: 4 (over z_hi, core).
Axes of the slice: x: 4, y: 4, z: 4 (z_hi: 2, z_lo: 2; z = z_hi * 2 + z_lo), core: 2. Of those that a mesh axis runs over, the one named last changes fastest.
Arguments:
- spectra: bfloat16 [256, 2, 250, 8192], P('tm', None, None, 'chan'), may hold values from -6 to 6
- src_blocks: int32 [2], replicated, may hold values from 0 to 127
- valid: int32 [256], P('tm'), may hold values 0 or 1
Outputs:
- stacked: bfloat16 [128, 101, 8192], P('tm', None, 'chan')
All inputs are finite; a program needn't handle non-finite values. No bound on the sum of `valid` on one device may be relied on, other than what follows from the above.
Results may differ from a plain program's by a relative error of at most 0.013.
Values may be sent and summed in bfloat16 or wider, within the bound.
No kernel may reach another device: no remote copies, remote signals or barrier semaphores. Data moves between devices by JAX's collectives and lax.ppermute only.
A program may use at most 192 MiB of HBM per device.

v0:
```python
import jax
import jax.numpy as jnp
from jax import lax
from jax.sharding import PartitionSpec as P

LAGS = 101
SRC_BLK = 64


def from_root(x, axis, root):
    mine = lax.axis_index(axis) == root
    return lax.psum(jnp.where(mine, x, jnp.zeros_like(x)), axis)


def lag_table(bin_count, lag_count, segment_total):
    bins_idx = jnp.arange(bin_count, dtype=jnp.int32) + 1
    lag_steps = jnp.arange(lag_count, dtype=jnp.int32) - (lag_count - 1) // 2
    phase_int = lag_steps[:, None] * bins_idx[None, :] % (2 * bin_count)
    phase = phase_int.astype(jnp.float32) * (2.0 * jnp.pi / (2.0 * bin_count))
    scale = 1.0 / jnp.sqrt(jnp.float32(segment_total * bin_count))
    return jnp.stack([jnp.cos(phase) * scale, -jnp.sin(phase) * scale]).astype(jnp.bfloat16)


def cross_spectra(source, spectra):
    rotated = jnp.concatenate([spectra[:, 1:2], -spectra[:, 0:1]], axis=1)
    real_part = jnp.einsum("scfk,scfr->fkr", source, spectra, preferred_element_type=jnp.float32)
    imag_part = jnp.einsum("scfk,scfr->fkr", source, rotated, preferred_element_type=jnp.float32)
    return jnp.stack([real_part, imag_part]).astype(jnp.bfloat16)


def to_lags(table, cross):
    return jnp.einsum("plf,pfkr->klr", table, cross, preferred_element_type=jnp.float32)


def fetch_block(window, owner):
    return from_root(window, "chan", owner)


def body(spectra, src_blocks, valid):
    seg_count, _, bin_count, chan_width = spectra.shape
    tm_count = lax.axis_size("tm")
    chan_index = lax.axis_index("chan")
    keep_mask = valid.astype(jnp.bfloat16)[:, None, None, None]
    starts = src_blocks * SRC_BLK
    owners = starts // chan_width
    windows = []
    for block in range(2):
        offset = jnp.clip(starts[block] - chan_index * chan_width, 0, chan_width - SRC_BLK)
        windows.append(lax.dynamic_slice_in_dim(spectra, offset, SRC_BLK, 3))
    sources = [fetch_block(windows[block], owners[block]) for block in range(2)]
    table = lag_table(bin_count, LAGS, seg_count * tm_count)
    pieces = [
        to_lags(table, cross_spectra(sources[block] * keep_mask, spectra)) for block in range(2)
    ]
    partial_value = jnp.concatenate(pieces, axis=0)
    row_count = partial_value.shape[0] // tm_count
    total = lax.psum(partial_value.astype(jnp.bfloat16), "tm").astype(jnp.float32)
    own_rows = lax.dynamic_slice_in_dim(total, lax.axis_index("tm") * row_count, row_count, 0)
    return own_rows.astype(jnp.bfloat16)


def solution(mesh):
    placed = (P("tm", None, None, "chan"), P(), P("tm"))
    return jax.shard_map(
        body, mesh=mesh, in_specs=placed, out_specs=P("tm", None, "chan"), check_vma=False
    )
```

profile of v0, /device:TPU:1, one launch (start us, length us, event | category | flops | bytes accessed | tf_op | source)
XLA Modules:
  0.0 756.0 jit_solution(6869578964841852418)
XLA Ops:
  6.5 0.7 and_select_fusion
  7.2 0.6 fusion.30
  9.1 24.8 %constant_dynamic-slice_fusion.1 = (bf16[64,2,250,64]{3,1,2,0:T(2,128)(2,1)}, bf16[64,2,250,64]{3,1,2,0:T(2,128)(2,1)}) fusion(bf16[64,2,250,256]{3,1,2,0:T(2,128)(2,1)} %param.3, s32[]{:T(128)S(6)} %min.7, s32[]{:T(128)S(6)} %min.8), kind=kLoop, calls=%fused_computation.46 | loop fusion | bytes 16384008 | tf_op jit(solution)/shard_map/dynamic_slice | solution.py:49
  33.9 17.2 %copy.35 = bf16[64,2,250,64]{2,3,1,0:T(8,128)(2,1)} copy(bf16[64,2,250,64]{3,1,2,0:T(2,128)(2,1)} %get-tuple-element.9) | data formatting | bytes 8192000
  51.8 17.3 %copy.36 = bf16[64,2,250,64]{2,3,1,0:T(8,128)(2,1)} copy(bf16[64,2,250,64]{3,1,2,0:T(2,128)(2,1)} %get-tuple-element.10) | data formatting | bytes 8192000
  69.6 2.4 broadcast_select_fusion.1
  72.0 1.3 copy-done
  73.3 2.3 broadcast_select_fusion
  75.6 0.0 all-reduce.6.cloned.1.call-update
  75.6 0.0 copy-start.1
  75.6 0.2 all-reduce.4.cloned.1.call-start
  75.9 11.3 %copy.17 = bf16[64,2,250,256]{3,0,1,2:T(8,128)(2,1)S(1)} copy(bf16[64,2,250,256]{3,1,2,0:T(2,128)(2,1)} %param.3) | data formatting | bytes 32768000 | tf_op args[0]
  87.2 0.5 multiply_convert_fusion.1
  87.7 5.9 fusion.29
  93.7 364.7 %all-reduce.6.cloned.1.call-done = (bf16[64,2,250,64]{2,3,1,0:T(8,128)(2,1)}, bf16[64,2,250,64]{2,3,1,0:T(8,128)(2,1)}) async-done(((bf16[64,2,250,64]{2,3,1,0:T(8,128)(2,1)}, bf16[64,2,250,64]{2,3,1,0:T(8,128)(2,1)}), (bf16[64,2,250,64]{2,3,1,0:T(8,128)(2,1)}, bf16[64,2,250,64]{2,3,1,0:T(8,128)(2,1)})) %all-reduce.6.cloned.1.call-update) | async-done | bytes 8192016 | tf_op jit(solution)/shard_map/psum | solution.py:12
  458.4 5.9 broadcast_multiply_fusion.1
  464.3 14.3 %copy.16 = bf16[64,2,250,64]{0,3,1,2:T(8,128)(2,1)} copy(bf16[64,2,250,64]{2,3,1,0:T(8,128)(2,1)} %get-tuple-element.13) | data formatting | bytes 8192000 | tf_op jit(solution)/shard_map/mul | solution.py:53
  478.6 13.0 %fusion.8 = bf16[1,250,64,256]{3,2,1,0:T(8,128)(2,1)} fusion(bf16[64,2,250,64]{0,3,1,2:T(8,128)(2,1)} %copy.16, bf16[64,2,250,256]{3,1,2,0:T(2,128)(2,1)} %param.3), kind=kOutput, calls=%fused_computation.19 | convolution fusion | flops 1052672000 | bytes 28672000 | tf_op jit(solution)/shard_map/scfk,scfr->fkr/dot_general | solution.py:26
  491.6 14.3 %copy.24 = bf16[64,2,250,64]{0,3,1,2:T(8,128)(2,1)} copy(bf16[64,2,250,64]{2,3,1,0:T(8,128)(2,1)} %get-tuple-element.14) | data formatting | bytes 8192000 | tf_op jit(solution)/shard_map/mul | solution.py:53
  505.9 12.3 %fusion.6 = bf16[1,250,64,256]{3,2,1,0:T(8,128)(2,1)} fusion(bf16[64,2,250,64]{0,3,1,2:T(8,128)(2,1)} %copy.16, bf16[64,1,250,256]{3,0,1,2:T(8,128)(2,1)} %get-tuple-element.8, bf16[64,1,250,256]{3,0,1,2:T(8,128)(2,1)} %get-tuple-element.7), kind=kOutput, calls=%fused_computation.13 | convolution fusion | flops 1060864000 | bytes 28672000 | tf_op jit(solution)/shard_map/scfk,scfr->fkr/dot_general | solution.py:27
  518.2 12.4 %fusion.7 = bf16[1,250,64,256]{3,2,1,0:T(8,128)(2,1)} fusion(bf16[64,2,250,64]{0,3,1,2:T(8,128)(2,1)} %copy.24, bf16[64,1,250,256]{3,0,1,2:T(8,128)(2,1)} %get-tuple-element.8, bf16[64,1,250,256]{3,0,1,2:T(8,128)(2,1)} %get-tuple-element.7), kind=kOutput, calls=%fused_computation.14 | convolution fusion | flops 1060864000 | bytes 28672000 | tf_op jit(solution)/shard_map/scfk,scfr->fkr/dot_general | solution.py:27
  530.6 13.4 %fusion.9 = bf16[1,250,64,256]{3,2,1,0:T(8,128)(2,1)} fusion(bf16[64,2,250,64]{0,3,1,2:T(8,128)(2,1)} %copy.24, bf16[64,2,250,256]{3,1,2,0:T(2,128)(2,1)} %param.3), kind=kOutput, calls=%fused_computation.20 | convolution fusion | flops 1052672000 | bytes 28672000 | tf_op jit(solution)/shard_map/scfk,scfr->fkr/dot_general | solution.py:26
  544.0 14.0 %pad_maximum_fusion.1 = bf16[2,250,64,256]{3,2,1,0:T(8,128)(2,1)} fusion(bf16[1,250,64,256]{3,2,1,0:T(8,128)(2,1)} %fusion.6, bf16[1,250,64,256]{3,2,1,0:T(8,128)(2,1)} %fusion.8), kind=kLoop, calls=%fused_computation.5 | loop fusion | flops 8192000 | bytes 32768000 | tf_op jit(solution)/shard_map/stack | solution.py:28
  558.0 17.9 %fusion.12 = bf16[64,256,101]{1,2,0:T(8,128)(2,1)} fusion(bf16[2,250,64,256]{3,2,1,0:T(8,128)(2,1)} %pad_maximum_fusion.1, bf16[1,101,250]{2,1,0:T(8,128)(2,1)S(1)} %get-tuple-element.12, bf16[1,101,250]{2,1,0:T(8,128)(2,1)S(1)} %get-tuple-element.11), kind=kOutput, calls=%fused_computation.26 | convolution fusion | flops 1654834560 | bytes 19794568 | tf_op jit(solution)/shard_map/plf,pfkr->klr/dot_general | solution.py:32
  575.9 2.7 copy.55
  578.7 10.8 %pad_maximum_fusion.2 = bf16[2,250,64,256]{3,2,1,0:T(8,128)(2,1)} fusion(bf16[1,250,64,256]{3,2,1,0:T(8,128)(2,1)} %fusion.7, bf16[1,250,64,256]{3,2,1,0:T(8,128)(2,1)S(1)} %bitcast.53), kind=kLoop, calls=%fused_computation.6 | loop fusion | flops 8192000 | bytes 32768000 | tf_op jit(solution)/shard_map/stack | solution.py:28
  589.5 17.6 %fusion.15 = bf16[64,256,101]{1,2,0:T(8,128)(2,1)} fusion(bf16[2,250,64,256]{3,2,1,0:T(8,128)(2,1)} %pad_maximum_fusion.2, bf16[1,101,250]{2,1,0:T(8,128)(2,1)S(1)} %get-tuple-element.12, bf16[1,101,250]{2,1,0:T(8,128)(2,1)S(1)} %get-tuple-element.11), kind=kOutput, calls=%fused_computation.27 | convolution fusion | flops 1654834560 | bytes 19794568 | tf_op jit(solution)/shard_map/plf,pfkr->klr/dot_general | solution.py:32
  607.1 2.7 copy.56
  609.8 3.6 pad_maximum_fusion.9
  613.5 0.0 all-reduce.4.cloned.1.call-update
  613.5 132.7 %all-reduce.4.cloned.1.call-done = bf16[128,101,256]{2,0,1:T(8,128)(2,1)} async-done(((bf16[128,101,256]{2,0,1:T(8,128)(2,1)}), bf16[128,101,256]{2,0,1:T(8,128)(2,1)}) %all-reduce.4.cloned.1.call-update) | async-done | bytes 6619152 | tf_op jit(solution)/shard_map/psum | solution.py:57
  746.2 2.7 convert_convert_fusion
  (11 shorter events, 0.0 us)
Async XLA Ops:
  6.5 451.9 %all-reduce.6.cloned.1.call-start = ((), (), s32[]{:S(2)}) async-start(), calls=%async_computation.1 | async-start | bytes 16777216 | tf_op jit(solution)/shard_map/psum | solution.py:12
  69.6 3.7 copy-start
  75.6 11.5 %copy-start.1 = (s32[64]{0:T(128)S(1)}, s32[64]{0:T(128)}, u32[]{:S(2)}) copy-start(s32[64]{0:T(128)} %param.5) | copy-start | bytes 772
  75.6 670.6 %all-reduce.4.cloned.1.call-start = ((), (), s32[]{:S(2)}) async-start(), calls=%async_computation | async-start | bytes 13238272 | tf_op jit(solution)/shard_map/psum | solution.py:57
  544.0 34.7 %slice-start = ((s8[8192000]{0:T(1024)(128)(4,1)}), s8[4194304]{0:T(1024)(128)(4,1)S(1)}, s32[]{:S(2)}) async-start(s8[8192000]{0:T(1024)(128)(4,1)} %bitcast.52), calls=%async_computation.2 | async-start | bytes 8388608
  558.0 20.6 %slice-start.1 = ((s8[8192000]{0:T(1024)(128)(4,1)}), s8[3997696]{0:T(1024)(128)(4,1)S(1)}, s32[]{:S(2)}) async-start(s8[8192000]{0:T(1024)(128)(4,1)} %bitcast.52), calls=%async_computation.3 | async-start | bytes 7995392
Sparse Core Ops, SparseCore 0:
  75.7 382.6 all-reduce.5
  613.6 132.5 all-reduce.3
where the time goes:
time: 760 us; the launch traced here: 756 us
  waiting for transfers between devices  497 us (65%)
  local copies, waits for them, and re-layouts  107 us (14%)
  matrix products  86.6 us (11%)
  other arithmetic  48.9 us (6%)
  between operations  16.2 us (2%)
    psum x1, waiting for transfers between devices, from_root(): return lax.psum(jnp.where(mine, x, jnp.zeros_like(x)), axis)  365 us
    psum x1, waiting for transfers between devices, body(): lax.psum(partial_value.astype(jnp.bfloat16), 'tm').astype(jnp.float32)  133 us
    unnamed x11, local copies, waits for them, and re-layouts  47.1 us
    dot_general x2, matrix products, to_lags(): jnp.einsum('plf,pfkr->klr', table, cross, preferred_element_type=jnp.floa...  35.5 us
    mul x2, local copies, waits for them, and re-layouts, body(): sources[block] * keep_mask  28.6 us
    dot_general x2, matrix products, cross_spectra(): jnp.einsum('scfk,scfr->fkr', source, spectra, preferred_element_type=jnp....  26.4 us
    another operation x2, other arithmetic, cross_spectra(): return jnp.stack([real_part, imag_part]).astype(jnp.bfloat16)  24.8 us
    dynamic_slice x1, local copies, waits for them, and re-layouts, body(): windows.append(lax.dynamic_slice_in_dim(spectra, offset, SRC_BLK, 3))  24.8 us
  transfers between devices with their start and end apart: 2, of which 2 were waited for; matrix products, arithmetic and copies ran while one was open for 2% of the time, Pallas kernels for 0%

commit v1 on v0

v1 whole, which is shorter than its diff:
```python
import jax
import jax.numpy as jnp
from jax import lax
from jax.experimental import pallas as pl
from jax.experimental.pallas import tpu as pltpu
from jax.sharding import PartitionSpec as P

LAGS = 101
SRC_BLK = 64
BINS = 250
CHUNKS = 2
ROWS = 128 // CHUNKS
LAG_PAD = 112


def shift_x(x, step):
    pairs = [((a * 4 + b) * 2 + c, (((a + step) % 4) * 4 + b) * 2 + c) for a in range(4) for b in range(4) for c in range(2)]
    return lax.ppermute(x, "chan", pairs)


def shift_y(x, step):
    pairs = [((a * 4 + b) * 2 + c, (a * 4 + (b + step) % 4) * 2 + c) for a in range(4) for b in range(4) for c in range(2)]
    return lax.ppermute(x, "chan", pairs)


def swap_z(x):
    return lax.ppermute(x, "chan", [(a, a ^ 1) for a in range(32)])


def swap_core(x):
    return lax.ppermute(x, "tm", [(a, a ^ 1) for a in range(4)])


def swap_far(x):
    return lax.ppermute(x, "tm", [(a, a ^ 2) for a in range(4)])


def lag_table(freqs, lag_count, segment_total):
    lag_steps = jnp.arange(lag_count, dtype=jnp.int32) - (LAGS - 1) // 2
    phase_int = lag_steps[:, None] * (freqs + 1)[None, :] % (2 * BINS)
    phase = phase_int.astype(jnp.float32) * (2.0 * jnp.pi / (2.0 * BINS))
    scale = 1.0 / jnp.sqrt(jnp.float32(segment_total * BINS))
    both = jnp.stack([jnp.cos(phase) * scale, -jnp.sin(phase) * scale])
    return jnp.where((freqs < BINS)[None, None, :], both, 0.0).astype(jnp.bfloat16)


def pick_kernel(first_ref, pick_ref, mask_ref, spec_ref, out_ref):
    step = pl.program_id(0)
    for w in range(8):
        rows = lax.dot_general(
            pick_ref[...], spec_ref[w], (((1,), (1,)), ((), ())), preferred_element_type=jnp.float32
        )
        kept = jnp.where((first_ref[0] + step) * 8 + w < BINS, rows * mask_ref[...], 0.0)
        out_ref[w] = kept.astype(jnp.bfloat16)


def pick_rows(first, pick, mask, spec):
    return pl.pallas_call(
        pick_kernel,
        grid_spec=pltpu.PrefetchScalarGridSpec(
            num_scalar_prefetch=1,
            grid=(4,),
            in_specs=[
                pl.BlockSpec((128, 256), lambda i, s: (0, 0)),
                pl.BlockSpec((1, 128), lambda i, s: (0, 0)),
                pl.BlockSpec((8, 128, 256), lambda i, s: (s[0] + i, 0, 0)),
            ],
            out_specs=pl.BlockSpec((8, 128, 128), lambda i, s: (i, 0, 0)),
        ),
        out_shape=jax.ShapeDtypeStruct((32, 128, 128), jnp.bfloat16),
        cost_estimate=pl.CostEstimate(flops=2 * 32 * 128 * 128 * 256, bytes_accessed=3 << 20, transcendentals=0),
        name="pick_rows",
    )(first, pick, mask, spec)


def correlate_kernel(blocks_ref, table_ref, sign_ref, spec_ref, src_ref, send_ref, keep_ref, left, right, acc):
    step = pl.program_id(0)
    base = lax.rem(step, 16) * 8
    for w in range(8):
        rows = src_ref[w]
        turned = jnp.concatenate([rows[:, 64:], rows[:, :64]], axis=1) * sign_ref[...]
        both = jnp.concatenate([rows, turned], axis=0)
        cross = jnp.dot(both, spec_ref[w], preferred_element_type=jnp.float32)
        for part in range(2):
            place = pl.ds(part * 128 + base + w, ROWS, stride=256)
            piece = cross[part * ROWS : (part + 1) * ROWS]
            left[place, :] = piece[:, :128]
            right[place, :] = piece[:, 128:]

    def lags(k):
        rows = pl.ds(pl.multiple_of(k * 256, 256), 256)
        cross = jnp.concatenate(
            [left[rows, :].astype(jnp.bfloat16), right[rows, :].astype(jnp.bfloat16)], axis=1
        )
        return jnp.dot(table_ref[0], cross, preferred_element_type=jnp.float32)

    @pl.when(step == 15)
    def _():
        @pl.loop(0, ROWS)
        def _(k):
            acc[k] = lags(k)

    @pl.when(step == 31)
    def _():
        @pl.loop(0, ROWS // 2)
        def _(k):
            send_ref[k] = (acc[k] + lags(k))[:LAGS].astype(jnp.bfloat16)

        @pl.loop(0, ROWS // 2)
        def _(k):
            high = k + ROWS // 2
            keep_ref[k] = (acc[high] + lags(high))[:LAGS].astype(jnp.bfloat16)


def correlate(blocks, table, sign, spec, src):
    half = jax.ShapeDtypeStruct((ROWS // 2, LAGS, 256), jnp.bfloat16)
    whole = pl.BlockSpec((ROWS // 2, LAGS, 256), lambda i, s: (0, 0, 0))
    return pl.pallas_call(
        correlate_kernel,
        grid_spec=pltpu.PrefetchScalarGridSpec(
            num_scalar_prefetch=1,
            grid=(32,),
            in_specs=[
                pl.BlockSpec((1, LAG_PAD, 256), lambda i, s: (i // 16, 0, 0)),
                pl.BlockSpec((1, 128), lambda i, s: (0, 0)),
                pl.BlockSpec((8, 128, 256), lambda i, s: (s[i], 0, 0)),
                pl.BlockSpec((8, ROWS, 128), lambda i, s: (i, 0, 0)),
            ],
            out_specs=[whole, whole],
            scratch_shapes=[
                pltpu.VMEM((ROWS * 256, 128), jnp.float32),
                pltpu.VMEM((ROWS * 256, 128), jnp.float32),
                pltpu.VMEM((ROWS, LAG_PAD, 256), jnp.float32),
            ],
        ),
        out_shape=[half, half],
        compiler_params=pltpu.CompilerParams(vmem_limit_bytes=44 << 20),
        cost_estimate=pl.CostEstimate(flops=20 * 10**9, bytes_accessed=24 << 20, transcendentals=0),
        name="correlate",
    )(blocks, table, sign, spec, src)


def body(spectra, src_blocks, valid):
    chan_index = lax.axis_index("chan")
    tm_index = lax.axis_index("tm")
    x, y = chan_index // 8, chan_index // 2 % 4
    core, far = tm_index % 2, tm_index // 2

    spec = jnp.transpose(spectra, (2, 1, 0, 3)).reshape(BINS, 128, 256)

    q = jnp.arange(128, dtype=jnp.int32)
    part, group, within = q // ROWS, q % ROWS // (ROWS // 4), q % (ROWS // 4)
    dest_core = jnp.where(group < 2, 1 - core, core)
    dest_far = jnp.where(group % 2 == 0, 1 - far, far)
    row = 32 * (2 * dest_far + dest_core) + (ROWS // 4) * part + within
    block = jnp.where(row < SRC_BLK, src_blocks[0], src_blocks[1])
    channel = block * SRC_BLK + row % SRC_BLK - chan_index * 256
    pick = (channel[:, None] == jnp.arange(256, dtype=jnp.int32)[None, :]).astype(jnp.bfloat16)
    mask = jnp.tile(valid.astype(jnp.float32), 2)[None, :]
    sign = jnp.where(jnp.arange(128) < 64, -1.0, 1.0).astype(jnp.bfloat16)[None, :]

    def scatter_first(base, at, shift):
        own = [pick_rows((base + 4 * ((at + d) % 4))[None], pick, mask, spec) for d in (1, 3, 2, 0)]
        return [own[3]] + [shift(own[i], d) for i, d in enumerate((1, 3, 2))]

    def scatter_second(quarters, at, shift):
        def piece(d):
            cut = [lax.dynamic_slice_in_dim(a, 8 * ((at + d) % 4), 8, 0) for a in quarters]
            return (cut[0] + cut[1]) + (cut[2] + cut[3])

        got = [shift(piece(d), d) for d in (1, 3, 2)]
        return (piece(0) + got[0]) + (got[1] + got[2])

    zero = jnp.int32(0)
    quarters_a = scatter_first(zero, x, shift_x)
    quarters_b = scatter_first(zero + 16, y, shift_y)
    piece_a = scatter_second(quarters_a, y, shift_y)
    piece_b = scatter_second(quarters_b, x, shift_x)
    piece_a = piece_a + swap_z(piece_a)
    piece_b = piece_b + swap_z(piece_b)

    def gather(a, shift):
        got = {d: shift(a, d) for d in (1, 3, 2)}
        return [a, got[1], got[2], got[3]]

    inner_a = gather(piece_a, shift_y)
    inner_b = gather(piece_b, shift_x)

    i = jnp.arange(256, dtype=jnp.int32)
    e, j, w = i % 128 // 32, i % 32 // 8, i % 8
    freqs = jnp.where(
        i < 128, 32 * ((x - e) % 4) + 8 * ((y - j) % 4) + w, 128 + 32 * ((y - e) % 4) + 8 * ((x - j) % 4) + w
    )
    table = lag_table(freqs, LAG_PAD, 256).reshape(2, LAG_PAD, 2, 128).transpose(2, 1, 0, 3).reshape(2, LAG_PAD, 256)
    blocks = freqs[::8] // 8

    outs = []
    for c in range(CHUNKS):
        rows = slice(c * ROWS, (c + 1) * ROWS)
        outer_a = gather(jnp.concatenate([a[:, rows] for a in inner_a]), shift_x)
        outer_b = gather(jnp.concatenate([a[:, rows] for a in inner_b]), shift_y)
        src = jnp.concatenate(outer_a + outer_b)
        send, keep = correlate(blocks, table, sign, spec, src)
        near = swap_core(send)
        quarter = ROWS // 4
        onward = (keep[:quarter].astype(jnp.float32) + near[:quarter].astype(jnp.float32)).astype(jnp.bfloat16)
        last = swap_far(onward)
        own = keep[quarter:].astype(jnp.float32) + near[quarter:].astype(jnp.float32)
        outs.append((own + last.astype(jnp.float32)).astype(jnp.bfloat16))
    return jnp.concatenate(outs)


def solution(mesh):
    placed = (P("tm", None, None, "chan"), P(), P("tm"))
    return jax.shard_map(
        body, mesh=mesh, in_specs=placed, out_specs=P("tm", None, "chan"), check_vma=False
    )
```

time: 760 us -> 396 us (0.52)
  waiting for transfers between devices: 497 us -> 138 us
  Pallas kernels: 0 us -> 148 us
  matrix products: 86.6 us -> 0 us
  local copies, waits for them, and re-layouts: 107 us -> 38.2 us
  starting transfers between devices: 0.22 us -> 57.4 us
  other arithmetic: 48.9 us -> 12.7 us
  between operations: 16.2 us -> 0.21 us
    psum x2 -> x0, waiting for transfers between devices: 497 us -> none  [the longest x1 365 us: from_root(): return lax.psum(jnp.where(mine, x, jnp.zeros_like(x)), axis)]
    pallas_call x0 -> x10, Pallas kernels: none -> 148 us  [the longest x2 115 us: correlate(): pl.pallas_call(correlate_kernel, grid_spec=pltpu.PrefetchScalarGridSpec(n...]
    ppermute x0 -> x36, waiting for transfers between devices: none -> 138 us  [the longest x15 62.2 us: shift_x(): return lax.ppermute(x, 'chan', pairs)]
    dot_general x6 -> x0, matrix products: 86.6 us -> none  [the longest x2 35.5 us: to_lags(): jnp.einsum('plf,pfkr->klr', table, cross, preferred_element_type=jnp.floa...]
    ppermute x0 -> x36, starting transfers between devices: none -> 57.4 us  [the longest x15 30.4 us: shift_y(): return lax.ppermute(x, 'chan', pairs)]
    unnamed x11 -> x14, local copies, waits for them, and re-layouts: 47.1 us -> 8.4 us
    mul x2 -> x0, local copies, waits for them, and re-layouts: 28.6 us -> none  [body(): sources[block] * keep_mask]
    another operation x3 -> x0, other arithmetic: 25.4 us -> none  [the longest x2 24.8 us: cross_spectra(): return jnp.stack([real_part, imag_part]).astype(jnp.bfloat16)]
  transfers between devices with their start and end apart: 2 -> 36, of which waited for: 2 -> 24; matrix products, arithmetic and copies ran while one was open for 2% -> 7% of each run, Pallas kernels for 0% -> 37%
where the time goes in v1:
time: 396 us; the launch traced here: 394 us
  Pallas kernels  148 us (37%)
  waiting for transfers between devices  138 us (35%)
  starting transfers between devices  57.4 us (14%)
  local copies, waits for them, and re-layouts  38.2 us (10%)
  other arithmetic  12.7 us (3%)
    pallas_call x2, Pallas kernels, correlate(): pl.pallas_call(correlate_kernel, grid_spec=pltpu.PrefetchScalarGridSpec(n...  115 us
    ppermute x15, waiting for transfers between devices, shift_x(): return lax.ppermute(x, 'chan', pairs)  62.2 us
    ppermute x15, waiting for transfers between devices, shift_y(): return lax.ppermute(x, 'chan', pairs)  42.7 us
    pallas_call x8, Pallas kernels, pick_rows(): pl.pallas_call(pick_kernel, grid_spec=pltpu.PrefetchScalarGridSpec(num_sc...  32.9 us
    ppermute x2, waiting for transfers between devices, swap_far(): return lax.ppermute(x, 'tm', [(a, a ^ 2) for a in range(4)])  31.8 us
    ppermute x15, starting transfers between devices, shift_y(): return lax.ppermute(x, 'chan', pairs)  30.4 us
    transpose x1, local copies, waits for them, and re-layouts, body(): spec = jnp.transpose(spectra, (2, 1, 0, 3)).reshape(BINS, 128, 256)  16.6 us
    ppermute x15, starting transfers between devices, shift_x(): return lax.ppermute(x, 'chan', pairs)  15.7 us
  transfers between devices with their start and end apart: 36, of which 24 were waited for; matrix products, arithmetic and copies ran while one was open for 7% of the time, Pallas kernels for 37%

profile of v1, /device:TPU:1, one launch (start us, length us, event | category | flops | bytes accessed | tf_op | source)
XLA Modules:
  0.0 394.5 jit_solution(7683752980510811475)
XLA Ops:
  3.2 16.6 %copy.19 = bf16[250,2,64,256]{3,2,1,0:T(8,128)(2,1)} copy(bf16[250,2,64,256]{3,1,0,2:T(2,128)(2,1)} %bitcast.28) | data formatting | bytes 32768000 | tf_op jit(solution)/shard_map/transpose | solution.py:149
  20.4 4.1 %pick_rows.9 = bf16[32,128,128]{2,1,0:T(8,128)(2,1)} custom-call(s32[1]{0:T(128)} %bitcast.6.first_ref, bf16[128,256]{1,0:T(8,128)(2,1)} %fusion.1.pick_ref, f32[1,128]{1,0:T(1,128)} %broadcast_in_dim_tile.3.mask_ref, bf16[250,128,256]{2,1,0:T(8,128)(2,1)} %bitcast.18), custom_call_target="tpu_custom_call" | custom-call | flops 268435456 | bytes 3145728 | tf_op jit(solution)/shard_map/pick_rows/pallas_call | solution.py:58
  26.5 4.1 %pick_rows.10 = bf16[32,128,128]{2,1,0:T(8,128)(2,1)} custom-call(s32[1]{0:T(128)} %bitcast.7.first_ref, bf16[128,256]{1,0:T(8,128)(2,1)} %fusion.1.pick_ref, f32[1,128]{1,0:T(1,128)} %broadcast_in_dim_tile.3.mask_ref, bf16[250,128,256]{2,1,0:T(8,128)(2,1)} %bitcast.19), custom_call_target="tpu_custom_call" | custom-call | flops 268435456 | bytes 3145728 | tf_op jit(solution)/shard_map/pick_rows/pallas_call | solution.py:58
  32.0 4.1 %pick_rows.11 = bf16[32,128,128]{2,1,0:T(8,128)(2,1)} custom-call(s32[1]{0:T(128)} %bitcast.8.first_ref, bf16[128,256]{1,0:T(8,128)(2,1)} %fusion.1.pick_ref, f32[1,128]{1,0:T(1,128)} %broadcast_in_dim_tile.3.mask_ref, bf16[250,128,256]{2,1,0:T(8,128)(2,1)} %bitcast.20), custom_call_target="tpu_custom_call" | custom-call | flops 268435456 | bytes 3145728 | tf_op jit(solution)/shard_map/pick_rows/pallas_call | solution.py:58
  37.8 4.1 %pick_rows.13 = bf16[32,128,128]{2,1,0:T(8,128)(2,1)} custom-call(s32[1]{0:T(128)} %bitcast.10.first_ref, bf16[128,256]{1,0:T(8,128)(2,1)} %fusion.1.pick_ref, f32[1,128]{1,0:T(1,128)} %broadcast_in_dim_tile.3.mask_ref, bf16[250,128,256]{2,1,0:T(8,128)(2,1)} %bitcast.21), custom_call_target="tpu_custom_call" | custom-call | flops 268435456 | bytes 3145728 | tf_op jit(solution)/shard_map/pick_rows/pallas_call | solution.py:58
  43.2 4.0 %pick_rows.14 = bf16[32,128,128]{2,1,0:T(8,128)(2,1)} custom-call(s32[1]{0:T(128)} %bitcast.11.first_ref, bf16[128,256]{1,0:T(8,128)(2,1)} %fusion.1.pick_ref, f32[1,128]{1,0:T(1,128)} %broadcast_in_dim_tile.3.mask_ref, bf16[250,128,256]{2,1,0:T(8,128)(2,1)} %bitcast.22), custom_call_target="tpu_custom_call" | custom-call | flops 268435456 | bytes 3145728 | tf_op jit(solution)/shard_map/pick_rows/pallas_call | solution.py:58
  48.8 4.1 %pick_rows.15 = bf16[32,128,128]{2,1,0:T(8,128)(2,1)} custom-call(s32[1]{0:T(128)} %bitcast.12.first_ref, bf16[128,256]{1,0:T(8,128)(2,1)} %fusion.1.pick_ref, f32[1,128]{1,0:T(1,128)} %broadcast_in_dim_tile.3.mask_ref, bf16[250,128,256]{2,1,0:T(8,128)(2,1)} %bitcast.23), custom_call_target="tpu_custom_call" | custom-call | flops 268435456 | bytes 3145728 | tf_op jit(solution)/shard_map/pick_rows/pallas_call | solution.py:58
  54.4 4.1 %pick_rows.8 = bf16[32,128,128]{2,1,0:T(8,128)(2,1)} custom-call(s32[1]{0:T(128)} %bitcast.3.first_ref, bf16[128,256]{1,0:T(8,128)(2,1)} %fusion.1.pick_ref, f32[1,128]{1,0:T(1,128)} %broadcast_in_dim_tile.3.mask_ref, bf16[250,128,256]{2,1,0:T(8,128)(2,1)} %bitcast.24), custom_call_target="tpu_custom_call" | custom-call | flops 268435456 | bytes 3145728 | tf_op jit(solution)/shard_map/pick_rows/pallas_call | solution.py:58
  58.6 15.7 %collective-permute-done.2 = bf16[32,128,128]{2,1,0:T(8,128)(2,1)S(1)} collective-permute-done((bf16[32,128,128]{2,1,0:T(8,128)(2,1)}, bf16[32,128,128]{2,1,0:T(8,128)(2,1)S(1)}, u32[]{:S(2)}, u32[]{:S(2)}) %collective-permute-start.2) | collective-permute-done | bytes 1048608 | tf_op jit(solution)/shard_map/ppermute | solution.py:18
  80.7 4.1 %pick_rows.12 = bf16[32,128,128]{2,1,0:T(8,128)(2,1)} custom-call(s32[1]{0:T(128)} %bitcast.9.first_ref, bf16[128,256]{1,0:T(8,128)(2,1)} %fusion.1.pick_ref, f32[1,128]{1,0:T(1,128)} %broadcast_in_dim_tile.3.mask_ref, bf16[250,128,256]{2,1,0:T(8,128)(2,1)} %bitcast.25), custom_call_target="tpu_custom_call" | custom-call | flops 268435456 | bytes 3145728 | tf_op jit(solution)/shard_map/pick_rows/pallas_call | solution.py:58
  84.8 5.5 %collective-permute-done.15 = bf16[32,128,128]{2,1,0:T(8,128)(2,1)} collective-permute-done((bf16[32,128,128]{2,1,0:T(8,128)(2,1)}, bf16[32,128,128]{2,1,0:T(8,128)(2,1)}, u32[]{:S(2)}, u32[]{:S(2)}) %collective-permute-start.15) | collective-permute-done | bytes 1048608 | tf_op jit(solution)/shard_map/ppermute | solution.py:23
  90.3 2.8 add_add_fusion.3
  93.1 6.6 %collective-permute-done.3 = bf16[8,128,128]{2,1,0:T(8,128)(2,1)S(1)} collective-permute-done((bf16[8,128,128]{2,1,0:T(8,128)(2,1)}, bf16[8,128,128]{2,1,0:T(8,128)(2,1)S(1)}, u32[]{:S(2)}, u32[]{:S(2)}) %collective-permute-start.3) | collective-permute-done | bytes 262176 | tf_op jit(solution)/shard_map/ppermute | solution.py:23
  108.7 4.5 %collective-permute-start.7 = (bf16[8,128,128]{2,1,0:T(8,128)(2,1)S(1)}, bf16[8,128,128]{2,1,0:T(8,128)(2,1)S(1)}, u32[]{:S(2)}, u32[]{:S(2)}) collective-permute-start(bf16[8,128,128]{2,1,0:T(8,128)(2,1)S(1)} %add.664), channel_id=1, source_target_pairs={{0,8},{4,12},{8,16},{12,20},{16,24},{20,28},{24,0},{28,4},{32,40},... | collective-permute-start | bytes 786440 | tf_op jit(solution)/shard_map/ppermute | solution.py:23
  117.5 4.4 %collective-permute-start.8 = (bf16[8,128,128]{2,1,0:T(8,128)(2,1)S(1)}, bf16[8,128,128]{2,1,0:T(8,128)(2,1)S(1)}, u32[]{:S(2)}, u32[]{:S(2)}) collective-permute-start(bf16[8,128,128]{2,1,0:T(8,128)(2,1)S(1)} %add.664), channel_id=1, source_target_pairs={{0,16},{4,20},{8,24},{12,28},{16,0},{20,4},{24,8},{28,12},{32,48},... | collective-permute-start | bytes 786440 | tf_op jit(solution)/shard_map/ppermute | solution.py:23
  122.7 5.1 %collective-permute-start.9 = (bf16[8,128,128]{2,1,0:T(8,128)(2,1)S(1)}, bf16[8,128,128]{2,1,0:T(8,128)(2,1)S(1)}, u32[]{:S(2)}, u32[]{:S(2)}) collective-permute-start(bf16[8,128,128]{2,1,0:T(8,128)(2,1)S(1)} %add.664), channel_id=1, source_target_pairs={{0,24},{4,28},{8,0},{12,4},{16,8},{20,12},{24,16},{28,20},{32,56},... | collective-permute-start | bytes 786440 | tf_op jit(solution)/shard_map/ppermute | solution.py:23
  130.8 7.8 %collective-permute-done.9 = bf16[8,128,128]{2,1,0:T(8,128)(2,1)S(1)} collective-permute-done((bf16[8,128,128]{2,1,0:T(8,128)(2,1)S(1)}, bf16[8,128,128]{2,1,0:T(8,128)(2,1)S(1)}, u32[]{:S(2)}, u32[]{:S(2)}) %collective-permute-start.9) | collective-permute-done | bytes 262176 | tf_op jit(solution)/shard_map/ppermute | solution.py:23
  146.8 6.5 %collective-permute-done.28 = bf16[32,64,128]{2,1,0:T(8,128)(2,1)S(1)} collective-permute-done((bf16[32,64,128]{2,1,0:T(8,128)(2,1)S(1)}, bf16[32,64,128]{2,1,0:T(8,128)(2,1)S(1)}, u32[]{:S(2)}, u32[]{:S(2)}) %collective-permute-start.28) | collective-permute-done | bytes 524320 | tf_op jit(solution)/shard_map/ppermute | solution.py:18
  154.1 8.2 %collective-permute-done.29 = bf16[32,64,128]{2,1,0:T(8,128)(2,1)S(1)} collective-permute-done((bf16[32,64,128]{2,1,0:T(8,128)(2,1)S(1)}, bf16[32,64,128]{2,1,0:T(8,128)(2,1)S(1)}, u32[]{:S(2)}, u32[]{:S(2)}) %collective-permute-start.29) | collective-permute-done | bytes 524320 | tf_op jit(solution)/shard_map/ppermute | solution.py:18
  163.1 5.1 %collective-permute-done.30 = bf16[32,64,128]{2,1,0:T(8,128)(2,1)S(1)} collective-permute-done((bf16[32,64,128]{2,1,0:T(8,128)(2,1)S(1)}, bf16[32,64,128]{2,1,0:T(8,128)(2,1)S(1)}, u32[]{:S(2)}, u32[]{:S(2)}) %collective-permute-start.30) | collective-permute-done | bytes 524320 | tf_op jit(solution)/shard_map/ppermute | solution.py:18
  170.2 5.4 %collective-permute-done.10 = bf16[32,64,128]{2,1,0:T(8,128)(2,1)S(1)} collective-permute-done((bf16[32,64,128]{2,1,0:T(8,128)(2,1)S(1)}, bf16[32,64,128]{2,1,0:T(8,128)(2,1)S(1)}, u32[]{:S(2)}, u32[]{:S(2)}) %collective-permute-start.10) | collective-permute-done | bytes 524320 | tf_op jit(solution)/shard_map/ppermute | solution.py:18
  176.5 8.3 %collective-permute-done.11 = bf16[32,64,128]{2,1,0:T(8,128)(2,1)S(1)} collective-permute-done((bf16[32,64,128]{2,1,0:T(8,128)(2,1)S(1)}, bf16[32,64,128]{2,1,0:T(8,128)(2,1)S(1)}, u32[]{:S(2)}, u32[]{:S(2)}) %collective-permute-start.11) | collective-permute-done | bytes 524320 | tf_op jit(solution)/shard_map/ppermute | solution.py:18
  185.6 4.8 %collective-permute-done.12 = bf16[32,64,128]{2,1,0:T(8,128)(2,1)S(1)} collective-permute-done((bf16[32,64,128]{2,1,0:T(8,128)(2,1)S(1)}, bf16[32,64,128]{2,1,0:T(8,128)(2,1)S(1)}, u32[]{:S(2)}, u32[]{:S(2)}) %collective-permute-start.12) | collective-permute-done | bytes 524320 | tf_op jit(solution)/shard_map/ppermute | solution.py:18
  200.8 4.5 %collective-permute-start.24 = (bf16[32,64,128]{2,1,0:T(8,128)(2,1)S(1)}, bf16[32,64,128]{2,1,0:T(8,128)(2,1)S(1)}, u32[]{:S(2)}, u32[]{:S(2)}) collective-permute-start(bf16[32,64,128]{2,1,0:T(8,128)(2,1)S(1)} %pad_maximum_fusion.2), channel_id=1, source_target_pairs={{0,16},{4,20},{8,24},{12,28},{16,0},{20,4},{24,8},{28,12},{32,48},... | collective-permute-start | bytes 1572872 | tf_op jit(solution)/shard_map/ppermute | solution.py:23
  207.1 7.0 %collective-permute-done.23 = bf16[32,64,128]{2,1,0:T(8,128)(2,1)S(1)} collective-permute-done((bf16[32,64,128]{2,1,0:T(8,128)(2,1)S(1)}, bf16[32,64,128]{2,1,0:T(8,128)(2,1)S(1)}, u32[]{:S(2)}, u32[]{:S(2)}) %collective-permute-start.23) | collective-permute-done | bytes 524320 | tf_op jit(solution)/shard_map/ppermute | solution.py:23
  216.1 10.2 %collective-permute-done.24 = bf16[32,64,128]{2,1,0:T(8,128)(2,1)S(1)} collective-permute-done((bf16[32,64,128]{2,1,0:T(8,128)(2,1)S(1)}, bf16[32,64,128]{2,1,0:T(8,128)(2,1)S(1)}, u32[]{:S(2)}, u32[]{:S(2)}) %collective-permute-start.24) | collective-permute-done | bytes 524320 | tf_op jit(solution)/shard_map/ppermute | solution.py:23
  230.1 57.7 %correlate.2 = (bf16[32,101,256]{2,1,0:T(8,128)(2,1)S(1)}, bf16[32,101,256]{2,1,0:T(8,128)(2,1)S(1)}) custom-call(s32[32]{0:T(128)S(1)} %and_select_fusion.15.blocks_ref, bf16[2,112,256]{2,1,0:T(8,128)(2,1)S(1)} %copy_bitcast_fusion.table_ref, bf16[1,128]{1,0:T(2,128)(2,1)S(1)} %fusion.36.sign_ref, bf16[250,128,256]{2,1,0:T(8,128)(2,1)} %bitcast.26, ...), custom_call_target="tpu_custom_call" | custom-call | flops 20000000000 | bytes 25165824 | tf_op jit(solution)/shard_map/correlate/pallas_call | solution.py:118
  288.2 3.5 collective-permute-start.26
  294.3 57.7 %correlate.3 = (bf16[32,101,256]{2,1,0:T(8,128)(2,1)S(1)}, bf16[32,101,256]{2,1,0:T(8,128)(2,1)S(1)}) custom-call(s32[32]{0:T(128)S(1)} %and_select_fusion.15.blocks_ref, bf16[2,112,256]{2,1,0:T(8,128)(2,1)S(1)} %copy_bitcast_fusion.table_ref, bf16[1,128]{1,0:T(2,128)(2,1)S(1)} %fusion.36.sign_ref, bf16[250,128,256]{2,1,0:T(8,128)(2,1)} %bitcast.27, ...), custom_call_target="tpu_custom_call" | custom-call | flops 20000000000 | bytes 25165824 | tf_op jit(solution)/shard_map/correlate/pallas_call | solution.py:118
  353.2 2.8 collective-permute-start.27
  359.5 14.8 %collective-permute-done.27 = bf16[16,101,256]{2,0,1:T(8,128)(2,1)S(1)} collective-permute-done((bf16[16,101,256]{2,0,1:T(8,128)(2,1)S(1)}, bf16[16,101,256]{2,0,1:T(8,128)(2,1)S(1)}, u32[]{:S(2)}, u32[]{:S(2)}) %collective-permute-start.27) | collective-permute-done | bytes 827424 | tf_op jit(solution)/shard_map/ppermute | solution.py:35
  375.0 17.0 %collective-permute-done.35 = bf16[16,101,256]{2,0,1:T(8,128)(2,1)S(1)} collective-permute-done((bf16[16,101,256]{2,0,1:T(8,128)(2,1)S(1)}, bf16[16,101,256]{2,0,1:T(8,128)(2,1)S(1)}, u32[]{:S(2)}, u32[]{:S(2)}) %collective-permute-start.35) | collective-permute-done | bytes 827424 | tf_op jit(solution)/shard_map/ppermute | solution.py:35
  (112 shorter events, 79.0 us)
Async XLA Ops:
  24.5 28.5 %collective-permute-start = (bf16[32,128,128]{2,1,0:T(8,128)(2,1)}, bf16[32,128,128]{2,1,0:T(8,128)(2,1)S(1)}, u32[]{:S(2)}, u32[]{:S(2)}) collective-permute-start(bf16[32,128,128]{2,1,0:T(8,128)(2,1)} %pick_rows.9), channel_id=1, source_target_pairs={{0,32},{4,36},{8,40},{12,44},{16,48},{20,52},{24,56},{28,60},{32,6... | collective-permute-start | bytes 3145736 | tf_op jit(solution)/shard_map/ppermute | solution.py:18
  30.7 27.9 %collective-permute-start.1 = (bf16[32,128,128]{2,1,0:T(8,128)(2,1)}, bf16[32,128,128]{2,1,0:T(8,128)(2,1)S(1)}, u32[]{:S(2)}, u32[]{:S(2)}) collective-permute-start(bf16[32,128,128]{2,1,0:T(8,128)(2,1)} %pick_rows.10), channel_id=1, source_target_pairs={{0,96},{4,100},{8,104},{12,108},{16,112},{20,116},{24,120},{28,124... | collective-permute-start | bytes 3145736 | tf_op jit(solution)/shard_map/ppermute | solution.py:18
  36.1 38.2 %collective-permute-start.2 = (bf16[32,128,128]{2,1,0:T(8,128)(2,1)}, bf16[32,128,128]{2,1,0:T(8,128)(2,1)S(1)}, u32[]{:S(2)}, u32[]{:S(2)}) collective-permute-start(bf16[32,128,128]{2,1,0:T(8,128)(2,1)} %pick_rows.11), channel_id=1, source_target_pairs={{0,64},{4,68},{8,72},{12,76},{16,80},{20,84},{24,88},{28,92},{32,9... | collective-permute-start | bytes 3145736 | tf_op jit(solution)/shard_map/ppermute | solution.py:18
  41.9 37.1 %collective-permute-start.13 = (bf16[32,128,128]{2,1,0:T(8,128)(2,1)}, bf16[32,128,128]{2,1,0:T(8,128)(2,1)}, u32[]{:S(2)}, u32[]{:S(2)}) collective-permute-start(bf16[32,128,128]{2,1,0:T(8,128)(2,1)} %pick_rows.13), channel_id=1, source_target_pairs={{0,8},{4,12},{8,16},{12,20},{16,24},{20,28},{24,0},{28,4},{32,40},... | collective-permute-start | bytes 3145736 | tf_op jit(solution)/shard_map/ppermute | solution.py:23
  47.2 37.6 %collective-permute-start.14 = (bf16[32,128,128]{2,1,0:T(8,128)(2,1)}, bf16[32,128,128]{2,1,0:T(8,128)(2,1)}, u32[]{:S(2)}, u32[]{:S(2)}) collective-permute-start(bf16[32,128,128]{2,1,0:T(8,128)(2,1)} %pick_rows.14), channel_id=1, source_target_pairs={{0,24},{4,28},{8,0},{12,4},{16,8},{20,12},{24,16},{28,20},{32,56},... | collective-permute-start | bytes 3145736 | tf_op jit(solution)/shard_map/ppermute | solution.py:23
  53.0 37.4 %collective-permute-start.15 = (bf16[32,128,128]{2,1,0:T(8,128)(2,1)}, bf16[32,128,128]{2,1,0:T(8,128)(2,1)}, u32[]{:S(2)}, u32[]{:S(2)}) collective-permute-start(bf16[32,128,128]{2,1,0:T(8,128)(2,1)} %pick_rows.15), channel_id=1, source_target_pairs={{0,16},{4,20},{8,24},{12,28},{16,0},{20,4},{24,8},{28,12},{32,48},... | collective-permute-start | bytes 3145736 | tf_op jit(solution)/shard_map/ppermute | solution.py:23
  76.4 23.3 %collective-permute-start.3 = (bf16[8,128,128]{2,1,0:T(8,128)(2,1)}, bf16[8,128,128]{2,1,0:T(8,128)(2,1)S(1)}, u32[]{:S(2)}, u32[]{:S(2)}) collective-permute-start(bf16[8,128,128]{2,1,0:T(8,128)(2,1)} %get-tuple-element.16), channel_id=1, source_target_pairs={{0,8},{4,12},{8,16},{12,20},{16,24},{20,28},{24,0},{28,4},{32,40},... | collective-permute-start | bytes 786440 | tf_op jit(solution)/shard_map/ppermute | solution.py:23
  77.6 24.3 %collective-permute-start.4 = (bf16[8,128,128]{2,1,0:T(8,128)(2,1)}, bf16[8,128,128]{2,1,0:T(8,128)(2,1)}, u32[]{:S(2)}, u32[]{:S(2)}) collective-permute-start(bf16[8,128,128]{2,1,0:T(8,128)(2,1)} %get-tuple-element.18), channel_id=1, source_target_pairs={{0,24},{4,28},{8,0},{12,4},{16,8},{20,12},{24,16},{28,20},{32,56},... | collective-permute-start | bytes 786440 | tf_op jit(solution)/shard_map/ppermute | solution.py:23
  79.1 22.8 %collective-permute-start.5 = (bf16[8,128,128]{2,1,0:T(8,128)(2,1)}, bf16[8,128,128]{2,1,0:T(8,128)(2,1)}, u32[]{:S(2)}, u32[]{:S(2)}) collective-permute-start(bf16[8,128,128]{2,1,0:T(8,128)(2,1)} %get-tuple-element.17), channel_id=1, source_target_pairs={{0,16},{4,20},{8,24},{12,28},{16,0},{20,4},{24,8},{28,12},{32,48},... | collective-permute-start | bytes 786440 | tf_op jit(solution)/shard_map/ppermute | solution.py:23
  105.2 8.8 %collective-permute-start.17 = (bf16[8,128,128]{2,1,0:T(8,128)(2,1)}, bf16[8,128,128]{2,1,0:T(8,128)(2,1)S(1)}, u32[]{:S(2)}, u32[]{:S(2)}) collective-permute-start(bf16[8,128,128]{2,1,0:T(8,128)(2,1)} %get-tuple-element.15), channel_id=1, source_target_pairs={{0,96},{4,100},{8,104},{12,108},{16,112},{20,116},{24,120},{28,124... | collective-permute-start | bytes 786440 | tf_op jit(solution)/shard_map/ppermute | solution.py:18
  108.7 19.1 %collective-permute-start.7 = (bf16[8,128,128]{2,1,0:T(8,128)(2,1)S(1)}, bf16[8,128,128]{2,1,0:T(8,128)(2,1)S(1)}, u32[]{:S(2)}, u32[]{:S(2)}) collective-permute-start(bf16[8,128,128]{2,1,0:T(8,128)(2,1)S(1)} %add.664), channel_id=1, source_target_pairs={{0,8},{4,12},{8,16},{12,20},{16,24},{20,28},{24,0},{28,4},{32,40},... | collective-permute-start | bytes 786440 | tf_op jit(solution)/shard_map/ppermute | solution.py:23
  117.0 27.6 %collective-permute-start.19 = (bf16[8,128,128]{2,1,0:T(8,128)(2,1)S(1)}, bf16[8,128,128]{2,1,0:T(8,128)(2,1)S(1)}, u32[]{:S(2)}, u32[]{:S(2)}) collective-permute-start(bf16[8,128,128]{2,1,0:T(8,128)(2,1)S(1)} %add_add_fusion), channel_id=1, source_target_pairs={{0,4},{4,0},{8,12},{12,8},{16,20},{20,16},{24,28},{28,24},{32,36},... | collective-permute-start | bytes 786440 | tf_op jit(solution)/shard_map/ppermute | solution.py:27
  117.5 12.4 %collective-permute-start.8 = (bf16[8,128,128]{2,1,0:T(8,128)(2,1)S(1)}, bf16[8,128,128]{2,1,0:T(8,128)(2,1)S(1)}, u32[]{:S(2)}, u32[]{:S(2)}) collective-permute-start(bf16[8,128,128]{2,1,0:T(8,128)(2,1)S(1)} %add.664), channel_id=1, source_target_pairs={{0,16},{4,20},{8,24},{12,28},{16,0},{20,4},{24,8},{28,12},{32,48},... | collective-permute-start | bytes 786440 | tf_op jit(solution)/shard_map/ppermute | solution.py:23
  122.7 15.8 %collective-permute-start.9 = (bf16[8,128,128]{2,1,0:T(8,128)(2,1)S(1)}, bf16[8,128,128]{2,1,0:T(8,128)(2,1)S(1)}, u32[]{:S(2)}, u32[]{:S(2)}) collective-permute-start(bf16[8,128,128]{2,1,0:T(8,128)(2,1)S(1)} %add.664), channel_id=1, source_target_pairs={{0,24},{4,28},{8,0},{12,4},{16,8},{20,12},{24,16},{28,20},{32,56},... | collective-permute-start | bytes 786440 | tf_op jit(solution)/shard_map/ppermute | solution.py:23
  139.4 13.8 %collective-permute-start.28 = (bf16[32,64,128]{2,1,0:T(8,128)(2,1)S(1)}, bf16[32,64,128]{2,1,0:T(8,128)(2,1)S(1)}, u32[]{:S(2)}, u32[]{:S(2)}) collective-permute-start(bf16[32,64,128]{2,1,0:T(8,128)(2,1)S(1)} %pad_maximum_fusion.3), channel_id=1, source_target_pairs={{0,32},{4,36},{8,40},{12,44},{16,48},{20,52},{24,56},{28,60},{32,6... | collective-permute-start | bytes 1572872 | tf_op jit(solution)/shard_map/ppermute | solution.py:18
  141.7 20.5 %collective-permute-start.29 = (bf16[32,64,128]{2,1,0:T(8,128)(2,1)S(1)}, bf16[32,64,128]{2,1,0:T(8,128)(2,1)S(1)}, u32[]{:S(2)}, u32[]{:S(2)}) collective-permute-start(bf16[32,64,128]{2,1,0:T(8,128)(2,1)S(1)} %pad_maximum_fusion.3), channel_id=1, source_target_pairs={{0,64},{4,68},{8,72},{12,76},{16,80},{20,84},{24,88},{28,92},{32,9... | collective-permute-start | bytes 1572872 | tf_op jit(solution)/shard_map/ppermute | solution.py:18
  142.4 25.7 %collective-permute-start.30 = (bf16[32,64,128]{2,1,0:T(8,128)(2,1)S(1)}, bf16[32,64,128]{2,1,0:T(8,128)(2,1)S(1)}, u32[]{:S(2)}, u32[]{:S(2)}) collective-permute-start(bf16[32,64,128]{2,1,0:T(8,128)(2,1)S(1)} %pad_maximum_fusion.3), channel_id=1, source_target_pairs={{0,96},{4,100},{8,104},{12,108},{16,112},{20,116},{24,120},{28,124... | collective-permute-start | bytes 1572872 | tf_op jit(solution)/shard_map/ppermute | solution.py:18
  144.5 31.1 %collective-permute-start.10 = (bf16[32,64,128]{2,1,0:T(8,128)(2,1)S(1)}, bf16[32,64,128]{2,1,0:T(8,128)(2,1)S(1)}, u32[]{:S(2)}, u32[]{:S(2)}) collective-permute-start(bf16[32,64,128]{2,1,0:T(8,128)(2,1)S(1)} %pad_maximum_fusion.1), channel_id=1, source_target_pairs={{0,32},{4,36},{8,40},{12,44},{16,48},{20,52},{24,56},{28,60},{32,6... | collective-permute-start | bytes 1572872 | tf_op jit(solution)/shard_map/ppermute | solution.py:18
  144.6 40.1 %collective-permute-start.11 = (bf16[32,64,128]{2,1,0:T(8,128)(2,1)S(1)}, bf16[32,64,128]{2,1,0:T(8,128)(2,1)S(1)}, u32[]{:S(2)}, u32[]{:S(2)}) collective-permute-start(bf16[32,64,128]{2,1,0:T(8,128)(2,1)S(1)} %pad_maximum_fusion.1), channel_id=1, source_target_pairs={{0,64},{4,68},{8,72},{12,76},{16,80},{20,84},{24,88},{28,92},{32,9... | collective-permute-start | bytes 1572872 | tf_op jit(solution)/shard_map/ppermute | solution.py:18
  153.2 37.2 %collective-permute-start.12 = (bf16[32,64,128]{2,1,0:T(8,128)(2,1)S(1)}, bf16[32,64,128]{2,1,0:T(8,128)(2,1)S(1)}, u32[]{:S(2)}, u32[]{:S(2)}) collective-permute-start(bf16[32,64,128]{2,1,0:T(8,128)(2,1)S(1)} %pad_maximum_fusion.1), channel_id=1, source_target_pairs={{0,96},{4,100},{8,104},{12,108},{16,112},{20,116},{24,120},{28,124... | collective-permute-start | bytes 1572872 | tf_op jit(solution)/shard_map/ppermute | solution.py:18
  162.2 30.2 %collective-permute-start.20 = (bf16[8,128,128]{2,1,0:T(8,128)(2,1)S(1)}, bf16[8,128,128]{2,1,0:T(8,128)(2,1)S(1)}, u32[]{:S(2)}, u32[]{:S(2)}) collective-permute-start(bf16[8,128,128]{2,1,0:T(8,128)(2,1)S(1)} %add.684), channel_id=1, source_target_pairs={{0,32},{4,36},{8,40},{12,44},{16,48},{20,52},{24,56},{28,60},{32,6... | collective-permute-start | bytes 786440 | tf_op jit(solution)/shard_map/ppermute | solution.py:18
  168.2 27.7 %collective-permute-start.21 = (bf16[8,128,128]{2,1,0:T(8,128)(2,1)S(1)}, bf16[8,128,128]{2,1,0:T(8,128)(2,1)S(1)}, u32[]{:S(2)}, u32[]{:S(2)}) collective-permute-start(bf16[8,128,128]{2,1,0:T(8,128)(2,1)S(1)} %add.684), channel_id=1, source_target_pairs={{0,64},{4,68},{8,72},{12,76},{16,80},{20,84},{24,88},{28,92},{32,9... | collective-permute-start | bytes 786440 | tf_op jit(solution)/shard_map/ppermute | solution.py:18
  175.6 23.8 %collective-permute-start.22 = (bf16[8,128,128]{2,1,0:T(8,128)(2,1)S(1)}, bf16[8,128,128]{2,1,0:T(8,128)(2,1)S(1)}, u32[]{:S(2)}, u32[]{:S(2)}) collective-permute-start(bf16[8,128,128]{2,1,0:T(8,128)(2,1)S(1)} %add.684), channel_id=1, source_target_pairs={{0,96},{4,100},{8,104},{12,108},{16,112},{20,116},{24,120},{28,124... | collective-permute-start | bytes 786440 | tf_op jit(solution)/shard_map/ppermute | solution.py:18
  200.3 13.8 %collective-permute-start.23 = (bf16[32,64,128]{2,1,0:T(8,128)(2,1)S(1)}, bf16[32,64,128]{2,1,0:T(8,128)(2,1)S(1)}, u32[]{:S(2)}, u32[]{:S(2)}) collective-permute-start(bf16[32,64,128]{2,1,0:T(8,128)(2,1)S(1)} %pad_maximum_fusion.2), channel_id=1, source_target_pairs={{0,8},{4,12},{8,16},{12,20},{16,24},{20,28},{24,0},{28,4},{32,40},... | collective-permute-start | bytes 1572872 | tf_op jit(solution)/shard_map/ppermute | solution.py:23
  200.8 25.4 %collective-permute-start.24 = (bf16[32,64,128]{2,1,0:T(8,128)(2,1)S(1)}, bf16[32,64,128]{2,1,0:T(8,128)(2,1)S(1)}, u32[]{:S(2)}, u32[]{:S(2)}) collective-permute-start(bf16[32,64,128]{2,1,0:T(8,128)(2,1)S(1)} %pad_maximum_fusion.2), channel_id=1, source_target_pairs={{0,16},{4,20},{8,24},{12,28},{16,0},{20,4},{24,8},{28,12},{32,48},... | collective-permute-start | bytes 1572872 | tf_op jit(solution)/shard_map/ppermute | solution.py:23
  205.4 24.0 %collective-permute-start.25 = (bf16[32,64,128]{2,1,0:T(8,128)(2,1)S(1)}, bf16[32,64,128]{2,1,0:T(8,128)(2,1)S(1)}, u32[]{:S(2)}, u32[]{:S(2)}) collective-permute-start(bf16[32,64,128]{2,1,0:T(8,128)(2,1)S(1)} %pad_maximum_fusion.2), channel_id=1, source_target_pairs={{0,24},{4,28},{8,0},{12,4},{16,8},{20,12},{24,16},{28,20},{32,56},... | collective-permute-start | bytes 1572872 | tf_op jit(solution)/shard_map/ppermute | solution.py:23
  205.5 86.3 %collective-permute-start.31 = (bf16[32,64,128]{2,1,0:T(8,128)(2,1)S(1)}, bf16[32,64,128]{2,1,0:T(8,128)(2,1)S(1)}, u32[]{:S(2)}, u32[]{:S(2)}) collective-permute-start(bf16[32,64,128]{2,1,0:T(8,128)(2,1)S(1)} %pad_maximum_fusion.4), channel_id=1, source_target_pairs={{0,8},{4,12},{8,16},{12,20},{16,24},{20,28},{24,0},{28,4},{32,40},... | collective-permute-start | bytes 1572872 | tf_op jit(solution)/shard_map/ppermute | solution.py:23
  207.0 85.6 %collective-permute-start.32 = (bf16[32,64,128]{2,1,0:T(8,128)(2,1)S(1)}, bf16[32,64,128]{2,1,0:T(8,128)(2,1)S(1)}, u32[]{:S(2)}, u32[]{:S(2)}) collective-permute-start(bf16[32,64,128]{2,1,0:T(8,128)(2,1)S(1)} %pad_maximum_fusion.4), channel_id=1, source_target_pairs={{0,16},{4,20},{8,24},{12,28},{16,0},{20,4},{24,8},{28,12},{32,48},... | collective-permute-start | bytes 1572872 | tf_op jit(solution)/shard_map/ppermute | solution.py:23
  214.1 79.3 %collective-permute-start.33 = (bf16[32,64,128]{2,1,0:T(8,128)(2,1)S(1)}, bf16[32,64,128]{2,1,0:T(8,128)(2,1)S(1)}, u32[]{:S(2)}, u32[]{:S(2)}) collective-permute-start(bf16[32,64,128]{2,1,0:T(8,128)(2,1)S(1)} %pad_maximum_fusion.4), channel_id=1, source_target_pairs={{0,24},{4,28},{8,0},{12,4},{16,8},{20,12},{24,16},{28,20},{32,56},... | collective-permute-start | bytes 1572872 | tf_op jit(solution)/shard_map/ppermute | solution.py:23
  288.2 64.3 %collective-permute-start.26 = (bf16[32,101,256]{2,0,1:T(8,128)(2,1)S(1)}, bf16[32,101,256]{2,0,1:T(8,128)(2,1)S(1)}, u32[]{:S(2)}, u32[]{:S(2)}) collective-permute-start(bf16[32,101,256]{2,0,1:T(8,128)(2,1)S(1)} %copy.20), channel_id=1, source_target_pairs={{0,1},{1,0},{2,3},{3,2},{4,5},{5,4},{6,7},{7,6},{8,9},{9,8},{10,11... | collective-permute-start | bytes 4964360 | tf_op jit(solution)/shard_map/ppermute | solution.py:31
  353.2 21.1 %collective-permute-start.27 = (bf16[16,101,256]{2,0,1:T(8,128)(2,1)S(1)}, bf16[16,101,256]{2,0,1:T(8,128)(2,1)S(1)}, u32[]{:S(2)}, u32[]{:S(2)}) collective-permute-start(bf16[16,101,256]{2,0,1:T(8,128)(2,1)S(1)} %copy.23), channel_id=1, source_target_pairs={{0,2},{1,3},{2,0},{3,1},{4,6},{5,7},{6,4},{7,5},{8,10},{9,11},{10,... | collective-permute-start | bytes 2482184 | tf_op jit(solution)/shard_map/ppermute | solution.py:35
  356.8 35.3 %collective-permute-start.35 = (bf16[16,101,256]{2,0,1:T(8,128)(2,1)S(1)}, bf16[16,101,256]{2,0,1:T(8,128)(2,1)S(1)}, u32[]{:S(2)}, u32[]{:S(2)}) collective-permute-start(bf16[16,101,256]{2,0,1:T(8,128)(2,1)S(1)} %copy.28), channel_id=1, source_target_pairs={{0,2},{1,3},{2,0},{3,1},{4,6},{5,7},{6,4},{7,5},{8,10},{9,11},{10,... | collective-permute-start | bytes 2482184 | tf_op jit(solution)/shard_map/ppermute | solution.py:35
  (6 other events, 44.4 us)

commit v2 on v1

v2 whole, which is shorter than its diff:
```python
import jax
import jax.numpy as jnp
from jax import lax
from jax.experimental import pallas as pl
from jax.experimental.pallas import tpu as pltpu
from jax.sharding import PartitionSpec as P

LAGS = 101
SRC_BLK = 64
BINS = 250
CHUNKS = 2
ROWS = 128 // CHUNKS
LAG_PAD = 112
STRIDE = 264


def shift_x(x, step):
    pairs = [((a * 4 + b) * 2 + c, (((a + step) % 4) * 4 + b) * 2 + c) for a in range(4) for b in range(4) for c in range(2)]
    return lax.ppermute(x, "chan", pairs)


def shift_y(x, step):
    pairs = [((a * 4 + b) * 2 + c, (a * 4 + (b + step) % 4) * 2 + c) for a in range(4) for b in range(4) for c in range(2)]
    return lax.ppermute(x, "chan", pairs)


def swap_z(x):
    return lax.ppermute(x, "chan", [(a, a ^ 1) for a in range(32)])


def swap_core(x):
    return lax.ppermute(x, "tm", [(a, a ^ 1) for a in range(4)])


def swap_far(x):
    return lax.ppermute(x, "tm", [(a, a ^ 2) for a in range(4)])


def lag_table(freqs, lag_count, segment_total):
    lag_steps = jnp.arange(lag_count, dtype=jnp.int32) - (LAGS - 1) // 2
    phase_int = lag_steps[:, None] * (freqs + 1)[None, :] % (2 * BINS)
    phase = phase_int.astype(jnp.float32) * (2.0 * jnp.pi / (2.0 * BINS))
    scale = 1.0 / jnp.sqrt(jnp.float32(segment_total * BINS))
    both = jnp.stack([jnp.cos(phase) * scale, -jnp.sin(phase) * scale])
    return jnp.where((freqs < BINS)[None, None, :], both, 0.0).astype(jnp.bfloat16)


def pick_kernel(first_ref, pick_ref, mask_ref, spec_a_ref, spec_b_ref, out_a_ref, out_b_ref):
    step = pl.program_id(0)
    for half, (spec_ref, out_ref) in enumerate(((spec_a_ref, out_a_ref), (spec_b_ref, out_b_ref))):
        for w in range(16):
            rows = lax.dot_general(
                pick_ref[...], spec_ref[w], (((1,), (1,)), ((), ())), preferred_element_type=jnp.float32
            )
            kept = jnp.where((first_ref[half] + step) * 16 + w < BINS, rows * mask_ref[...], 0.0)
            out_ref[w] = kept.astype(jnp.bfloat16)


def pick_rows(first, pick, mask, spec):
    part = jax.ShapeDtypeStruct((32, 128, 128), jnp.bfloat16)
    return pl.pallas_call(
        pick_kernel,
        grid_spec=pltpu.PrefetchScalarGridSpec(
            num_scalar_prefetch=1,
            grid=(2,),
            in_specs=[
                pl.BlockSpec((128, 256), lambda i, s: (0, 0)),
                pl.BlockSpec((1, 128), lambda i, s: (0, 0)),
                pl.BlockSpec((16, 128, 256), lambda i, s: (s[0] + i, 0, 0)),
                pl.BlockSpec((16, 128, 256), lambda i, s: (s[1] + i, 0, 0)),
            ],
            out_specs=[pl.BlockSpec((16, 128, 128), lambda i, s: (i, 0, 0))] * 2,
        ),
        out_shape=[part, part],
        compiler_params=pltpu.CompilerParams(vmem_limit_bytes=50 << 20),
        cost_estimate=pl.CostEstimate(flops=4 * 32 * 128 * 128 * 256, bytes_accessed=6 << 20, transcendentals=0),
        name="pick_rows",
    )(first, pick, mask, spec, spec)


def assemble_kernel(at_ref, *refs):
    for e in range(4):
        place = pl.ds(8 * lax.rem(at_ref[0] + 4 - e, 4), 8)
        for c in range(CHUNKS):
            refs[4 + c][place] = refs[e][:, c * ROWS : (c + 1) * ROWS]


def assemble(at, pieces):
    piece = pl.BlockSpec((8, 128, 128), lambda i, s: (0, 0, 0))
    return pl.pallas_call(
        assemble_kernel,
        grid_spec=pltpu.PrefetchScalarGridSpec(
            num_scalar_prefetch=1,
            grid=(1,),
            in_specs=[piece] * 4,
            out_specs=[pl.BlockSpec((32, ROWS, 128), lambda i, s: (0, 0, 0))] * CHUNKS,
        ),
        out_shape=[jax.ShapeDtypeStruct((32, ROWS, 128), jnp.bfloat16)] * CHUNKS,
        compiler_params=pltpu.CompilerParams(vmem_limit_bytes=8 << 20),
        cost_estimate=pl.CostEstimate(flops=0, bytes_accessed=2 << 20, transcendentals=0),
        name="assemble",
    )(at, *pieces)


def correlate_kernel(blocks_ref, table_ref, sign_ref, spec_ref, *refs):
    sources, (send_ref, keep_ref, src, left, right, acc) = refs[:8], refs[8:]
    step = pl.program_id(0)
    for m in range(8):

        @pl.when(step == m)
        def _():
            src[...] = sources[m][...]

    base = lax.rem(step, 4) * 32
    last = BINS - 1 - 32 * blocks_ref[step]
    sign = sign_ref[...]

    @pl.loop(0, 2)
    def _(group):
        for w in range(16):
            i = group * 16 + w
            rows = src[i]
            turned = jnp.concatenate([rows[:, 64:], rows[:, :64]], axis=1) * sign
            both = jnp.concatenate([rows, turned], axis=0)
            cross = jnp.dot(both, spec_ref[jnp.minimum(i, last)], preferred_element_type=jnp.float32)
            for part in range(2):
                place = pl.ds(part * 128 + base + i, ROWS, stride=STRIDE)
                piece = cross[part * ROWS : (part + 1) * ROWS]
                left[place, :] = piece[:, :128]
                right[place, :] = piece[:, 128:]

    def lags(k):
        rows = pl.ds(pl.multiple_of(k * STRIDE, 8), 256)
        cross = jnp.concatenate(
            [left[rows, :].astype(jnp.bfloat16), right[rows, :].astype(jnp.bfloat16)], axis=1
        )
        return jnp.dot(table_ref[0], cross, preferred_element_type=jnp.float32)

    @pl.when(step == 3)
    def _():
        @pl.loop(0, ROWS, step=8)
        def _(first):
            for u in range(8):
                acc[first + u] = lags(first + u)

    @pl.when(step == 7)
    def _():
        @pl.loop(0, ROWS // 2, step=8)
        def _(first):
            for u in range(8):
                k = first + u
                send_ref[k] = (acc[k] + lags(k))[:LAGS].astype(jnp.bfloat16)

        @pl.loop(0, ROWS // 2, step=8)
        def _(first):
            for u in range(8):
                k = first + u + ROWS // 2
                keep_ref[first + u] = (acc[k] + lags(k))[:LAGS].astype(jnp.bfloat16)


def correlate(blocks, table, sign, spec, sources):
    half = jax.ShapeDtypeStruct((ROWS // 2, LAGS, 256), jnp.bfloat16)
    whole = pl.BlockSpec((ROWS // 2, LAGS, 256), lambda i, s: (0, 0, 0))
    return pl.pallas_call(
        correlate_kernel,
        grid_spec=pltpu.PrefetchScalarGridSpec(
            num_scalar_prefetch=1,
            grid=(8,),
            in_specs=[
                pl.BlockSpec((1, LAG_PAD, 256), lambda i, s: (i // 4, 0, 0)),
                pl.BlockSpec((1, 128), lambda i, s: (0, 0)),
                pl.BlockSpec((32, 128, 256), lambda i, s: (s[i], 0, 0)),
            ]
            + [pl.BlockSpec((32, ROWS, 128), lambda i, s: (0, 0, 0))] * 8,
            out_specs=[whole, whole],
            scratch_shapes=[
                pltpu.VMEM((32, ROWS, 128), jnp.bfloat16),
                pltpu.VMEM((ROWS * STRIDE, 128), jnp.float32),
                pltpu.VMEM((ROWS * STRIDE, 128), jnp.float32),
                pltpu.VMEM((ROWS, LAG_PAD, 256), jnp.float32),
            ],
        ),
        out_shape=[half, half],
        compiler_params=pltpu.CompilerParams(vmem_limit_bytes=50 << 20),
        cost_estimate=pl.CostEstimate(flops=20 * 10**9, bytes_accessed=24 << 20, transcendentals=0),
        name="correlate",
    )(blocks, table, sign, spec, *sources)


def body(spectra, src_blocks, valid):
    chan_index = lax.axis_index("chan")
    tm_index = lax.axis_index("tm")
    x, y = chan_index // 8, chan_index // 2 % 4
    core, far = tm_index % 2, tm_index // 2

    spec = jnp.transpose(spectra, (2, 1, 0, 3)).reshape(BINS, 128, 256)

    q = jnp.arange(128, dtype=jnp.int32)
    part, group, within = q // ROWS, q % ROWS // (ROWS // 4), q % (ROWS // 4)
    dest_core = jnp.where(group < 2, 1 - core, core)
    dest_far = jnp.where(group % 2 == 0, 1 - far, far)
    row = 32 * (2 * dest_far + dest_core) + (ROWS // 4) * part + within
    block = jnp.where(row < SRC_BLK, src_blocks[0], src_blocks[1])
    channel = block * SRC_BLK + row % SRC_BLK - chan_index * 256
    pick = (channel[:, None] == jnp.arange(256, dtype=jnp.int32)[None, :]).astype(jnp.bfloat16)
    mask = jnp.tile(valid.astype(jnp.float32), 2)[None, :]
    sign = jnp.where(jnp.arange(128) < 64, -1.0, 1.0).astype(jnp.bfloat16)[None, :]

    own = {d: pick_rows(jnp.stack([2 * ((x + d) % 4), 8 + 2 * ((y + d) % 4)]), pick, mask, spec) for d in (1, 3, 2, 0)}
    quarters_a = [own[0][0]] + [shift_x(own[d][0], d) for d in (1, 3, 2)]
    quarters_b = [own[0][1]] + [shift_y(own[d][1], d) for d in (1, 3, 2)]

    def scatter(quarters, at, shift):
        def piece(d):
            cut = [lax.dynamic_slice_in_dim(a, 8 * ((at + d) % 4), 8, 0) for a in quarters]
            return (cut[0] + cut[1]) + (cut[2] + cut[3])

        got = [shift(piece(d), d) for d in (1, 3, 2)]
        return (piece(0) + got[0]) + (got[1] + got[2])

    piece_a = scatter(quarters_a, y, shift_y)
    piece_b = scatter(quarters_b, x, shift_x)
    piece_a = piece_a + swap_z(piece_a)
    piece_b = piece_b + swap_z(piece_b)

    def gather(a, shift):
        got = {d: shift(a, d) for d in (1, 3, 2)}
        return [a, got[1], got[2], got[3]]

    inner_a = assemble(y[None], gather(piece_a, shift_y))
    inner_b = assemble(x[None], gather(piece_b, shift_x))

    i = jnp.arange(256, dtype=jnp.int32)
    e = i % 128 // 32
    blocks_at = jnp.where(i < 128, (x - e) % 4, 4 + (y - e) % 4)
    table = lag_table(32 * blocks_at + i % 32, LAG_PAD, 256)
    table = table.reshape(2, LAG_PAD, 2, 128).transpose(2, 1, 0, 3).reshape(2, LAG_PAD, 256)
    blocks = blocks_at[::32]

    outs, waiting = [], None
    quarter = ROWS // 4
    arrived = gather(inner_a[0], shift_x) + gather(inner_b[0], shift_y)
    for c in range(CHUNKS):
        following = None
        if c + 1 < CHUNKS:
            following = gather(inner_a[c + 1], shift_x) + gather(inner_b[c + 1], shift_y)
        if waiting is not None:
            last = swap_far(waiting[0])
        send, keep = correlate(blocks, table, sign, spec, arrived)
        if waiting is not None:
            outs.append(finish(waiting, last))
        arrived = following
        near = swap_core(send)
        onward = (keep[:quarter].astype(jnp.float32) + near[:quarter].astype(jnp.float32)).astype(jnp.bfloat16)
        waiting = (onward, keep[quarter:], near[quarter:])
    outs.append(finish(waiting, swap_far(onward)))
    return jnp.concatenate(outs)


def finish(waiting, last):
    own = waiting[1].astype(jnp.float32) + waiting[2].astype(jnp.float32)
    return (own + last.astype(jnp.float32)).astype(jnp.bfloat16)


def solution(mesh):
    placed = (P("tm", None, None, "chan"), P(), P("tm"))
    return jax.shard_map(
        body, mesh=mesh, in_specs=placed, out_specs=P("tm", None, "chan"), check_vma=False
    )
```

time: 396 us -> 297 us (0.75)
  Pallas kernels: 148 us -> 55.4 us
  local copies, waits for them, and re-layouts: 38.2 us -> 25.8 us
  waiting for transfers between devices: 138 us -> 150 us
  starting transfers between devices: 57.4 us -> 49.9 us
    pallas_call x2, Pallas kernels: 115 us -> 39.3 us  [correlate(): pl.pallas_call(correlate_kernel, grid_spec=pltpu.PrefetchScalarGridSpec(n...]
    ppermute x15, waiting for transfers between devices: 42.7 us -> 65 us  [shift_y(): return lax.ppermute(x, 'chan', pairs)]
    pallas_call x8 -> x4, Pallas kernels: 32.9 us -> 15.9 us  [pick_rows(): pl.pallas_call(pick_kernel, grid_spec=pltpu.PrefetchScalarGridSpec(num_sc...]
    ppermute x15, waiting for transfers between devices: 62.2 us -> 52 us  [shift_x(): return lax.ppermute(x, 'chan', pairs)]
    ppermute x15, starting transfers between devices: 30.4 us -> 21.8 us  [shift_y(): return lax.ppermute(x, 'chan', pairs)]
    slice x9 -> x1, local copies, waits for them, and re-layouts: 6.74 us -> 0.09 us  [body(): blocks = blocks_at[::32]]
    unnamed x14 -> x10, local copies, waits for them, and re-layouts: 8.4 us -> 2.01 us
    ppermute x15, starting transfers between devices: 15.7 us -> 21.3 us  [shift_x(): return lax.ppermute(x, 'chan', pairs)]
  transfers between devices with their start and end apart: 36 -> 36, of which waited for: 24 -> 15; matrix products, arithmetic and copies ran while one was open for 7% -> 5% of each run, Pallas kernels for 37% -> 18%
where the time goes in v2:
time: 297 us; the launch traced here: 294 us
  waiting for transfers between devices  150 us (51%)
  Pallas kernels  55.4 us (19%)
  starting transfers between devices  49.9 us (17%)
  local copies, waits for them, and re-layouts  25.8 us (9%)
  other arithmetic  12.4 us (4%)
    ppermute x15, waiting for transfers between devices, shift_y(): return lax.ppermute(x, 'chan', pairs)  65 us
    ppermute x15, waiting for transfers between devices, shift_x(): return lax.ppermute(x, 'chan', pairs)  52 us
    pallas_call x2, Pallas kernels, correlate(): pl.pallas_call(correlate_kernel, grid_spec=pltpu.PrefetchScalarGridSpec(n...  39.3 us
    ppermute x2, waiting for transfers between devices, swap_far(): return lax.ppermute(x, 'tm', [(a, a ^ 2) for a in range(4)])  33.4 us
    ppermute x15, starting transfers between devices, shift_y(): return lax.ppermute(x, 'chan', pairs)  21.8 us
    ppermute x15, starting transfers between devices, shift_x(): return lax.ppermute(x, 'chan', pairs)  21.3 us
    transpose x1, local copies, waits for them, and re-layouts, body(): spec = jnp.transpose(spectra, (2, 1, 0, 3)).reshape(BINS, 128, 256)  16.6 us
    pallas_call x4, Pallas kernels, pick_rows(): pl.pallas_call(pick_kernel, grid_spec=pltpu.PrefetchScalarGridSpec(num_sc...  15.9 us
  transfers between devices with their start and end apart: 36, of which 15 were waited for; matrix products, arithmetic and copies ran while one was open for 5% of the time, Pallas kernels for 18%

profile of v2, /device:TPU:1, one launch (start us, length us, event | category | flops | bytes accessed | tf_op | source)
XLA Modules:
  0.0 294.2 jit_solution(608599280247081482)
XLA Ops:
  2.7 16.6 %copy.19 = bf16[250,2,64,256]{3,2,1,0:T(8,128)(2,1)} copy(bf16[250,2,64,256]{3,1,0,2:T(2,128)(2,1)} %bitcast.30) | data formatting | bytes 32768000 | tf_op jit(solution)/shard_map/transpose | solution.py:196
  19.4 3.6 %pick_rows.6 = (bf16[32,128,128]{2,1,0:T(8,128)(2,1)S(1)}, bf16[32,128,128]{2,1,0:T(8,128)(2,1)S(1)}) custom-call(s32[2]{0:T(128)S(1)} %get-tuple-element.53.first_ref, bf16[128,256]{1,0:T(8,128)(2,1)S(1)} %fusion.1.pick_ref, f32[1,128]{1,0:T(1,128)S(1)} %broadcast_in_dim_tile.3.mask_ref, bf16[250,128,256]{2,1,0:T(8,128)(2,1)} %bitcast.20, ...), custom_call_target="tpu_custom_call" | custom-call | flops 536870912 | bytes 6291456 | tf_op jit(solution)/shard_map/pick_rows/pallas_call | solution.py:61
  23.0 3.6 %collective-permute-start.14 = (bf16[32,128,128]{2,1,0:T(8,128)(2,1)S(1)}, bf16[32,128,128]{2,1,0:T(8,128)(2,1)}, u32[]{:S(2)}, u32[]{:S(2)}) collective-permute-start(bf16[32,128,128]{2,1,0:T(8,128)(2,1)S(1)} %get-tuple-element.28), channel_id=1, source_target_pairs={{0,24},{4,28},{8,0},{12,4},{16,8},{20,12},{24,16},{28,20},{32,56},... | collective-permute-start | bytes 3145736 | tf_op jit(solution)/shard_map/ppermute | solution.py:24
  26.7 4.4 %pick_rows.5 = (bf16[32,128,128]{2,1,0:T(8,128)(2,1)}, bf16[32,128,128]{2,1,0:T(8,128)(2,1)}) custom-call(s32[2]{0:T(128)S(1)} %get-tuple-element.52.first_ref, bf16[128,256]{1,0:T(8,128)(2,1)S(1)} %fusion.1.pick_ref, f32[1,128]{1,0:T(1,128)S(1)} %broadcast_in_dim_tile.3.mask_ref, bf16[250,128,256]{2,1,0:T(8,128)(2,1)} %bitcast.22, ...), custom_call_target="tpu_custom_call" | custom-call | flops 536870912 | bytes 6291456 | tf_op jit(solution)/shard_map/pick_rows/pallas_call | solution.py:61
  31.1 4.4 %pick_rows.7 = (bf16[32,128,128]{2,1,0:T(8,128)(2,1)}, bf16[32,128,128]{2,1,0:T(8,128)(2,1)}) custom-call(s32[2]{0:T(128)S(1)} %get-tuple-element.54.first_ref, bf16[128,256]{1,0:T(8,128)(2,1)S(1)} %fusion.1.pick_ref, f32[1,128]{1,0:T(1,128)S(1)} %broadcast_in_dim_tile.3.mask_ref, bf16[250,128,256]{2,1,0:T(8,128)(2,1)} %bitcast.24, ...), custom_call_target="tpu_custom_call" | custom-call | flops 536870912 | bytes 6291456 | tf_op jit(solution)/shard_map/pick_rows/pallas_call | solution.py:61
  37.1 2.5 collective-permute-start.1
  39.6 31.2 %collective-permute-done.14 = bf16[32,128,128]{2,1,0:T(8,128)(2,1)} collective-permute-done((bf16[32,128,128]{2,1,0:T(8,128)(2,1)S(1)}, bf16[32,128,128]{2,1,0:T(8,128)(2,1)}, u32[]{:S(2)}, u32[]{:S(2)}) %collective-permute-start.14) | collective-permute-done | bytes 1048608 | tf_op jit(solution)/shard_map/ppermute | solution.py:24
  70.8 3.6 %pick_rows.4 = (bf16[32,128,128]{2,1,0:T(8,128)(2,1)S(1)}, bf16[32,128,128]{2,1,0:T(8,128)(2,1)S(1)}) custom-call(s32[2]{0:T(128)S(1)} %get-tuple-element.51.first_ref, bf16[128,256]{1,0:T(8,128)(2,1)S(1)} %fusion.1.pick_ref, f32[1,128]{1,0:T(1,128)S(1)} %broadcast_in_dim_tile.3.mask_ref, bf16[250,128,256]{2,1,0:T(8,128)(2,1)} %bitcast.26, ...), custom_call_target="tpu_custom_call" | custom-call | flops 536870912 | bytes 6291456 | tf_op jit(solution)/shard_map/pick_rows/pallas_call | solution.py:61
  74.4 3.5 %collective-permute-done.15 = bf16[32,128,128]{2,1,0:T(8,128)(2,1)} collective-permute-done((bf16[32,128,128]{2,1,0:T(8,128)(2,1)}, bf16[32,128,128]{2,1,0:T(8,128)(2,1)}, u32[]{:S(2)}, u32[]{:S(2)}) %collective-permute-start.15) | collective-permute-done | bytes 1048608 | tf_op jit(solution)/shard_map/ppermute | solution.py:24
  77.9 2.4 add_add_fusion.3
  83.0 20.3 %collective-permute-done.16 = bf16[8,128,128]{2,1,0:T(8,128)(2,1)} collective-permute-done((bf16[8,128,128]{2,1,0:T(8,128)(2,1)S(1)}, bf16[8,128,128]{2,1,0:T(8,128)(2,1)}, u32[]{:S(2)}, u32[]{:S(2)}) %collective-permute-start.16) | collective-permute-done | bytes 262176 | tf_op jit(solution)/shard_map/ppermute | solution.py:19
  103.3 9.0 %collective-permute-done.18 = bf16[8,128,128]{2,1,0:T(8,128)(2,1)} collective-permute-done((bf16[8,128,128]{2,1,0:T(8,128)(2,1)S(1)}, bf16[8,128,128]{2,1,0:T(8,128)(2,1)}, u32[]{:S(2)}, u32[]{:S(2)}) %collective-permute-start.18) | collective-permute-done | bytes 262176 | tf_op jit(solution)/shard_map/ppermute | solution.py:19
  115.7 5.3 %collective-permute-start.4 = (bf16[8,128,128]{2,1,0:T(8,128)(2,1)S(1)}, bf16[8,128,128]{2,1,0:T(8,128)(2,1)S(1)}, u32[]{:S(2)}, u32[]{:S(2)}) collective-permute-start(bf16[8,128,128]{2,1,0:T(8,128)(2,1)S(1)} %get-tuple-element.42), channel_id=1, source_target_pairs={{0,24},{4,28},{8,0},{12,4},{16,8},{20,12},{24,16},{28,20},{32,56},... | collective-permute-start | bytes 786440 | tf_op jit(solution)/shard_map/ppermute | solution.py:24
  123.2 2.8 collective-permute-start.21
  126.1 2.0 collective-permute-start.22
  128.0 2.9 collective-permute-done.4
  134.0 2.1 collective-permute-done.21.refs_2_
  137.2 3.1 %collective-permute-start.24 = (bf16[32,64,128]{2,1,0:T(8,128)(2,1)S(1)}, bf16[32,64,128]{2,1,0:T(8,128)(2,1)S(1)}, u32[]{:S(2)}, u32[]{:S(2)}) collective-permute-start(bf16[32,64,128]{2,1,0:T(8,128)(2,1)S(1)} %get-tuple-element.30.refs_4_), channel_id=1, source_target_pairs={{0,16},{4,20},{8,24},{12,28},{16,0},{20,4},{24,8},{28,12},{32,48},... | collective-permute-start | bytes 1572872 | tf_op jit(solution)/shard_map/ppermute | solution.py:24
  140.5 2.0 collective-permute-start.8
  143.4 20.6 %collective-permute-done.7.refs_1_ = bf16[8,128,128]{2,1,0:T(8,128)(2,1)S(1)} collective-permute-done((bf16[8,128,128]{2,1,0:T(8,128)(2,1)S(1)}, bf16[8,128,128]{2,1,0:T(8,128)(2,1)S(1)}, u32[]{:S(2)}, u32[]{:S(2)}) %collective-permute-start.7) | collective-permute-done | bytes 262176 | tf_op jit(solution)/shard_map/ppermute | solution.py:24
  164.0 2.6 collective-permute-start.25
  166.6 5.3 %collective-permute-done.8.refs_2_ = bf16[8,128,128]{2,1,0:T(8,128)(2,1)S(1)} collective-permute-done((bf16[8,128,128]{2,1,0:T(8,128)(2,1)S(1)}, bf16[8,128,128]{2,1,0:T(8,128)(2,1)S(1)}, u32[]{:S(2)}, u32[]{:S(2)}) %collective-permute-start.8) | collective-permute-done | bytes 262176 | tf_op jit(solution)/shard_map/ppermute | solution.py:24
  172.0 4.0 %collective-permute-start.10 = (bf16[32,64,128]{2,1,0:T(8,128)(2,1)S(1)}, bf16[32,64,128]{2,1,0:T(8,128)(2,1)S(1)}, u32[]{:S(2)}, u32[]{:S(2)}) collective-permute-start(bf16[32,64,128]{2,1,0:T(8,128)(2,1)S(1)} %get-tuple-element.25.refs_0_), channel_id=1, source_target_pairs={{0,32},{4,36},{8,40},{12,44},{16,48},{20,52},{24,56},{28,60},{32,6... | collective-permute-start | bytes 1572872 | tf_op jit(solution)/shard_map/ppermute | solution.py:19
  176.0 2.0 collective-permute-start.11
  180.1 6.4 %collective-permute-done.10.refs_1_ = bf16[32,64,128]{2,1,0:T(8,128)(2,1)S(1)} collective-permute-done((bf16[32,64,128]{2,1,0:T(8,128)(2,1)S(1)}, bf16[32,64,128]{2,1,0:T(8,128)(2,1)S(1)}, u32[]{:S(2)}, u32[]{:S(2)}) %collective-permute-start.10) | collective-permute-done | bytes 524320 | tf_op jit(solution)/shard_map/ppermute | solution.py:19
  186.6 12.1 %collective-permute-done.11.refs_2_ = bf16[32,64,128]{2,1,0:T(8,128)(2,1)S(1)} collective-permute-done((bf16[32,64,128]{2,1,0:T(8,128)(2,1)S(1)}, bf16[32,64,128]{2,1,0:T(8,128)(2,1)S(1)}, u32[]{:S(2)}, u32[]{:S(2)}) %collective-permute-start.11) | collective-permute-done | bytes 524320 | tf_op jit(solution)/shard_map/ppermute | solution.py:19
  202.0 2.8 collective-permute-start.30
  204.8 19.6 %correlate.2 = (bf16[32,101,256]{2,1,0:T(8,128)(2,1)}, bf16[32,101,256]{2,1,0:T(8,128)(2,1)}) custom-call(s32[8]{0:T(128)S(1)} %slice.33.blocks_ref, bf16[2,112,256]{2,1,0:T(8,128)(2,1)S(1)} %copy_bitcast_fusion.table_ref, bf16[1,128]{1,0:T(2,128)(2,1)S(1)} %fusion.17.sign_ref, bf16[250,128,256]{2,1,0:T(8,128)(2,1)} %bitcast.28, ...), custom_call_target="tpu_custom_call" | custom-call | flops 20000000000 | bytes 25165824 | tf_op jit(solution)/shard_map/correlate/pallas_call | solution.py:164
  228.7 19.7 %correlate.3 = (bf16[32,101,256]{2,1,0:T(8,128)(2,1)}, bf16[32,101,256]{2,1,0:T(8,128)(2,1)}) custom-call(s32[8]{0:T(128)S(1)} %slice.33.blocks_ref, bf16[2,112,256]{2,1,0:T(8,128)(2,1)S(1)} %copy_bitcast_fusion.table_ref, bf16[1,128]{1,0:T(2,128)(2,1)S(1)} %fusion.17.sign_ref, bf16[250,128,256]{2,1,0:T(8,128)(2,1)} %bitcast.29, ...), custom_call_target="tpu_custom_call" | custom-call | flops 20000000000 | bytes 25165824 | tf_op jit(solution)/shard_map/correlate/pallas_call | solution.py:164
  252.3 3.1 %collective-permute-start.27 = (bf16[16,101,256]{2,0,1:T(8,128)(2,1)S(1)}, bf16[16,101,256]{2,0,1:T(8,128)(2,1)S(1)}, u32[]{:S(2)}, u32[]{:S(2)}) collective-permute-start(bf16[16,101,256]{2,0,1:T(8,128)(2,1)S(1)} %copy.23), channel_id=1, source_target_pairs={{0,2},{1,3},{2,0},{3,1},{4,6},{5,7},{6,4},{7,5},{8,10},{9,11},{10,... | collective-permute-start | bytes 2482184 | tf_op jit(solution)/shard_map/ppermute | solution.py:36
  257.7 16.3 %collective-permute-done.27 = bf16[16,101,256]{2,0,1:T(8,128)(2,1)S(1)} collective-permute-done((bf16[16,101,256]{2,0,1:T(8,128)(2,1)S(1)}, bf16[16,101,256]{2,0,1:T(8,128)(2,1)S(1)}, u32[]{:S(2)}, u32[]{:S(2)}) %collective-permute-start.27) | collective-permute-done | bytes 827424 | tf_op jit(solution)/shard_map/ppermute | solution.py:36
  274.7 17.1 %collective-permute-done.35 = bf16[16,101,256]{2,0,1:T(8,128)(2,1)S(1)} collective-permute-done((bf16[16,101,256]{2,0,1:T(8,128)(2,1)S(1)}, bf16[16,101,256]{2,0,1:T(8,128)(2,1)S(1)}, u32[]{:S(2)}, u32[]{:S(2)}) %collective-permute-start.35) | collective-permute-done | bytes 827424 | tf_op jit(solution)/shard_map/ppermute | solution.py:36
  (93 shorter events, 37.0 us)
Async XLA Ops:
  23.0 47.8 %collective-permute-start.14 = (bf16[32,128,128]{2,1,0:T(8,128)(2,1)S(1)}, bf16[32,128,128]{2,1,0:T(8,128)(2,1)}, u32[]{:S(2)}, u32[]{:S(2)}) collective-permute-start(bf16[32,128,128]{2,1,0:T(8,128)(2,1)S(1)} %get-tuple-element.28), channel_id=1, source_target_pairs={{0,24},{4,28},{8,0},{12,4},{16,8},{20,12},{24,16},{28,20},{32,56},... | collective-permute-start | bytes 3145736 | tf_op jit(solution)/shard_map/ppermute | solution.py:24
  31.1 43.3 %collective-permute-start.13 = (bf16[32,128,128]{2,1,0:T(8,128)(2,1)}, bf16[32,128,128]{2,1,0:T(8,128)(2,1)}, u32[]{:S(2)}, u32[]{:S(2)}) collective-permute-start(bf16[32,128,128]{2,1,0:T(8,128)(2,1)} %get-tuple-element.27), channel_id=1, source_target_pairs={{0,8},{4,12},{8,16},{12,20},{16,24},{20,28},{24,0},{28,4},{32,40},... | collective-permute-start | bytes 3145736 | tf_op jit(solution)/shard_map/ppermute | solution.py:24
  35.5 42.4 %collective-permute-start.15 = (bf16[32,128,128]{2,1,0:T(8,128)(2,1)}, bf16[32,128,128]{2,1,0:T(8,128)(2,1)}, u32[]{:S(2)}, u32[]{:S(2)}) collective-permute-start(bf16[32,128,128]{2,1,0:T(8,128)(2,1)} %get-tuple-element.29), channel_id=1, source_target_pairs={{0,16},{4,20},{8,24},{12,28},{16,0},{20,4},{24,8},{28,12},{32,48},... | collective-permute-start | bytes 3145736 | tf_op jit(solution)/shard_map/ppermute | solution.py:24
  37.1 76.7 %collective-permute-start.1 = (bf16[32,128,128]{2,1,0:T(8,128)(2,1)S(1)}, bf16[32,128,128]{2,1,0:T(8,128)(2,1)}, u32[]{:S(2)}, u32[]{:S(2)}) collective-permute-start(bf16[32,128,128]{2,1,0:T(8,128)(2,1)S(1)} %get-tuple-element.23), channel_id=1, source_target_pairs={{0,96},{4,100},{8,104},{12,108},{16,112},{20,116},{24,120},{28,124... | collective-permute-start | bytes 3145736 | tf_op jit(solution)/shard_map/ppermute | solution.py:19
  39.6 74.2 %collective-permute-start = (bf16[32,128,128]{2,1,0:T(8,128)(2,1)}, bf16[32,128,128]{2,1,0:T(8,128)(2,1)}, u32[]{:S(2)}, u32[]{:S(2)}) collective-permute-start(bf16[32,128,128]{2,1,0:T(8,128)(2,1)} %get-tuple-element.22), channel_id=1, source_target_pairs={{0,32},{4,36},{8,40},{12,44},{16,48},{20,52},{24,56},{28,60},{32,6... | collective-permute-start | bytes 3145736 | tf_op jit(solution)/shard_map/ppermute | solution.py:19
  70.8 43.1 %collective-permute-start.2 = (bf16[32,128,128]{2,1,0:T(8,128)(2,1)}, bf16[32,128,128]{2,1,0:T(8,128)(2,1)}, u32[]{:S(2)}, u32[]{:S(2)}) collective-permute-start(bf16[32,128,128]{2,1,0:T(8,128)(2,1)} %get-tuple-element.24), channel_id=1, source_target_pairs={{0,64},{4,68},{8,72},{12,76},{16,80},{20,84},{24,88},{28,92},{32,9... | collective-permute-start | bytes 3145736 | tf_op jit(solution)/shard_map/ppermute | solution.py:19
  80.3 23.0 %collective-permute-start.16 = (bf16[8,128,128]{2,1,0:T(8,128)(2,1)S(1)}, bf16[8,128,128]{2,1,0:T(8,128)(2,1)}, u32[]{:S(2)}, u32[]{:S(2)}) collective-permute-start(bf16[8,128,128]{2,1,0:T(8,128)(2,1)S(1)} %get-tuple-element.37), channel_id=1, source_target_pairs={{0,32},{4,36},{8,40},{12,44},{16,48},{20,52},{24,56},{28,60},{32,6... | collective-permute-start | bytes 786440 | tf_op jit(solution)/shard_map/ppermute | solution.py:19
  81.5 21.8 %collective-permute-start.17 = (bf16[8,128,128]{2,1,0:T(8,128)(2,1)}, bf16[8,128,128]{2,1,0:T(8,128)(2,1)}, u32[]{:S(2)}, u32[]{:S(2)}) collective-permute-start(bf16[8,128,128]{2,1,0:T(8,128)(2,1)} %get-tuple-element.39), channel_id=1, source_target_pairs={{0,96},{4,100},{8,104},{12,108},{16,112},{20,116},{24,120},{28,124... | collective-permute-start | bytes 786440 | tf_op jit(solution)/shard_map/ppermute | solution.py:19
  115.6 10.5 %collective-permute-start.3 = (bf16[8,128,128]{2,1,0:T(8,128)(2,1)S(1)}, bf16[8,128,128]{2,1,0:T(8,128)(2,1)S(1)}, u32[]{:S(2)}, u32[]{:S(2)}) collective-permute-start(bf16[8,128,128]{2,1,0:T(8,128)(2,1)S(1)} %get-tuple-element.40), channel_id=1, source_target_pairs={{0,8},{4,12},{8,16},{12,20},{16,24},{20,28},{24,0},{28,4},{32,40},... | collective-permute-start | bytes 786440 | tf_op jit(solution)/shard_map/ppermute | solution.py:24
  115.7 15.2 %collective-permute-start.4 = (bf16[8,128,128]{2,1,0:T(8,128)(2,1)S(1)}, bf16[8,128,128]{2,1,0:T(8,128)(2,1)S(1)}, u32[]{:S(2)}, u32[]{:S(2)}) collective-permute-start(bf16[8,128,128]{2,1,0:T(8,128)(2,1)S(1)} %get-tuple-element.42), channel_id=1, source_target_pairs={{0,24},{4,28},{8,0},{12,4},{16,8},{20,12},{24,16},{28,20},{32,56},... | collective-permute-start | bytes 786440 | tf_op jit(solution)/shard_map/ppermute | solution.py:24
  121.0 11.4 %collective-permute-start.5 = (bf16[8,128,128]{2,1,0:T(8,128)(2,1)S(1)}, bf16[8,128,128]{2,1,0:T(8,128)(2,1)S(1)}, u32[]{:S(2)}, u32[]{:S(2)}) collective-permute-start(bf16[8,128,128]{2,1,0:T(8,128)(2,1)S(1)} %get-tuple-element.41), channel_id=1, source_target_pairs={{0,16},{4,20},{8,24},{12,28},{16,0},{20,4},{24,8},{28,12},{32,48},... | collective-permute-start | bytes 786440 | tf_op jit(solution)/shard_map/ppermute | solution.py:24
  123.1 10.8 %collective-permute-start.20 = (bf16[8,128,128]{2,1,0:T(8,128)(2,1)S(1)}, bf16[8,128,128]{2,1,0:T(8,128)(2,1)S(1)}, u32[]{:S(2)}, u32[]{:S(2)}) collective-permute-start(bf16[8,128,128]{2,1,0:T(8,128)(2,1)S(1)} %add.575.refs_0_), channel_id=1, source_target_pairs={{0,32},{4,36},{8,40},{12,44},{16,48},{20,52},{24,56},{28,60},{32,6... | collective-permute-start | bytes 786440 | tf_op jit(solution)/shard_map/ppermute | solution.py:19
  123.2 12.8 %collective-permute-start.21 = (bf16[8,128,128]{2,1,0:T(8,128)(2,1)S(1)}, bf16[8,128,128]{2,1,0:T(8,128)(2,1)S(1)}, u32[]{:S(2)}, u32[]{:S(2)}) collective-permute-start(bf16[8,128,128]{2,1,0:T(8,128)(2,1)S(1)} %add.575.refs_0_), channel_id=1, source_target_pairs={{0,64},{4,68},{8,72},{12,76},{16,80},{20,84},{24,88},{28,92},{32,9... | collective-permute-start | bytes 786440 | tf_op jit(solution)/shard_map/ppermute | solution.py:19
  126.1 10.6 %collective-permute-start.22 = (bf16[8,128,128]{2,1,0:T(8,128)(2,1)S(1)}, bf16[8,128,128]{2,1,0:T(8,128)(2,1)S(1)}, u32[]{:S(2)}, u32[]{:S(2)}) collective-permute-start(bf16[8,128,128]{2,1,0:T(8,128)(2,1)S(1)} %add.575.refs_0_), channel_id=1, source_target_pairs={{0,96},{4,100},{8,104},{12,108},{16,112},{20,116},{24,120},{28,124... | collective-permute-start | bytes 786440 | tf_op jit(solution)/shard_map/ppermute | solution.py:19
  136.7 41.3 %collective-permute-start.23 = (bf16[32,64,128]{2,1,0:T(8,128)(2,1)S(1)}, bf16[32,64,128]{2,1,0:T(8,128)(2,1)S(1)}, u32[]{:S(2)}, u32[]{:S(2)}) collective-permute-start(bf16[32,64,128]{2,1,0:T(8,128)(2,1)S(1)} %get-tuple-element.30.refs_4_), channel_id=1, source_target_pairs={{0,8},{4,12},{8,16},{12,20},{16,24},{20,28},{24,0},{28,4},{32,40},... | collective-permute-start | bytes 1572872 | tf_op jit(solution)/shard_map/ppermute | solution.py:24
  137.2 41.3 %collective-permute-start.24 = (bf16[32,64,128]{2,1,0:T(8,128)(2,1)S(1)}, bf16[32,64,128]{2,1,0:T(8,128)(2,1)S(1)}, u32[]{:S(2)}, u32[]{:S(2)}) collective-permute-start(bf16[32,64,128]{2,1,0:T(8,128)(2,1)S(1)} %get-tuple-element.30.refs_4_), channel_id=1, source_target_pairs={{0,16},{4,20},{8,24},{12,28},{16,0},{20,4},{24,8},{28,12},{32,48},... | collective-permute-start | bytes 1572872 | tf_op jit(solution)/shard_map/ppermute | solution.py:24
  140.5 23.5 %collective-permute-start.7 = (bf16[8,128,128]{2,1,0:T(8,128)(2,1)S(1)}, bf16[8,128,128]{2,1,0:T(8,128)(2,1)S(1)}, u32[]{:S(2)}, u32[]{:S(2)}) collective-permute-start(bf16[8,128,128]{2,1,0:T(8,128)(2,1)S(1)} %add.555.refs_0_), channel_id=1, source_target_pairs={{0,8},{4,12},{8,16},{12,20},{16,24},{20,28},{24,0},{28,4},{32,40},... | collective-permute-start | bytes 786440 | tf_op jit(solution)/shard_map/ppermute | solution.py:24
  140.5 31.4 %collective-permute-start.8 = (bf16[8,128,128]{2,1,0:T(8,128)(2,1)S(1)}, bf16[8,128,128]{2,1,0:T(8,128)(2,1)S(1)}, u32[]{:S(2)}, u32[]{:S(2)}) collective-permute-start(bf16[8,128,128]{2,1,0:T(8,128)(2,1)S(1)} %add.555.refs_0_), channel_id=1, source_target_pairs={{0,16},{4,20},{8,24},{12,28},{16,0},{20,4},{24,8},{28,12},{32,48},... | collective-permute-start | bytes 786440 | tf_op jit(solution)/shard_map/ppermute | solution.py:24
  142.5 29.4 %collective-permute-start.9 = (bf16[8,128,128]{2,1,0:T(8,128)(2,1)S(1)}, bf16[8,128,128]{2,1,0:T(8,128)(2,1)S(1)}, u32[]{:S(2)}, u32[]{:S(2)}) collective-permute-start(bf16[8,128,128]{2,1,0:T(8,128)(2,1)S(1)} %add.555.refs_0_), channel_id=1, source_target_pairs={{0,24},{4,28},{8,0},{12,4},{16,8},{20,12},{24,16},{28,20},{32,56},... | collective-permute-start | bytes 786440 | tf_op jit(solution)/shard_map/ppermute | solution.py:24
  164.0 15.2 %collective-permute-start.25 = (bf16[32,64,128]{2,1,0:T(8,128)(2,1)S(1)}, bf16[32,64,128]{2,1,0:T(8,128)(2,1)S(1)}, u32[]{:S(2)}, u32[]{:S(2)}) collective-permute-start(bf16[32,64,128]{2,1,0:T(8,128)(2,1)S(1)} %get-tuple-element.30.refs_4_), channel_id=1, source_target_pairs={{0,24},{4,28},{8,0},{12,4},{16,8},{20,12},{24,16},{28,20},{32,56},... | collective-permute-start | bytes 1572872 | tf_op jit(solution)/shard_map/ppermute | solution.py:24
  172.0 14.5 %collective-permute-start.10 = (bf16[32,64,128]{2,1,0:T(8,128)(2,1)S(1)}, bf16[32,64,128]{2,1,0:T(8,128)(2,1)S(1)}, u32[]{:S(2)}, u32[]{:S(2)}) collective-permute-start(bf16[32,64,128]{2,1,0:T(8,128)(2,1)S(1)} %get-tuple-element.25.refs_0_), channel_id=1, source_target_pairs={{0,32},{4,36},{8,40},{12,44},{16,48},{20,52},{24,56},{28,60},{32,6... | collective-permute-start | bytes 1572872 | tf_op jit(solution)/shard_map/ppermute | solution.py:19
  176.0 22.7 %collective-permute-start.11 = (bf16[32,64,128]{2,1,0:T(8,128)(2,1)S(1)}, bf16[32,64,128]{2,1,0:T(8,128)(2,1)S(1)}, u32[]{:S(2)}, u32[]{:S(2)}) collective-permute-start(bf16[32,64,128]{2,1,0:T(8,128)(2,1)S(1)} %get-tuple-element.25.refs_0_), channel_id=1, source_target_pairs={{0,64},{4,68},{8,72},{12,76},{16,80},{20,84},{24,88},{28,92},{32,9... | collective-permute-start | bytes 1572872 | tf_op jit(solution)/shard_map/ppermute | solution.py:19
  178.0 22.1 %collective-permute-start.12 = (bf16[32,64,128]{2,1,0:T(8,128)(2,1)S(1)}, bf16[32,64,128]{2,1,0:T(8,128)(2,1)S(1)}, u32[]{:S(2)}, u32[]{:S(2)}) collective-permute-start(bf16[32,64,128]{2,1,0:T(8,128)(2,1)S(1)} %get-tuple-element.25.refs_0_), channel_id=1, source_target_pairs={{0,96},{4,100},{8,104},{12,108},{16,112},{20,116},{24,120},{28,124... | collective-permute-start | bytes 1572872 | tf_op jit(solution)/shard_map/ppermute | solution.py:19
  178.5 23.5 %collective-permute-start.31 = (bf16[32,64,128]{2,1,0:T(8,128)(2,1)S(1)}, bf16[32,64,128]{2,1,0:T(8,128)(2,1)S(1)}, u32[]{:S(2)}, u32[]{:S(2)}) collective-permute-start(bf16[32,64,128]{2,1,0:T(8,128)(2,1)S(1)} %get-tuple-element.34.refs_4_), channel_id=1, source_target_pairs={{0,8},{4,12},{8,16},{12,20},{16,24},{20,28},{24,0},{28,4},{32,40},... | collective-permute-start | bytes 1572872 | tf_op jit(solution)/shard_map/ppermute | solution.py:24
  179.1 47.2 %collective-permute-start.32 = (bf16[32,64,128]{2,1,0:T(8,128)(2,1)S(1)}, bf16[32,64,128]{2,1,0:T(8,128)(2,1)S(1)}, u32[]{:S(2)}, u32[]{:S(2)}) collective-permute-start(bf16[32,64,128]{2,1,0:T(8,128)(2,1)S(1)} %get-tuple-element.34.refs_4_), channel_id=1, source_target_pairs={{0,16},{4,20},{8,24},{12,28},{16,0},{20,4},{24,8},{28,12},{32,48},... | collective-permute-start | bytes 1572872 | tf_op jit(solution)/shard_map/ppermute | solution.py:24
  186.5 41.4 %collective-permute-start.33 = (bf16[32,64,128]{2,1,0:T(8,128)(2,1)S(1)}, bf16[32,64,128]{2,1,0:T(8,128)(2,1)S(1)}, u32[]{:S(2)}, u32[]{:S(2)}) collective-permute-start(bf16[32,64,128]{2,1,0:T(8,128)(2,1)S(1)} %get-tuple-element.34.refs_4_), channel_id=1, source_target_pairs={{0,24},{4,28},{8,0},{12,4},{16,8},{20,12},{24,16},{28,20},{32,56},... | collective-permute-start | bytes 1572872 | tf_op jit(solution)/shard_map/ppermute | solution.py:24
  198.7 29.2 %collective-permute-start.28 = (bf16[32,64,128]{2,1,0:T(8,128)(2,1)S(1)}, bf16[32,64,128]{2,1,0:T(8,128)(2,1)S(1)}, u32[]{:S(2)}, u32[]{:S(2)}) collective-permute-start(bf16[32,64,128]{2,1,0:T(8,128)(2,1)S(1)} %get-tuple-element.33.refs_0_), channel_id=1, source_target_pairs={{0,32},{4,36},{8,40},{12,44},{16,48},{20,52},{24,56},{28,60},{32,6... | collective-permute-start | bytes 1572872 | tf_op jit(solution)/shard_map/ppermute | solution.py:19
  200.1 27.9 %collective-permute-start.29 = (bf16[32,64,128]{2,1,0:T(8,128)(2,1)S(1)}, bf16[32,64,128]{2,1,0:T(8,128)(2,1)S(1)}, u32[]{:S(2)}, u32[]{:S(2)}) collective-permute-start(bf16[32,64,128]{2,1,0:T(8,128)(2,1)S(1)} %get-tuple-element.33.refs_0_), channel_id=1, source_target_pairs={{0,64},{4,68},{8,72},{12,76},{16,80},{20,84},{24,88},{28,92},{32,9... | collective-permute-start | bytes 1572872 | tf_op jit(solution)/shard_map/ppermute | solution.py:19
  202.0 25.9 %collective-permute-start.30 = (bf16[32,64,128]{2,1,0:T(8,128)(2,1)S(1)}, bf16[32,64,128]{2,1,0:T(8,128)(2,1)S(1)}, u32[]{:S(2)}, u32[]{:S(2)}) collective-permute-start(bf16[32,64,128]{2,1,0:T(8,128)(2,1)S(1)} %get-tuple-element.33.refs_0_), channel_id=1, source_target_pairs={{0,96},{4,100},{8,104},{12,108},{16,112},{20,116},{24,120},{28,124... | collective-permute-start | bytes 1572872 | tf_op jit(solution)/shard_map/ppermute | solution.py:19
  226.3 24.1 %collective-permute-start.26 = (bf16[32,101,256]{2,0,1:T(8,128)(2,1)S(1)}, bf16[32,101,256]{2,0,1:T(8,128)(2,1)S(1)}, u32[]{:S(2)}, u32[]{:S(2)}) collective-permute-start(bf16[32,101,256]{2,0,1:T(8,128)(2,1)S(1)} %copy.20), channel_id=1, source_target_pairs={{0,1},{1,0},{2,3},{3,2},{4,5},{5,4},{6,7},{7,6},{8,9},{9,8},{10,11... | collective-permute-start | bytes 4964360 | tf_op jit(solution)/shard_map/ppermute | solution.py:32
  252.3 21.7 %collective-permute-start.27 = (bf16[16,101,256]{2,0,1:T(8,128)(2,1)S(1)}, bf16[16,101,256]{2,0,1:T(8,128)(2,1)S(1)}, u32[]{:S(2)}, u32[]{:S(2)}) collective-permute-start(bf16[16,101,256]{2,0,1:T(8,128)(2,1)S(1)} %copy.23), channel_id=1, source_target_pairs={{0,2},{1,3},{2,0},{3,1},{4,6},{5,7},{6,4},{7,5},{8,10},{9,11},{10,... | collective-permute-start | bytes 2482184 | tf_op jit(solution)/shard_map/ppermute | solution.py:36
  256.1 35.6 %collective-permute-start.35 = (bf16[16,101,256]{2,0,1:T(8,128)(2,1)S(1)}, bf16[16,101,256]{2,0,1:T(8,128)(2,1)S(1)}, u32[]{:S(2)}, u32[]{:S(2)}) collective-permute-start(bf16[16,101,256]{2,0,1:T(8,128)(2,1)S(1)} %copy.28), channel_id=1, source_target_pairs={{0,2},{1,3},{2,0},{3,1},{4,6},{5,7},{6,4},{7,5},{8,10},{9,11},{10,... | collective-permute-start | bytes 2482184 | tf_op jit(solution)/shard_map/ppermute | solution.py:36
  (9 other events, 77.0 us)

commit v3 on v2

--- a/solution.py
+++ b/solution.py
@@ -9,8 +9,12 @@
 SRC_BLK = 64
 BINS = 250
 CHUNKS = 2
-ROWS = 128 // CHUNKS
+PARTS = 4
+WIDE = 128 // CHUNKS
+ROWS = 128 // PARTS
 LAG_PAD = 112
+LAG = 2
+SMALL = pl.CostEstimate(flops=1 << 20, bytes_accessed=1 << 16, transcendentals=0)
 STRIDE = 264
 
 
@@ -73,7 +77,7 @@
         ),
         out_shape=[part, part],
         compiler_params=pltpu.CompilerParams(vmem_limit_bytes=50 << 20),
-        cost_estimate=pl.CostEstimate(flops=4 * 32 * 128 * 128 * 256, bytes_accessed=6 << 20, transcendentals=0),
+        cost_estimate=SMALL,
         name="pick_rows",
     )(first, pick, mask, spec, spec)
 
@@ -82,7 +86,7 @@
     for e in range(4):
         place = pl.ds(8 * lax.rem(at_ref[0] + 4 - e, 4), 8)
         for c in range(CHUNKS):
-            refs[4 + c][place] = refs[e][:, c * ROWS : (c + 1) * ROWS]
+            refs[4 + c][place] = refs[e][:, c * WIDE : (c + 1) * WIDE]
 
 
 def assemble(at, pieces):
@@ -93,11 +97,11 @@
             num_scalar_prefetch=1,
             grid=(1,),
             in_specs=[piece] * 4,
-            out_specs=[pl.BlockSpec((32, ROWS, 128), lambda i, s: (0, 0, 0))] * CHUNKS,
+            out_specs=[pl.BlockSpec((32, WIDE, 128), lambda i, s: (0, 0, 0))] * CHUNKS,
         ),
-        out_shape=[jax.ShapeDtypeStruct((32, ROWS, 128), jnp.bfloat16)] * CHUNKS,
+        out_shape=[jax.ShapeDtypeStruct((32, WIDE, 128), jnp.bfloat16)] * CHUNKS,
         compiler_params=pltpu.CompilerParams(vmem_limit_bytes=8 << 20),
-        cost_estimate=pl.CostEstimate(flops=0, bytes_accessed=2 << 20, transcendentals=0),
+        cost_estimate=SMALL,
         name="assemble",
     )(at, *pieces)
 
@@ -158,7 +162,7 @@
                 keep_ref[first + u] = (acc[k] + lags(k))[:LAGS].astype(jnp.bfloat16)
 
 
-def correlate(blocks, table, sign, spec, sources):
+def correlate(part, blocks, table, sign, spec, sources):
     half = jax.ShapeDtypeStruct((ROWS // 2, LAGS, 256), jnp.bfloat16)
     whole = pl.BlockSpec((ROWS // 2, LAGS, 256), lambda i, s: (0, 0, 0))
     return pl.pallas_call(
@@ -171,7 +175,7 @@
                 pl.BlockSpec((1, 128), lambda i, s: (0, 0)),
                 pl.BlockSpec((32, 128, 256), lambda i, s: (s[i], 0, 0)),
             ]
-            + [pl.BlockSpec((32, ROWS, 128), lambda i, s: (0, 0, 0))] * 8,
+            + [pl.BlockSpec((32, ROWS, 128), lambda i, s: (0, part, 0))] * 8,
             out_specs=[whole, whole],
             scratch_shapes=[
                 pltpu.VMEM((32, ROWS, 128), jnp.bfloat16),
@@ -182,7 +186,7 @@
         ),
         out_shape=[half, half],
         compiler_params=pltpu.CompilerParams(vmem_limit_bytes=50 << 20),
-        cost_estimate=pl.CostEstimate(flops=20 * 10**9, bytes_accessed=24 << 20, transcendentals=0),
+        cost_estimate=SMALL,
         name="correlate",
     )(blocks, table, sign, spec, *sources)
 
@@ -206,29 +210,29 @@
     mask = jnp.tile(valid.astype(jnp.float32), 2)[None, :]
     sign = jnp.where(jnp.arange(128) < 64, -1.0, 1.0).astype(jnp.bfloat16)[None, :]
 
+    barrier = lax.optimization_barrier
     own = {d: pick_rows(jnp.stack([2 * ((x + d) % 4), 8 + 2 * ((y + d) % 4)]), pick, mask, spec) for d in (1, 3, 2, 0)}
-    quarters_a = [own[0][0]] + [shift_x(own[d][0], d) for d in (1, 3, 2)]
-    quarters_b = [own[0][1]] + [shift_y(own[d][1], d) for d in (1, 3, 2)]
-
-    def scatter(quarters, at, shift):
-        def piece(d):
-            cut = [lax.dynamic_slice_in_dim(a, 8 * ((at + d) % 4), 8, 0) for a in quarters]
-            return (cut[0] + cut[1]) + (cut[2] + cut[3])
-
-        got = [shift(piece(d), d) for d in (1, 3, 2)]
-        return (piece(0) + got[0]) + (got[1] + got[2])
-
-    piece_a = scatter(quarters_a, y, shift_y)
-    piece_b = scatter(quarters_b, x, shift_x)
-    piece_a = piece_a + swap_z(piece_a)
-    piece_b = piece_b + swap_z(piece_b)
-
-    def gather(a, shift):
-        got = {d: shift(a, d) for d in (1, 3, 2)}
-        return [a, got[1], got[2], got[3]]
-
-    inner_a = assemble(y[None], gather(piece_a, shift_y))
-    inner_b = assemble(x[None], gather(piece_b, shift_x))
+    got = {d: (shift_x(own[d][0], d), shift_y(own[d][1], d)) for d in (1, 3, 2)}
+    got = barrier(got)
+
+    def piece(half, at, d):
+        parts = (own[0][half], got[1][half], got[2][half], got[3][half])
+        cut = [lax.dynamic_slice_in_dim(a, 8 * ((at + d) % 4), 8, 0) for a in parts]
+        return (cut[0] + cut[1]) + (cut[2] + cut[3])
+
+    pieces = {d: (piece(0, y, d), piece(1, x, d)) for d in range(4)}
+    more = barrier({d: (shift_y(pieces[d][0], d), shift_x(pieces[d][1], d)) for d in (1, 3, 2)})
+    piece_a, piece_b = [(pieces[0][h] + more[1][h]) + (more[2][h] + more[3][h]) for h in range(2)]
+    far_a, far_b = barrier((swap_z(piece_a), swap_z(piece_b)))
+    piece_a, piece_b = piece_a + far_a, piece_b + far_b
+
+    def gather(a, b, shift_a, shift_b):
+        come = {d: (shift_a(a, d), shift_b(b, d)) for d in (1, 3, 2)}
+        come = barrier(come)
+        return [a, come[1][0], come[2][0], come[3][0]], [b, come[1][1], come[2][1], come[3][1]]
+
+    near_a, near_b = gather(piece_a, piece_b, shift_y, shift_x)
+    inner_a, inner_b = assemble(y[None], near_a), assemble(x[None], near_b)
 
     i = jnp.arange(256, dtype=jnp.int32)
     e = i % 128 // 32
@@ -237,28 +241,26 @@
     table = table.reshape(2, LAG_PAD, 2, 128).transpose(2, 1, 0, 3).reshape(2, LAG_PAD, 256)
     blocks = blocks_at[::32]
 
-    outs, waiting = [], None
+    arrivals = []
+    for c in range(CHUNKS):
+        far_a, far_b = gather(inner_a[c], inner_b[c], shift_x, shift_y)
+        arrivals.append(far_a + far_b)
+    outs = []
     quarter = ROWS // 4
-    arrived = gather(inner_a[0], shift_x) + gather(inner_b[0], shift_y)
-    for c in range(CHUNKS):
-        following = None
-        if c + 1 < CHUNKS:
-            following = gather(inner_a[c + 1], shift_x) + gather(inner_b[c + 1], shift_y)
-        if waiting is not None:
-            last = swap_far(waiting[0])
-        send, keep = correlate(blocks, table, sign, spec, arrived)
-        if waiting is not None:
-            outs.append(finish(waiting, last))
-        arrived = following
+    for part in range(PARTS):
+        at = blocks
+        if part >= LAG:
+            at, outs[part - LAG] = barrier((blocks, outs[part - LAG]))
+        c = part * CHUNKS // PARTS
+        send, keep = correlate(part - c * PARTS // CHUNKS, at, table, sign, spec, arrivals[c])
         near = swap_core(send)
         onward = (keep[:quarter].astype(jnp.float32) + near[:quarter].astype(jnp.float32)).astype(jnp.bfloat16)
-        waiting = (onward, keep[quarter:], near[quarter:])
-    outs.append(finish(waiting, swap_far(onward)))
+        outs.append(finish((keep[quarter:], near[quarter:]), swap_far(onward)))
     return jnp.concatenate(outs)
 
 
-def finish(waiting, last):
-    own = waiting[1].astype(jnp.float32) + waiting[2].astype(jnp.float32)
+def finish(own_rows, last):
+    own = own_rows[0].astype(jnp.float32) + own_rows[1].astype(jnp.float32)
     return (own + last.astype(jnp.float32)).astype(jnp.bfloat16)
 
 

time: 297 us -> 284 us (0.956)
  waiting for transfers between devices: 150 us -> 99.4 us
  Pallas kernels: 55.4 us -> 77.2 us
  starting transfers between devices: 49.9 us -> 65.7 us
  local copies, waits for them, and re-layouts: 25.8 us -> 29 us
    ppermute x15, waiting for transfers between devices: 65 us -> 35.1 us  [shift_y(): return lax.ppermute(x, 'chan', pairs)]
    pallas_call x2 -> x4, Pallas kernels: 39.3 us -> 60.4 us  [correlate(): pl.pallas_call(correlate_kernel, grid_spec=pltpu.PrefetchScalarGridSpec(n...]
    ppermute x15, waiting for transfers between devices: 52 us -> 34.8 us  [shift_x(): return lax.ppermute(x, 'chan', pairs)]
    ppermute x2 -> x4, waiting for transfers between devices: 33.4 us -> 23.7 us  [swap_far(): return lax.ppermute(x, 'tm', [(a, a ^ 2) for a in range(4)])]
    ppermute x2 -> x4, starting transfers between devices: 1.7 us -> 10.8 us  [swap_core(): return lax.ppermute(x, 'tm', [(a, a ^ 1) for a in range(4)])]
    ppermute x2, waiting for transfers between devices: 0.01 us -> 5.74 us  [swap_z(): return lax.ppermute(x, 'chan', [(a, a ^ 1) for a in range(32)])]
    ppermute x15, starting transfers between devices: 21.8 us -> 27 us  [shift_y(): return lax.ppermute(x, 'chan', pairs)]
    ppermute x2 -> x4, starting transfers between devices: 4.69 us -> 9.21 us  [swap_far(): return lax.ppermute(x, 'tm', [(a, a ^ 2) for a in range(4)])]
  transfers between devices with their start and end apart: 36 -> 40, of which waited for: 15 -> 18; matrix products, arithmetic and copies ran while one was open for 5% -> 4% of each run, Pallas kernels for 18% -> 26%
where the time goes in v3:
time: 284 us; the launch traced here: 283 us
  waiting for transfers between devices  99.4 us (35%)
  Pallas kernels  77.2 us (27%)
  starting transfers between devices  65.7 us (23%)
  local copies, waits for them, and re-layouts  29 us (10%)
  other arithmetic  11.4 us (4%)
    pallas_call x4, Pallas kernels, correlate(): pl.pallas_call(correlate_kernel, grid_spec=pltpu.PrefetchScalarGridSpec(n...  60.4 us
    ppermute x15, waiting for transfers between devices, shift_y(): return lax.ppermute(x, 'chan', pairs)  35.1 us
    ppermute x15, waiting for transfers between devices, shift_x(): return lax.ppermute(x, 'chan', pairs)  34.8 us
    ppermute x15, starting transfers between devices, shift_y(): return lax.ppermute(x, 'chan', pairs)  27 us
    ppermute x4, waiting for transfers between devices, swap_far(): return lax.ppermute(x, 'tm', [(a, a ^ 2) for a in range(4)])  23.7 us
    ppermute x15, starting transfers between devices, shift_x(): return lax.ppermute(x, 'chan', pairs)  16.9 us
    transpose x1, local copies, waits for them, and re-layouts, body(): spec = jnp.transpose(spectra, (2, 1, 0, 3)).reshape(BINS, 128, 256)  16.5 us
    pallas_call x4, Pallas kernels, pick_rows(): pl.pallas_call(pick_kernel, grid_spec=pltpu.PrefetchScalarGridSpec(num_sc...  15.9 us
  transfers between devices with their start and end apart: 40, of which 18 were waited for; matrix products, arithmetic and copies ran while one was open for 4% of the time, Pallas kernels for 26%

profile of v3, /device:TPU:1, one launch (start us, length us, event | category | flops | bytes accessed | tf_op | source)
XLA Modules:
  0.0 283.0 jit_solution(16993517226930633582)
XLA Ops:
  2.7 16.5 %copy.21 = bf16[250,2,64,256]{3,2,1,0:T(8,128)(2,1)} copy(bf16[250,2,64,256]{3,1,0,2:T(2,128)(2,1)} %bitcast.32) | data formatting | bytes 32768000 | tf_op jit(solution)/shard_map/transpose | solution.py:200
  19.4 3.6 %pick_rows.6 = (bf16[32,128,128]{2,1,0:T(8,128)(2,1)S(1)}, bf16[32,128,128]{2,1,0:T(8,128)(2,1)S(1)}) custom-call(s32[2]{0:T(128)S(1)} %get-tuple-element.137.first_ref, bf16[128,256]{1,0:T(8,128)(2,1)S(1)} %fusion.1.pick_ref, f32[1,128]{1,0:T(1,128)S(1)} %broadcast_in_dim_tile.3.mask_ref, bf16[250,128,256]{2,1,0:T(8,128)(2,1)} %bitcast.20, ...), custom_call_target="tpu_custom_call" | custom-call | flops 1048576 | bytes 65536 | tf_op jit(solution)/shard_map/pick_rows/pallas_call | solution.py:65
  23.0 3.7 %collective-permute-start.2 = (bf16[32,128,128]{2,1,0:T(8,128)(2,1)S(1)}, bf16[32,128,128]{2,1,0:T(8,128)(2,1)S(1)}, u32[]{:S(2)}, u32[]{:S(2)}) collective-permute-start(bf16[32,128,128]{2,1,0:T(8,128)(2,1)S(1)} %get-tuple-element.64), channel_id=1, source_target_pairs={{0,64},{4,68},{8,72},{12,76},{16,80},{20,84},{24,88},{28,92},{32,9... | collective-permute-start | bytes 3145736 | tf_op jit(solution)/shard_map/ppermute | solution.py:23
  26.7 2.9 %collective-permute-start.3 = (bf16[32,128,128]{2,1,0:T(8,128)(2,1)S(1)}, bf16[32,128,128]{2,1,0:T(8,128)(2,1)}, u32[]{:S(2)}, u32[]{:S(2)}) collective-permute-start(bf16[32,128,128]{2,1,0:T(8,128)(2,1)S(1)} %get-tuple-element.65), channel_id=1, source_target_pairs={{0,16},{4,20},{8,24},{12,28},{16,0},{20,4},{24,8},{28,12},{32,48},... | collective-permute-start | bytes 3145736 | tf_op jit(solution)/shard_map/ppermute | solution.py:28
  29.6 4.4 %pick_rows.7 = (bf16[32,128,128]{2,1,0:T(8,128)(2,1)}, bf16[32,128,128]{2,1,0:T(8,128)(2,1)}) custom-call(s32[2]{0:T(128)S(1)} %get-tuple-element.138.first_ref, bf16[128,256]{1,0:T(8,128)(2,1)S(1)} %fusion.1.pick_ref, f32[1,128]{1,0:T(1,128)S(1)} %broadcast_in_dim_tile.3.mask_ref, bf16[250,128,256]{2,1,0:T(8,128)(2,1)} %bitcast.22, ...), custom_call_target="tpu_custom_call" | custom-call | flops 1048576 | bytes 65536 | tf_op jit(solution)/shard_map/pick_rows/pallas_call | solution.py:65
  35.7 4.4 %pick_rows.5 = (bf16[32,128,128]{2,1,0:T(8,128)(2,1)}, bf16[32,128,128]{2,1,0:T(8,128)(2,1)}) custom-call(s32[2]{0:T(128)S(1)} %get-tuple-element.136.first_ref, bf16[128,256]{1,0:T(8,128)(2,1)S(1)} %fusion.1.pick_ref, f32[1,128]{1,0:T(1,128)S(1)} %broadcast_in_dim_tile.3.mask_ref, bf16[250,128,256]{2,1,0:T(8,128)(2,1)} %bitcast.24, ...), custom_call_target="tpu_custom_call" | custom-call | flops 1048576 | bytes 65536 | tf_op jit(solution)/shard_map/pick_rows/pallas_call | solution.py:65
  40.7 8.5 %collective-permute-done.2 = bf16[32,128,128]{2,1,0:T(8,128)(2,1)S(1)} collective-permute-done((bf16[32,128,128]{2,1,0:T(8,128)(2,1)S(1)}, bf16[32,128,128]{2,1,0:T(8,128)(2,1)S(1)}, u32[]{:S(2)}, u32[]{:S(2)}) %collective-permute-start.2) | collective-permute-done | bytes 1048608 | tf_op jit(solution)/shard_map/ppermute | solution.py:23
  50.8 3.6 %pick_rows.4 = (bf16[32,128,128]{2,1,0:T(8,128)(2,1)S(1)}, bf16[32,128,128]{2,1,0:T(8,128)(2,1)S(1)}) custom-call(s32[2]{0:T(128)S(1)} %get-tuple-element.135.first_ref, bf16[128,256]{1,0:T(8,128)(2,1)S(1)} %fusion.1.pick_ref, f32[1,128]{1,0:T(1,128)S(1)} %broadcast_in_dim_tile.3.mask_ref, bf16[250,128,256]{2,1,0:T(8,128)(2,1)} %bitcast.26, ...), custom_call_target="tpu_custom_call" | custom-call | flops 1048576 | bytes 65536 | tf_op jit(solution)/shard_map/pick_rows/pallas_call | solution.py:65
  54.4 17.8 %collective-permute-done.4 = bf16[32,128,128]{2,1,0:T(8,128)(2,1)} collective-permute-done((bf16[32,128,128]{2,1,0:T(8,128)(2,1)}, bf16[32,128,128]{2,1,0:T(8,128)(2,1)}, u32[]{:S(2)}, u32[]{:S(2)}) %collective-permute-start.4) | collective-permute-done | bytes 1048608 | tf_op jit(solution)/shard_map/ppermute | solution.py:23
  72.2 3.0 %collective-permute-done.5 = bf16[32,128,128]{2,1,0:T(8,128)(2,1)} collective-permute-done((bf16[32,128,128]{2,1,0:T(8,128)(2,1)}, bf16[32,128,128]{2,1,0:T(8,128)(2,1)}, u32[]{:S(2)}, u32[]{:S(2)}) %collective-permute-start.5) | collective-permute-done | bytes 1048608 | tf_op jit(solution)/shard_map/ppermute | solution.py:28
  82.5 3.2 %collective-permute-start.10 = (bf16[8,128,128]{2,1,0:T(8,128)(2,1)}, bf16[8,128,128]{2,1,0:T(8,128)(2,1)}, u32[]{:S(2)}, u32[]{:S(2)}) collective-permute-start(bf16[8,128,128]{2,1,0:T(8,128)(2,1)} %get-tuple-element.120), channel_id=1, source_target_pairs={{0,24},{4,28},{8,0},{12,4},{16,8},{20,12},{24,16},{28,20},{32,56},... | collective-permute-start | bytes 786440 | tf_op jit(solution)/shard_map/ppermute | solution.py:28
  89.3 7.1 %collective-permute-done.6 = bf16[8,128,128]{2,1,0:T(8,128)(2,1)} collective-permute-done((bf16[8,128,128]{2,1,0:T(8,128)(2,1)}, bf16[8,128,128]{2,1,0:T(8,128)(2,1)}, u32[]{:S(2)}, u32[]{:S(2)}) %collective-permute-start.6) | collective-permute-done | bytes 262176 | tf_op jit(solution)/shard_map/ppermute | solution.py:28
  103.3 3.4 %collective-permute-done.12 = bf16[8,128,128]{2,1,0:T(8,128)(2,1)S(1)} collective-permute-done((bf16[8,128,128]{2,1,0:T(8,128)(2,1)S(1)}, bf16[8,128,128]{2,1,0:T(8,128)(2,1)S(1)}, u32[]{:S(2)}, u32[]{:S(2)}) %collective-permute-start.12) | collective-permute-done | bytes 262176 | tf_op jit(solution)/shard_map/ppermute | solution.py:32
  113.3 3.7 %collective-permute-start.16 = (bf16[8,128,128]{2,1,0:T(8,128)(2,1)S(1)}, bf16[8,128,128]{2,1,0:T(8,128)(2,1)S(1)}, u32[]{:S(2)}, u32[]{:S(2)}) collective-permute-start(bf16[8,128,128]{2,1,0:T(8,128)(2,1)S(1)} %add.592.refs_0_), channel_id=1, source_target_pairs={{0,16},{4,20},{8,24},{12,28},{16,0},{20,4},{24,8},{28,12},{32,48},... | collective-permute-start | bytes 786440 | tf_op jit(solution)/shard_map/ppermute | solution.py:28
  117.0 4.7 %collective-permute-start.18 = (bf16[8,128,128]{2,1,0:T(8,128)(2,1)S(1)}, bf16[8,128,128]{2,1,0:T(8,128)(2,1)S(1)}, u32[]{:S(2)}, u32[]{:S(2)}) collective-permute-start(bf16[8,128,128]{2,1,0:T(8,128)(2,1)S(1)} %add.592.refs_0_), channel_id=1, source_target_pairs={{0,24},{4,28},{8,0},{12,4},{16,8},{20,12},{24,16},{28,20},{32,56},... | collective-permute-start | bytes 786440 | tf_op jit(solution)/shard_map/ppermute | solution.py:28
  121.7 3.2 %collective-permute-done.16.refs_2_ = bf16[8,128,128]{2,1,0:T(8,128)(2,1)S(1)} collective-permute-done((bf16[8,128,128]{2,1,0:T(8,128)(2,1)S(1)}, bf16[8,128,128]{2,1,0:T(8,128)(2,1)S(1)}, u32[]{:S(2)}, u32[]{:S(2)}) %collective-permute-start.16) | collective-permute-done | bytes 262176 | tf_op jit(solution)/shard_map/ppermute | solution.py:28
  128.2 4.4 %collective-permute-start.23 = (bf16[32,64,128]{2,1,0:T(8,128)(2,1)S(1)}, bf16[32,64,128]{2,1,0:T(8,128)(2,1)S(1)}, u32[]{:S(2)}, u32[]{:S(2)}) collective-permute-start(bf16[32,64,128]{2,1,0:T(8,128)(2,1)S(1)} %get-tuple-element.90.refs_4_), channel_id=1, source_target_pairs={{0,16},{4,20},{8,24},{12,28},{16,0},{20,4},{24,8},{28,12},{32,48},... | collective-permute-start | bytes 1572872 | tf_op jit(solution)/shard_map/ppermute | solution.py:28
  135.0 4.3 %collective-permute-done.21.refs_5_ = bf16[32,64,128]{2,1,0:T(8,128)(2,1)S(1)} collective-permute-done((bf16[32,64,128]{2,1,0:T(8,128)(2,1)S(1)}, bf16[32,64,128]{2,1,0:T(8,128)(2,1)S(1)}, u32[]{:S(2)}, u32[]{:S(2)}) %collective-permute-start.21) | collective-permute-done | bytes 524320 | tf_op jit(solution)/shard_map/ppermute | solution.py:28
  139.4 12.1 %collective-permute-done.23.refs_6_ = bf16[32,64,128]{2,1,0:T(8,128)(2,1)S(1)} collective-permute-done((bf16[32,64,128]{2,1,0:T(8,128)(2,1)S(1)}, bf16[32,64,128]{2,1,0:T(8,128)(2,1)S(1)}, u32[]{:S(2)}, u32[]{:S(2)}) %collective-permute-start.23) | collective-permute-done | bytes 524320 | tf_op jit(solution)/shard_map/ppermute | solution.py:28
  155.9 3.1 %collective-permute-start.35 = (bf16[32,64,128]{2,1,0:T(8,128)(2,1)S(1)}, bf16[32,64,128]{2,1,0:T(8,128)(2,1)}, u32[]{:S(2)}, u32[]{:S(2)}) collective-permute-start(bf16[32,64,128]{2,1,0:T(8,128)(2,1)S(1)} %get-tuple-element.105.refs_4_), channel_id=1, source_target_pairs={{0,24},{4,28},{8,0},{12,4},{16,8},{20,12},{24,16},{28,20},{32,56},... | collective-permute-start | bytes 1572872 | tf_op jit(solution)/shard_map/ppermute | solution.py:28
  161.2 15.2 %correlate.4 = (bf16[16,101,256]{2,1,0:T(8,128)(2,1)}, bf16[16,101,256]{2,1,0:T(8,128)(2,1)}) custom-call(s32[8]{0:T(128)S(1)} %slice.57.blocks_ref, bf16[2,112,256]{2,1,0:T(8,128)(2,1)S(1)} %copy_bitcast_fusion.table_ref, bf16[1,128]{1,0:T(2,128)(2,1)S(1)} %fusion.17.sign_ref, bf16[250,128,256]{2,1,0:T(8,128)(2,1)} %bitcast.28, ...), custom_call_target="tpu_custom_call" | custom-call | flops 1048576 | bytes 65536 | tf_op jit(solution)/shard_map/correlate/pallas_call | solution.py:168
  177.8 5.9 %collective-permute-start.26 = (bf16[16,101,256]{2,0,1:T(8,128)(2,1)S(1)}, bf16[16,101,256]{2,0,1:T(8,128)(2,1)S(1)}, u32[]{:S(2)}, u32[]{:S(2)}) collective-permute-start(bf16[16,101,256]{2,0,1:T(8,128)(2,1)S(1)} %copy.22), channel_id=1, source_target_pairs={{0,1},{1,0},{2,3},{3,2},{4,5},{5,4},{6,7},{7,6},{8,9},{9,8},{10,11... | collective-permute-start | bytes 2482184 | tf_op jit(solution)/shard_map/ppermute | solution.py:36
  186.5 15.2 %correlate.5 = (bf16[16,101,256]{2,1,0:T(8,128)(2,1)}, bf16[16,101,256]{2,1,0:T(8,128)(2,1)}) custom-call(s32[8]{0:T(128)S(1)} %slice.57.blocks_ref, bf16[2,112,256]{2,1,0:T(8,128)(2,1)S(1)} %copy_bitcast_fusion.table_ref, bf16[1,128]{1,0:T(2,128)(2,1)S(1)} %fusion.17.sign_ref, bf16[250,128,256]{2,1,0:T(8,128)(2,1)} %bitcast.29, ...), custom_call_target="tpu_custom_call" | custom-call | flops 1048576 | bytes 65536 | tf_op jit(solution)/shard_map/correlate/pallas_call | solution.py:168
  203.9 5.8 %collective-permute-done.30.refs_1_ = bf16[32,64,128]{2,1,0:T(8,128)(2,1)S(1)} collective-permute-done((bf16[32,64,128]{2,1,0:T(8,128)(2,1)S(1)}, bf16[32,64,128]{2,1,0:T(8,128)(2,1)S(1)}, u32[]{:S(2)}, u32[]{:S(2)}) %collective-permute-start.30) | collective-permute-done | bytes 524320 | tf_op jit(solution)/shard_map/ppermute | solution.py:23
  210.2 3.1 %collective-permute-start.27 = (bf16[8,101,256]{2,1,0:T(8,128)(2,1)S(1)}, bf16[8,101,256]{2,1,0:T(8,128)(2,1)S(1)}, u32[]{:S(2)}, u32[]{:S(2)}) collective-permute-start(bf16[8,101,256]{2,1,0:T(8,128)(2,1)S(1)} %add_convert_fusion.7), channel_id=1, source_target_pairs={{0,2},{1,3},{2,0},{3,1},{4,6},{5,7},{6,4},{7,5},{8,10},{9,11},{10,... | collective-permute-start | bytes 1241096 | tf_op jit(solution)/shard_map/ppermute | solution.py:40
  214.4 7.6 %collective-permute-done.27 = bf16[8,101,256]{2,1,0:T(8,128)(2,1)S(1)} collective-permute-done((bf16[8,101,256]{2,1,0:T(8,128)(2,1)S(1)}, bf16[8,101,256]{2,1,0:T(8,128)(2,1)S(1)}, u32[]{:S(2)}, u32[]{:S(2)}) %collective-permute-start.27) | collective-permute-done | bytes 413728 | tf_op jit(solution)/shard_map/ppermute | solution.py:40
  222.2 15.0 %correlate.6 = (bf16[16,101,256]{2,1,0:T(8,128)(2,1)}, bf16[16,101,256]{2,1,0:T(8,128)(2,1)}) custom-call(s32[8]{0:T(128)S(1)} %slice.57.blocks_ref, bf16[2,112,256]{2,1,0:T(8,128)(2,1)S(1)} %copy_bitcast_fusion.table_ref, bf16[1,128]{1,0:T(2,128)(2,1)S(1)} %fusion.17.sign_ref, bf16[250,128,256]{2,1,0:T(8,128)(2,1)} %bitcast.30, ...), custom_call_target="tpu_custom_call" | custom-call | flops 1048576 | bytes 65536 | tf_op jit(solution)/shard_map/correlate/pallas_call | solution.py:168
  238.4 4.0 %collective-permute-start.36 = (bf16[16,101,256]{2,0,1:T(8,128)(2,1)S(1)}, bf16[16,101,256]{2,0,1:T(8,128)(2,1)S(1)}, u32[]{:S(2)}, u32[]{:S(2)}) collective-permute-start(bf16[16,101,256]{2,0,1:T(8,128)(2,1)S(1)} %copy.28), channel_id=1, source_target_pairs={{0,1},{1,0},{2,3},{3,2},{4,5},{5,4},{6,7},{7,6},{8,9},{9,8},{10,11... | collective-permute-start | bytes 2482184 | tf_op jit(solution)/shard_map/ppermute | solution.py:36
  242.6 15.0 %correlate.7 = (bf16[16,101,256]{2,1,0:T(8,128)(2,1)}, bf16[16,101,256]{2,1,0:T(8,128)(2,1)}) custom-call(s32[8]{0:T(128)S(1)} %slice.57.blocks_ref, bf16[2,112,256]{2,1,0:T(8,128)(2,1)S(1)} %copy_bitcast_fusion.table_ref, bf16[1,128]{1,0:T(2,128)(2,1)S(1)} %fusion.17.sign_ref, bf16[250,128,256]{2,1,0:T(8,128)(2,1)} %bitcast.31, ...), custom_call_target="tpu_custom_call" | custom-call | flops 1048576 | bytes 65536 | tf_op jit(solution)/shard_map/correlate/pallas_call | solution.py:168
  259.3 3.1 %collective-permute-start.37 = (bf16[8,101,256]{2,1,0:T(8,128)(2,1)S(1)}, bf16[8,101,256]{2,1,0:T(8,128)(2,1)S(1)}, u32[]{:S(2)}, u32[]{:S(2)}) collective-permute-start(bf16[8,101,256]{2,1,0:T(8,128)(2,1)S(1)} %add_convert_fusion.3), channel_id=1, source_target_pairs={{0,2},{1,3},{2,0},{3,1},{4,6},{5,7},{6,4},{7,5},{8,10},{9,11},{10,... | collective-permute-start | bytes 1241096 | tf_op jit(solution)/shard_map/ppermute | solution.py:40
  264.7 7.2 %collective-permute-done.37 = bf16[8,101,256]{2,1,0:T(8,128)(2,1)S(1)} collective-permute-done((bf16[8,101,256]{2,1,0:T(8,128)(2,1)S(1)}, bf16[8,101,256]{2,1,0:T(8,128)(2,1)S(1)}, u32[]{:S(2)}, u32[]{:S(2)}) %collective-permute-start.37) | collective-permute-done | bytes 413728 | tf_op jit(solution)/shard_map/ppermute | solution.py:40
  272.1 9.0 %collective-permute-done.39 = bf16[8,101,256]{2,1,0:T(8,128)(2,1)S(1)} collective-permute-done((bf16[8,101,256]{2,1,0:T(8,128)(2,1)S(1)}, bf16[8,101,256]{2,1,0:T(8,128)(2,1)S(1)}, u32[]{:S(2)}, u32[]{:S(2)}) %collective-permute-start.39) | collective-permute-done | bytes 413728 | tf_op jit(solution)/shard_map/ppermute | solution.py:40
  (125 shorter events, 59.1 us)
Async XLA Ops:
  23.0 26.2 %collective-permute-start.2 = (bf16[32,128,128]{2,1,0:T(8,128)(2,1)S(1)}, bf16[32,128,128]{2,1,0:T(8,128)(2,1)S(1)}, u32[]{:S(2)}, u32[]{:S(2)}) collective-permute-start(bf16[32,128,128]{2,1,0:T(8,128)(2,1)S(1)} %get-tuple-element.64), channel_id=1, source_target_pairs={{0,64},{4,68},{8,72},{12,76},{16,80},{20,84},{24,88},{28,92},{32,9... | collective-permute-start | bytes 3145736 | tf_op jit(solution)/shard_map/ppermute | solution.py:23
  26.7 27.7 %collective-permute-start.3 = (bf16[32,128,128]{2,1,0:T(8,128)(2,1)S(1)}, bf16[32,128,128]{2,1,0:T(8,128)(2,1)}, u32[]{:S(2)}, u32[]{:S(2)}) collective-permute-start(bf16[32,128,128]{2,1,0:T(8,128)(2,1)S(1)} %get-tuple-element.65), channel_id=1, source_target_pairs={{0,16},{4,20},{8,24},{12,28},{16,0},{20,4},{24,8},{28,12},{32,48},... | collective-permute-start | bytes 3145736 | tf_op jit(solution)/shard_map/ppermute | solution.py:28
  34.0 38.2 %collective-permute-start.4 = (bf16[32,128,128]{2,1,0:T(8,128)(2,1)}, bf16[32,128,128]{2,1,0:T(8,128)(2,1)}, u32[]{:S(2)}, u32[]{:S(2)}) collective-permute-start(bf16[32,128,128]{2,1,0:T(8,128)(2,1)} %get-tuple-element.66), channel_id=1, source_target_pairs={{0,96},{4,100},{8,104},{12,108},{16,112},{20,116},{24,120},{28,124... | collective-permute-start | bytes 3145736 | tf_op jit(solution)/shard_map/ppermute | solution.py:23
  34.8 40.3 %collective-permute-start.5 = (bf16[32,128,128]{2,1,0:T(8,128)(2,1)}, bf16[32,128,128]{2,1,0:T(8,128)(2,1)}, u32[]{:S(2)}, u32[]{:S(2)}) collective-permute-start(bf16[32,128,128]{2,1,0:T(8,128)(2,1)} %get-tuple-element.67), channel_id=1, source_target_pairs={{0,24},{4,28},{8,0},{12,4},{16,8},{20,12},{24,16},{28,20},{32,56},... | collective-permute-start | bytes 3145736 | tf_op jit(solution)/shard_map/ppermute | solution.py:28
  40.1 35.1 %collective-permute-start = (bf16[32,128,128]{2,1,0:T(8,128)(2,1)}, bf16[32,128,128]{2,1,0:T(8,128)(2,1)}, u32[]{:S(2)}, u32[]{:S(2)}) collective-permute-start(bf16[32,128,128]{2,1,0:T(8,128)(2,1)} %get-tuple-element.62), channel_id=1, source_target_pairs={{0,32},{4,36},{8,40},{12,44},{16,48},{20,52},{24,56},{28,60},{32,6... | collective-permute-start | bytes 3145736 | tf_op jit(solution)/shard_map/ppermute | solution.py:23
  49.2 25.9 %collective-permute-start.1 = (bf16[32,128,128]{2,1,0:T(8,128)(2,1)}, bf16[32,128,128]{2,1,0:T(8,128)(2,1)}, u32[]{:S(2)}, u32[]{:S(2)}) collective-permute-start(bf16[32,128,128]{2,1,0:T(8,128)(2,1)} %get-tuple-element.63), channel_id=1, source_target_pairs={{0,8},{4,12},{8,16},{12,20},{16,24},{20,28},{24,0},{28,4},{32,40},... | collective-permute-start | bytes 3145736 | tf_op jit(solution)/shard_map/ppermute | solution.py:28
  78.7 10.5 %collective-permute-start.7 = (bf16[8,128,128]{2,1,0:T(8,128)(2,1)}, bf16[8,128,128]{2,1,0:T(8,128)(2,1)}, u32[]{:S(2)}, u32[]{:S(2)}) collective-permute-start(bf16[8,128,128]{2,1,0:T(8,128)(2,1)} %get-tuple-element.119), channel_id=1, source_target_pairs={{0,32},{4,36},{8,40},{12,44},{16,48},{20,52},{24,56},{28,60},{32,6... | collective-permute-start | bytes 786440 | tf_op jit(solution)/shard_map/ppermute | solution.py:23
  85.7 10.8 %collective-permute-start.6 = (bf16[8,128,128]{2,1,0:T(8,128)(2,1)}, bf16[8,128,128]{2,1,0:T(8,128)(2,1)}, u32[]{:S(2)}, u32[]{:S(2)}) collective-permute-start(bf16[8,128,128]{2,1,0:T(8,128)(2,1)} %get-tuple-element.122), channel_id=1, source_target_pairs={{0,8},{4,12},{8,16},{12,20},{16,24},{20,28},{24,0},{28,4},{32,40},... | collective-permute-start | bytes 786440 | tf_op jit(solution)/shard_map/ppermute | solution.py:28
  85.7 10.8 %collective-permute-start.8 = (bf16[8,128,128]{2,1,0:T(8,128)(2,1)}, bf16[8,128,128]{2,1,0:T(8,128)(2,1)}, u32[]{:S(2)}, u32[]{:S(2)}) collective-permute-start(bf16[8,128,128]{2,1,0:T(8,128)(2,1)} %get-tuple-element.121), channel_id=1, source_target_pairs={{0,16},{4,20},{8,24},{12,28},{16,0},{20,4},{24,8},{28,12},{32,48},... | collective-permute-start | bytes 786440 | tf_op jit(solution)/shard_map/ppermute | solution.py:28
  106.8 10.3 %collective-permute-start.15 = (bf16[8,128,128]{2,1,0:T(8,128)(2,1)S(1)}, bf16[8,128,128]{2,1,0:T(8,128)(2,1)S(1)}, u32[]{:S(2)}, u32[]{:S(2)}) collective-permute-start(bf16[8,128,128]{2,1,0:T(8,128)(2,1)S(1)} %add.593.refs_0_), channel_id=1, source_target_pairs={{0,32},{4,36},{8,40},{12,44},{16,48},{20,52},{24,56},{28,60},{32,6... | collective-permute-start | bytes 786440 | tf_op jit(solution)/shard_map/ppermute | solution.py:23
  108.8 12.9 %collective-permute-start.17 = (bf16[8,128,128]{2,1,0:T(8,128)(2,1)S(1)}, bf16[8,128,128]{2,1,0:T(8,128)(2,1)S(1)}, u32[]{:S(2)}, u32[]{:S(2)}) collective-permute-start(bf16[8,128,128]{2,1,0:T(8,128)(2,1)S(1)} %add.593.refs_0_), channel_id=1, source_target_pairs={{0,64},{4,68},{8,72},{12,76},{16,80},{20,84},{24,88},{28,92},{32,9... | collective-permute-start | bytes 786440 | tf_op jit(solution)/shard_map/ppermute | solution.py:23
  110.6 11.1 %collective-permute-start.19 = (bf16[8,128,128]{2,1,0:T(8,128)(2,1)S(1)}, bf16[8,128,128]{2,1,0:T(8,128)(2,1)S(1)}, u32[]{:S(2)}, u32[]{:S(2)}) collective-permute-start(bf16[8,128,128]{2,1,0:T(8,128)(2,1)S(1)} %add.593.refs_0_), channel_id=1, source_target_pairs={{0,96},{4,100},{8,104},{12,108},{16,112},{20,116},{24,120},{28,124... | collective-permute-start | bytes 786440 | tf_op jit(solution)/shard_map/ppermute | solution.py:23
  113.3 11.6 %collective-permute-start.16 = (bf16[8,128,128]{2,1,0:T(8,128)(2,1)S(1)}, bf16[8,128,128]{2,1,0:T(8,128)(2,1)S(1)}, u32[]{:S(2)}, u32[]{:S(2)}) collective-permute-start(bf16[8,128,128]{2,1,0:T(8,128)(2,1)S(1)} %add.592.refs_0_), channel_id=1, source_target_pairs={{0,16},{4,20},{8,24},{12,28},{16,0},{20,4},{24,8},{28,12},{32,48},... | collective-permute-start | bytes 786440 | tf_op jit(solution)/shard_map/ppermute | solution.py:28
  117.0 10.8 %collective-permute-start.18 = (bf16[8,128,128]{2,1,0:T(8,128)(2,1)S(1)}, bf16[8,128,128]{2,1,0:T(8,128)(2,1)S(1)}, u32[]{:S(2)}, u32[]{:S(2)}) collective-permute-start(bf16[8,128,128]{2,1,0:T(8,128)(2,1)S(1)} %add.592.refs_0_), channel_id=1, source_target_pairs={{0,24},{4,28},{8,0},{12,4},{16,8},{20,12},{24,16},{28,20},{32,56},... | collective-permute-start | bytes 786440 | tf_op jit(solution)/shard_map/ppermute | solution.py:28
  127.9 11.4 %collective-permute-start.21 = (bf16[32,64,128]{2,1,0:T(8,128)(2,1)S(1)}, bf16[32,64,128]{2,1,0:T(8,128)(2,1)S(1)}, u32[]{:S(2)}, u32[]{:S(2)}) collective-permute-start(bf16[32,64,128]{2,1,0:T(8,128)(2,1)S(1)} %get-tuple-element.90.refs_4_), channel_id=1, source_target_pairs={{0,8},{4,12},{8,16},{12,20},{16,24},{20,28},{24,0},{28,4},{32,40},... | collective-permute-start | bytes 1572872 | tf_op jit(solution)/shard_map/ppermute | solution.py:28
  128.2 23.2 %collective-permute-start.23 = (bf16[32,64,128]{2,1,0:T(8,128)(2,1)S(1)}, bf16[32,64,128]{2,1,0:T(8,128)(2,1)S(1)}, u32[]{:S(2)}, u32[]{:S(2)}) collective-permute-start(bf16[32,64,128]{2,1,0:T(8,128)(2,1)S(1)} %get-tuple-element.90.refs_4_), channel_id=1, source_target_pairs={{0,16},{4,20},{8,24},{12,28},{16,0},{20,4},{24,8},{28,12},{32,48},... | collective-permute-start | bytes 1572872 | tf_op jit(solution)/shard_map/ppermute | solution.py:28
  132.6 22.0 %collective-permute-start.25 = (bf16[32,64,128]{2,1,0:T(8,128)(2,1)S(1)}, bf16[32,64,128]{2,1,0:T(8,128)(2,1)S(1)}, u32[]{:S(2)}, u32[]{:S(2)}) collective-permute-start(bf16[32,64,128]{2,1,0:T(8,128)(2,1)S(1)} %get-tuple-element.90.refs_4_), channel_id=1, source_target_pairs={{0,24},{4,28},{8,0},{12,4},{16,8},{20,12},{24,16},{28,20},{32,56},... | collective-permute-start | bytes 1572872 | tf_op jit(solution)/shard_map/ppermute | solution.py:28
  133.4 21.7 %collective-permute-start.20 = (bf16[32,64,128]{2,1,0:T(8,128)(2,1)}, bf16[32,64,128]{2,1,0:T(8,128)(2,1)S(1)}, u32[]{:S(2)}, u32[]{:S(2)}) collective-permute-start(bf16[32,64,128]{2,1,0:T(8,128)(2,1)} %get-tuple-element.86.refs_0_), channel_id=1, source_target_pairs={{0,32},{4,36},{8,40},{12,44},{16,48},{20,52},{24,56},{28,60},{32,6... | collective-permute-start | bytes 1572872 | tf_op jit(solution)/shard_map/ppermute | solution.py:23
  134.0 25.1 %collective-permute-start.22 = (bf16[32,64,128]{2,1,0:T(8,128)(2,1)}, bf16[32,64,128]{2,1,0:T(8,128)(2,1)}, u32[]{:S(2)}, u32[]{:S(2)}) collective-permute-start(bf16[32,64,128]{2,1,0:T(8,128)(2,1)} %get-tuple-element.86.refs_0_), channel_id=1, source_target_pairs={{0,64},{4,68},{8,72},{12,76},{16,80},{20,84},{24,88},{28,92},{32,9... | collective-permute-start | bytes 1572872 | tf_op jit(solution)/shard_map/ppermute | solution.py:23
  139.3 19.8 %collective-permute-start.24 = (bf16[32,64,128]{2,1,0:T(8,128)(2,1)}, bf16[32,64,128]{2,1,0:T(8,128)(2,1)}, u32[]{:S(2)}, u32[]{:S(2)}) collective-permute-start(bf16[32,64,128]{2,1,0:T(8,128)(2,1)} %get-tuple-element.86.refs_0_), channel_id=1, source_target_pairs={{0,96},{4,100},{8,104},{12,108},{16,112},{20,116},{24,120},{28,124... | collective-permute-start | bytes 1572872 | tf_op jit(solution)/shard_map/ppermute | solution.py:23
  152.2 31.5 %collective-permute-start.31 = (bf16[32,64,128]{2,1,0:T(8,128)(2,1)S(1)}, bf16[32,64,128]{2,1,0:T(8,128)(2,1)S(1)}, u32[]{:S(2)}, u32[]{:S(2)}) collective-permute-start(bf16[32,64,128]{2,1,0:T(8,128)(2,1)S(1)} %get-tuple-element.105.refs_4_), channel_id=1, source_target_pairs={{0,8},{4,12},{8,16},{12,20},{16,24},{20,28},{24,0},{28,4},{32,40},... | collective-permute-start | bytes 1572872 | tf_op jit(solution)/shard_map/ppermute | solution.py:28
  154.6 29.7 %collective-permute-start.33 = (bf16[32,64,128]{2,1,0:T(8,128)(2,1)S(1)}, bf16[32,64,128]{2,1,0:T(8,128)(2,1)S(1)}, u32[]{:S(2)}, u32[]{:S(2)}) collective-permute-start(bf16[32,64,128]{2,1,0:T(8,128)(2,1)S(1)} %get-tuple-element.105.refs_4_), channel_id=1, source_target_pairs={{0,16},{4,20},{8,24},{12,28},{16,0},{20,4},{24,8},{28,12},{32,48},... | collective-permute-start | bytes 1572872 | tf_op jit(solution)/shard_map/ppermute | solution.py:28
  155.9 47.2 %collective-permute-start.35 = (bf16[32,64,128]{2,1,0:T(8,128)(2,1)S(1)}, bf16[32,64,128]{2,1,0:T(8,128)(2,1)}, u32[]{:S(2)}, u32[]{:S(2)}) collective-permute-start(bf16[32,64,128]{2,1,0:T(8,128)(2,1)S(1)} %get-tuple-element.105.refs_4_), channel_id=1, source_target_pairs={{0,24},{4,28},{8,0},{12,4},{16,8},{20,12},{24,16},{28,20},{32,56},... | collective-permute-start | bytes 1572872 | tf_op jit(solution)/shard_map/ppermute | solution.py:28
  177.8 32.2 %collective-permute-start.26 = (bf16[16,101,256]{2,0,1:T(8,128)(2,1)S(1)}, bf16[16,101,256]{2,0,1:T(8,128)(2,1)S(1)}, u32[]{:S(2)}, u32[]{:S(2)}) collective-permute-start(bf16[16,101,256]{2,0,1:T(8,128)(2,1)S(1)} %copy.22), channel_id=1, source_target_pairs={{0,1},{1,0},{2,3},{3,2},{4,5},{5,4},{6,7},{7,6},{8,9},{9,8},{10,11... | collective-permute-start | bytes 2482184 | tf_op jit(solution)/shard_map/ppermute | solution.py:36
  183.7 25.9 %collective-permute-start.30 = (bf16[32,64,128]{2,1,0:T(8,128)(2,1)S(1)}, bf16[32,64,128]{2,1,0:T(8,128)(2,1)S(1)}, u32[]{:S(2)}, u32[]{:S(2)}) collective-permute-start(bf16[32,64,128]{2,1,0:T(8,128)(2,1)S(1)} %get-tuple-element.104.refs_0_), channel_id=1, source_target_pairs={{0,32},{4,36},{8,40},{12,44},{16,48},{20,52},{24,56},{28,60},{32,6... | collective-permute-start | bytes 1572872 | tf_op jit(solution)/shard_map/ppermute | solution.py:23
  183.7 25.9 %collective-permute-start.32 = (bf16[32,64,128]{2,1,0:T(8,128)(2,1)S(1)}, bf16[32,64,128]{2,1,0:T(8,128)(2,1)S(1)}, u32[]{:S(2)}, u32[]{:S(2)}) collective-permute-start(bf16[32,64,128]{2,1,0:T(8,128)(2,1)S(1)} %get-tuple-element.104.refs_0_), channel_id=1, source_target_pairs={{0,64},{4,68},{8,72},{12,76},{16,80},{20,84},{24,88},{28,92},{32,9... | collective-permute-start | bytes 1572872 | tf_op jit(solution)/shard_map/ppermute | solution.py:23
  184.2 25.7 %collective-permute-start.34 = (bf16[32,64,128]{2,1,0:T(8,128)(2,1)S(1)}, bf16[32,64,128]{2,1,0:T(8,128)(2,1)S(1)}, u32[]{:S(2)}, u32[]{:S(2)}) collective-permute-start(bf16[32,64,128]{2,1,0:T(8,128)(2,1)S(1)} %get-tuple-element.104.refs_0_), channel_id=1, source_target_pairs={{0,96},{4,100},{8,104},{12,108},{16,112},{20,116},{24,120},{28,124... | collective-permute-start | bytes 1572872 | tf_op jit(solution)/shard_map/ppermute | solution.py:23
  210.2 11.8 %collective-permute-start.27 = (bf16[8,101,256]{2,1,0:T(8,128)(2,1)S(1)}, bf16[8,101,256]{2,1,0:T(8,128)(2,1)S(1)}, u32[]{:S(2)}, u32[]{:S(2)}) collective-permute-start(bf16[8,101,256]{2,1,0:T(8,128)(2,1)S(1)} %add_convert_fusion.7), channel_id=1, source_target_pairs={{0,2},{1,3},{2,0},{3,1},{4,6},{5,7},{6,4},{7,5},{8,10},{9,11},{10,... | collective-permute-start | bytes 1241096 | tf_op jit(solution)/shard_map/ppermute | solution.py:40
  213.5 29.0 %collective-permute-start.29 = (bf16[8,101,256]{2,1,0:T(8,128)(2,1)S(1)}, bf16[8,101,256]{2,1,0:T(8,128)(2,1)S(1)}, u32[]{:S(2)}, u32[]{:S(2)}) collective-permute-start(bf16[8,101,256]{2,1,0:T(8,128)(2,1)S(1)} %add_convert_fusion.5), channel_id=1, source_target_pairs={{0,2},{1,3},{2,0},{3,1},{4,6},{5,7},{6,4},{7,5},{8,10},{9,11},{10,... | collective-permute-start | bytes 1241096 | tf_op jit(solution)/shard_map/ppermute | solution.py:40
  238.4 20.7 %collective-permute-start.36 = (bf16[16,101,256]{2,0,1:T(8,128)(2,1)S(1)}, bf16[16,101,256]{2,0,1:T(8,128)(2,1)S(1)}, u32[]{:S(2)}, u32[]{:S(2)}) collective-permute-start(bf16[16,101,256]{2,0,1:T(8,128)(2,1)S(1)} %copy.28), channel_id=1, source_target_pairs={{0,1},{1,0},{2,3},{3,2},{4,5},{5,4},{6,7},{7,6},{8,9},{9,8},{10,11... | collective-permute-start | bytes 2482184 | tf_op jit(solution)/shard_map/ppermute | solution.py:36
  259.3 12.6 %collective-permute-start.37 = (bf16[8,101,256]{2,1,0:T(8,128)(2,1)S(1)}, bf16[8,101,256]{2,1,0:T(8,128)(2,1)S(1)}, u32[]{:S(2)}, u32[]{:S(2)}) collective-permute-start(bf16[8,101,256]{2,1,0:T(8,128)(2,1)S(1)} %add_convert_fusion.3), channel_id=1, source_target_pairs={{0,2},{1,3},{2,0},{3,1},{4,6},{5,7},{6,4},{7,5},{8,10},{9,11},{10,... | collective-permute-start | bytes 1241096 | tf_op jit(solution)/shard_map/ppermute | solution.py:40
  262.6 18.4 %collective-permute-start.39 = (bf16[8,101,256]{2,1,0:T(8,128)(2,1)S(1)}, bf16[8,101,256]{2,1,0:T(8,128)(2,1)S(1)}, u32[]{:S(2)}, u32[]{:S(2)}) collective-permute-start(bf16[8,101,256]{2,1,0:T(8,128)(2,1)S(1)} %add_convert_fusion.1), channel_id=1, source_target_pairs={{0,2},{1,3},{2,0},{3,1},{4,6},{5,7},{6,4},{7,5},{8,10},{9,11},{10,... | collective-permute-start | bytes 1241096 | tf_op jit(solution)/shard_map/ppermute | solution.py:40
  (21 other events, 116.4 us)

commit v4 on v3

--- a/solution.py
+++ b/solution.py
@@ -8,12 +8,11 @@
 LAGS = 101
 SRC_BLK = 64
 BINS = 250
-CHUNKS = 2
-PARTS = 4
+CHUNKS = 1
+PARTS = 2
 WIDE = 128 // CHUNKS
 ROWS = 128 // PARTS
 LAG_PAD = 112
-LAG = 2
 SMALL = pl.CostEstimate(flops=1 << 20, bytes_accessed=1 << 16, transcendentals=0)
 STRIDE = 264
 
@@ -186,7 +185,7 @@
         ),
         out_shape=[half, half],
         compiler_params=pltpu.CompilerParams(vmem_limit_bytes=50 << 20),
-        cost_estimate=SMALL,
+        cost_estimate=pl.CostEstimate(flops=20 * 10**9, bytes_accessed=24 << 20, transcendentals=0),
         name="correlate",
     )(blocks, table, sign, spec, *sources)
 
@@ -247,15 +246,18 @@
         arrivals.append(far_a + far_b)
     outs = []
     quarter = ROWS // 4
+    last = own_rows = None
     for part in range(PARTS):
-        at = blocks
-        if part >= LAG:
-            at, outs[part - LAG] = barrier((blocks, outs[part - LAG]))
         c = part * CHUNKS // PARTS
-        send, keep = correlate(part - c * PARTS // CHUNKS, at, table, sign, spec, arrivals[c])
+        send, keep = correlate(part - c * PARTS // CHUNKS, blocks, table, sign, spec, arrivals[c])
+        if last is not None:
+            send, last = barrier((send, last))
+            outs.append(finish(own_rows, last))
         near = swap_core(send)
+        own_rows = (keep[quarter:], near[quarter:])
         onward = (keep[:quarter].astype(jnp.float32) + near[:quarter].astype(jnp.float32)).astype(jnp.bfloat16)
-        outs.append(finish((keep[quarter:], near[quarter:]), swap_far(onward)))
+        last = swap_far(onward)
+    outs.append(finish(own_rows, last))
     return jnp.concatenate(outs)
 
 

time: 284 us -> 269 us (0.947); the launches traced: 283 us -> 264 us
  Pallas kernels: 77.2 us -> 57.5 us
  waiting for transfers between devices: 99.4 us -> 117 us
  starting transfers between devices: 65.7 us -> 52.2 us
  local copies, waits for them, and re-layouts: 29 us -> 24.9 us
    ppermute x15 -> x12, waiting for transfers between devices: 35.1 us -> 57.3 us  [shift_y(): return lax.ppermute(x, 'chan', pairs)]
    pallas_call x4 -> x2, Pallas kernels: 60.4 us -> 41.4 us  [correlate(): pl.pallas_call(correlate_kernel, grid_spec=pltpu.PrefetchScalarGridSpec(n...]
    ppermute x4 -> x2, waiting for transfers between devices: 0.01 us -> 6.31 us  [swap_core(): return lax.ppermute(x, 'tm', [(a, a ^ 1) for a in range(4)])]
    ppermute x4 -> x2, starting transfers between devices: 9.21 us -> 3.13 us  [swap_far(): return lax.ppermute(x, 'tm', [(a, a ^ 2) for a in range(4)])]
    ppermute x15 -> x12, waiting for transfers between devices: 34.8 us -> 28.9 us  [shift_x(): return lax.ppermute(x, 'chan', pairs)]
    ppermute x4 -> x2, waiting for transfers between devices: 23.7 us -> 18.8 us  [swap_far(): return lax.ppermute(x, 'tm', [(a, a ^ 2) for a in range(4)])]
    ppermute x15 -> x12, starting transfers between devices: 27 us -> 22.4 us  [shift_y(): return lax.ppermute(x, 'chan', pairs)]
    pallas_call x4 -> x1, local copies, waits for them, and re-layouts: 5.48 us -> 1.83 us  [correlate(): pl.pallas_call(correlate_kernel, grid_spec=pltpu.PrefetchScalarGridSpec(n...]
  transfers between devices with their start and end apart: 40 -> 30, of which waited for: 18 -> 17; matrix products, arithmetic and copies ran while one was open for 4% -> 2% of each run, Pallas kernels for 26% -> 13%
where the time goes in v4:
time: 269 us; the launch traced here: 264 us
  waiting for transfers between devices  117 us (43%)
  Pallas kernels  57.5 us (21%)
  starting transfers between devices  52.2 us (19%)
  local copies, waits for them, and re-layouts  24.9 us (9%)
  other arithmetic  12.4 us (5%)
    ppermute x12, waiting for transfers between devices, shift_y(): return lax.ppermute(x, 'chan', pairs)  57.3 us
    pallas_call x2, Pallas kernels, correlate(): pl.pallas_call(correlate_kernel, grid_spec=pltpu.PrefetchScalarGridSpec(n...  41.4 us
    ppermute x12, waiting for transfers between devices, shift_x(): return lax.ppermute(x, 'chan', pairs)  28.9 us
    ppermute x12, starting transfers between devices, shift_y(): return lax.ppermute(x, 'chan', pairs)  22.4 us
    ppermute x2, waiting for transfers between devices, swap_far(): return lax.ppermute(x, 'tm', [(a, a ^ 2) for a in range(4)])  18.8 us
    transpose x1, local copies, waits for them, and re-layouts, body(): spec = jnp.transpose(spectra, (2, 1, 0, 3)).reshape(BINS, 128, 256)  16.5 us
    pallas_call x4, Pallas kernels, pick_rows(): pl.pallas_call(pick_kernel, grid_spec=pltpu.PrefetchScalarGridSpec(num_sc...  15.9 us
    ppermute x12, starting transfers between devices, shift_x(): return lax.ppermute(x, 'chan', pairs)  15 us
  transfers between devices with their start and end apart: 30, of which 17 were waited for; matrix products, arithmetic and copies ran while one was open for 2% of the time, Pallas kernels for 13%

profile of v4, /device:TPU:1, one launch (start us, length us, event | category | flops | bytes accessed | tf_op | source)
XLA Modules:
  0.0 264.2 jit_solution(10452775150245388049)
XLA Ops:
  2.7 16.5 %copy.19 = bf16[250,2,64,256]{3,2,1,0:T(8,128)(2,1)} copy(bf16[250,2,64,256]{3,1,0,2:T(2,128)(2,1)} %bitcast.30) | data formatting | bytes 32768000 | tf_op jit(solution)/shard_map/transpose | solution.py:199
  19.4 3.6 %pick_rows.6 = (bf16[32,128,128]{2,1,0:T(8,128)(2,1)S(1)}, bf16[32,128,128]{2,1,0:T(8,128)(2,1)S(1)}) custom-call(s32[2]{0:T(128)S(1)} %get-tuple-element.101.first_ref, bf16[128,256]{1,0:T(8,128)(2,1)S(1)} %fusion.1.pick_ref, f32[1,128]{1,0:T(1,128)S(1)} %broadcast_in_dim_tile.3.mask_ref, bf16[250,128,256]{2,1,0:T(8,128)(2,1)} %bitcast.20, ...), custom_call_target="tpu_custom_call" | custom-call | flops 1048576 | bytes 65536 | tf_op jit(solution)/shard_map/pick_rows/pallas_call | solution.py:64
  23.0 3.7 %collective-permute-start.2 = (bf16[32,128,128]{2,1,0:T(8,128)(2,1)S(1)}, bf16[32,128,128]{2,1,0:T(8,128)(2,1)S(1)}, u32[]{:S(2)}, u32[]{:S(2)}) collective-permute-start(bf16[32,128,128]{2,1,0:T(8,128)(2,1)S(1)} %get-tuple-element.48), channel_id=1, source_target_pairs={{0,64},{4,68},{8,72},{12,76},{16,80},{20,84},{24,88},{28,92},{32,9... | collective-permute-start | bytes 3145736 | tf_op jit(solution)/shard_map/ppermute | solution.py:22
  26.7 2.9 %collective-permute-start.3 = (bf16[32,128,128]{2,1,0:T(8,128)(2,1)S(1)}, bf16[32,128,128]{2,1,0:T(8,128)(2,1)}, u32[]{:S(2)}, u32[]{:S(2)}) collective-permute-start(bf16[32,128,128]{2,1,0:T(8,128)(2,1)S(1)} %get-tuple-element.49), channel_id=1, source_target_pairs={{0,16},{4,20},{8,24},{12,28},{16,0},{20,4},{24,8},{28,12},{32,48},... | collective-permute-start | bytes 3145736 | tf_op jit(solution)/shard_map/ppermute | solution.py:27
  29.6 4.4 %pick_rows.7 = (bf16[32,128,128]{2,1,0:T(8,128)(2,1)}, bf16[32,128,128]{2,1,0:T(8,128)(2,1)}) custom-call(s32[2]{0:T(128)S(1)} %get-tuple-element.102.first_ref, bf16[128,256]{1,0:T(8,128)(2,1)S(1)} %fusion.1.pick_ref, f32[1,128]{1,0:T(1,128)S(1)} %broadcast_in_dim_tile.3.mask_ref, bf16[250,128,256]{2,1,0:T(8,128)(2,1)} %bitcast.22, ...), custom_call_target="tpu_custom_call" | custom-call | flops 1048576 | bytes 65536 | tf_op jit(solution)/shard_map/pick_rows/pallas_call | solution.py:64
  35.7 4.4 %pick_rows.5 = (bf16[32,128,128]{2,1,0:T(8,128)(2,1)}, bf16[32,128,128]{2,1,0:T(8,128)(2,1)}) custom-call(s32[2]{0:T(128)S(1)} %get-tuple-element.100.first_ref, bf16[128,256]{1,0:T(8,128)(2,1)S(1)} %fusion.1.pick_ref, f32[1,128]{1,0:T(1,128)S(1)} %broadcast_in_dim_tile.3.mask_ref, bf16[250,128,256]{2,1,0:T(8,128)(2,1)} %bitcast.24, ...), custom_call_target="tpu_custom_call" | custom-call | flops 1048576 | bytes 65536 | tf_op jit(solution)/shard_map/pick_rows/pallas_call | solution.py:64
  40.7 8.6 %collective-permute-done.2 = bf16[32,128,128]{2,1,0:T(8,128)(2,1)S(1)} collective-permute-done((bf16[32,128,128]{2,1,0:T(8,128)(2,1)S(1)}, bf16[32,128,128]{2,1,0:T(8,128)(2,1)S(1)}, u32[]{:S(2)}, u32[]{:S(2)}) %collective-permute-start.2) | collective-permute-done | bytes 1048608 | tf_op jit(solution)/shard_map/ppermute | solution.py:22
  50.8 3.6 %pick_rows.4 = (bf16[32,128,128]{2,1,0:T(8,128)(2,1)S(1)}, bf16[32,128,128]{2,1,0:T(8,128)(2,1)S(1)}) custom-call(s32[2]{0:T(128)S(1)} %get-tuple-element.99.first_ref, bf16[128,256]{1,0:T(8,128)(2,1)S(1)} %fusion.1.pick_ref, f32[1,128]{1,0:T(1,128)S(1)} %broadcast_in_dim_tile.3.mask_ref, bf16[250,128,256]{2,1,0:T(8,128)(2,1)} %bitcast.26, ...), custom_call_target="tpu_custom_call" | custom-call | flops 1048576 | bytes 65536 | tf_op jit(solution)/shard_map/pick_rows/pallas_call | solution.py:64
  54.4 17.8 %collective-permute-done.4 = bf16[32,128,128]{2,1,0:T(8,128)(2,1)} collective-permute-done((bf16[32,128,128]{2,1,0:T(8,128)(2,1)}, bf16[32,128,128]{2,1,0:T(8,128)(2,1)}, u32[]{:S(2)}, u32[]{:S(2)}) %collective-permute-start.4) | collective-permute-done | bytes 1048608 | tf_op jit(solution)/shard_map/ppermute | solution.py:22
  72.2 3.0 %collective-permute-done.5 = bf16[32,128,128]{2,1,0:T(8,128)(2,1)} collective-permute-done((bf16[32,128,128]{2,1,0:T(8,128)(2,1)}, bf16[32,128,128]{2,1,0:T(8,128)(2,1)}, u32[]{:S(2)}, u32[]{:S(2)}) %collective-permute-start.5) | collective-permute-done | bytes 1048608 | tf_op jit(solution)/shard_map/ppermute | solution.py:27
  75.2 2.7 %add_add_fusion.2 = (bf16[8,128,128]{2,1,0:T(8,128)(2,1)}, bf16[8,128,128]{2,1,0:T(8,128)(2,1)}, bf16[8,128,128]{2,1,0:T(8,128)(2,1)}) fusion(bf16[32,128,128]{2,1,0:T(8,128)(2,1)} %collective-permute-done.5, s32[]{:T(128)S(6)} %select_n.418, bf16[32,128,128]{2,1,0:T(8,128)(2,1)} %collective-permute-done.3, bf16[32,128,128]{2,1,0:T(8,128)(2,1)} %collective-permute-done.1, ...), kind=kLoop, calls=%fused_computation.7 | loop fusion | flops 1179648 | bytes 3932172 | tf_op jit(solution)/shard_map/add | solution.py:220
  80.2 2.3 add_add_fusion.3
  82.5 3.2 %collective-permute-start.10 = (bf16[8,128,128]{2,1,0:T(8,128)(2,1)}, bf16[8,128,128]{2,1,0:T(8,128)(2,1)}, u32[]{:S(2)}, u32[]{:S(2)}) collective-permute-start(bf16[8,128,128]{2,1,0:T(8,128)(2,1)} %get-tuple-element.88), channel_id=1, source_target_pairs={{0,24},{4,28},{8,0},{12,4},{16,8},{20,12},{24,16},{28,20},{32,56},... | collective-permute-start | bytes 786440 | tf_op jit(solution)/shard_map/ppermute | solution.py:27
  86.9 2.3 collective-permute-done.7
  89.3 7.1 %collective-permute-done.6 = bf16[8,128,128]{2,1,0:T(8,128)(2,1)} collective-permute-done((bf16[8,128,128]{2,1,0:T(8,128)(2,1)}, bf16[8,128,128]{2,1,0:T(8,128)(2,1)}, u32[]{:S(2)}, u32[]{:S(2)}) %collective-permute-start.6) | collective-permute-done | bytes 262176 | tf_op jit(solution)/shard_map/ppermute | solution.py:27
  101.0 2.3 collective-permute-done.13
  103.3 3.4 %collective-permute-done.12 = bf16[8,128,128]{2,1,0:T(8,128)(2,1)S(1)} collective-permute-done((bf16[8,128,128]{2,1,0:T(8,128)(2,1)S(1)}, bf16[8,128,128]{2,1,0:T(8,128)(2,1)S(1)}, u32[]{:S(2)}, u32[]{:S(2)}) %collective-permute-start.12) | collective-permute-done | bytes 262176 | tf_op jit(solution)/shard_map/ppermute | solution.py:31
  106.8 2.0 collective-permute-start.15
  113.3 3.8 %collective-permute-start.16 = (bf16[8,128,128]{2,1,0:T(8,128)(2,1)S(1)}, bf16[8,128,128]{2,1,0:T(8,128)(2,1)S(1)}, u32[]{:S(2)}, u32[]{:S(2)}) collective-permute-start(bf16[8,128,128]{2,1,0:T(8,128)(2,1)S(1)} %add.574.refs_0_), channel_id=1, source_target_pairs={{0,16},{4,20},{8,24},{12,28},{16,0},{20,4},{24,8},{28,12},{32,48},... | collective-permute-start | bytes 786440 | tf_op jit(solution)/shard_map/ppermute | solution.py:27
  117.1 3.9 %collective-permute-start.18 = (bf16[8,128,128]{2,1,0:T(8,128)(2,1)S(1)}, bf16[8,128,128]{2,1,0:T(8,128)(2,1)S(1)}, u32[]{:S(2)}, u32[]{:S(2)}) collective-permute-start(bf16[8,128,128]{2,1,0:T(8,128)(2,1)S(1)} %add.574.refs_0_), channel_id=1, source_target_pairs={{0,24},{4,28},{8,0},{12,4},{16,8},{20,12},{24,16},{28,20},{32,56},... | collective-permute-start | bytes 786440 | tf_op jit(solution)/shard_map/ppermute | solution.py:27
  121.0 4.0 %collective-permute-done.16.refs_2_ = bf16[8,128,128]{2,1,0:T(8,128)(2,1)S(1)} collective-permute-done((bf16[8,128,128]{2,1,0:T(8,128)(2,1)S(1)}, bf16[8,128,128]{2,1,0:T(8,128)(2,1)S(1)}, u32[]{:S(2)}, u32[]{:S(2)}) %collective-permute-start.16) | collective-permute-done | bytes 262176 | tf_op jit(solution)/shard_map/ppermute | solution.py:27
  125.0 2.1 collective-permute-done.18.refs_3_
  127.3 4.3 %collective-permute-start.23 = (bf16[32,128,128]{2,1,0:T(8,128)(2,1)S(1)}, bf16[32,128,128]{2,1,0:T(8,128)(2,1)}, u32[]{:S(2)}, u32[]{:S(2)}) collective-permute-start(bf16[32,128,128]{2,1,0:T(8,128)(2,1)S(1)} %assemble.3.refs_4_), channel_id=1, source_target_pairs={{0,16},{4,20},{8,24},{12,28},{16,0},{20,4},{24,8},{28,12},{32,48},... | collective-permute-start | bytes 3145736 | tf_op jit(solution)/shard_map/ppermute | solution.py:27
  133.5 15.5 %collective-permute-done.21.refs_5_ = bf16[32,128,128]{2,1,0:T(8,128)(2,1)S(1)} collective-permute-done((bf16[32,128,128]{2,1,0:T(8,128)(2,1)S(1)}, bf16[32,128,128]{2,1,0:T(8,128)(2,1)S(1)}, u32[]{:S(2)}, u32[]{:S(2)}) %collective-permute-start.21) | collective-permute-done | bytes 1048608 | tf_op jit(solution)/shard_map/ppermute | solution.py:27
  150.8 21.7 %collective-permute-done.23.refs_6_ = bf16[32,128,128]{2,1,0:T(8,128)(2,1)} collective-permute-done((bf16[32,128,128]{2,1,0:T(8,128)(2,1)S(1)}, bf16[32,128,128]{2,1,0:T(8,128)(2,1)}, u32[]{:S(2)}, u32[]{:S(2)}) %collective-permute-start.23) | collective-permute-done | bytes 1048608 | tf_op jit(solution)/shard_map/ppermute | solution.py:27
  172.5 3.7 %collective-permute-done.25.refs_7_ = bf16[32,128,128]{2,1,0:T(8,128)(2,1)} collective-permute-done((bf16[32,128,128]{2,1,0:T(8,128)(2,1)S(1)}, bf16[32,128,128]{2,1,0:T(8,128)(2,1)}, u32[]{:S(2)}, u32[]{:S(2)}) %collective-permute-start.25) | collective-permute-done | bytes 1048608 | tf_op jit(solution)/shard_map/ppermute | solution.py:27
  176.4 20.7 %correlate.2 = (bf16[32,101,256]{2,1,0:T(8,128)(2,1)}, bf16[32,101,256]{2,1,0:T(8,128)(2,1)}) custom-call(s32[8]{0:T(128)S(1)} %slice.33.blocks_ref, bf16[2,112,256]{2,1,0:T(8,128)(2,1)S(1)} %copy_bitcast_fusion.table_ref, bf16[1,128]{1,0:T(2,128)(2,1)S(1)} %fusion.17.sign_ref, bf16[250,128,256]{2,1,0:T(8,128)(2,1)} %bitcast.28, ...), custom_call_target="tpu_custom_call" | custom-call | flops 20000000000 | bytes 25165824 | tf_op jit(solution)/shard_map/correlate/pallas_call | solution.py:167
  198.9 9.2 %collective-permute-start.26 = (bf16[32,101,256]{2,0,1:T(8,128)(2,1)S(1)}, bf16[32,101,256]{2,0,1:T(8,128)(2,1)S(1)}, u32[]{:S(2)}, u32[]{:S(2)}) collective-permute-start(bf16[32,101,256]{2,0,1:T(8,128)(2,1)S(1)} %copy.20), channel_id=1, source_target_pairs={{0,1},{1,0},{2,3},{3,2},{4,5},{5,4},{6,7},{7,6},{8,9},{9,8},{10,11... | collective-permute-start | bytes 4964360 | tf_op jit(solution)/shard_map/ppermute | solution.py:35
  208.1 3.2 %collective-permute-done.26 = bf16[32,101,256]{2,0,1:T(8,128)(2,1)S(1)} collective-permute-done((bf16[32,101,256]{2,0,1:T(8,128)(2,1)S(1)}, bf16[32,101,256]{2,0,1:T(8,128)(2,1)S(1)}, u32[]{:S(2)}, u32[]{:S(2)}) %collective-permute-start.26) | collective-permute-done | bytes 1654816 | tf_op jit(solution)/shard_map/ppermute | solution.py:35
  213.3 20.7 %correlate.3 = (bf16[32,101,256]{2,1,0:T(8,128)(2,1)}, bf16[32,101,256]{2,1,0:T(8,128)(2,1)}) custom-call(s32[8]{0:T(128)S(1)} %slice.33.blocks_ref, bf16[2,112,256]{2,1,0:T(8,128)(2,1)S(1)} %copy_bitcast_fusion.table_ref, bf16[1,128]{1,0:T(2,128)(2,1)S(1)} %fusion.17.sign_ref, bf16[250,128,256]{2,1,0:T(8,128)(2,1)} %bitcast.29, ...), custom_call_target="tpu_custom_call" | custom-call | flops 20000000000 | bytes 25165824 | tf_op jit(solution)/shard_map/correlate/pallas_call | solution.py:167
  236.6 3.2 %collective-permute-done.28 = bf16[32,101,256]{2,0,1:T(8,128)(2,1)S(1)} collective-permute-done((bf16[32,101,256]{2,0,1:T(8,128)(2,1)S(1)}, bf16[32,101,256]{2,0,1:T(8,128)(2,1)S(1)}, u32[]{:S(2)}, u32[]{:S(2)}) %collective-permute-start.28) | collective-permute-done | bytes 1654816 | tf_op jit(solution)/shard_map/ppermute | solution.py:35
  243.0 18.8 %collective-permute-done.29 = bf16[16,101,256]{2,0,1:T(8,128)(2,1)S(1)} collective-permute-done((bf16[16,101,256]{2,0,1:T(8,128)(2,1)S(1)}, bf16[16,101,256]{2,0,1:T(8,128)(2,1)S(1)}, u32[]{:S(2)}, u32[]{:S(2)}) %collective-permute-start.29) | collective-permute-done | bytes 827424 | tf_op jit(solution)/shard_map/ppermute | solution.py:39
  (85 shorter events, 35.6 us)
Async XLA Ops:
  2.7 16.6 %copy-start.6 = (s32[64]{0:T(128)S(1)}, s32[64]{0:T(128)}, u32[]{:S(2)}) copy-start(s32[64]{0:T(128)} %param.5) | copy-start | bytes 772
  23.0 26.2 %collective-permute-start.2 = (bf16[32,128,128]{2,1,0:T(8,128)(2,1)S(1)}, bf16[32,128,128]{2,1,0:T(8,128)(2,1)S(1)}, u32[]{:S(2)}, u32[]{:S(2)}) collective-permute-start(bf16[32,128,128]{2,1,0:T(8,128)(2,1)S(1)} %get-tuple-element.48), channel_id=1, source_target_pairs={{0,64},{4,68},{8,72},{12,76},{16,80},{20,84},{24,88},{28,92},{32,9... | collective-permute-start | bytes 3145736 | tf_op jit(solution)/shard_map/ppermute | solution.py:22
  26.7 27.7 %collective-permute-start.3 = (bf16[32,128,128]{2,1,0:T(8,128)(2,1)S(1)}, bf16[32,128,128]{2,1,0:T(8,128)(2,1)}, u32[]{:S(2)}, u32[]{:S(2)}) collective-permute-start(bf16[32,128,128]{2,1,0:T(8,128)(2,1)S(1)} %get-tuple-element.49), channel_id=1, source_target_pairs={{0,16},{4,20},{8,24},{12,28},{16,0},{20,4},{24,8},{28,12},{32,48},... | collective-permute-start | bytes 3145736 | tf_op jit(solution)/shard_map/ppermute | solution.py:27
  34.0 38.2 %collective-permute-start.4 = (bf16[32,128,128]{2,1,0:T(8,128)(2,1)}, bf16[32,128,128]{2,1,0:T(8,128)(2,1)}, u32[]{:S(2)}, u32[]{:S(2)}) collective-permute-start(bf16[32,128,128]{2,1,0:T(8,128)(2,1)} %get-tuple-element.50), channel_id=1, source_target_pairs={{0,96},{4,100},{8,104},{12,108},{16,112},{20,116},{24,120},{28,124... | collective-permute-start | bytes 3145736 | tf_op jit(solution)/shard_map/ppermute | solution.py:22
  34.8 40.3 %collective-permute-start.5 = (bf16[32,128,128]{2,1,0:T(8,128)(2,1)}, bf16[32,128,128]{2,1,0:T(8,128)(2,1)}, u32[]{:S(2)}, u32[]{:S(2)}) collective-permute-start(bf16[32,128,128]{2,1,0:T(8,128)(2,1)} %get-tuple-element.51), channel_id=1, source_target_pairs={{0,24},{4,28},{8,0},{12,4},{16,8},{20,12},{24,16},{28,20},{32,56},... | collective-permute-start | bytes 3145736 | tf_op jit(solution)/shard_map/ppermute | solution.py:27
  40.1 35.1 %collective-permute-start = (bf16[32,128,128]{2,1,0:T(8,128)(2,1)}, bf16[32,128,128]{2,1,0:T(8,128)(2,1)}, u32[]{:S(2)}, u32[]{:S(2)}) collective-permute-start(bf16[32,128,128]{2,1,0:T(8,128)(2,1)} %get-tuple-element.46), channel_id=1, source_target_pairs={{0,32},{4,36},{8,40},{12,44},{16,48},{20,52},{24,56},{28,60},{32,6... | collective-permute-start | bytes 3145736 | tf_op jit(solution)/shard_map/ppermute | solution.py:22
  49.2 25.9 %collective-permute-start.1 = (bf16[32,128,128]{2,1,0:T(8,128)(2,1)}, bf16[32,128,128]{2,1,0:T(8,128)(2,1)}, u32[]{:S(2)}, u32[]{:S(2)}) collective-permute-start(bf16[32,128,128]{2,1,0:T(8,128)(2,1)} %get-tuple-element.47), channel_id=1, source_target_pairs={{0,8},{4,12},{8,16},{12,20},{16,24},{20,28},{24,0},{28,4},{32,40},... | collective-permute-start | bytes 3145736 | tf_op jit(solution)/shard_map/ppermute | solution.py:27
  77.9 7.8 %collective-permute-start.11 = (bf16[8,128,128]{2,1,0:T(8,128)(2,1)}, bf16[8,128,128]{2,1,0:T(8,128)(2,1)S(1)}, u32[]{:S(2)}, u32[]{:S(2)}) collective-permute-start(bf16[8,128,128]{2,1,0:T(8,128)(2,1)} %get-tuple-element.85), channel_id=1, source_target_pairs={{0,96},{4,100},{8,104},{12,108},{16,112},{20,116},{24,120},{28,124... | collective-permute-start | bytes 786440 | tf_op jit(solution)/shard_map/ppermute | solution.py:22
  78.7 10.5 %collective-permute-start.7 = (bf16[8,128,128]{2,1,0:T(8,128)(2,1)}, bf16[8,128,128]{2,1,0:T(8,128)(2,1)}, u32[]{:S(2)}, u32[]{:S(2)}) collective-permute-start(bf16[8,128,128]{2,1,0:T(8,128)(2,1)} %get-tuple-element.87), channel_id=1, source_target_pairs={{0,32},{4,36},{8,40},{12,44},{16,48},{20,52},{24,56},{28,60},{32,6... | collective-permute-start | bytes 786440 | tf_op jit(solution)/shard_map/ppermute | solution.py:22
  79.3 9.9 %collective-permute-start.9 = (bf16[8,128,128]{2,1,0:T(8,128)(2,1)}, bf16[8,128,128]{2,1,0:T(8,128)(2,1)}, u32[]{:S(2)}, u32[]{:S(2)}) collective-permute-start(bf16[8,128,128]{2,1,0:T(8,128)(2,1)} %get-tuple-element.86), channel_id=1, source_target_pairs={{0,64},{4,68},{8,72},{12,76},{16,80},{20,84},{24,88},{28,92},{32,9... | collective-permute-start | bytes 786440 | tf_op jit(solution)/shard_map/ppermute | solution.py:22
  82.5 6.8 %collective-permute-start.10 = (bf16[8,128,128]{2,1,0:T(8,128)(2,1)}, bf16[8,128,128]{2,1,0:T(8,128)(2,1)}, u32[]{:S(2)}, u32[]{:S(2)}) collective-permute-start(bf16[8,128,128]{2,1,0:T(8,128)(2,1)} %get-tuple-element.88), channel_id=1, source_target_pairs={{0,24},{4,28},{8,0},{12,4},{16,8},{20,12},{24,16},{28,20},{32,56},... | collective-permute-start | bytes 786440 | tf_op jit(solution)/shard_map/ppermute | solution.py:27
  85.7 10.8 %collective-permute-start.6 = (bf16[8,128,128]{2,1,0:T(8,128)(2,1)}, bf16[8,128,128]{2,1,0:T(8,128)(2,1)}, u32[]{:S(2)}, u32[]{:S(2)}) collective-permute-start(bf16[8,128,128]{2,1,0:T(8,128)(2,1)} %get-tuple-element.90), channel_id=1, source_target_pairs={{0,8},{4,12},{8,16},{12,20},{16,24},{20,28},{24,0},{28,4},{32,40},... | collective-permute-start | bytes 786440 | tf_op jit(solution)/shard_map/ppermute | solution.py:27
  85.7 10.8 %collective-permute-start.8 = (bf16[8,128,128]{2,1,0:T(8,128)(2,1)}, bf16[8,128,128]{2,1,0:T(8,128)(2,1)}, u32[]{:S(2)}, u32[]{:S(2)}) collective-permute-start(bf16[8,128,128]{2,1,0:T(8,128)(2,1)} %get-tuple-element.89), channel_id=1, source_target_pairs={{0,16},{4,20},{8,24},{12,28},{16,0},{20,4},{24,8},{28,12},{32,48},... | collective-permute-start | bytes 786440 | tf_op jit(solution)/shard_map/ppermute | solution.py:27
  97.8 5.5 %collective-permute-start.13 = (bf16[8,128,128]{2,1,0:T(8,128)(2,1)S(1)}, bf16[8,128,128]{2,1,0:T(8,128)(2,1)S(1)}, u32[]{:S(2)}, u32[]{:S(2)}) collective-permute-start(bf16[8,128,128]{2,1,0:T(8,128)(2,1)S(1)} %add_add_fusion), channel_id=1, source_target_pairs={{0,4},{4,0},{8,12},{12,8},{16,20},{20,16},{24,28},{28,24},{32,36},... | collective-permute-start | bytes 786440 | tf_op jit(solution)/shard_map/ppermute | solution.py:31
  100.9 5.8 %collective-permute-start.12 = (bf16[8,128,128]{2,1,0:T(8,128)(2,1)S(1)}, bf16[8,128,128]{2,1,0:T(8,128)(2,1)S(1)}, u32[]{:S(2)}, u32[]{:S(2)}) collective-permute-start(bf16[8,128,128]{2,1,0:T(8,128)(2,1)S(1)} %add_add_fusion.1), channel_id=1, source_target_pairs={{0,4},{4,0},{8,12},{12,8},{16,20},{20,16},{24,28},{28,24},{32,36},... | collective-permute-start | bytes 786440 | tf_op jit(solution)/shard_map/ppermute | solution.py:31
  106.8 10.3 %collective-permute-start.15 = (bf16[8,128,128]{2,1,0:T(8,128)(2,1)S(1)}, bf16[8,128,128]{2,1,0:T(8,128)(2,1)S(1)}, u32[]{:S(2)}, u32[]{:S(2)}) collective-permute-start(bf16[8,128,128]{2,1,0:T(8,128)(2,1)S(1)} %add.575.refs_0_), channel_id=1, source_target_pairs={{0,32},{4,36},{8,40},{12,44},{16,48},{20,52},{24,56},{28,60},{32,6... | collective-permute-start | bytes 786440 | tf_op jit(solution)/shard_map/ppermute | solution.py:22
  108.9 12.1 %collective-permute-start.17 = (bf16[8,128,128]{2,1,0:T(8,128)(2,1)S(1)}, bf16[8,128,128]{2,1,0:T(8,128)(2,1)S(1)}, u32[]{:S(2)}, u32[]{:S(2)}) collective-permute-start(bf16[8,128,128]{2,1,0:T(8,128)(2,1)S(1)} %add.575.refs_0_), channel_id=1, source_target_pairs={{0,64},{4,68},{8,72},{12,76},{16,80},{20,84},{24,88},{28,92},{32,9... | collective-permute-start | bytes 786440 | tf_op jit(solution)/shard_map/ppermute | solution.py:22
  110.6 10.4 %collective-permute-start.19 = (bf16[8,128,128]{2,1,0:T(8,128)(2,1)S(1)}, bf16[8,128,128]{2,1,0:T(8,128)(2,1)S(1)}, u32[]{:S(2)}, u32[]{:S(2)}) collective-permute-start(bf16[8,128,128]{2,1,0:T(8,128)(2,1)S(1)} %add.575.refs_0_), channel_id=1, source_target_pairs={{0,96},{4,100},{8,104},{12,108},{16,112},{20,116},{24,120},{28,124... | collective-permute-start | bytes 786440 | tf_op jit(solution)/shard_map/ppermute | solution.py:22
  112.6 8.4 %collective-permute-start.14 = (bf16[8,128,128]{2,1,0:T(8,128)(2,1)S(1)}, bf16[8,128,128]{2,1,0:T(8,128)(2,1)S(1)}, u32[]{:S(2)}, u32[]{:S(2)}) collective-permute-start(bf16[8,128,128]{2,1,0:T(8,128)(2,1)S(1)} %add.574.refs_0_), channel_id=1, source_target_pairs={{0,8},{4,12},{8,16},{12,20},{16,24},{20,28},{24,0},{28,4},{32,40},... | collective-permute-start | bytes 786440 | tf_op jit(solution)/shard_map/ppermute | solution.py:27
  113.3 11.7 %collective-permute-start.16 = (bf16[8,128,128]{2,1,0:T(8,128)(2,1)S(1)}, bf16[8,128,128]{2,1,0:T(8,128)(2,1)S(1)}, u32[]{:S(2)}, u32[]{:S(2)}) collective-permute-start(bf16[8,128,128]{2,1,0:T(8,128)(2,1)S(1)} %add.574.refs_0_), channel_id=1, source_target_pairs={{0,16},{4,20},{8,24},{12,28},{16,0},{20,4},{24,8},{28,12},{32,48},... | collective-permute-start | bytes 786440 | tf_op jit(solution)/shard_map/ppermute | solution.py:27
  117.1 10.0 %collective-permute-start.18 = (bf16[8,128,128]{2,1,0:T(8,128)(2,1)S(1)}, bf16[8,128,128]{2,1,0:T(8,128)(2,1)S(1)}, u32[]{:S(2)}, u32[]{:S(2)}) collective-permute-start(bf16[8,128,128]{2,1,0:T(8,128)(2,1)S(1)} %add.574.refs_0_), channel_id=1, source_target_pairs={{0,24},{4,28},{8,0},{12,4},{16,8},{20,12},{24,16},{28,20},{32,56},... | collective-permute-start | bytes 786440 | tf_op jit(solution)/shard_map/ppermute | solution.py:27
  127.2 49.2 %copy-start = (bf16[32,128,128]{2,1,0:T(8,128)(2,1)}, bf16[32,128,128]{2,1,0:T(8,128)(2,1)S(1)}, u32[]{:S(2)}) copy-start(bf16[32,128,128]{2,1,0:T(8,128)(2,1)S(1)} %assemble.3.refs_4_) | copy-start | bytes 3145732
  127.2 21.8 %collective-permute-start.21 = (bf16[32,128,128]{2,1,0:T(8,128)(2,1)S(1)}, bf16[32,128,128]{2,1,0:T(8,128)(2,1)S(1)}, u32[]{:S(2)}, u32[]{:S(2)}) collective-permute-start(bf16[32,128,128]{2,1,0:T(8,128)(2,1)S(1)} %assemble.3.refs_4_), channel_id=1, source_target_pairs={{0,8},{4,12},{8,16},{12,20},{16,24},{20,28},{24,0},{28,4},{32,40},... | collective-permute-start | bytes 3145736 | tf_op jit(solution)/shard_map/ppermute | solution.py:27
  127.3 45.2 %collective-permute-start.23 = (bf16[32,128,128]{2,1,0:T(8,128)(2,1)S(1)}, bf16[32,128,128]{2,1,0:T(8,128)(2,1)}, u32[]{:S(2)}, u32[]{:S(2)}) collective-permute-start(bf16[32,128,128]{2,1,0:T(8,128)(2,1)S(1)} %assemble.3.refs_4_), channel_id=1, source_target_pairs={{0,16},{4,20},{8,24},{12,28},{16,0},{20,4},{24,8},{28,12},{32,48},... | collective-permute-start | bytes 3145736 | tf_op jit(solution)/shard_map/ppermute | solution.py:27
  131.6 44.6 %collective-permute-start.25 = (bf16[32,128,128]{2,1,0:T(8,128)(2,1)S(1)}, bf16[32,128,128]{2,1,0:T(8,128)(2,1)}, u32[]{:S(2)}, u32[]{:S(2)}) collective-permute-start(bf16[32,128,128]{2,1,0:T(8,128)(2,1)S(1)} %assemble.3.refs_4_), channel_id=1, source_target_pairs={{0,24},{4,28},{8,0},{12,4},{16,8},{20,12},{24,16},{28,20},{32,56},... | collective-permute-start | bytes 3145736 | tf_op jit(solution)/shard_map/ppermute | solution.py:27
  131.7 44.5 %collective-permute-start.20 = (bf16[32,128,128]{2,1,0:T(8,128)(2,1)S(1)}, bf16[32,128,128]{2,1,0:T(8,128)(2,1)S(1)}, u32[]{:S(2)}, u32[]{:S(2)}) collective-permute-start(bf16[32,128,128]{2,1,0:T(8,128)(2,1)S(1)} %assemble.2.refs_0_), channel_id=1, source_target_pairs={{0,32},{4,36},{8,40},{12,44},{16,48},{20,52},{24,56},{28,60},{32,6... | collective-permute-start | bytes 3145736 | tf_op jit(solution)/shard_map/ppermute | solution.py:22
  131.7 44.4 %collective-permute-start.22 = (bf16[32,128,128]{2,1,0:T(8,128)(2,1)S(1)}, bf16[32,128,128]{2,1,0:T(8,128)(2,1)}, u32[]{:S(2)}, u32[]{:S(2)}) collective-permute-start(bf16[32,128,128]{2,1,0:T(8,128)(2,1)S(1)} %assemble.2.refs_0_), channel_id=1, source_target_pairs={{0,64},{4,68},{8,72},{12,76},{16,80},{20,84},{24,88},{28,92},{32,9... | collective-permute-start | bytes 3145736 | tf_op jit(solution)/shard_map/ppermute | solution.py:22
  150.0 26.4 %collective-permute-start.24 = (bf16[32,128,128]{2,1,0:T(8,128)(2,1)S(1)}, bf16[32,128,128]{2,1,0:T(8,128)(2,1)}, u32[]{:S(2)}, u32[]{:S(2)}) collective-permute-start(bf16[32,128,128]{2,1,0:T(8,128)(2,1)S(1)} %assemble.2.refs_0_), channel_id=1, source_target_pairs={{0,96},{4,100},{8,104},{12,108},{16,112},{20,116},{24,120},{28,124... | collective-permute-start | bytes 3145736 | tf_op jit(solution)/shard_map/ppermute | solution.py:22
  198.9 12.3 %collective-permute-start.26 = (bf16[32,101,256]{2,0,1:T(8,128)(2,1)S(1)}, bf16[32,101,256]{2,0,1:T(8,128)(2,1)S(1)}, u32[]{:S(2)}, u32[]{:S(2)}) collective-permute-start(bf16[32,101,256]{2,0,1:T(8,128)(2,1)S(1)} %copy.20), channel_id=1, source_target_pairs={{0,1},{1,0},{2,3},{3,2},{4,5},{5,4},{6,7},{7,6},{8,9},{9,8},{10,11... | collective-permute-start | bytes 4964360 | tf_op jit(solution)/shard_map/ppermute | solution.py:35
  212.0 22.1 %collective-permute-start.27 = (bf16[16,101,256]{2,0,1:T(8,128)(2,1)S(1)}, bf16[16,101,256]{2,0,1:T(8,128)(2,1)S(1)}, u32[]{:S(2)}, u32[]{:S(2)}) collective-permute-start(bf16[16,101,256]{2,0,1:T(8,128)(2,1)S(1)} %copy.23), channel_id=1, source_target_pairs={{0,2},{1,3},{2,0},{3,1},{4,6},{5,7},{6,4},{7,5},{8,10},{9,11},{10,... | collective-permute-start | bytes 2482184 | tf_op jit(solution)/shard_map/ppermute | solution.py:39
  235.9 3.9 %collective-permute-start.28 = (bf16[32,101,256]{2,0,1:T(8,128)(2,1)S(1)}, bf16[32,101,256]{2,0,1:T(8,128)(2,1)S(1)}, u32[]{:S(2)}, u32[]{:S(2)}) collective-permute-start(bf16[32,101,256]{2,0,1:T(8,128)(2,1)S(1)} %copy.25), channel_id=1, source_target_pairs={{0,1},{1,0},{2,3},{3,2},{4,5},{5,4},{6,7},{7,6},{8,9},{9,8},{10,11... | collective-permute-start | bytes 4964360 | tf_op jit(solution)/shard_map/ppermute | solution.py:35
  240.5 21.2 %collective-permute-start.29 = (bf16[16,101,256]{2,0,1:T(8,128)(2,1)S(1)}, bf16[16,101,256]{2,0,1:T(8,128)(2,1)S(1)}, u32[]{:S(2)}, u32[]{:S(2)}) collective-permute-start(bf16[16,101,256]{2,0,1:T(8,128)(2,1)S(1)} %copy.28), channel_id=1, source_target_pairs={{0,2},{1,3},{2,0},{3,1},{4,6},{5,7},{6,4},{7,5},{8,10},{9,11},{10,... | collective-permute-start | bytes 2482184 | tf_op jit(solution)/shard_map/ppermute | solution.py:39
  (5 other events, 24.1 us)

commit v5 on v4

--- a/solution.py
+++ b/solution.py
@@ -8,9 +8,7 @@
 LAGS = 101
 SRC_BLK = 64
 BINS = 250
-CHUNKS = 1
 PARTS = 2
-WIDE = 128 // CHUNKS
 ROWS = 128 // PARTS
 LAG_PAD = 112
 SMALL = pl.CostEstimate(flops=1 << 20, bytes_accessed=1 << 16, transcendentals=0)
@@ -82,10 +80,9 @@
 
 
 def assemble_kernel(at_ref, *refs):
-    for e in range(4):
+    for m, e in enumerate((0, 1, 3, 2)):
         place = pl.ds(8 * lax.rem(at_ref[0] + 4 - e, 4), 8)
-        for c in range(CHUNKS):
-            refs[4 + c][place] = refs[e][:, c * WIDE : (c + 1) * WIDE]
+        refs[4][place] = refs[m][...]
 
 
 def assemble(at, pieces):
@@ -96,25 +93,23 @@
             num_scalar_prefetch=1,
             grid=(1,),
             in_specs=[piece] * 4,
-            out_specs=[pl.BlockSpec((32, WIDE, 128), lambda i, s: (0, 0, 0))] * CHUNKS,
+            out_specs=pl.BlockSpec((32, 128, 128), lambda i, s: (0, 0, 0)),
         ),
-        out_shape=[jax.ShapeDtypeStruct((32, WIDE, 128), jnp.bfloat16)] * CHUNKS,
+        out_shape=jax.ShapeDtypeStruct((32, 128, 128), jnp.bfloat16),
         compiler_params=pltpu.CompilerParams(vmem_limit_bytes=8 << 20),
         cost_estimate=SMALL,
         name="assemble",
     )(at, *pieces)
 
 
-def correlate_kernel(blocks_ref, table_ref, sign_ref, spec_ref, *refs):
-    sources, (send_ref, keep_ref, src, left, right, acc) = refs[:8], refs[8:]
+def cross_blocks(blocks_ref, sign_ref, spec_ref, sources, src, left, right):
     step = pl.program_id(0)
-    for m in range(8):
+    for m in range(4):
 
         @pl.when(step == m)
         def _():
             src[...] = sources[m][...]
 
-    base = lax.rem(step, 4) * 32
     last = BINS - 1 - 32 * blocks_ref[step]
     sign = sign_ref[...]
 
@@ -127,67 +122,90 @@
             both = jnp.concatenate([rows, turned], axis=0)
             cross = jnp.dot(both, spec_ref[jnp.minimum(i, last)], preferred_element_type=jnp.float32)
             for part in range(2):
-                place = pl.ds(part * 128 + base + i, ROWS, stride=STRIDE)
+                place = pl.ds(part * 128 + step * 32 + i, ROWS, stride=STRIDE)
                 piece = cross[part * ROWS : (part + 1) * ROWS]
                 left[place, :] = piece[:, :128]
                 right[place, :] = piece[:, 128:]
 
-    def lags(k):
-        rows = pl.ds(pl.multiple_of(k * STRIDE, 8), 256)
-        cross = jnp.concatenate(
-            [left[rows, :].astype(jnp.bfloat16), right[rows, :].astype(jnp.bfloat16)], axis=1
-        )
-        return jnp.dot(table_ref[0], cross, preferred_element_type=jnp.float32)
-
-    @pl.when(step == 3)
+
+def lag_sums(k, table_ref, left, right):
+    rows = pl.ds(pl.multiple_of(k * STRIDE, 8), 256)
+    cross = jnp.concatenate([left[rows, :].astype(jnp.bfloat16), right[rows, :].astype(jnp.bfloat16)], axis=1)
+    return jnp.dot(table_ref[...], cross, preferred_element_type=jnp.float32)
+
+
+def early_kernel(blocks_ref, table_ref, sign_ref, spec_ref, *refs):
+    sources, (acc_ref, src, left, right) = refs[:4], refs[4:]
+    cross_blocks(blocks_ref, sign_ref, spec_ref, sources, src, left, right)
+
+    @pl.when(pl.program_id(0) == 3)
     def _():
         @pl.loop(0, ROWS, step=8)
         def _(first):
             for u in range(8):
-                acc[first + u] = lags(first + u)
-
-    @pl.when(step == 7)
+                acc_ref[first + u] = lag_sums(first + u, table_ref, left, right)
+
+
+def late_kernel(blocks_ref, table_ref, sign_ref, spec_ref, *refs):
+    sources, (before_ref, send_ref, keep_ref, src, left, right, acc, sem) = refs[:4], refs[4:]
+    step = pl.program_id(0)
+    fetch = pltpu.make_async_copy(before_ref, acc, sem)
+
+    @pl.when(step == 0)
     def _():
+        fetch.start()
+
+    cross_blocks(blocks_ref, sign_ref, spec_ref, sources, src, left, right)
+
+    @pl.when(step == 3)
+    def _():
+        fetch.wait()
+
         @pl.loop(0, ROWS // 2, step=8)
         def _(first):
             for u in range(8):
                 k = first + u
-                send_ref[k] = (acc[k] + lags(k))[:LAGS].astype(jnp.bfloat16)
+                send_ref[k] = (acc[k] + lag_sums(k, table_ref, left, right))[:LAGS].astype(jnp.bfloat16)
 
         @pl.loop(0, ROWS // 2, step=8)
         def _(first):
             for u in range(8):
                 k = first + u + ROWS // 2
-                keep_ref[first + u] = (acc[k] + lags(k))[:LAGS].astype(jnp.bfloat16)
-
-
-def correlate(part, blocks, table, sign, spec, sources):
+                keep_ref[first + u] = (acc[k] + lag_sums(k, table_ref, left, right))[:LAGS].astype(jnp.bfloat16)
+
+
+def correlate(part, blocks, table, sign, spec, sources, before=None):
     half = jax.ShapeDtypeStruct((ROWS // 2, LAGS, 256), jnp.bfloat16)
+    sums = jax.ShapeDtypeStruct((ROWS, LAG_PAD, 256), jnp.float32)
+    early = before is None
     whole = pl.BlockSpec((ROWS // 2, LAGS, 256), lambda i, s: (0, 0, 0))
+    scratch = [
+        pltpu.VMEM((32, ROWS, 128), jnp.bfloat16),
+        pltpu.VMEM((ROWS * STRIDE, 128), jnp.float32),
+        pltpu.VMEM((ROWS * STRIDE, 128), jnp.float32),
+    ]
+    if not early:
+        scratch += [pltpu.VMEM((ROWS, LAG_PAD, 256), jnp.float32), pltpu.SemaphoreType.DMA]
     return pl.pallas_call(
-        correlate_kernel,
+        early_kernel if early else late_kernel,
         grid_spec=pltpu.PrefetchScalarGridSpec(
             num_scalar_prefetch=1,
-            grid=(8,),
+            grid=(4,),
             in_specs=[
-                pl.BlockSpec((1, LAG_PAD, 256), lambda i, s: (i // 4, 0, 0)),
+                pl.BlockSpec((LAG_PAD, 256), lambda i, s: (0, 0)),
                 pl.BlockSpec((1, 128), lambda i, s: (0, 0)),
                 pl.BlockSpec((32, 128, 256), lambda i, s: (s[i], 0, 0)),
             ]
-            + [pl.BlockSpec((32, ROWS, 128), lambda i, s: (0, part, 0))] * 8,
-            out_specs=[whole, whole],
-            scratch_shapes=[
-                pltpu.VMEM((32, ROWS, 128), jnp.bfloat16),
-                pltpu.VMEM((ROWS * STRIDE, 128), jnp.float32),
-                pltpu.VMEM((ROWS * STRIDE, 128), jnp.float32),
-                pltpu.VMEM((ROWS, LAG_PAD, 256), jnp.float32),
-            ],
+            + [pl.BlockSpec((32, ROWS, 128), lambda i, s: (0, part, 0))] * 4
+            + ([] if early else [pl.BlockSpec(memory_space=pl.ANY)]),
+            out_specs=pl.BlockSpec((ROWS, LAG_PAD, 256), lambda i, s: (0, 0, 0)) if early else [whole, whole],
+            scratch_shapes=scratch,
         ),
-        out_shape=[half, half],
-        compiler_params=pltpu.CompilerParams(vmem_limit_bytes=50 << 20),
-        cost_estimate=pl.CostEstimate(flops=20 * 10**9, bytes_accessed=24 << 20, transcendentals=0),
-        name="correlate",
-    )(blocks, table, sign, spec, *sources)
+        out_shape=sums if early else [half, half],
+        compiler_params=pltpu.CompilerParams(vmem_limit_bytes=46 << 20),
+        cost_estimate=pl.CostEstimate(flops=12 * 10**9, bytes_accessed=16 << 20, transcendentals=0),
+        name="correlate_early" if early else "correlate_late",
+    )(blocks, table, sign, spec, *sources, *([] if early else [before]))
 
 
 def body(spectra, src_blocks, valid):
@@ -226,30 +244,29 @@
     piece_a, piece_b = piece_a + far_a, piece_b + far_b
 
     def gather(a, b, shift_a, shift_b):
-        come = {d: (shift_a(a, d), shift_b(b, d)) for d in (1, 3, 2)}
-        come = barrier(come)
-        return [a, come[1][0], come[2][0], come[3][0]], [b, come[1][1], come[2][1], come[3][1]]
+        return [a] + [shift_a(a, d) for d in (1, 3, 2)], [b] + [shift_b(b, d) for d in (1, 3, 2)]
 
     near_a, near_b = gather(piece_a, piece_b, shift_y, shift_x)
+    near_a, near_b = barrier((near_a, near_b))
     inner_a, inner_b = assemble(y[None], near_a), assemble(x[None], near_b)
 
-    i = jnp.arange(256, dtype=jnp.int32)
-    e = i % 128 // 32
-    blocks_at = jnp.where(i < 128, (x - e) % 4, 4 + (y - e) % 4)
-    table = lag_table(32 * blocks_at + i % 32, LAG_PAD, 256)
+    far_a, far_b = gather(inner_a, inner_b, shift_x, shift_y)
+    arrivals = [far_a[0], far_b[0], far_a[1], far_a[2], far_b[1], far_b[2], far_a[3], far_b[3]]
+    blocks = jnp.stack(
+        [x, 4 + y, (x + 3) % 4, (x + 1) % 4, 4 + (y + 3) % 4, 4 + (y + 1) % 4, (x + 2) % 4, 4 + (y + 2) % 4]
+    )
+    freqs = (32 * blocks[:, None] + jnp.arange(32, dtype=jnp.int32)[None, :]).reshape(256)
+    table = lag_table(freqs, LAG_PAD, 256)
     table = table.reshape(2, LAG_PAD, 2, 128).transpose(2, 1, 0, 3).reshape(2, LAG_PAD, 256)
-    blocks = blocks_at[::32]
-
-    arrivals = []
-    for c in range(CHUNKS):
-        far_a, far_b = gather(inner_a[c], inner_b[c], shift_x, shift_y)
-        arrivals.append(far_a + far_b)
+    sums = [correlate(part, blocks[:4], table[0], sign, spec, arrivals[:4]) for part in range(PARTS)]
+
+    sums = barrier(sums)
+
     outs = []
     quarter = ROWS // 4
     last = own_rows = None
     for part in range(PARTS):
-        c = part * CHUNKS // PARTS
-        send, keep = correlate(part - c * PARTS // CHUNKS, blocks, table, sign, spec, arrivals[c])
+        send, keep = correlate(part, blocks[4:], table[1], sign, spec, arrivals[4:], sums[part])
         if last is not None:
             send, last = barrier((send, last))
             outs.append(finish(own_rows, last))

time: 269 us -> 276 us (1.026); the launches traced: 264 us -> 276 us
  starting transfers between devices: 52.2 us -> 77.6 us
  waiting for transfers between devices: 117 us -> 101 us
  Pallas kernels: 57.5 us -> 63 us
  local copies, waits for them, and re-layouts: 24.9 us -> 21.5 us
    ppermute x12, waiting for transfers between devices: 57.3 us -> 14.9 us  [shift_y(): return lax.ppermute(x, 'chan', pairs)]
    ppermute x12, waiting for transfers between devices: 28.9 us -> 47.4 us  [shift_x(): return lax.ppermute(x, 'chan', pairs)]
    ppermute x2, starting transfers between devices: 9.93 us -> 27.3 us  [swap_core(): return lax.ppermute(x, 'tm', [(a, a ^ 1) for a in range(4)])]
    ppermute x2, waiting for transfers between devices: 18.8 us -> 25.3 us  [swap_far(): return lax.ppermute(x, 'tm', [(a, a ^ 2) for a in range(4)])]
    pallas_call x2 -> x4, Pallas kernels: 41.4 us -> 47 us  [correlate(): pl.pallas_call(early_kernel if early else late_kernel, grid_spec=pltpu.Pr...]
    ppermute x12, starting transfers between devices: 22.4 us -> 26.5 us  [shift_y(): return lax.ppermute(x, 'chan', pairs)]
    ppermute x2, starting transfers between devices: 3.13 us -> 6.44 us  [swap_far(): return lax.ppermute(x, 'tm', [(a, a ^ 2) for a in range(4)])]
  transfers between devices with their start and end apart: 30 -> 30, of which waited for: 17 -> 18; matrix products, arithmetic and copies ran while one was open for 2% -> 2% of each run, Pallas kernels for 13% -> 18%
where the time goes in v5:
time: 276 us
  waiting for transfers between devices  101 us (37%)
  starting transfers between devices  77.6 us (28%)
  Pallas kernels  63 us (23%)
  local copies, waits for them, and re-layouts  21.5 us (8%)
  other arithmetic  12.4 us (4%)
    ppermute x12, waiting for transfers between devices, shift_x(): return lax.ppermute(x, 'chan', pairs)  47.4 us
    pallas_call x4, Pallas kernels, correlate(): pl.pallas_call(early_kernel if early else late_kernel, grid_spec=pltpu.Pr...  47 us
    ppermute x2, starting transfers between devices, swap_core(): return lax.ppermute(x, 'tm', [(a, a ^ 1) for a in range(4)])  27.3 us
    ppermute x12, starting transfers between devices, shift_y(): return lax.ppermute(x, 'chan', pairs)  26.5 us
    ppermute x2, waiting for transfers between devices, swap_far(): return lax.ppermute(x, 'tm', [(a, a ^ 2) for a in range(4)])  25.3 us
    transpose x1, local copies, waits for them, and re-layouts, body(): spec = jnp.transpose(spectra, (2, 1, 0, 3)).reshape(BINS, 128, 256)  16.6 us
    pallas_call x4, Pallas kernels, pick_rows(): pl.pallas_call(pick_kernel, grid_spec=pltpu.PrefetchScalarGridSpec(num_sc...  15.9 us
    ppermute x12, starting transfers between devices, shift_x(): return lax.ppermute(x, 'chan', pairs)  15.4 us
  transfers between devices with their start and end apart: 30, of which 18 were waited for; matrix products, arithmetic and copies ran while one was open for 2% of the time, Pallas kernels for 18%

profile of v5, /device:TPU:1, one launch (start us, length us, event | category | flops | bytes accessed | tf_op | source)
XLA Modules:
  0.0 276.0 jit_solution(18161291178357157300)
XLA Ops:
  2.9 16.6 %copy.19 = bf16[250,2,64,256]{3,2,1,0:T(8,128)(2,1)} copy(bf16[250,2,64,256]{3,1,0,2:T(2,128)(2,1)} %bitcast.49) | data formatting | bytes 32768000 | tf_op jit(solution)/shard_map/transpose | solution.py:217
  19.6 3.6 %pick_rows.5 = (bf16[32,128,128]{2,1,0:T(8,128)(2,1)S(1)}, bf16[32,128,128]{2,1,0:T(8,128)(2,1)S(1)}) custom-call(s32[2]{0:T(128)S(1)} %get-tuple-element.98.first_ref, bf16[128,256]{1,0:T(8,128)(2,1)S(1)} %fusion.1.pick_ref, f32[1,128]{1,0:T(1,128)S(1)} %broadcast_in_dim_tile.3.mask_ref, bf16[250,128,256]{2,1,0:T(8,128)(2,1)} %bitcast.37, ...), custom_call_target="tpu_custom_call" | custom-call | flops 1048576 | bytes 65536 | tf_op jit(solution)/shard_map/pick_rows/pallas_call | solution.py:62
  26.7 4.4 %pick_rows.6 = (bf16[32,128,128]{2,1,0:T(8,128)(2,1)}, bf16[32,128,128]{2,1,0:T(8,128)(2,1)}) custom-call(s32[2]{0:T(128)S(1)} %get-tuple-element.99.first_ref, bf16[128,256]{1,0:T(8,128)(2,1)S(1)} %fusion.1.pick_ref, f32[1,128]{1,0:T(1,128)S(1)} %broadcast_in_dim_tile.3.mask_ref, bf16[250,128,256]{2,1,0:T(8,128)(2,1)} %bitcast.39, ...), custom_call_target="tpu_custom_call" | custom-call | flops 1048576 | bytes 65536 | tf_op jit(solution)/shard_map/pick_rows/pallas_call | solution.py:62
  31.1 2.4 collective-permute-start.2
  33.5 2.6 collective-permute-start.3
  36.2 4.4 %pick_rows.7 = (bf16[32,128,128]{2,1,0:T(8,128)(2,1)}, bf16[32,128,128]{2,1,0:T(8,128)(2,1)}) custom-call(s32[2]{0:T(128)S(1)} %get-tuple-element.100.first_ref, bf16[128,256]{1,0:T(8,128)(2,1)S(1)} %fusion.1.pick_ref, f32[1,128]{1,0:T(1,128)S(1)} %broadcast_in_dim_tile.3.mask_ref, bf16[250,128,256]{2,1,0:T(8,128)(2,1)} %bitcast.41, ...), custom_call_target="tpu_custom_call" | custom-call | flops 1048576 | bytes 65536 | tf_op jit(solution)/shard_map/pick_rows/pallas_call | solution.py:62
  41.7 7.4 %collective-permute-done = bf16[32,128,128]{2,1,0:T(8,128)(2,1)S(1)} collective-permute-done((bf16[32,128,128]{2,1,0:T(8,128)(2,1)S(1)}, bf16[32,128,128]{2,1,0:T(8,128)(2,1)S(1)}, u32[]{:S(2)}, u32[]{:S(2)}) %collective-permute-start) | collective-permute-done | bytes 1048608 | tf_op jit(solution)/shard_map/ppermute | solution.py:20
  49.1 3.1 %collective-permute-start.5 = (bf16[32,128,128]{2,1,0:T(8,128)(2,1)}, bf16[32,128,128]{2,1,0:T(8,128)(2,1)}, u32[]{:S(2)}, u32[]{:S(2)}) collective-permute-start(bf16[32,128,128]{2,1,0:T(8,128)(2,1)} %get-tuple-element.49), channel_id=1, source_target_pairs={{0,24},{4,28},{8,0},{12,4},{16,8},{20,12},{24,16},{28,20},{32,56},... | collective-permute-start | bytes 3145736 | tf_op jit(solution)/shard_map/ppermute | solution.py:25
  52.2 3.6 %pick_rows.4 = (bf16[32,128,128]{2,1,0:T(8,128)(2,1)S(1)}, bf16[32,128,128]{2,1,0:T(8,128)(2,1)S(1)}) custom-call(s32[2]{0:T(128)S(1)} %get-tuple-element.97.first_ref, bf16[128,256]{1,0:T(8,128)(2,1)S(1)} %fusion.1.pick_ref, f32[1,128]{1,0:T(1,128)S(1)} %broadcast_in_dim_tile.3.mask_ref, bf16[250,128,256]{2,1,0:T(8,128)(2,1)} %bitcast.43, ...), custom_call_target="tpu_custom_call" | custom-call | flops 1048576 | bytes 65536 | tf_op jit(solution)/shard_map/pick_rows/pallas_call | solution.py:62
  55.8 17.1 %collective-permute-done.2 = bf16[32,128,128]{2,1,0:T(8,128)(2,1)} collective-permute-done((bf16[32,128,128]{2,1,0:T(8,128)(2,1)}, bf16[32,128,128]{2,1,0:T(8,128)(2,1)}, u32[]{:S(2)}, u32[]{:S(2)}) %collective-permute-start.2) | collective-permute-done | bytes 1048608 | tf_op jit(solution)/shard_map/ppermute | solution.py:20
  74.0 4.5 %collective-permute-done.4 = bf16[32,128,128]{2,1,0:T(8,128)(2,1)} collective-permute-done((bf16[32,128,128]{2,1,0:T(8,128)(2,1)}, bf16[32,128,128]{2,1,0:T(8,128)(2,1)}, u32[]{:S(2)}, u32[]{:S(2)}) %collective-permute-start.4) | collective-permute-done | bytes 1048608 | tf_op jit(solution)/shard_map/ppermute | solution.py:20
  81.0 2.6 add_add_fusion.2
  88.4 3.2 %collective-permute-start.10 = (bf16[8,128,128]{2,1,0:T(8,128)(2,1)}, bf16[8,128,128]{2,1,0:T(8,128)(2,1)}, u32[]{:S(2)}, u32[]{:S(2)}) collective-permute-start(bf16[8,128,128]{2,1,0:T(8,128)(2,1)} %get-tuple-element.84), channel_id=1, source_target_pairs={{0,24},{4,28},{8,0},{12,4},{16,8},{20,12},{24,16},{28,20},{32,56},... | collective-permute-start | bytes 786440 | tf_op jit(solution)/shard_map/ppermute | solution.py:25
  93.3 3.7 %collective-permute-done.9 = bf16[8,128,128]{2,1,0:T(8,128)(2,1)} collective-permute-done((bf16[8,128,128]{2,1,0:T(8,128)(2,1)}, bf16[8,128,128]{2,1,0:T(8,128)(2,1)}, u32[]{:S(2)}, u32[]{:S(2)}) %collective-permute-start.9) | collective-permute-done | bytes 262176 | tf_op jit(solution)/shard_map/ppermute | solution.py:20
  97.4 3.6 %collective-permute-done.6 = bf16[8,128,128]{2,1,0:T(8,128)(2,1)} collective-permute-done((bf16[8,128,128]{2,1,0:T(8,128)(2,1)}, bf16[8,128,128]{2,1,0:T(8,128)(2,1)}, u32[]{:S(2)}, u32[]{:S(2)}) %collective-permute-start.6) | collective-permute-done | bytes 262176 | tf_op jit(solution)/shard_map/ppermute | solution.py:25
  101.0 3.0 %collective-permute-done.8 = bf16[8,128,128]{2,1,0:T(8,128)(2,1)} collective-permute-done((bf16[8,128,128]{2,1,0:T(8,128)(2,1)}, bf16[8,128,128]{2,1,0:T(8,128)(2,1)}, u32[]{:S(2)}, u32[]{:S(2)}) %collective-permute-start.8) | collective-permute-done | bytes 262176 | tf_op jit(solution)/shard_map/ppermute | solution.py:25
  110.8 5.1 %collective-permute-done.12 = bf16[8,128,128]{2,1,0:T(8,128)(2,1)S(1)} collective-permute-done((bf16[8,128,128]{2,1,0:T(8,128)(2,1)S(1)}, bf16[8,128,128]{2,1,0:T(8,128)(2,1)S(1)}, u32[]{:S(2)}, u32[]{:S(2)}) %collective-permute-start.12) | collective-permute-done | bytes 262176 | tf_op jit(solution)/shard_map/ppermute | solution.py:29
  122.7 2.9 %collective-permute-start.16 = (bf16[8,128,128]{2,1,0:T(8,128)(2,1)S(1)}, bf16[8,128,128]{2,1,0:T(8,128)(2,1)S(1)}, u32[]{:S(2)}, u32[]{:S(2)}) collective-permute-start(bf16[8,128,128]{2,1,0:T(8,128)(2,1)S(1)} %add.520.refs_0_), channel_id=1, source_target_pairs={{0,16},{4,20},{8,24},{12,28},{16,0},{20,4},{24,8},{28,12},{32,48},... | collective-permute-start | bytes 786440 | tf_op jit(solution)/shard_map/ppermute | solution.py:25
  127.5 4.4 %collective-permute-done.16.refs_3_ = bf16[8,128,128]{2,1,0:T(8,128)(2,1)S(1)} collective-permute-done((bf16[8,128,128]{2,1,0:T(8,128)(2,1)S(1)}, bf16[8,128,128]{2,1,0:T(8,128)(2,1)S(1)}, u32[]{:S(2)}, u32[]{:S(2)}) %collective-permute-start.16) | collective-permute-done | bytes 262176 | tf_op jit(solution)/shard_map/ppermute | solution.py:25
  139.6 12.8 %collective-permute-done.24.refs_2_ = bf16[32,128,128]{2,1,0:T(8,128)(2,1)S(1)} collective-permute-done((bf16[32,128,128]{2,1,0:T(8,128)(2,1)S(1)}, bf16[32,128,128]{2,1,0:T(8,128)(2,1)S(1)}, u32[]{:S(2)}, u32[]{:S(2)}) %collective-permute-start.24) | collective-permute-done | bytes 1048608 | tf_op jit(solution)/shard_map/ppermute | solution.py:20
  152.4 6.1 %collective-permute-start.23 = (bf16[32,128,128]{2,1,0:T(8,128)(2,1)S(1)}, bf16[32,128,128]{2,1,0:T(8,128)(2,1)S(1)}, u32[]{:S(2)}, u32[]{:S(2)}) collective-permute-start(bf16[32,128,128]{2,1,0:T(8,128)(2,1)S(1)} %assemble.2.refs_1_), channel_id=1, source_target_pairs={{0,16},{4,20},{8,24},{12,28},{16,0},{20,4},{24,8},{28,12},{32,48},... | collective-permute-start | bytes 3145736 | tf_op jit(solution)/shard_map/ppermute | solution.py:25
  158.5 12.7 %correlate_early.3.refs_4_ = f32[64,112,256]{2,1,0:T(8,128)} custom-call(s32[4]{0:T(128)S(1)} %pad_add_fusion.5.blocks_ref, bf16[112,256]{1,0:T(8,128)(2,1)S(1)} %bitcast.35, bf16[1,128]{1,0:T(2,128)(2,1)S(1)} %fusion.10.sign_ref, bf16[250,128,256]{2,1,0:T(8,128)(2,1)} %bitcast.45, bf16[32,128,128]{2,1,0:T(8,128)(2,1)S(1)} %assemble.3.refs_0_, ...), custom_call_target="tpu_custom_call" | custom-call | flops 12000000000 | bytes 16777216 | tf_op jit(solution)/shard_map/correlate_early/pallas_call | solution.py:189
  171.2 12.8 %correlate_early.2.refs_4_ = f32[64,112,256]{2,1,0:T(8,128)} custom-call(s32[4]{0:T(128)S(1)} %pad_add_fusion.5.blocks_ref, bf16[112,256]{1,0:T(8,128)(2,1)S(1)} %bitcast.36, bf16[1,128]{1,0:T(2,128)(2,1)S(1)} %fusion.10.sign_ref, bf16[250,128,256]{2,1,0:T(8,128)(2,1)} %bitcast.46, bf16[32,128,128]{2,1,0:T(8,128)(2,1)S(1)} %assemble.3.refs_0_, ...), custom_call_target="tpu_custom_call" | custom-call | flops 12000000000 | bytes 16777216 | tf_op jit(solution)/shard_map/correlate_early/pallas_call | solution.py:189
  184.0 10.7 %correlate_late.2 = (bf16[32,101,256]{2,1,0:T(8,128)(2,1)S(1)}, bf16[32,101,256]{2,1,0:T(8,128)(2,1)S(1)}) custom-call(s32[4]{0:T(128)S(1)} %pad_add_fusion.blocks_ref, bf16[112,256]{1,0:T(8,128)(2,1)S(1)} %bitcast.33, bf16[1,128]{1,0:T(2,128)(2,1)S(1)} %fusion.10.sign_ref, bf16[250,128,256]{2,1,0:T(8,128)(2,1)} %bitcast.47, ...), custom_call_target="tpu_custom_call" | custom-call | flops 12000000000 | bytes 16777216 | tf_op jit(solution)/shard_map/correlate_late/pallas_call | solution.py:189
  195.1 26.4 %collective-permute-start.26 = (bf16[32,101,256]{2,0,1:T(8,128)(2,1)S(1)}, bf16[32,101,256]{2,0,1:T(8,128)(2,1)S(1)}, u32[]{:S(2)}, u32[]{:S(2)}) collective-permute-start(bf16[32,101,256]{2,0,1:T(8,128)(2,1)S(1)} %copy.21), channel_id=1, source_target_pairs={{0,1},{1,0},{2,3},{3,2},{4,5},{5,4},{6,7},{7,6},{8,9},{9,8},{10,11... | collective-permute-start | bytes 4964360 | tf_op jit(solution)/shard_map/ppermute | solution.py:33
  221.5 3.2 %collective-permute-done.26 = bf16[32,101,256]{2,0,1:T(8,128)(2,1)S(1)} collective-permute-done((bf16[32,101,256]{2,0,1:T(8,128)(2,1)S(1)}, bf16[32,101,256]{2,0,1:T(8,128)(2,1)S(1)}, u32[]{:S(2)}, u32[]{:S(2)}) %collective-permute-start.26) | collective-permute-done | bytes 1654816 | tf_op jit(solution)/shard_map/ppermute | solution.py:33
  225.3 3.4 %collective-permute-start.27 = (bf16[16,101,256]{2,0,1:T(8,128)(2,1)S(1)}, bf16[16,101,256]{2,0,1:T(8,128)(2,1)S(1)}, u32[]{:S(2)}, u32[]{:S(2)}) collective-permute-start(bf16[16,101,256]{2,0,1:T(8,128)(2,1)S(1)} %copy.24), channel_id=1, source_target_pairs={{0,2},{1,3},{2,0},{3,1},{4,6},{5,7},{6,4},{7,5},{8,10},{9,11},{10,... | collective-permute-start | bytes 2482184 | tf_op jit(solution)/shard_map/ppermute | solution.py:37
  228.7 10.7 %correlate_late.3 = (bf16[32,101,256]{2,1,0:T(8,128)(2,1)S(1)}, bf16[32,101,256]{2,1,0:T(8,128)(2,1)S(1)}) custom-call(s32[4]{0:T(128)S(1)} %pad_add_fusion.blocks_ref, bf16[112,256]{1,0:T(8,128)(2,1)S(1)} %bitcast.34, bf16[1,128]{1,0:T(2,128)(2,1)S(1)} %fusion.10.sign_ref, bf16[250,128,256]{2,1,0:T(8,128)(2,1)} %bitcast.48, ...), custom_call_target="tpu_custom_call" | custom-call | flops 12000000000 | bytes 16777216 | tf_op jit(solution)/shard_map/correlate_late/pallas_call | solution.py:189
  239.4 7.8 %collective-permute-done.27 = bf16[16,101,256]{2,0,1:T(8,128)(2,1)S(1)} collective-permute-done((bf16[16,101,256]{2,0,1:T(8,128)(2,1)S(1)}, bf16[16,101,256]{2,0,1:T(8,128)(2,1)S(1)}, u32[]{:S(2)}, u32[]{:S(2)}) %collective-permute-start.27) | collective-permute-done | bytes 827424 | tf_op jit(solution)/shard_map/ppermute | solution.py:37
  248.6 3.2 %collective-permute-done.28 = bf16[32,101,256]{2,0,1:T(8,128)(2,1)S(1)} collective-permute-done((bf16[32,101,256]{2,0,1:T(8,128)(2,1)S(1)}, bf16[32,101,256]{2,0,1:T(8,128)(2,1)S(1)}, u32[]{:S(2)}, u32[]{:S(2)}) %collective-permute-start.28) | collective-permute-done | bytes 1654816 | tf_op jit(solution)/shard_map/ppermute | solution.py:33
  252.4 3.0 %collective-permute-start.29 = (bf16[16,101,256]{2,0,1:T(8,128)(2,1)S(1)}, bf16[16,101,256]{2,0,1:T(8,128)(2,1)S(1)}, u32[]{:S(2)}, u32[]{:S(2)}) collective-permute-start(bf16[16,101,256]{2,0,1:T(8,128)(2,1)S(1)} %copy.29), channel_id=1, source_target_pairs={{0,2},{1,3},{2,0},{3,1},{4,6},{5,7},{6,4},{7,5},{8,10},{9,11},{10,... | collective-permute-start | bytes 2482184 | tf_op jit(solution)/shard_map/ppermute | solution.py:37
  256.0 17.5 %collective-permute-done.29 = bf16[16,101,256]{2,0,1:T(8,128)(2,1)S(1)} collective-permute-done((bf16[16,101,256]{2,0,1:T(8,128)(2,1)S(1)}, bf16[16,101,256]{2,0,1:T(8,128)(2,1)S(1)}, u32[]{:S(2)}, u32[]{:S(2)}) %collective-permute-start.29) | collective-permute-done | bytes 827424 | tf_op jit(solution)/shard_map/ppermute | solution.py:37
  (91 shorter events, 47.3 us)
Async XLA Ops:
  2.9 16.6 %copy-start.2 = (s32[64]{0:T(128)S(1)}, s32[64]{0:T(128)}, u32[]{:S(2)}) copy-start(s32[64]{0:T(128)} %param.5) | copy-start | bytes 772
  23.2 25.9 %collective-permute-start = (bf16[32,128,128]{2,1,0:T(8,128)(2,1)S(1)}, bf16[32,128,128]{2,1,0:T(8,128)(2,1)S(1)}, u32[]{:S(2)}, u32[]{:S(2)}) collective-permute-start(bf16[32,128,128]{2,1,0:T(8,128)(2,1)S(1)} %get-tuple-element.44), channel_id=1, source_target_pairs={{0,32},{4,36},{8,40},{12,44},{16,48},{20,52},{24,56},{28,60},{32,6... | collective-permute-start | bytes 3145736 | tf_op jit(solution)/shard_map/ppermute | solution.py:20
  25.3 30.5 %collective-permute-start.1 = (bf16[32,128,128]{2,1,0:T(8,128)(2,1)S(1)}, bf16[32,128,128]{2,1,0:T(8,128)(2,1)}, u32[]{:S(2)}, u32[]{:S(2)}) collective-permute-start(bf16[32,128,128]{2,1,0:T(8,128)(2,1)S(1)} %get-tuple-element.45), channel_id=1, source_target_pairs={{0,8},{4,12},{8,16},{12,20},{16,24},{20,28},{24,0},{28,4},{32,40},... | collective-permute-start | bytes 3145736 | tf_op jit(solution)/shard_map/ppermute | solution.py:25
  31.1 41.8 %collective-permute-start.2 = (bf16[32,128,128]{2,1,0:T(8,128)(2,1)}, bf16[32,128,128]{2,1,0:T(8,128)(2,1)}, u32[]{:S(2)}, u32[]{:S(2)}) collective-permute-start(bf16[32,128,128]{2,1,0:T(8,128)(2,1)} %get-tuple-element.46), channel_id=1, source_target_pairs={{0,64},{4,68},{8,72},{12,76},{16,80},{20,84},{24,88},{28,92},{32,9... | collective-permute-start | bytes 3145736 | tf_op jit(solution)/shard_map/ppermute | solution.py:20
  33.5 40.5 %collective-permute-start.3 = (bf16[32,128,128]{2,1,0:T(8,128)(2,1)}, bf16[32,128,128]{2,1,0:T(8,128)(2,1)}, u32[]{:S(2)}, u32[]{:S(2)}) collective-permute-start(bf16[32,128,128]{2,1,0:T(8,128)(2,1)} %get-tuple-element.47), channel_id=1, source_target_pairs={{0,16},{4,20},{8,24},{12,28},{16,0},{20,4},{24,8},{28,12},{32,48},... | collective-permute-start | bytes 3145736 | tf_op jit(solution)/shard_map/ppermute | solution.py:25
  40.5 38.0 %collective-permute-start.4 = (bf16[32,128,128]{2,1,0:T(8,128)(2,1)}, bf16[32,128,128]{2,1,0:T(8,128)(2,1)}, u32[]{:S(2)}, u32[]{:S(2)}) collective-permute-start(bf16[32,128,128]{2,1,0:T(8,128)(2,1)} %get-tuple-element.48), channel_id=1, source_target_pairs={{0,96},{4,100},{8,104},{12,108},{16,112},{20,116},{24,120},{28,124... | collective-permute-start | bytes 3145736 | tf_op jit(solution)/shard_map/ppermute | solution.py:20
  49.1 31.8 %collective-permute-start.5 = (bf16[32,128,128]{2,1,0:T(8,128)(2,1)}, bf16[32,128,128]{2,1,0:T(8,128)(2,1)}, u32[]{:S(2)}, u32[]{:S(2)}) collective-permute-start(bf16[32,128,128]{2,1,0:T(8,128)(2,1)} %get-tuple-element.49), channel_id=1, source_target_pairs={{0,24},{4,28},{8,0},{12,4},{16,8},{20,12},{24,16},{28,20},{32,56},... | collective-permute-start | bytes 3145736 | tf_op jit(solution)/shard_map/ppermute | solution.py:25
  81.0 5.2 %copy-start.1 = (bf16[32,128,128]{2,1,0:T(8,128)(2,1)S(1)}, bf16[32,128,128]{2,1,0:T(8,128)(2,1)}, u32[]{:S(2)}) copy-start(bf16[32,128,128]{2,1,0:T(8,128)(2,1)} %copy-done) | copy-start | bytes 3145732
  83.6 8.1 %collective-permute-start.11 = (bf16[8,128,128]{2,1,0:T(8,128)(2,1)}, bf16[8,128,128]{2,1,0:T(8,128)(2,1)S(1)}, u32[]{:S(2)}, u32[]{:S(2)}) collective-permute-start(bf16[8,128,128]{2,1,0:T(8,128)(2,1)} %get-tuple-element.81), channel_id=1, source_target_pairs={{0,96},{4,100},{8,104},{12,108},{16,112},{20,116},{24,120},{28,124... | collective-permute-start | bytes 786440 | tf_op jit(solution)/shard_map/ppermute | solution.py:20
  84.7 8.6 %collective-permute-start.7 = (bf16[8,128,128]{2,1,0:T(8,128)(2,1)}, bf16[8,128,128]{2,1,0:T(8,128)(2,1)}, u32[]{:S(2)}, u32[]{:S(2)}) collective-permute-start(bf16[8,128,128]{2,1,0:T(8,128)(2,1)} %get-tuple-element.83), channel_id=1, source_target_pairs={{0,32},{4,36},{8,40},{12,44},{16,48},{20,52},{24,56},{28,60},{32,6... | collective-permute-start | bytes 786440 | tf_op jit(solution)/shard_map/ppermute | solution.py:20
  85.0 12.0 %collective-permute-start.9 = (bf16[8,128,128]{2,1,0:T(8,128)(2,1)}, bf16[8,128,128]{2,1,0:T(8,128)(2,1)}, u32[]{:S(2)}, u32[]{:S(2)}) collective-permute-start(bf16[8,128,128]{2,1,0:T(8,128)(2,1)} %get-tuple-element.82), channel_id=1, source_target_pairs={{0,64},{4,68},{8,72},{12,76},{16,80},{20,84},{24,88},{28,92},{32,9... | collective-permute-start | bytes 786440 | tf_op jit(solution)/shard_map/ppermute | solution.py:20
  88.4 9.0 %collective-permute-start.10 = (bf16[8,128,128]{2,1,0:T(8,128)(2,1)}, bf16[8,128,128]{2,1,0:T(8,128)(2,1)}, u32[]{:S(2)}, u32[]{:S(2)}) collective-permute-start(bf16[8,128,128]{2,1,0:T(8,128)(2,1)} %get-tuple-element.84), channel_id=1, source_target_pairs={{0,24},{4,28},{8,0},{12,4},{16,8},{20,12},{24,16},{28,20},{32,56},... | collective-permute-start | bytes 786440 | tf_op jit(solution)/shard_map/ppermute | solution.py:25
  91.7 9.3 %collective-permute-start.6 = (bf16[8,128,128]{2,1,0:T(8,128)(2,1)}, bf16[8,128,128]{2,1,0:T(8,128)(2,1)}, u32[]{:S(2)}, u32[]{:S(2)}) collective-permute-start(bf16[8,128,128]{2,1,0:T(8,128)(2,1)} %get-tuple-element.86), channel_id=1, source_target_pairs={{0,8},{4,12},{8,16},{12,20},{16,24},{20,28},{24,0},{28,4},{32,40},... | collective-permute-start | bytes 786440 | tf_op jit(solution)/shard_map/ppermute | solution.py:25
  91.7 12.3 %collective-permute-start.8 = (bf16[8,128,128]{2,1,0:T(8,128)(2,1)}, bf16[8,128,128]{2,1,0:T(8,128)(2,1)}, u32[]{:S(2)}, u32[]{:S(2)}) collective-permute-start(bf16[8,128,128]{2,1,0:T(8,128)(2,1)} %get-tuple-element.85), channel_id=1, source_target_pairs={{0,16},{4,20},{8,24},{12,28},{16,0},{20,4},{24,8},{28,12},{32,48},... | collective-permute-start | bytes 786440 | tf_op jit(solution)/shard_map/ppermute | solution.py:25
  105.4 5.5 %collective-permute-start.13 = (bf16[8,128,128]{2,1,0:T(8,128)(2,1)S(1)}, bf16[8,128,128]{2,1,0:T(8,128)(2,1)S(1)}, u32[]{:S(2)}, u32[]{:S(2)}) collective-permute-start(bf16[8,128,128]{2,1,0:T(8,128)(2,1)S(1)} %add_add_fusion), channel_id=1, source_target_pairs={{0,4},{4,0},{8,12},{12,8},{16,20},{20,16},{24,28},{28,24},{32,36},... | collective-permute-start | bytes 786440 | tf_op jit(solution)/shard_map/ppermute | solution.py:29
  108.4 7.5 %collective-permute-start.12 = (bf16[8,128,128]{2,1,0:T(8,128)(2,1)S(1)}, bf16[8,128,128]{2,1,0:T(8,128)(2,1)S(1)}, u32[]{:S(2)}, u32[]{:S(2)}) collective-permute-start(bf16[8,128,128]{2,1,0:T(8,128)(2,1)S(1)} %add_add_fusion.1), channel_id=1, source_target_pairs={{0,4},{4,0},{8,12},{12,8},{16,20},{20,16},{24,28},{28,24},{32,36},... | collective-permute-start | bytes 786440 | tf_op jit(solution)/shard_map/ppermute | solution.py:29
  116.0 6.7 %collective-permute-start.17 = (bf16[8,128,128]{2,1,0:T(8,128)(2,1)S(1)}, bf16[8,128,128]{2,1,0:T(8,128)(2,1)S(1)}, u32[]{:S(2)}, u32[]{:S(2)}) collective-permute-start(bf16[8,128,128]{2,1,0:T(8,128)(2,1)S(1)} %add.521.refs_0_), channel_id=1, source_target_pairs={{0,32},{4,36},{8,40},{12,44},{16,48},{20,52},{24,56},{28,60},{32,6... | collective-permute-start | bytes 786440 | tf_op jit(solution)/shard_map/ppermute | solution.py:20
  117.9 7.8 %collective-permute-start.18 = (bf16[8,128,128]{2,1,0:T(8,128)(2,1)S(1)}, bf16[8,128,128]{2,1,0:T(8,128)(2,1)S(1)}, u32[]{:S(2)}, u32[]{:S(2)}) collective-permute-start(bf16[8,128,128]{2,1,0:T(8,128)(2,1)S(1)} %add.521.refs_0_), channel_id=1, source_target_pairs={{0,96},{4,100},{8,104},{12,108},{16,112},{20,116},{24,120},{28,124... | collective-permute-start | bytes 786440 | tf_op jit(solution)/shard_map/ppermute | solution.py:20
  119.2 8.3 %collective-permute-start.19 = (bf16[8,128,128]{2,1,0:T(8,128)(2,1)S(1)}, bf16[8,128,128]{2,1,0:T(8,128)(2,1)S(1)}, u32[]{:S(2)}, u32[]{:S(2)}) collective-permute-start(bf16[8,128,128]{2,1,0:T(8,128)(2,1)S(1)} %add.521.refs_0_), channel_id=1, source_target_pairs={{0,64},{4,68},{8,72},{12,76},{16,80},{20,84},{24,88},{28,92},{32,9... | collective-permute-start | bytes 786440 | tf_op jit(solution)/shard_map/ppermute | solution.py:20
  119.8 7.7 %collective-permute-start.14 = (bf16[8,128,128]{2,1,0:T(8,128)(2,1)S(1)}, bf16[8,128,128]{2,1,0:T(8,128)(2,1)S(1)}, u32[]{:S(2)}, u32[]{:S(2)}) collective-permute-start(bf16[8,128,128]{2,1,0:T(8,128)(2,1)S(1)} %add.520.refs_0_), channel_id=1, source_target_pairs={{0,8},{4,12},{8,16},{12,20},{16,24},{20,28},{24,0},{28,4},{32,40},... | collective-permute-start | bytes 786440 | tf_op jit(solution)/shard_map/ppermute | solution.py:25
  121.1 6.3 %collective-permute-start.15 = (bf16[8,128,128]{2,1,0:T(8,128)(2,1)S(1)}, bf16[8,128,128]{2,1,0:T(8,128)(2,1)S(1)}, u32[]{:S(2)}, u32[]{:S(2)}) collective-permute-start(bf16[8,128,128]{2,1,0:T(8,128)(2,1)S(1)} %add.520.refs_0_), channel_id=1, source_target_pairs={{0,24},{4,28},{8,0},{12,4},{16,8},{20,12},{24,16},{28,20},{32,56},... | collective-permute-start | bytes 786440 | tf_op jit(solution)/shard_map/ppermute | solution.py:25
  122.7 9.1 %collective-permute-start.16 = (bf16[8,128,128]{2,1,0:T(8,128)(2,1)S(1)}, bf16[8,128,128]{2,1,0:T(8,128)(2,1)S(1)}, u32[]{:S(2)}, u32[]{:S(2)}) collective-permute-start(bf16[8,128,128]{2,1,0:T(8,128)(2,1)S(1)} %add.520.refs_0_), channel_id=1, source_target_pairs={{0,16},{4,20},{8,24},{12,28},{16,0},{20,4},{24,8},{28,12},{32,48},... | collective-permute-start | bytes 786440 | tf_op jit(solution)/shard_map/ppermute | solution.py:25
  131.9 20.5 %collective-permute-start.24 = (bf16[32,128,128]{2,1,0:T(8,128)(2,1)S(1)}, bf16[32,128,128]{2,1,0:T(8,128)(2,1)S(1)}, u32[]{:S(2)}, u32[]{:S(2)}) collective-permute-start(bf16[32,128,128]{2,1,0:T(8,128)(2,1)S(1)} %assemble.3.refs_0_), channel_id=1, source_target_pairs={{0,32},{4,36},{8,40},{12,44},{16,48},{20,52},{24,56},{28,60},{32,6... | collective-permute-start | bytes 3145736 | tf_op jit(solution)/shard_map/ppermute | solution.py:20
  132.2 26.3 %collective-permute-start.25 = (bf16[32,128,128]{2,1,0:T(8,128)(2,1)S(1)}, bf16[32,128,128]{2,1,0:T(8,128)(2,1)S(1)}, u32[]{:S(2)}, u32[]{:S(2)}) collective-permute-start(bf16[32,128,128]{2,1,0:T(8,128)(2,1)S(1)} %assemble.3.refs_0_), channel_id=1, source_target_pairs={{0,96},{4,100},{8,104},{12,108},{16,112},{20,116},{24,120},{28,124... | collective-permute-start | bytes 3145736 | tf_op jit(solution)/shard_map/ppermute | solution.py:20
  135.6 48.4 %collective-permute-start.22 = (bf16[32,128,128]{2,1,0:T(8,128)(2,1)S(1)}, bf16[32,128,128]{2,1,0:T(8,128)(2,1)S(1)}, u32[]{:S(2)}, u32[]{:S(2)}) collective-permute-start(bf16[32,128,128]{2,1,0:T(8,128)(2,1)S(1)} %assemble.3.refs_0_), channel_id=1, source_target_pairs={{0,64},{4,68},{8,72},{12,76},{16,80},{20,84},{24,88},{28,92},{32,9... | collective-permute-start | bytes 3145736 | tf_op jit(solution)/shard_map/ppermute | solution.py:20
  136.9 47.1 %collective-permute-start.20 = (bf16[32,128,128]{2,1,0:T(8,128)(2,1)S(1)}, bf16[32,128,128]{2,1,0:T(8,128)(2,1)S(1)}, u32[]{:S(2)}, u32[]{:S(2)}) collective-permute-start(bf16[32,128,128]{2,1,0:T(8,128)(2,1)S(1)} %assemble.2.refs_1_), channel_id=1, source_target_pairs={{0,8},{4,12},{8,16},{12,20},{16,24},{20,28},{24,0},{28,4},{32,40},... | collective-permute-start | bytes 3145736 | tf_op jit(solution)/shard_map/ppermute | solution.py:25
  137.5 46.5 %collective-permute-start.21 = (bf16[32,128,128]{2,1,0:T(8,128)(2,1)S(1)}, bf16[32,128,128]{2,1,0:T(8,128)(2,1)S(1)}, u32[]{:S(2)}, u32[]{:S(2)}) collective-permute-start(bf16[32,128,128]{2,1,0:T(8,128)(2,1)S(1)} %assemble.2.refs_1_), channel_id=1, source_target_pairs={{0,24},{4,28},{8,0},{12,4},{16,8},{20,12},{24,16},{28,20},{32,56},... | collective-permute-start | bytes 3145736 | tf_op jit(solution)/shard_map/ppermute | solution.py:25
  152.4 31.6 %collective-permute-start.23 = (bf16[32,128,128]{2,1,0:T(8,128)(2,1)S(1)}, bf16[32,128,128]{2,1,0:T(8,128)(2,1)S(1)}, u32[]{:S(2)}, u32[]{:S(2)}) collective-permute-start(bf16[32,128,128]{2,1,0:T(8,128)(2,1)S(1)} %assemble.2.refs_1_), channel_id=1, source_target_pairs={{0,16},{4,20},{8,24},{12,28},{16,0},{20,4},{24,8},{28,12},{32,48},... | collective-permute-start | bytes 3145736 | tf_op jit(solution)/shard_map/ppermute | solution.py:25
  195.1 29.5 %collective-permute-start.26 = (bf16[32,101,256]{2,0,1:T(8,128)(2,1)S(1)}, bf16[32,101,256]{2,0,1:T(8,128)(2,1)S(1)}, u32[]{:S(2)}, u32[]{:S(2)}) collective-permute-start(bf16[32,101,256]{2,0,1:T(8,128)(2,1)S(1)} %copy.21), channel_id=1, source_target_pairs={{0,1},{1,0},{2,3},{3,2},{4,5},{5,4},{6,7},{7,6},{8,9},{9,8},{10,11... | collective-permute-start | bytes 4964360 | tf_op jit(solution)/shard_map/ppermute | solution.py:33
  225.3 21.9 %collective-permute-start.27 = (bf16[16,101,256]{2,0,1:T(8,128)(2,1)S(1)}, bf16[16,101,256]{2,0,1:T(8,128)(2,1)S(1)}, u32[]{:S(2)}, u32[]{:S(2)}) collective-permute-start(bf16[16,101,256]{2,0,1:T(8,128)(2,1)S(1)} %copy.24), channel_id=1, source_target_pairs={{0,2},{1,3},{2,0},{3,1},{4,6},{5,7},{6,4},{7,5},{8,10},{9,11},{10,... | collective-permute-start | bytes 2482184 | tf_op jit(solution)/shard_map/ppermute | solution.py:37
  247.6 4.1 %collective-permute-start.28 = (bf16[32,101,256]{2,0,1:T(8,128)(2,1)S(1)}, bf16[32,101,256]{2,0,1:T(8,128)(2,1)S(1)}, u32[]{:S(2)}, u32[]{:S(2)}) collective-permute-start(bf16[32,101,256]{2,0,1:T(8,128)(2,1)S(1)} %copy.26), channel_id=1, source_target_pairs={{0,1},{1,0},{2,3},{3,2},{4,5},{5,4},{6,7},{7,6},{8,9},{9,8},{10,11... | collective-permute-start | bytes 4964360 | tf_op jit(solution)/shard_map/ppermute | solution.py:33
  252.4 21.2 %collective-permute-start.29 = (bf16[16,101,256]{2,0,1:T(8,128)(2,1)S(1)}, bf16[16,101,256]{2,0,1:T(8,128)(2,1)S(1)}, u32[]{:S(2)}, u32[]{:S(2)}) collective-permute-start(bf16[16,101,256]{2,0,1:T(8,128)(2,1)S(1)} %copy.29), channel_id=1, source_target_pairs={{0,2},{1,3},{2,0},{3,1},{4,6},{5,7},{6,4},{7,5},{8,10},{9,11},{10,... | collective-permute-start | bytes 2482184 | tf_op jit(solution)/shard_map/ppermute | solution.py:37
  (1 other events, 3.1 us)

commit v6 on v5

--- a/solution.py
+++ b/solution.py
@@ -108,7 +108,10 @@
 
         @pl.when(step == m)
         def _():
-            src[...] = sources[m][...]
+            at = 0
+            for piece in sources[m]:
+                src[at : at + piece.shape[0]] = piece[...]
+                at += piece.shape[0]
 
     last = BINS - 1 - 32 * blocks_ref[step]
     sign = sign_ref[...]
@@ -135,7 +138,7 @@
 
 
 def early_kernel(blocks_ref, table_ref, sign_ref, spec_ref, *refs):
-    sources, (acc_ref, src, left, right) = refs[:4], refs[4:]
+    sources, (acc_ref, src, left, right) = [[r] for r in refs[:4]], refs[4:]
     cross_blocks(blocks_ref, sign_ref, spec_ref, sources, src, left, right)
 
     @pl.when(pl.program_id(0) == 3)
@@ -147,7 +150,8 @@
 
 
 def late_kernel(blocks_ref, table_ref, sign_ref, spec_ref, *refs):
-    sources, (before_ref, send_ref, keep_ref, src, left, right, acc, sem) = refs[:4], refs[4:]
+    sources = [refs[:1], refs[1:2], refs[2:4], refs[4:6]]
+    before_ref, send_ref, keep_ref, src, left, right, acc, sem = refs[6:]
     step = pl.program_id(0)
     fetch = pltpu.make_async_copy(before_ref, acc, sem)
 
@@ -196,7 +200,7 @@
                 pl.BlockSpec((1, 128), lambda i, s: (0, 0)),
                 pl.BlockSpec((32, 128, 256), lambda i, s: (s[i], 0, 0)),
             ]
-            + [pl.BlockSpec((32, ROWS, 128), lambda i, s: (0, part, 0))] * 4
+            + [pl.BlockSpec((a.shape[0], ROWS, 128), lambda i, s: (0, part, 0)) for a in sources]
             + ([] if early else [pl.BlockSpec(memory_space=pl.ANY)]),
             out_specs=pl.BlockSpec((ROWS, LAG_PAD, 256), lambda i, s: (0, 0, 0)) if early else [whole, whole],
             scratch_shapes=scratch,
@@ -250,15 +254,20 @@
     near_a, near_b = barrier((near_a, near_b))
     inner_a, inner_b = assemble(y[None], near_a), assemble(x[None], near_b)
 
-    far_a, far_b = gather(inner_a, inner_b, shift_x, shift_y)
-    arrivals = [far_a[0], far_b[0], far_a[1], far_a[2], far_b[1], far_b[2], far_a[3], far_b[3]]
+    next_a = [shift_x(inner_a, 1), shift_x(inner_a, 3)]
+    next_b = [shift_y(inner_b, 1), shift_y(inner_b, 3)]
+    next_a, next_b = barrier((next_a, next_b))
+    over_a = [shift_x(next_a[0][:16], 1), shift_x(next_a[1][16:], 3)]
+    over_b = [shift_y(next_b[0][:16], 1), shift_y(next_b[1][16:], 3)]
+    first_sources = [inner_a, inner_b] + next_a
+    last_sources = next_b + over_a + over_b
     blocks = jnp.stack(
         [x, 4 + y, (x + 3) % 4, (x + 1) % 4, 4 + (y + 3) % 4, 4 + (y + 1) % 4, (x + 2) % 4, 4 + (y + 2) % 4]
     )
     freqs = (32 * blocks[:, None] + jnp.arange(32, dtype=jnp.int32)[None, :]).reshape(256)
     table = lag_table(freqs, LAG_PAD, 256)
     table = table.reshape(2, LAG_PAD, 2, 128).transpose(2, 1, 0, 3).reshape(2, LAG_PAD, 256)
-    sums = [correlate(part, blocks[:4], table[0], sign, spec, arrivals[:4]) for part in range(PARTS)]
+    sums = [correlate(part, blocks[:4], table[0], sign, spec, first_sources) for part in range(PARTS)]
 
     sums = barrier(sums)
 
@@ -266,7 +275,7 @@
     quarter = ROWS // 4
     last = own_rows = None
     for part in range(PARTS):
-        send, keep = correlate(part, blocks[4:], table[1], sign, spec, arrivals[4:], sums[part])
+        send, keep = correlate(part, blocks[4:], table[1], sign, spec, last_sources, sums[part])
         if last is not None:
             send, last = barrier((send, last))
             outs.append(finish(own_rows, last))

time: 276 us -> 264 us (0.957)
  starting transfers between devices: 77.6 us -> 62 us
  waiting for transfers between devices: 101 us -> 104 us
    ppermute x12 -> x13, waiting for transfers between devices: 14.9 us -> 30.9 us  [shift_y(): return lax.ppermute(x, 'chan', pairs)]
    ppermute x2, starting transfers between devices: 27.3 us -> 13.3 us  [swap_core(): return lax.ppermute(x, 'tm', [(a, a ^ 1) for a in range(4)])]
    ppermute x12 -> x13, waiting for transfers between devices: 47.4 us -> 34.6 us  [shift_x(): return lax.ppermute(x, 'chan', pairs)]
    ppermute x12 -> x13, starting transfers between devices: 26.5 us -> 23.3 us  [shift_y(): return lax.ppermute(x, 'chan', pairs)]
    ppermute x12 -> x13, starting transfers between devices: 15.4 us -> 17 us  [shift_x(): return lax.ppermute(x, 'chan', pairs)]
  transfers between devices with their start and end apart: 30 -> 32, of which waited for: 18 -> 19; matrix products, arithmetic and copies ran while one was open for 2% -> 2% of each run, Pallas kernels for 18% -> 18%
where the time goes in v6:
time: 264 us
  waiting for transfers between devices  104 us (39%)
  Pallas kernels  63 us (24%)
  starting transfers between devices  62 us (23%)
  local copies, waits for them, and re-layouts  21.6 us (8%)
  other arithmetic  12.6 us (5%)
    pallas_call x4, Pallas kernels, correlate(): pl.pallas_call(early_kernel if early else late_kernel, grid_spec=pltpu.Pr...  46.9 us
    ppermute x13, waiting for transfers between devices, shift_x(): return lax.ppermute(x, 'chan', pairs)  34.6 us
    ppermute x13, waiting for transfers between devices, shift_y(): return lax.ppermute(x, 'chan', pairs)  30.9 us
    ppermute x2, waiting for transfers between devices, swap_far(): return lax.ppermute(x, 'tm', [(a, a ^ 2) for a in range(4)])  25.2 us
    ppermute x13, starting transfers between devices, shift_y(): return lax.ppermute(x, 'chan', pairs)  23.3 us
    ppermute x13, starting transfers between devices, shift_x(): return lax.ppermute(x, 'chan', pairs)  17 us
    transpose x1, local copies, waits for them, and re-layouts, body(): spec = jnp.transpose(spectra, (2, 1, 0, 3)).reshape(BINS, 128, 256)  16.6 us
    pallas_call x4, Pallas kernels, pick_rows(): pl.pallas_call(pick_kernel, grid_spec=pltpu.PrefetchScalarGridSpec(num_sc...  15.9 us
  transfers between devices with their start and end apart: 32, of which 19 were waited for; matrix products, arithmetic and copies ran while one was open for 2% of the time, Pallas kernels for 18%

profile of v6, /device:TPU:1, one launch (start us, length us, event | category | flops | bytes accessed | tf_op | source)
XLA Modules:
  0.0 263.8 jit_solution(10712670178609932797)
XLA Ops:
  2.7 16.6 %copy.19 = bf16[250,2,64,256]{3,2,1,0:T(8,128)(2,1)} copy(bf16[250,2,64,256]{3,1,0,2:T(2,128)(2,1)} %bitcast.49) | data formatting | bytes 32768000 | tf_op jit(solution)/shard_map/transpose | solution.py:221
  19.5 3.6 %pick_rows.5 = (bf16[32,128,128]{2,1,0:T(8,128)(2,1)S(1)}, bf16[32,128,128]{2,1,0:T(8,128)(2,1)S(1)}) custom-call(s32[2]{0:T(128)S(1)} %get-tuple-element.106.first_ref, bf16[128,256]{1,0:T(8,128)(2,1)S(1)} %fusion.1.pick_ref, f32[1,128]{1,0:T(1,128)S(1)} %broadcast_in_dim_tile.3.mask_ref, bf16[250,128,256]{2,1,0:T(8,128)(2,1)} %bitcast.37, ...), custom_call_target="tpu_custom_call" | custom-call | flops 1048576 | bytes 65536 | tf_op jit(solution)/shard_map/pick_rows/pallas_call | solution.py:62
  26.5 4.4 %pick_rows.6 = (bf16[32,128,128]{2,1,0:T(8,128)(2,1)}, bf16[32,128,128]{2,1,0:T(8,128)(2,1)}) custom-call(s32[2]{0:T(128)S(1)} %get-tuple-element.107.first_ref, bf16[128,256]{1,0:T(8,128)(2,1)S(1)} %fusion.1.pick_ref, f32[1,128]{1,0:T(1,128)S(1)} %broadcast_in_dim_tile.3.mask_ref, bf16[250,128,256]{2,1,0:T(8,128)(2,1)} %bitcast.39, ...), custom_call_target="tpu_custom_call" | custom-call | flops 1048576 | bytes 65536 | tf_op jit(solution)/shard_map/pick_rows/pallas_call | solution.py:62
  36.0 4.4 %pick_rows.7 = (bf16[32,128,128]{2,1,0:T(8,128)(2,1)}, bf16[32,128,128]{2,1,0:T(8,128)(2,1)}) custom-call(s32[2]{0:T(128)S(1)} %get-tuple-element.108.first_ref, bf16[128,256]{1,0:T(8,128)(2,1)S(1)} %fusion.1.pick_ref, f32[1,128]{1,0:T(1,128)S(1)} %broadcast_in_dim_tile.3.mask_ref, bf16[250,128,256]{2,1,0:T(8,128)(2,1)} %bitcast.41, ...), custom_call_target="tpu_custom_call" | custom-call | flops 1048576 | bytes 65536 | tf_op jit(solution)/shard_map/pick_rows/pallas_call | solution.py:62
  41.5 7.4 %collective-permute-done = bf16[32,128,128]{2,1,0:T(8,128)(2,1)S(1)} collective-permute-done((bf16[32,128,128]{2,1,0:T(8,128)(2,1)S(1)}, bf16[32,128,128]{2,1,0:T(8,128)(2,1)S(1)}, u32[]{:S(2)}, u32[]{:S(2)}) %collective-permute-start) | collective-permute-done | bytes 1048608 | tf_op jit(solution)/shard_map/ppermute | solution.py:20
  49.0 3.1 %collective-permute-start.5 = (bf16[32,128,128]{2,1,0:T(8,128)(2,1)}, bf16[32,128,128]{2,1,0:T(8,128)(2,1)}, u32[]{:S(2)}, u32[]{:S(2)}) collective-permute-start(bf16[32,128,128]{2,1,0:T(8,128)(2,1)} %get-tuple-element.53), channel_id=1, source_target_pairs={{0,24},{4,28},{8,0},{12,4},{16,8},{20,12},{24,16},{28,20},{32,56},... | collective-permute-start | bytes 3145736 | tf_op jit(solution)/shard_map/ppermute | solution.py:25
  52.0 3.6 %pick_rows.4 = (bf16[32,128,128]{2,1,0:T(8,128)(2,1)S(1)}, bf16[32,128,128]{2,1,0:T(8,128)(2,1)S(1)}) custom-call(s32[2]{0:T(128)S(1)} %get-tuple-element.105.first_ref, bf16[128,256]{1,0:T(8,128)(2,1)S(1)} %fusion.1.pick_ref, f32[1,128]{1,0:T(1,128)S(1)} %broadcast_in_dim_tile.3.mask_ref, bf16[250,128,256]{2,1,0:T(8,128)(2,1)} %bitcast.43, ...), custom_call_target="tpu_custom_call" | custom-call | flops 1048576 | bytes 65536 | tf_op jit(solution)/shard_map/pick_rows/pallas_call | solution.py:62
  55.6 17.1 %collective-permute-done.2 = bf16[32,128,128]{2,1,0:T(8,128)(2,1)} collective-permute-done((bf16[32,128,128]{2,1,0:T(8,128)(2,1)}, bf16[32,128,128]{2,1,0:T(8,128)(2,1)}, u32[]{:S(2)}, u32[]{:S(2)}) %collective-permute-start.2) | collective-permute-done | bytes 1048608 | tf_op jit(solution)/shard_map/ppermute | solution.py:20
  73.9 4.5 %collective-permute-done.4 = bf16[32,128,128]{2,1,0:T(8,128)(2,1)} collective-permute-done((bf16[32,128,128]{2,1,0:T(8,128)(2,1)}, bf16[32,128,128]{2,1,0:T(8,128)(2,1)}, u32[]{:S(2)}, u32[]{:S(2)}) %collective-permute-start.4) | collective-permute-done | bytes 1048608 | tf_op jit(solution)/shard_map/ppermute | solution.py:20
  80.8 2.6 add_add_fusion.2
  88.3 3.2 %collective-permute-start.10 = (bf16[8,128,128]{2,1,0:T(8,128)(2,1)}, bf16[8,128,128]{2,1,0:T(8,128)(2,1)}, u32[]{:S(2)}, u32[]{:S(2)}) collective-permute-start(bf16[8,128,128]{2,1,0:T(8,128)(2,1)} %get-tuple-element.92), channel_id=1, source_target_pairs={{0,24},{4,28},{8,0},{12,4},{16,8},{20,12},{24,16},{28,20},{32,56},... | collective-permute-start | bytes 786440 | tf_op jit(solution)/shard_map/ppermute | solution.py:25
  93.2 3.7 %collective-permute-done.9 = bf16[8,128,128]{2,1,0:T(8,128)(2,1)} collective-permute-done((bf16[8,128,128]{2,1,0:T(8,128)(2,1)}, bf16[8,128,128]{2,1,0:T(8,128)(2,1)}, u32[]{:S(2)}, u32[]{:S(2)}) %collective-permute-start.9) | collective-permute-done | bytes 262176 | tf_op jit(solution)/shard_map/ppermute | solution.py:20
  97.3 3.6 %collective-permute-done.6 = bf16[8,128,128]{2,1,0:T(8,128)(2,1)} collective-permute-done((bf16[8,128,128]{2,1,0:T(8,128)(2,1)}, bf16[8,128,128]{2,1,0:T(8,128)(2,1)}, u32[]{:S(2)}, u32[]{:S(2)}) %collective-permute-start.6) | collective-permute-done | bytes 262176 | tf_op jit(solution)/shard_map/ppermute | solution.py:25
  100.9 2.9 %collective-permute-done.8 = bf16[8,128,128]{2,1,0:T(8,128)(2,1)} collective-permute-done((bf16[8,128,128]{2,1,0:T(8,128)(2,1)}, bf16[8,128,128]{2,1,0:T(8,128)(2,1)}, u32[]{:S(2)}, u32[]{:S(2)}) %collective-permute-start.8) | collective-permute-done | bytes 262176 | tf_op jit(solution)/shard_map/ppermute | solution.py:25
  110.7 5.1 %collective-permute-done.12 = bf16[8,128,128]{2,1,0:T(8,128)(2,1)S(1)} collective-permute-done((bf16[8,128,128]{2,1,0:T(8,128)(2,1)S(1)}, bf16[8,128,128]{2,1,0:T(8,128)(2,1)S(1)}, u32[]{:S(2)}, u32[]{:S(2)}) %collective-permute-start.12) | collective-permute-done | bytes 262176 | tf_op jit(solution)/shard_map/ppermute | solution.py:29
  122.6 2.9 %collective-permute-start.16 = (bf16[8,128,128]{2,1,0:T(8,128)(2,1)S(1)}, bf16[8,128,128]{2,1,0:T(8,128)(2,1)S(1)}, u32[]{:S(2)}, u32[]{:S(2)}) collective-permute-start(bf16[8,128,128]{2,1,0:T(8,128)(2,1)S(1)} %add.520.refs_0_), channel_id=1, source_target_pairs={{0,16},{4,20},{8,24},{12,28},{16,0},{20,4},{24,8},{28,12},{32,48},... | collective-permute-start | bytes 786440 | tf_op jit(solution)/shard_map/ppermute | solution.py:25
  127.4 4.4 %collective-permute-done.16.refs_3_ = bf16[8,128,128]{2,1,0:T(8,128)(2,1)S(1)} collective-permute-done((bf16[8,128,128]{2,1,0:T(8,128)(2,1)S(1)}, bf16[8,128,128]{2,1,0:T(8,128)(2,1)S(1)}, u32[]{:S(2)}, u32[]{:S(2)}) %collective-permute-start.16) | collective-permute-done | bytes 262176 | tf_op jit(solution)/shard_map/ppermute | solution.py:25
  138.3 12.3 %collective-permute-done.22.refs_0_ = bf16[32,128,128]{2,1,0:T(8,128)(2,1)S(1)} collective-permute-done((bf16[32,128,128]{2,1,0:T(8,128)(2,1)S(1)}, bf16[32,128,128]{2,1,0:T(8,128)(2,1)S(1)}, u32[]{:S(2)}, u32[]{:S(2)}) %collective-permute-start.22) | collective-permute-done | bytes 1048608 | tf_op jit(solution)/shard_map/ppermute | solution.py:25
  150.6 3.7 %collective-permute-done.23.refs_1_ = bf16[32,128,128]{2,1,0:T(8,128)(2,1)S(1)} collective-permute-done((bf16[32,128,128]{2,1,0:T(8,128)(2,1)S(1)}, bf16[32,128,128]{2,1,0:T(8,128)(2,1)S(1)}, u32[]{:S(2)}, u32[]{:S(2)}) %collective-permute-start.23) | collective-permute-done | bytes 1048608 | tf_op jit(solution)/shard_map/ppermute | solution.py:25
  154.5 2.6 %collective-permute-start.25 = (bf16[16,128,128]{2,1,0:T(8,128)(2,1)S(1)}, bf16[16,128,128]{2,1,0:T(8,128)(2,1)S(1)}, u32[]{:S(2)}, u32[]{:S(2)}) collective-permute-start(bf16[16,128,128]{2,1,0:T(8,128)(2,1)S(1)} %slice.62), channel_id=1, source_target_pairs={{0,96},{4,100},{8,104},{12,108},{16,112},{20,116},{24,120},{28,124... | collective-permute-start | bytes 1572872 | tf_op jit(solution)/shard_map/ppermute | solution.py:20
  157.4 2.7 %collective-permute-start.27 = (bf16[16,128,128]{2,1,0:T(8,128)(2,1)S(1)}, bf16[16,128,128]{2,1,0:T(8,128)(2,1)S(1)}, u32[]{:S(2)}, u32[]{:S(2)}) collective-permute-start(bf16[16,128,128]{2,1,0:T(8,128)(2,1)S(1)} %slice.64), channel_id=1, source_target_pairs={{0,24},{4,28},{8,0},{12,4},{16,8},{20,12},{24,16},{28,20},{32,56},... | collective-permute-start | bytes 1572872 | tf_op jit(solution)/shard_map/ppermute | solution.py:25
  160.1 12.7 %correlate_early.3.refs_6_ = f32[64,112,256]{2,1,0:T(8,128)} custom-call(s32[4]{0:T(128)S(1)} %pad_add_fusion.5.blocks_ref, bf16[112,256]{1,0:T(8,128)(2,1)S(1)} %bitcast.35, bf16[1,128]{1,0:T(2,128)(2,1)S(1)} %fusion.10.sign_ref, bf16[250,128,256]{2,1,0:T(8,128)(2,1)} %bitcast.45, bf16[32,128,128]{2,1,0:T(8,128)(2,1)S(1)} %assemble.2.refs_0_, ...), custom_call_target="tpu_custom_call" | custom-call | flops 12000000000 | bytes 16777216 | tf_op jit(solution)/shard_map/correlate_early/pallas_call | solution.py:193
  172.8 12.8 %correlate_early.2.refs_6_ = f32[64,112,256]{2,1,0:T(8,128)} custom-call(s32[4]{0:T(128)S(1)} %pad_add_fusion.5.blocks_ref, bf16[112,256]{1,0:T(8,128)(2,1)S(1)} %bitcast.36, bf16[1,128]{1,0:T(2,128)(2,1)S(1)} %fusion.10.sign_ref, bf16[250,128,256]{2,1,0:T(8,128)(2,1)} %bitcast.46, bf16[32,128,128]{2,1,0:T(8,128)(2,1)S(1)} %assemble.2.refs_0_, ...), custom_call_target="tpu_custom_call" | custom-call | flops 12000000000 | bytes 16777216 | tf_op jit(solution)/shard_map/correlate_early/pallas_call | solution.py:193
  185.6 10.7 %correlate_late.2 = (bf16[32,101,256]{2,1,0:T(8,128)(2,1)S(1)}, bf16[32,101,256]{2,1,0:T(8,128)(2,1)S(1)}) custom-call(s32[4]{0:T(128)S(1)} %pad_add_fusion.blocks_ref, bf16[112,256]{1,0:T(8,128)(2,1)S(1)} %bitcast.33, bf16[1,128]{1,0:T(2,128)(2,1)S(1)} %fusion.10.sign_ref, bf16[250,128,256]{2,1,0:T(8,128)(2,1)} %bitcast.47, ...), custom_call_target="tpu_custom_call" | custom-call | flops 12000000000 | bytes 16777216 | tf_op jit(solution)/shard_map/correlate_late/pallas_call | solution.py:193
  196.7 12.4 %collective-permute-start.28 = (bf16[32,101,256]{2,0,1:T(8,128)(2,1)S(1)}, bf16[32,101,256]{2,0,1:T(8,128)(2,1)S(1)}, u32[]{:S(2)}, u32[]{:S(2)}) collective-permute-start(bf16[32,101,256]{2,0,1:T(8,128)(2,1)S(1)} %copy.21), channel_id=1, source_target_pairs={{0,1},{1,0},{2,3},{3,2},{4,5},{5,4},{6,7},{7,6},{8,9},{9,8},{10,11... | collective-permute-start | bytes 4964360 | tf_op jit(solution)/shard_map/ppermute | solution.py:33
  209.1 3.2 %collective-permute-done.28 = bf16[32,101,256]{2,0,1:T(8,128)(2,1)S(1)} collective-permute-done((bf16[32,101,256]{2,0,1:T(8,128)(2,1)S(1)}, bf16[32,101,256]{2,0,1:T(8,128)(2,1)S(1)}, u32[]{:S(2)}, u32[]{:S(2)}) %collective-permute-start.28) | collective-permute-done | bytes 1654816 | tf_op jit(solution)/shard_map/ppermute | solution.py:33
  212.9 3.5 %collective-permute-start.29 = (bf16[16,101,256]{2,0,1:T(8,128)(2,1)S(1)}, bf16[16,101,256]{2,0,1:T(8,128)(2,1)S(1)}, u32[]{:S(2)}, u32[]{:S(2)}) collective-permute-start(bf16[16,101,256]{2,0,1:T(8,128)(2,1)S(1)} %copy.24), channel_id=1, source_target_pairs={{0,2},{1,3},{2,0},{3,1},{4,6},{5,7},{6,4},{7,5},{8,10},{9,11},{10,... | collective-permute-start | bytes 2482184 | tf_op jit(solution)/shard_map/ppermute | solution.py:37
  216.4 10.7 %correlate_late.3 = (bf16[32,101,256]{2,1,0:T(8,128)(2,1)S(1)}, bf16[32,101,256]{2,1,0:T(8,128)(2,1)S(1)}) custom-call(s32[4]{0:T(128)S(1)} %pad_add_fusion.blocks_ref, bf16[112,256]{1,0:T(8,128)(2,1)S(1)} %bitcast.34, bf16[1,128]{1,0:T(2,128)(2,1)S(1)} %fusion.10.sign_ref, bf16[250,128,256]{2,1,0:T(8,128)(2,1)} %bitcast.48, ...), custom_call_target="tpu_custom_call" | custom-call | flops 12000000000 | bytes 16777216 | tf_op jit(solution)/shard_map/correlate_late/pallas_call | solution.py:193
  227.2 7.7 %collective-permute-done.29 = bf16[16,101,256]{2,0,1:T(8,128)(2,1)S(1)} collective-permute-done((bf16[16,101,256]{2,0,1:T(8,128)(2,1)S(1)}, bf16[16,101,256]{2,0,1:T(8,128)(2,1)S(1)}, u32[]{:S(2)}, u32[]{:S(2)}) %collective-permute-start.29) | collective-permute-done | bytes 827424 | tf_op jit(solution)/shard_map/ppermute | solution.py:37
  236.3 3.2 %collective-permute-done.30 = bf16[32,101,256]{2,0,1:T(8,128)(2,1)S(1)} collective-permute-done((bf16[32,101,256]{2,0,1:T(8,128)(2,1)S(1)}, bf16[32,101,256]{2,0,1:T(8,128)(2,1)S(1)}, u32[]{:S(2)}, u32[]{:S(2)}) %collective-permute-start.30) | collective-permute-done | bytes 1654816 | tf_op jit(solution)/shard_map/ppermute | solution.py:33
  240.1 3.0 %collective-permute-start.31 = (bf16[16,101,256]{2,0,1:T(8,128)(2,1)S(1)}, bf16[16,101,256]{2,0,1:T(8,128)(2,1)S(1)}, u32[]{:S(2)}, u32[]{:S(2)}) collective-permute-start(bf16[16,101,256]{2,0,1:T(8,128)(2,1)S(1)} %copy.29), channel_id=1, source_target_pairs={{0,2},{1,3},{2,0},{3,1},{4,6},{5,7},{6,4},{7,5},{8,10},{9,11},{10,... | collective-permute-start | bytes 2482184 | tf_op jit(solution)/shard_map/ppermute | solution.py:37
  243.9 17.5 %collective-permute-done.31 = bf16[16,101,256]{2,0,1:T(8,128)(2,1)S(1)} collective-permute-done((bf16[16,101,256]{2,0,1:T(8,128)(2,1)S(1)}, bf16[16,101,256]{2,0,1:T(8,128)(2,1)S(1)}, u32[]{:S(2)}, u32[]{:S(2)}) %collective-permute-start.31) | collective-permute-done | bytes 827424 | tf_op jit(solution)/shard_map/ppermute | solution.py:37
  (99 shorter events, 51.7 us)
Async XLA Ops:
  23.1 25.9 %collective-permute-start = (bf16[32,128,128]{2,1,0:T(8,128)(2,1)S(1)}, bf16[32,128,128]{2,1,0:T(8,128)(2,1)S(1)}, u32[]{:S(2)}, u32[]{:S(2)}) collective-permute-start(bf16[32,128,128]{2,1,0:T(8,128)(2,1)S(1)} %get-tuple-element.48), channel_id=1, source_target_pairs={{0,32},{4,36},{8,40},{12,44},{16,48},{20,52},{24,56},{28,60},{32,6... | collective-permute-start | bytes 3145736 | tf_op jit(solution)/shard_map/ppermute | solution.py:20
  25.2 30.5 %collective-permute-start.1 = (bf16[32,128,128]{2,1,0:T(8,128)(2,1)S(1)}, bf16[32,128,128]{2,1,0:T(8,128)(2,1)}, u32[]{:S(2)}, u32[]{:S(2)}) collective-permute-start(bf16[32,128,128]{2,1,0:T(8,128)(2,1)S(1)} %get-tuple-element.49), channel_id=1, source_target_pairs={{0,8},{4,12},{8,16},{12,20},{16,24},{20,28},{24,0},{28,4},{32,40},... | collective-permute-start | bytes 3145736 | tf_op jit(solution)/shard_map/ppermute | solution.py:25
  31.0 41.8 %collective-permute-start.2 = (bf16[32,128,128]{2,1,0:T(8,128)(2,1)}, bf16[32,128,128]{2,1,0:T(8,128)(2,1)}, u32[]{:S(2)}, u32[]{:S(2)}) collective-permute-start(bf16[32,128,128]{2,1,0:T(8,128)(2,1)} %get-tuple-element.50), channel_id=1, source_target_pairs={{0,64},{4,68},{8,72},{12,76},{16,80},{20,84},{24,88},{28,92},{32,9... | collective-permute-start | bytes 3145736 | tf_op jit(solution)/shard_map/ppermute | solution.py:20
  33.4 40.5 %collective-permute-start.3 = (bf16[32,128,128]{2,1,0:T(8,128)(2,1)}, bf16[32,128,128]{2,1,0:T(8,128)(2,1)}, u32[]{:S(2)}, u32[]{:S(2)}) collective-permute-start(bf16[32,128,128]{2,1,0:T(8,128)(2,1)} %get-tuple-element.51), channel_id=1, source_target_pairs={{0,16},{4,20},{8,24},{12,28},{16,0},{20,4},{24,8},{28,12},{32,48},... | collective-permute-start | bytes 3145736 | tf_op jit(solution)/shard_map/ppermute | solution.py:25
  40.4 38.0 %collective-permute-start.4 = (bf16[32,128,128]{2,1,0:T(8,128)(2,1)}, bf16[32,128,128]{2,1,0:T(8,128)(2,1)}, u32[]{:S(2)}, u32[]{:S(2)}) collective-permute-start(bf16[32,128,128]{2,1,0:T(8,128)(2,1)} %get-tuple-element.52), channel_id=1, source_target_pairs={{0,96},{4,100},{8,104},{12,108},{16,112},{20,116},{24,120},{28,124... | collective-permute-start | bytes 3145736 | tf_op jit(solution)/shard_map/ppermute | solution.py:20
  49.0 31.8 %collective-permute-start.5 = (bf16[32,128,128]{2,1,0:T(8,128)(2,1)}, bf16[32,128,128]{2,1,0:T(8,128)(2,1)}, u32[]{:S(2)}, u32[]{:S(2)}) collective-permute-start(bf16[32,128,128]{2,1,0:T(8,128)(2,1)} %get-tuple-element.53), channel_id=1, source_target_pairs={{0,24},{4,28},{8,0},{12,4},{16,8},{20,12},{24,16},{28,20},{32,56},... | collective-permute-start | bytes 3145736 | tf_op jit(solution)/shard_map/ppermute | solution.py:25
  83.4 8.1 %collective-permute-start.11 = (bf16[8,128,128]{2,1,0:T(8,128)(2,1)}, bf16[8,128,128]{2,1,0:T(8,128)(2,1)S(1)}, u32[]{:S(2)}, u32[]{:S(2)}) collective-permute-start(bf16[8,128,128]{2,1,0:T(8,128)(2,1)} %get-tuple-element.89), channel_id=1, source_target_pairs={{0,96},{4,100},{8,104},{12,108},{16,112},{20,116},{24,120},{28,124... | collective-permute-start | bytes 786440 | tf_op jit(solution)/shard_map/ppermute | solution.py:20
  84.6 8.6 %collective-permute-start.7 = (bf16[8,128,128]{2,1,0:T(8,128)(2,1)}, bf16[8,128,128]{2,1,0:T(8,128)(2,1)}, u32[]{:S(2)}, u32[]{:S(2)}) collective-permute-start(bf16[8,128,128]{2,1,0:T(8,128)(2,1)} %get-tuple-element.91), channel_id=1, source_target_pairs={{0,32},{4,36},{8,40},{12,44},{16,48},{20,52},{24,56},{28,60},{32,6... | collective-permute-start | bytes 786440 | tf_op jit(solution)/shard_map/ppermute | solution.py:20
  84.9 12.0 %collective-permute-start.9 = (bf16[8,128,128]{2,1,0:T(8,128)(2,1)}, bf16[8,128,128]{2,1,0:T(8,128)(2,1)}, u32[]{:S(2)}, u32[]{:S(2)}) collective-permute-start(bf16[8,128,128]{2,1,0:T(8,128)(2,1)} %get-tuple-element.90), channel_id=1, source_target_pairs={{0,64},{4,68},{8,72},{12,76},{16,80},{20,84},{24,88},{28,92},{32,9... | collective-permute-start | bytes 786440 | tf_op jit(solution)/shard_map/ppermute | solution.py:20
  88.3 9.0 %collective-permute-start.10 = (bf16[8,128,128]{2,1,0:T(8,128)(2,1)}, bf16[8,128,128]{2,1,0:T(8,128)(2,1)}, u32[]{:S(2)}, u32[]{:S(2)}) collective-permute-start(bf16[8,128,128]{2,1,0:T(8,128)(2,1)} %get-tuple-element.92), channel_id=1, source_target_pairs={{0,24},{4,28},{8,0},{12,4},{16,8},{20,12},{24,16},{28,20},{32,56},... | collective-permute-start | bytes 786440 | tf_op jit(solution)/shard_map/ppermute | solution.py:25
  91.5 9.3 %collective-permute-start.6 = (bf16[8,128,128]{2,1,0:T(8,128)(2,1)}, bf16[8,128,128]{2,1,0:T(8,128)(2,1)}, u32[]{:S(2)}, u32[]{:S(2)}) collective-permute-start(bf16[8,128,128]{2,1,0:T(8,128)(2,1)} %get-tuple-element.94), channel_id=1, source_target_pairs={{0,8},{4,12},{8,16},{12,20},{16,24},{20,28},{24,0},{28,4},{32,40},... | collective-permute-start | bytes 786440 | tf_op jit(solution)/shard_map/ppermute | solution.py:25
  91.5 12.3 %collective-permute-start.8 = (bf16[8,128,128]{2,1,0:T(8,128)(2,1)}, bf16[8,128,128]{2,1,0:T(8,128)(2,1)}, u32[]{:S(2)}, u32[]{:S(2)}) collective-permute-start(bf16[8,128,128]{2,1,0:T(8,128)(2,1)} %get-tuple-element.93), channel_id=1, source_target_pairs={{0,16},{4,20},{8,24},{12,28},{16,0},{20,4},{24,8},{28,12},{32,48},... | collective-permute-start | bytes 786440 | tf_op jit(solution)/shard_map/ppermute | solution.py:25
  105.2 5.5 %collective-permute-start.13 = (bf16[8,128,128]{2,1,0:T(8,128)(2,1)S(1)}, bf16[8,128,128]{2,1,0:T(8,128)(2,1)S(1)}, u32[]{:S(2)}, u32[]{:S(2)}) collective-permute-start(bf16[8,128,128]{2,1,0:T(8,128)(2,1)S(1)} %add_add_fusion), channel_id=1, source_target_pairs={{0,4},{4,0},{8,12},{12,8},{16,20},{20,16},{24,28},{28,24},{32,36},... | collective-permute-start | bytes 786440 | tf_op jit(solution)/shard_map/ppermute | solution.py:29
  108.3 7.5 %collective-permute-start.12 = (bf16[8,128,128]{2,1,0:T(8,128)(2,1)S(1)}, bf16[8,128,128]{2,1,0:T(8,128)(2,1)S(1)}, u32[]{:S(2)}, u32[]{:S(2)}) collective-permute-start(bf16[8,128,128]{2,1,0:T(8,128)(2,1)S(1)} %add_add_fusion.1), channel_id=1, source_target_pairs={{0,4},{4,0},{8,12},{12,8},{16,20},{20,16},{24,28},{28,24},{32,36},... | collective-permute-start | bytes 786440 | tf_op jit(solution)/shard_map/ppermute | solution.py:29
  115.9 6.7 %collective-permute-start.17 = (bf16[8,128,128]{2,1,0:T(8,128)(2,1)S(1)}, bf16[8,128,128]{2,1,0:T(8,128)(2,1)S(1)}, u32[]{:S(2)}, u32[]{:S(2)}) collective-permute-start(bf16[8,128,128]{2,1,0:T(8,128)(2,1)S(1)} %add.521.refs_0_), channel_id=1, source_target_pairs={{0,32},{4,36},{8,40},{12,44},{16,48},{20,52},{24,56},{28,60},{32,6... | collective-permute-start | bytes 786440 | tf_op jit(solution)/shard_map/ppermute | solution.py:20
  117.8 7.8 %collective-permute-start.18 = (bf16[8,128,128]{2,1,0:T(8,128)(2,1)S(1)}, bf16[8,128,128]{2,1,0:T(8,128)(2,1)S(1)}, u32[]{:S(2)}, u32[]{:S(2)}) collective-permute-start(bf16[8,128,128]{2,1,0:T(8,128)(2,1)S(1)} %add.521.refs_0_), channel_id=1, source_target_pairs={{0,96},{4,100},{8,104},{12,108},{16,112},{20,116},{24,120},{28,124... | collective-permute-start | bytes 786440 | tf_op jit(solution)/shard_map/ppermute | solution.py:20
  119.1 8.3 %collective-permute-start.19 = (bf16[8,128,128]{2,1,0:T(8,128)(2,1)S(1)}, bf16[8,128,128]{2,1,0:T(8,128)(2,1)S(1)}, u32[]{:S(2)}, u32[]{:S(2)}) collective-permute-start(bf16[8,128,128]{2,1,0:T(8,128)(2,1)S(1)} %add.521.refs_0_), channel_id=1, source_target_pairs={{0,64},{4,68},{8,72},{12,76},{16,80},{20,84},{24,88},{28,92},{32,9... | collective-permute-start | bytes 786440 | tf_op jit(solution)/shard_map/ppermute | solution.py:20
  119.6 7.7 %collective-permute-start.14 = (bf16[8,128,128]{2,1,0:T(8,128)(2,1)S(1)}, bf16[8,128,128]{2,1,0:T(8,128)(2,1)S(1)}, u32[]{:S(2)}, u32[]{:S(2)}) collective-permute-start(bf16[8,128,128]{2,1,0:T(8,128)(2,1)S(1)} %add.520.refs_0_), channel_id=1, source_target_pairs={{0,8},{4,12},{8,16},{12,20},{16,24},{20,28},{24,0},{28,4},{32,40},... | collective-permute-start | bytes 786440 | tf_op jit(solution)/shard_map/ppermute | solution.py:25
  121.0 6.4 %collective-permute-start.15 = (bf16[8,128,128]{2,1,0:T(8,128)(2,1)S(1)}, bf16[8,128,128]{2,1,0:T(8,128)(2,1)S(1)}, u32[]{:S(2)}, u32[]{:S(2)}) collective-permute-start(bf16[8,128,128]{2,1,0:T(8,128)(2,1)S(1)} %add.520.refs_0_), channel_id=1, source_target_pairs={{0,24},{4,28},{8,0},{12,4},{16,8},{20,12},{24,16},{28,20},{32,56},... | collective-permute-start | bytes 786440 | tf_op jit(solution)/shard_map/ppermute | solution.py:25
  122.6 9.1 %collective-permute-start.16 = (bf16[8,128,128]{2,1,0:T(8,128)(2,1)S(1)}, bf16[8,128,128]{2,1,0:T(8,128)(2,1)S(1)}, u32[]{:S(2)}, u32[]{:S(2)}) collective-permute-start(bf16[8,128,128]{2,1,0:T(8,128)(2,1)S(1)} %add.520.refs_0_), channel_id=1, source_target_pairs={{0,16},{4,20},{8,24},{12,28},{16,0},{20,4},{24,8},{28,12},{32,48},... | collective-permute-start | bytes 786440 | tf_op jit(solution)/shard_map/ppermute | solution.py:25
  131.8 18.8 %collective-permute-start.22 = (bf16[32,128,128]{2,1,0:T(8,128)(2,1)S(1)}, bf16[32,128,128]{2,1,0:T(8,128)(2,1)S(1)}, u32[]{:S(2)}, u32[]{:S(2)}) collective-permute-start(bf16[32,128,128]{2,1,0:T(8,128)(2,1)S(1)} %assemble.3.refs_1_), channel_id=1, source_target_pairs={{0,8},{4,12},{8,16},{12,20},{16,24},{20,28},{24,0},{28,4},{32,40},... | collective-permute-start | bytes 3145736 | tf_op jit(solution)/shard_map/ppermute | solution.py:25
  132.4 21.8 %collective-permute-start.23 = (bf16[32,128,128]{2,1,0:T(8,128)(2,1)S(1)}, bf16[32,128,128]{2,1,0:T(8,128)(2,1)S(1)}, u32[]{:S(2)}, u32[]{:S(2)}) collective-permute-start(bf16[32,128,128]{2,1,0:T(8,128)(2,1)S(1)} %assemble.3.refs_1_), channel_id=1, source_target_pairs={{0,24},{4,28},{8,0},{12,4},{16,8},{20,12},{24,16},{28,20},{32,56},... | collective-permute-start | bytes 3145736 | tf_op jit(solution)/shard_map/ppermute | solution.py:25
  134.6 19.7 %collective-permute-start.20 = (bf16[32,128,128]{2,1,0:T(8,128)(2,1)S(1)}, bf16[32,128,128]{2,1,0:T(8,128)(2,1)S(1)}, u32[]{:S(2)}, u32[]{:S(2)}) collective-permute-start(bf16[32,128,128]{2,1,0:T(8,128)(2,1)S(1)} %assemble.2.refs_0_), channel_id=1, source_target_pairs={{0,32},{4,36},{8,40},{12,44},{16,48},{20,52},{24,56},{28,60},{32,6... | collective-permute-start | bytes 3145736 | tf_op jit(solution)/shard_map/ppermute | solution.py:20
  134.9 19.4 %collective-permute-start.21 = (bf16[32,128,128]{2,1,0:T(8,128)(2,1)S(1)}, bf16[32,128,128]{2,1,0:T(8,128)(2,1)S(1)}, u32[]{:S(2)}, u32[]{:S(2)}) collective-permute-start(bf16[32,128,128]{2,1,0:T(8,128)(2,1)S(1)} %assemble.2.refs_0_), channel_id=1, source_target_pairs={{0,96},{4,100},{8,104},{12,108},{16,112},{20,116},{24,120},{28,124... | collective-permute-start | bytes 3145736 | tf_op jit(solution)/shard_map/ppermute | solution.py:20
  154.3 31.2 %collective-permute-start.24 = (bf16[16,128,128]{2,1,0:T(8,128)(2,1)S(1)}, bf16[16,128,128]{2,1,0:T(8,128)(2,1)S(1)}, u32[]{:S(2)}, u32[]{:S(2)}) collective-permute-start(bf16[16,128,128]{2,1,0:T(8,128)(2,1)S(1)} %slice.61), channel_id=1, source_target_pairs={{0,32},{4,36},{8,40},{12,44},{16,48},{20,52},{24,56},{28,60},{32,6... | collective-permute-start | bytes 1572872 | tf_op jit(solution)/shard_map/ppermute | solution.py:20
  154.5 31.0 %collective-permute-start.25 = (bf16[16,128,128]{2,1,0:T(8,128)(2,1)S(1)}, bf16[16,128,128]{2,1,0:T(8,128)(2,1)S(1)}, u32[]{:S(2)}, u32[]{:S(2)}) collective-permute-start(bf16[16,128,128]{2,1,0:T(8,128)(2,1)S(1)} %slice.62), channel_id=1, source_target_pairs={{0,96},{4,100},{8,104},{12,108},{16,112},{20,116},{24,120},{28,124... | collective-permute-start | bytes 1572872 | tf_op jit(solution)/shard_map/ppermute | solution.py:20
  157.2 28.3 %collective-permute-start.26 = (bf16[16,128,128]{2,1,0:T(8,128)(2,1)S(1)}, bf16[16,128,128]{2,1,0:T(8,128)(2,1)S(1)}, u32[]{:S(2)}, u32[]{:S(2)}) collective-permute-start(bf16[16,128,128]{2,1,0:T(8,128)(2,1)S(1)} %slice.63), channel_id=1, source_target_pairs={{0,8},{4,12},{8,16},{12,20},{16,24},{20,28},{24,0},{28,4},{32,40},... | collective-permute-start | bytes 1572872 | tf_op jit(solution)/shard_map/ppermute | solution.py:25
  157.4 28.2 %collective-permute-start.27 = (bf16[16,128,128]{2,1,0:T(8,128)(2,1)S(1)}, bf16[16,128,128]{2,1,0:T(8,128)(2,1)S(1)}, u32[]{:S(2)}, u32[]{:S(2)}) collective-permute-start(bf16[16,128,128]{2,1,0:T(8,128)(2,1)S(1)} %slice.64), channel_id=1, source_target_pairs={{0,24},{4,28},{8,0},{12,4},{16,8},{20,12},{24,16},{28,20},{32,56},... | collective-permute-start | bytes 1572872 | tf_op jit(solution)/shard_map/ppermute | solution.py:25
  196.7 15.5 %collective-permute-start.28 = (bf16[32,101,256]{2,0,1:T(8,128)(2,1)S(1)}, bf16[32,101,256]{2,0,1:T(8,128)(2,1)S(1)}, u32[]{:S(2)}, u32[]{:S(2)}) collective-permute-start(bf16[32,101,256]{2,0,1:T(8,128)(2,1)S(1)} %copy.21), channel_id=1, source_target_pairs={{0,1},{1,0},{2,3},{3,2},{4,5},{5,4},{6,7},{7,6},{8,9},{9,8},{10,11... | collective-permute-start | bytes 4964360 | tf_op jit(solution)/shard_map/ppermute | solution.py:33
  212.9 22.0 %collective-permute-start.29 = (bf16[16,101,256]{2,0,1:T(8,128)(2,1)S(1)}, bf16[16,101,256]{2,0,1:T(8,128)(2,1)S(1)}, u32[]{:S(2)}, u32[]{:S(2)}) collective-permute-start(bf16[16,101,256]{2,0,1:T(8,128)(2,1)S(1)} %copy.24), channel_id=1, source_target_pairs={{0,2},{1,3},{2,0},{3,1},{4,6},{5,7},{6,4},{7,5},{8,10},{9,11},{10,... | collective-permute-start | bytes 2482184 | tf_op jit(solution)/shard_map/ppermute | solution.py:37
  235.3 4.1 %collective-permute-start.30 = (bf16[32,101,256]{2,0,1:T(8,128)(2,1)S(1)}, bf16[32,101,256]{2,0,1:T(8,128)(2,1)S(1)}, u32[]{:S(2)}, u32[]{:S(2)}) collective-permute-start(bf16[32,101,256]{2,0,1:T(8,128)(2,1)S(1)} %copy.26), channel_id=1, source_target_pairs={{0,1},{1,0},{2,3},{3,2},{4,5},{5,4},{6,7},{7,6},{8,9},{9,8},{10,11... | collective-permute-start | bytes 4964360 | tf_op jit(solution)/shard_map/ppermute | solution.py:33
  240.1 21.2 %collective-permute-start.31 = (bf16[16,101,256]{2,0,1:T(8,128)(2,1)S(1)}, bf16[16,101,256]{2,0,1:T(8,128)(2,1)S(1)}, u32[]{:S(2)}, u32[]{:S(2)}) collective-permute-start(bf16[16,101,256]{2,0,1:T(8,128)(2,1)S(1)} %copy.29), channel_id=1, source_target_pairs={{0,2},{1,3},{2,0},{3,1},{4,6},{5,7},{6,4},{7,5},{8,10},{9,11},{10,... | collective-permute-start | bytes 2482184 | tf_op jit(solution)/shard_map/ppermute | solution.py:37
  (3 other events, 24.8 us)

commit v7 on v6

--- a/solution.py
+++ b/solution.py
@@ -104,7 +104,7 @@
 
 def cross_blocks(blocks_ref, sign_ref, spec_ref, sources, src, left, right):
     step = pl.program_id(0)
-    for m in range(4):
+    for m in range(len(sources)):
 
         @pl.when(step == m)
         def _():
@@ -125,7 +125,7 @@
             both = jnp.concatenate([rows, turned], axis=0)
             cross = jnp.dot(both, spec_ref[jnp.minimum(i, last)], preferred_element_type=jnp.float32)
             for part in range(2):
-                place = pl.ds(part * 128 + step * 32 + i, ROWS, stride=STRIDE)
+                place = pl.ds(part * 128 + lax.rem(step, 4) * 32 + i, ROWS, stride=STRIDE)
                 piece = cross[part * ROWS : (part + 1) * ROWS]
                 left[place, :] = piece[:, :128]
                 right[place, :] = piece[:, 128:]
@@ -134,7 +134,7 @@
 def lag_sums(k, table_ref, left, right):
     rows = pl.ds(pl.multiple_of(k * STRIDE, 8), 256)
     cross = jnp.concatenate([left[rows, :].astype(jnp.bfloat16), right[rows, :].astype(jnp.bfloat16)], axis=1)
-    return jnp.dot(table_ref[...], cross, preferred_element_type=jnp.float32)
+    return jnp.dot(table_ref[0], cross, preferred_element_type=jnp.float32)
 
 
 def early_kernel(blocks_ref, table_ref, sign_ref, spec_ref, *refs):
@@ -147,6 +147,17 @@
         def _(first):
             for u in range(8):
                 acc_ref[first + u] = lag_sums(first + u, table_ref, left, right)
+
+
+def finish_sums(table_ref, left, right, acc, send_ref, keep_ref):
+    for start, out_ref in ((0, send_ref), (ROWS // 2, keep_ref)):
+
+        @pl.loop(0, ROWS // 2, step=8)
+        def _(first):
+            for u in range(8):
+                k = first + u + start
+                total = acc[k] + lag_sums(k, table_ref, left, right)
+                out_ref[first + u] = total[:LAGS].astype(jnp.bfloat16)
 
 
 def late_kernel(blocks_ref, table_ref, sign_ref, spec_ref, *refs):
@@ -164,52 +175,63 @@
     @pl.when(step == 3)
     def _():
         fetch.wait()
-
-        @pl.loop(0, ROWS // 2, step=8)
+        finish_sums(table_ref, left, right, acc, send_ref, keep_ref)
+
+
+def whole_kernel(blocks_ref, table_ref, sign_ref, spec_ref, *refs):
+    sources = [[r] for r in refs[:6]] + [refs[6:8], refs[8:10]]
+    send_ref, keep_ref, src, left, right, acc = refs[10:]
+    step = pl.program_id(0)
+    cross_blocks(blocks_ref, sign_ref, spec_ref, sources, src, left, right)
+
+    @pl.when(step == 3)
+    def _():
+        @pl.loop(0, ROWS, step=8)
         def _(first):
             for u in range(8):
-                k = first + u
-                send_ref[k] = (acc[k] + lag_sums(k, table_ref, left, right))[:LAGS].astype(jnp.bfloat16)
-
-        @pl.loop(0, ROWS // 2, step=8)
-        def _(first):
-            for u in range(8):
-                k = first + u + ROWS // 2
-                keep_ref[first + u] = (acc[k] + lag_sums(k, table_ref, left, right))[:LAGS].astype(jnp.bfloat16)
-
-
-def correlate(part, blocks, table, sign, spec, sources, before=None):
+                acc[first + u] = lag_sums(first + u, table_ref, left, right)
+
+    @pl.when(step == 7)
+    def _():
+        finish_sums(table_ref, left, right, acc, send_ref, keep_ref)
+
+
+def correlate(kernel, part, blocks, table, sign, spec, sources, before=None):
+    sums = jax.ShapeDtypeStruct((ROWS, LAG_PAD, 256), jnp.float32)
     half = jax.ShapeDtypeStruct((ROWS // 2, LAGS, 256), jnp.bfloat16)
-    sums = jax.ShapeDtypeStruct((ROWS, LAG_PAD, 256), jnp.float32)
-    early = before is None
-    whole = pl.BlockSpec((ROWS // 2, LAGS, 256), lambda i, s: (0, 0, 0))
+    sums_block = pl.BlockSpec((ROWS, LAG_PAD, 256), lambda i, s: (0, 0, 0))
+    half_block = pl.BlockSpec((ROWS // 2, LAGS, 256), lambda i, s: (0, 0, 0))
+    early = kernel is early_kernel
+    steps = blocks.shape[0]
     scratch = [
         pltpu.VMEM((32, ROWS, 128), jnp.bfloat16),
         pltpu.VMEM((ROWS * STRIDE, 128), jnp.float32),
         pltpu.VMEM((ROWS * STRIDE, 128), jnp.float32),
     ]
     if not early:
-        scratch += [pltpu.VMEM((ROWS, LAG_PAD, 256), jnp.float32), pltpu.SemaphoreType.DMA]
+        scratch.append(pltpu.VMEM((ROWS, LAG_PAD, 256), jnp.float32))
+    if before is not None:
+        scratch.append(pltpu.SemaphoreType.DMA)
     return pl.pallas_call(
-        early_kernel if early else late_kernel,
+        kernel,
         grid_spec=pltpu.PrefetchScalarGridSpec(
             num_scalar_prefetch=1,
-            grid=(4,),
+            grid=(steps,),
             in_specs=[
-                pl.BlockSpec((LAG_PAD, 256), lambda i, s: (0, 0)),
+                pl.BlockSpec((1, LAG_PAD, 256), lambda i, s: (i // 4, 0, 0)),
                 pl.BlockSpec((1, 128), lambda i, s: (0, 0)),
                 pl.BlockSpec((32, 128, 256), lambda i, s: (s[i], 0, 0)),
             ]
             + [pl.BlockSpec((a.shape[0], ROWS, 128), lambda i, s: (0, part, 0)) for a in sources]
-            + ([] if early else [pl.BlockSpec(memory_space=pl.ANY)]),
-            out_specs=pl.BlockSpec((ROWS, LAG_PAD, 256), lambda i, s: (0, 0, 0)) if early else [whole, whole],
+            + ([] if before is None else [pl.BlockSpec(memory_space=pl.ANY)]),
+            out_specs=sums_block if early else [half_block, half_block],
             scratch_shapes=scratch,
         ),
         out_shape=sums if early else [half, half],
-        compiler_params=pltpu.CompilerParams(vmem_limit_bytes=46 << 20),
-        cost_estimate=pl.CostEstimate(flops=12 * 10**9, bytes_accessed=16 << 20, transcendentals=0),
-        name="correlate_early" if early else "correlate_late",
-    )(blocks, table, sign, spec, *sources, *([] if early else [before]))
+        compiler_params=pltpu.CompilerParams(vmem_limit_bytes=50 << 20),
+        cost_estimate=pl.CostEstimate(flops=steps * 3 * 10**9, bytes_accessed=steps * (4 << 20), transcendentals=0),
+        name=kernel.__name__,
+    )(blocks, table, sign, spec, *sources, *([] if before is None else [before]))
 
 
 def body(spectra, src_blocks, valid):
@@ -267,15 +289,16 @@
     freqs = (32 * blocks[:, None] + jnp.arange(32, dtype=jnp.int32)[None, :]).reshape(256)
     table = lag_table(freqs, LAG_PAD, 256)
     table = table.reshape(2, LAG_PAD, 2, 128).transpose(2, 1, 0, 3).reshape(2, LAG_PAD, 256)
-    sums = [correlate(part, blocks[:4], table[0], sign, spec, first_sources) for part in range(PARTS)]
-
-    sums = barrier(sums)
+    sums = correlate(early_kernel, 0, blocks[:4], table[:1], sign, spec, first_sources)
 
     outs = []
     quarter = ROWS // 4
     last = own_rows = None
     for part in range(PARTS):
-        send, keep = correlate(part, blocks[4:], table[1], sign, spec, last_sources, sums[part])
+        if part == 0:
+            send, keep = correlate(late_kernel, 0, blocks[4:], table[1:], sign, spec, last_sources, sums)
+        else:
+            send, keep = correlate(whole_kernel, part, blocks, table, sign, spec, first_sources + last_sources)
         if last is not None:
             send, last = barrier((send, last))
             outs.append(finish(own_rows, last))

time: 264 us -> 271 us (1.027)
  waiting for transfers between devices: 104 us -> 112 us
  starting transfers between devices: 62 us -> 58.5 us
  local copies, waits for them, and re-layouts: 21.6 us -> 24.5 us
    ppermute x13, waiting for transfers between devices: 34.6 us -> 58.7 us  [shift_x(): return lax.ppermute(x, 'chan', pairs)]
    ppermute x13, waiting for transfers between devices: 30.9 us -> 19.1 us  [shift_y(): return lax.ppermute(x, 'chan', pairs)]
    ppermute x13, starting transfers between devices: 17 us -> 28.6 us  [shift_x(): return lax.ppermute(x, 'chan', pairs)]
    ppermute x2, starting transfers between devices: 13.3 us -> 6.21 us  [swap_core(): return lax.ppermute(x, 'tm', [(a, a ^ 1) for a in range(4)])]
    ppermute x2, waiting for transfers between devices: 25.2 us -> 19.5 us  [swap_far(): return lax.ppermute(x, 'tm', [(a, a ^ 2) for a in range(4)])]
    ppermute x13, starting transfers between devices: 23.3 us -> 17.7 us  [shift_y(): return lax.ppermute(x, 'chan', pairs)]
    pallas_call x4 -> x3, Pallas kernels: 46.9 us -> 46.2 us  [correlate(): pl.pallas_call(kernel, grid_spec=pltpu.PrefetchScalarGridSpec(num_scalar_...]
  transfers between devices with their start and end apart: 32 -> 32, of which waited for: 19 -> 17; matrix products, arithmetic and copies ran while one was open for 2% -> 2% of each run, Pallas kernels for 18% -> 17%
where the time goes in v7:
time: 271 us; the launch traced here: 270 us
  waiting for transfers between devices  112 us (41%)
  Pallas kernels  62.3 us (23%)
  starting transfers between devices  58.5 us (22%)
  local copies, waits for them, and re-layouts  24.5 us (9%)
  other arithmetic  12.7 us (5%)
    ppermute x13, waiting for transfers between devices, shift_x(): return lax.ppermute(x, 'chan', pairs)  58.7 us
    pallas_call x3, Pallas kernels, correlate(): pl.pallas_call(kernel, grid_spec=pltpu.PrefetchScalarGridSpec(num_scalar_...  46.2 us
    ppermute x13, starting transfers between devices, shift_x(): return lax.ppermute(x, 'chan', pairs)  28.6 us
    ppermute x2, waiting for transfers between devices, swap_far(): return lax.ppermute(x, 'tm', [(a, a ^ 2) for a in range(4)])  19.5 us
    ppermute x13, waiting for transfers between devices, shift_y(): return lax.ppermute(x, 'chan', pairs)  19.1 us
    ppermute x13, starting transfers between devices, shift_y(): return lax.ppermute(x, 'chan', pairs)  17.7 us
    transpose x1, local copies, waits for them, and re-layouts, body(): spec = jnp.transpose(spectra, (2, 1, 0, 3)).reshape(BINS, 128, 256)  16.6 us
    pallas_call x4, Pallas kernels, pick_rows(): pl.pallas_call(pick_kernel, grid_spec=pltpu.PrefetchScalarGridSpec(num_sc...  15.9 us
  transfers between devices with their start and end apart: 32, of which 17 were waited for; matrix products, arithmetic and copies ran while one was open for 2% of the time, Pallas kernels for 17%

profile of v7, /device:TPU:1, one launch (start us, length us, event | category | flops | bytes accessed | tf_op | source)
XLA Modules:
  0.0 270.4 jit_solution(18177489071202907564)
XLA Ops:
  3.4 16.6 %copy.19 = bf16[250,2,64,256]{3,2,1,0:T(8,128)(2,1)} copy(bf16[250,2,64,256]{3,1,0,2:T(2,128)(2,1)} %bitcast.52) | data formatting | bytes 32768000 | tf_op jit(solution)/shard_map/transpose | solution.py:243
  20.1 3.6 %pick_rows.7 = (bf16[32,128,128]{2,1,0:T(8,128)(2,1)S(1)}, bf16[32,128,128]{2,1,0:T(8,128)(2,1)S(1)}) custom-call(s32[2]{0:T(128)S(1)} %get-tuple-element.106.first_ref, bf16[128,256]{1,0:T(8,128)(2,1)S(1)} %fusion.1.pick_ref, f32[1,128]{1,0:T(1,128)S(1)} %broadcast_in_dim_tile.3.mask_ref, bf16[250,128,256]{2,1,0:T(8,128)(2,1)} %bitcast.41, ...), custom_call_target="tpu_custom_call" | custom-call | flops 1048576 | bytes 65536 | tf_op jit(solution)/shard_map/pick_rows/pallas_call | solution.py:62
  23.6 3.4 %collective-permute-start.4 = (bf16[32,128,128]{2,1,0:T(8,128)(2,1)S(1)}, bf16[32,128,128]{2,1,0:T(8,128)(2,1)S(1)}, u32[]{:S(2)}, u32[]{:S(2)}) collective-permute-start(bf16[32,128,128]{2,1,0:T(8,128)(2,1)S(1)} %get-tuple-element.50), channel_id=1, source_target_pairs={{0,96},{4,100},{8,104},{12,108},{16,112},{20,116},{24,120},{28,124... | collective-permute-start | bytes 3145736 | tf_op jit(solution)/shard_map/ppermute | solution.py:20
  27.0 2.7 %collective-permute-start.5 = (bf16[32,128,128]{2,1,0:T(8,128)(2,1)S(1)}, bf16[32,128,128]{2,1,0:T(8,128)(2,1)}, u32[]{:S(2)}, u32[]{:S(2)}) collective-permute-start(bf16[32,128,128]{2,1,0:T(8,128)(2,1)S(1)} %get-tuple-element.51), channel_id=1, source_target_pairs={{0,24},{4,28},{8,0},{12,4},{16,8},{20,12},{24,16},{28,20},{32,56},... | collective-permute-start | bytes 3145736 | tf_op jit(solution)/shard_map/ppermute | solution.py:25
  29.8 4.4 %pick_rows.6 = (bf16[32,128,128]{2,1,0:T(8,128)(2,1)}, bf16[32,128,128]{2,1,0:T(8,128)(2,1)}) custom-call(s32[2]{0:T(128)S(1)} %get-tuple-element.105.first_ref, bf16[128,256]{1,0:T(8,128)(2,1)S(1)} %fusion.1.pick_ref, f32[1,128]{1,0:T(1,128)S(1)} %broadcast_in_dim_tile.3.mask_ref, bf16[250,128,256]{2,1,0:T(8,128)(2,1)} %bitcast.43, ...), custom_call_target="tpu_custom_call" | custom-call | flops 1048576 | bytes 65536 | tf_op jit(solution)/shard_map/pick_rows/pallas_call | solution.py:62
  35.1 4.4 %pick_rows.5 = (bf16[32,128,128]{2,1,0:T(8,128)(2,1)}, bf16[32,128,128]{2,1,0:T(8,128)(2,1)}) custom-call(s32[2]{0:T(128)S(1)} %get-tuple-element.104.first_ref, bf16[128,256]{1,0:T(8,128)(2,1)S(1)} %fusion.1.pick_ref, f32[1,128]{1,0:T(1,128)S(1)} %broadcast_in_dim_tile.3.mask_ref, bf16[250,128,256]{2,1,0:T(8,128)(2,1)} %bitcast.45, ...), custom_call_target="tpu_custom_call" | custom-call | flops 1048576 | bytes 65536 | tf_op jit(solution)/shard_map/pick_rows/pallas_call | solution.py:62
  40.1 10.0 %collective-permute-done.4 = bf16[32,128,128]{2,1,0:T(8,128)(2,1)S(1)} collective-permute-done((bf16[32,128,128]{2,1,0:T(8,128)(2,1)S(1)}, bf16[32,128,128]{2,1,0:T(8,128)(2,1)S(1)}, u32[]{:S(2)}, u32[]{:S(2)}) %collective-permute-start.4) | collective-permute-done | bytes 1048608 | tf_op jit(solution)/shard_map/ppermute | solution.py:20
  51.0 3.6 %pick_rows.4 = (bf16[32,128,128]{2,1,0:T(8,128)(2,1)S(1)}, bf16[32,128,128]{2,1,0:T(8,128)(2,1)S(1)}) custom-call(s32[2]{0:T(128)S(1)} %get-tuple-element.103.first_ref, bf16[128,256]{1,0:T(8,128)(2,1)S(1)} %fusion.1.pick_ref, f32[1,128]{1,0:T(1,128)S(1)} %broadcast_in_dim_tile.3.mask_ref, bf16[250,128,256]{2,1,0:T(8,128)(2,1)} %bitcast.47, ...), custom_call_target="tpu_custom_call" | custom-call | flops 1048576 | bytes 65536 | tf_op jit(solution)/shard_map/pick_rows/pallas_call | solution.py:62
  54.6 4.8 %collective-permute-done.2 = bf16[32,128,128]{2,1,0:T(8,128)(2,1)} collective-permute-done((bf16[32,128,128]{2,1,0:T(8,128)(2,1)}, bf16[32,128,128]{2,1,0:T(8,128)(2,1)}, u32[]{:S(2)}, u32[]{:S(2)}) %collective-permute-start.2) | collective-permute-done | bytes 1048608 | tf_op jit(solution)/shard_map/ppermute | solution.py:20
  59.6 23.9 %collective-permute-done = bf16[32,128,128]{2,1,0:T(8,128)(2,1)} collective-permute-done((bf16[32,128,128]{2,1,0:T(8,128)(2,1)}, bf16[32,128,128]{2,1,0:T(8,128)(2,1)}, u32[]{:S(2)}, u32[]{:S(2)}) %collective-permute-start) | collective-permute-done | bytes 1048608 | tf_op jit(solution)/shard_map/ppermute | solution.py:20
  87.2 2.5 add_add_fusion.2
  89.7 17.0 %collective-permute-start.11 = (bf16[8,128,128]{2,1,0:T(8,128)(2,1)}, bf16[8,128,128]{2,1,0:T(8,128)(2,1)}, u32[]{:S(2)}, u32[]{:S(2)}) collective-permute-start(bf16[8,128,128]{2,1,0:T(8,128)(2,1)} %get-tuple-element.85), channel_id=1, source_target_pairs={{0,96},{4,100},{8,104},{12,108},{16,112},{20,116},{24,120},{28,124... | collective-permute-start | bytes 786440 | tf_op jit(solution)/shard_map/ppermute | solution.py:20
  107.3 10.5 %collective-permute-done.11 = bf16[8,128,128]{2,1,0:T(8,128)(2,1)} collective-permute-done((bf16[8,128,128]{2,1,0:T(8,128)(2,1)}, bf16[8,128,128]{2,1,0:T(8,128)(2,1)}, u32[]{:S(2)}, u32[]{:S(2)}) %collective-permute-start.11) | collective-permute-done | bytes 262176 | tf_op jit(solution)/shard_map/ppermute | solution.py:20
  117.7 2.8 %collective-permute-done.7 = bf16[8,128,128]{2,1,0:T(8,128)(2,1)} collective-permute-done((bf16[8,128,128]{2,1,0:T(8,128)(2,1)}, bf16[8,128,128]{2,1,0:T(8,128)(2,1)}, u32[]{:S(2)}, u32[]{:S(2)}) %collective-permute-start.7) | collective-permute-done | bytes 262176 | tf_op jit(solution)/shard_map/ppermute | solution.py:20
  124.9 2.9 %collective-permute-done.12 = bf16[8,128,128]{2,1,0:T(8,128)(2,1)S(1)} collective-permute-done((bf16[8,128,128]{2,1,0:T(8,128)(2,1)S(1)}, bf16[8,128,128]{2,1,0:T(8,128)(2,1)S(1)}, u32[]{:S(2)}, u32[]{:S(2)}) %collective-permute-start.12) | collective-permute-done | bytes 262176 | tf_op jit(solution)/shard_map/ppermute | solution.py:29
  127.8 5.6 %collective-permute-done.13 = bf16[8,128,128]{2,1,0:T(8,128)(2,1)S(1)} collective-permute-done((bf16[8,128,128]{2,1,0:T(8,128)(2,1)S(1)}, bf16[8,128,128]{2,1,0:T(8,128)(2,1)S(1)}, u32[]{:S(2)}, u32[]{:S(2)}) %collective-permute-start.13) | collective-permute-done | bytes 262176 | tf_op jit(solution)/shard_map/ppermute | solution.py:29
  135.6 4.0 %collective-permute-start.16 = (bf16[8,128,128]{2,1,0:T(8,128)(2,1)S(1)}, bf16[8,128,128]{2,1,0:T(8,128)(2,1)S(1)}, u32[]{:S(2)}, u32[]{:S(2)}) collective-permute-start(bf16[8,128,128]{2,1,0:T(8,128)(2,1)S(1)} %add.520.refs_0_), channel_id=1, source_target_pairs={{0,16},{4,20},{8,24},{12,28},{16,0},{20,4},{24,8},{28,12},{32,48},... | collective-permute-start | bytes 786440 | tf_op jit(solution)/shard_map/ppermute | solution.py:25
  140.9 2.4 collective-permute-start.14
  143.2 2.4 collective-permute-done.18.refs_2_
  145.6 2.3 collective-permute-done.17.refs_1_
  154.8 14.5 %collective-permute-done.23.refs_1_.refs_5_ = bf16[32,128,128]{2,1,0:T(8,128)(2,1)S(1)} collective-permute-done((bf16[32,128,128]{2,1,0:T(8,128)(2,1)S(1)}, bf16[32,128,128]{2,1,0:T(8,128)(2,1)S(1)}, u32[]{:S(2)}, u32[]{:S(2)}) %collective-permute-start.23) | collective-permute-done | bytes 1048608 | tf_op jit(solution)/shard_map/ppermute | solution.py:25
  169.2 3.1 %collective-permute-done.22.refs_0_.refs_4_ = bf16[32,128,128]{2,1,0:T(8,128)(2,1)S(1)} collective-permute-done((bf16[32,128,128]{2,1,0:T(8,128)(2,1)S(1)}, bf16[32,128,128]{2,1,0:T(8,128)(2,1)S(1)}, u32[]{:S(2)}, u32[]{:S(2)}) %collective-permute-start.22) | collective-permute-done | bytes 1048608 | tf_op jit(solution)/shard_map/ppermute | solution.py:25
  174.7 2.7 collective-permute-start.25
  177.3 2.4 collective-permute-start.27
  179.7 12.9 %early_kernel.1.refs_6_ = f32[64,112,256]{2,1,0:T(8,128)} custom-call(s32[4]{0:T(128)S(1)} %pad_add_fusion.5.blocks_ref, bf16[1,112,256]{2,1,0:T(8,128)(2,1)S(1)} %bitcast.40, bf16[1,128]{1,0:T(2,128)(2,1)S(1)} %fusion.11.sign_ref, bf16[250,128,256]{2,1,0:T(8,128)(2,1)} %bitcast.49, bf16[32,128,128]{2,1,0:T(8,128)(2,1)S(1)} %assemble.2.refs_0_, ...), custom_call_target="tpu_custom_call" | custom-call | flops 12000000000 | bytes 16777216 | tf_op jit(solution)/shard_map/early_kernel/pallas_call | solution.py:215
  192.7 12.7 %late_kernel.1 = (bf16[32,101,256]{2,1,0:T(8,128)(2,1)}, bf16[32,101,256]{2,1,0:T(8,128)(2,1)}) custom-call(s32[4]{0:T(128)S(1)} %pad_add_fusion.blocks_ref, bf16[1,112,256]{2,1,0:T(8,128)(2,1)S(1)} %bitcast.39, bf16[1,128]{1,0:T(2,128)(2,1)S(1)} %fusion.11.sign_ref, bf16[250,128,256]{2,1,0:T(8,128)(2,1)} %bitcast.50, ...), custom_call_target="tpu_custom_call" | custom-call | flops 12000000000 | bytes 16777216 | tf_op jit(solution)/shard_map/late_kernel/pallas_call | solution.py:215
  207.2 5.5 %collective-permute-start.28 = (bf16[32,101,256]{2,0,1:T(8,128)(2,1)S(1)}, bf16[32,101,256]{2,0,1:T(8,128)(2,1)S(1)}, u32[]{:S(2)}, u32[]{:S(2)}) collective-permute-start(bf16[32,101,256]{2,0,1:T(8,128)(2,1)S(1)} %copy.21), channel_id=1, source_target_pairs={{0,1},{1,0},{2,3},{3,2},{4,5},{5,4},{6,7},{7,6},{8,9},{9,8},{10,11... | collective-permute-start | bytes 4964360 | tf_op jit(solution)/shard_map/ppermute | solution.py:33
  212.7 3.1 %collective-permute-done.28 = bf16[32,101,256]{2,0,1:T(8,128)(2,1)S(1)} collective-permute-done((bf16[32,101,256]{2,0,1:T(8,128)(2,1)S(1)}, bf16[32,101,256]{2,0,1:T(8,128)(2,1)S(1)}, u32[]{:S(2)}, u32[]{:S(2)}) %collective-permute-start.28) | collective-permute-done | bytes 1654816 | tf_op jit(solution)/shard_map/ppermute | solution.py:33
  216.5 3.1 %collective-permute-start.29 = (bf16[16,101,256]{2,0,1:T(8,128)(2,1)S(1)}, bf16[16,101,256]{2,0,1:T(8,128)(2,1)S(1)}, u32[]{:S(2)}, u32[]{:S(2)}) collective-permute-start(bf16[16,101,256]{2,0,1:T(8,128)(2,1)S(1)} %copy.25), channel_id=1, source_target_pairs={{0,2},{1,3},{2,0},{3,1},{4,6},{5,7},{6,4},{7,5},{8,10},{9,11},{10,... | collective-permute-start | bytes 2482184 | tf_op jit(solution)/shard_map/ppermute | solution.py:37
  219.6 20.7 %whole_kernel.1 = (bf16[32,101,256]{2,1,0:T(8,128)(2,1)}, bf16[32,101,256]{2,1,0:T(8,128)(2,1)}) custom-call(s32[8]{0:T(128)S(1)} %stack.81.blocks_ref, bf16[2,112,256]{2,1,0:T(8,128)(2,1)S(1)} %bitcast.38, bf16[1,128]{1,0:T(2,128)(2,1)S(1)} %fusion.11.sign_ref, bf16[250,128,256]{2,1,0:T(8,128)(2,1)} %bitcast.51, bf16[32,128,128]{2,1,0:T(8,128)(2,1)S(1)} %assemble.2.refs_0_, ...), custom_call_target="tpu_custom_call" | custom-call | flops 24000000000 | bytes 33554432 | tf_op jit(solution)/shard_map/whole_kernel/pallas_call | solution.py:215
  242.9 3.2 %collective-permute-done.30 = bf16[32,101,256]{2,0,1:T(8,128)(2,1)S(1)} collective-permute-done((bf16[32,101,256]{2,0,1:T(8,128)(2,1)S(1)}, bf16[32,101,256]{2,0,1:T(8,128)(2,1)S(1)}, u32[]{:S(2)}, u32[]{:S(2)}) %collective-permute-start.30) | collective-permute-done | bytes 1654816 | tf_op jit(solution)/shard_map/ppermute | solution.py:33
  248.5 19.5 %collective-permute-done.31 = bf16[16,101,256]{2,0,1:T(8,128)(2,1)S(1)} collective-permute-done((bf16[16,101,256]{2,0,1:T(8,128)(2,1)S(1)}, bf16[16,101,256]{2,0,1:T(8,128)(2,1)S(1)}, u32[]{:S(2)}, u32[]{:S(2)}) %collective-permute-start.31) | collective-permute-done | bytes 827424 | tf_op jit(solution)/shard_map/ppermute | solution.py:37
  (109 shorter events, 37.3 us)
Async XLA Ops:
  23.6 26.4 %collective-permute-start.4 = (bf16[32,128,128]{2,1,0:T(8,128)(2,1)S(1)}, bf16[32,128,128]{2,1,0:T(8,128)(2,1)S(1)}, u32[]{:S(2)}, u32[]{:S(2)}) collective-permute-start(bf16[32,128,128]{2,1,0:T(8,128)(2,1)S(1)} %get-tuple-element.50), channel_id=1, source_target_pairs={{0,96},{4,100},{8,104},{12,108},{16,112},{20,116},{24,120},{28,124... | collective-permute-start | bytes 3145736 | tf_op jit(solution)/shard_map/ppermute | solution.py:20
  27.0 27.6 %collective-permute-start.5 = (bf16[32,128,128]{2,1,0:T(8,128)(2,1)S(1)}, bf16[32,128,128]{2,1,0:T(8,128)(2,1)}, u32[]{:S(2)}, u32[]{:S(2)}) collective-permute-start(bf16[32,128,128]{2,1,0:T(8,128)(2,1)S(1)} %get-tuple-element.51), channel_id=1, source_target_pairs={{0,24},{4,28},{8,0},{12,4},{16,8},{20,12},{24,16},{28,20},{32,56},... | collective-permute-start | bytes 3145736 | tf_op jit(solution)/shard_map/ppermute | solution.py:25
  34.1 25.3 %collective-permute-start.2 = (bf16[32,128,128]{2,1,0:T(8,128)(2,1)}, bf16[32,128,128]{2,1,0:T(8,128)(2,1)}, u32[]{:S(2)}, u32[]{:S(2)}) collective-permute-start(bf16[32,128,128]{2,1,0:T(8,128)(2,1)} %get-tuple-element.48), channel_id=1, source_target_pairs={{0,64},{4,68},{8,72},{12,76},{16,80},{20,84},{24,88},{28,92},{32,9... | collective-permute-start | bytes 3145736 | tf_op jit(solution)/shard_map/ppermute | solution.py:20
  34.6 25.0 %collective-permute-start.3 = (bf16[32,128,128]{2,1,0:T(8,128)(2,1)}, bf16[32,128,128]{2,1,0:T(8,128)(2,1)}, u32[]{:S(2)}, u32[]{:S(2)}) collective-permute-start(bf16[32,128,128]{2,1,0:T(8,128)(2,1)} %get-tuple-element.49), channel_id=1, source_target_pairs={{0,16},{4,20},{8,24},{12,28},{16,0},{20,4},{24,8},{28,12},{32,48},... | collective-permute-start | bytes 3145736 | tf_op jit(solution)/shard_map/ppermute | solution.py:25
  39.5 44.0 %collective-permute-start = (bf16[32,128,128]{2,1,0:T(8,128)(2,1)}, bf16[32,128,128]{2,1,0:T(8,128)(2,1)}, u32[]{:S(2)}, u32[]{:S(2)}) collective-permute-start(bf16[32,128,128]{2,1,0:T(8,128)(2,1)} %get-tuple-element.46), channel_id=1, source_target_pairs={{0,32},{4,36},{8,40},{12,44},{16,48},{20,52},{24,56},{28,60},{32,6... | collective-permute-start | bytes 3145736 | tf_op jit(solution)/shard_map/ppermute | solution.py:20
  50.1 33.4 %collective-permute-start.1 = (bf16[32,128,128]{2,1,0:T(8,128)(2,1)}, bf16[32,128,128]{2,1,0:T(8,128)(2,1)}, u32[]{:S(2)}, u32[]{:S(2)}) collective-permute-start(bf16[32,128,128]{2,1,0:T(8,128)(2,1)} %get-tuple-element.47), channel_id=1, source_target_pairs={{0,8},{4,12},{8,16},{12,20},{16,24},{20,28},{24,0},{28,4},{32,40},... | collective-permute-start | bytes 3145736 | tf_op jit(solution)/shard_map/ppermute | solution.py:25
  85.7 21.0 %collective-permute-start.10 = (bf16[8,128,128]{2,1,0:T(8,128)(2,1)}, bf16[8,128,128]{2,1,0:T(8,128)(2,1)S(1)}, u32[]{:S(2)}, u32[]{:S(2)}) collective-permute-start(bf16[8,128,128]{2,1,0:T(8,128)(2,1)} %get-tuple-element.88), channel_id=1, source_target_pairs={{0,24},{4,28},{8,0},{12,4},{16,8},{20,12},{24,16},{28,20},{32,56},... | collective-permute-start | bytes 786440 | tf_op jit(solution)/shard_map/ppermute | solution.py:25
  86.2 21.1 %collective-permute-start.8 = (bf16[8,128,128]{2,1,0:T(8,128)(2,1)S(1)}, bf16[8,128,128]{2,1,0:T(8,128)(2,1)S(1)}, u32[]{:S(2)}, u32[]{:S(2)}) collective-permute-start(bf16[8,128,128]{2,1,0:T(8,128)(2,1)S(1)} %get-tuple-element.89), channel_id=1, source_target_pairs={{0,16},{4,20},{8,24},{12,28},{16,0},{20,4},{24,8},{28,12},{32,48},... | collective-permute-start | bytes 786440 | tf_op jit(solution)/shard_map/ppermute | solution.py:25
  86.2 21.1 %collective-permute-start.6 = (bf16[8,128,128]{2,1,0:T(8,128)(2,1)S(1)}, bf16[8,128,128]{2,1,0:T(8,128)(2,1)S(1)}, u32[]{:S(2)}, u32[]{:S(2)}) collective-permute-start(bf16[8,128,128]{2,1,0:T(8,128)(2,1)S(1)} %get-tuple-element.90), channel_id=1, source_target_pairs={{0,8},{4,12},{8,16},{12,20},{16,24},{20,28},{24,0},{28,4},{32,40},... | collective-permute-start | bytes 786440 | tf_op jit(solution)/shard_map/ppermute | solution.py:25
  89.7 28.0 %collective-permute-start.11 = (bf16[8,128,128]{2,1,0:T(8,128)(2,1)}, bf16[8,128,128]{2,1,0:T(8,128)(2,1)}, u32[]{:S(2)}, u32[]{:S(2)}) collective-permute-start(bf16[8,128,128]{2,1,0:T(8,128)(2,1)} %get-tuple-element.85), channel_id=1, source_target_pairs={{0,96},{4,100},{8,104},{12,108},{16,112},{20,116},{24,120},{28,124... | collective-permute-start | bytes 786440 | tf_op jit(solution)/shard_map/ppermute | solution.py:20
  106.7 11.0 %collective-permute-start.9 = (bf16[8,128,128]{2,1,0:T(8,128)(2,1)}, bf16[8,128,128]{2,1,0:T(8,128)(2,1)}, u32[]{:S(2)}, u32[]{:S(2)}) collective-permute-start(bf16[8,128,128]{2,1,0:T(8,128)(2,1)} %get-tuple-element.86), channel_id=1, source_target_pairs={{0,64},{4,68},{8,72},{12,76},{16,80},{20,84},{24,88},{28,92},{32,9... | collective-permute-start | bytes 786440 | tf_op jit(solution)/shard_map/ppermute | solution.py:20
  106.7 13.8 %collective-permute-start.7 = (bf16[8,128,128]{2,1,0:T(8,128)(2,1)}, bf16[8,128,128]{2,1,0:T(8,128)(2,1)}, u32[]{:S(2)}, u32[]{:S(2)}) collective-permute-start(bf16[8,128,128]{2,1,0:T(8,128)(2,1)} %get-tuple-element.87), channel_id=1, source_target_pairs={{0,32},{4,36},{8,40},{12,44},{16,48},{20,52},{24,56},{28,60},{32,6... | collective-permute-start | bytes 786440 | tf_op jit(solution)/shard_map/ppermute | solution.py:20
  121.7 6.1 %collective-permute-start.12 = (bf16[8,128,128]{2,1,0:T(8,128)(2,1)S(1)}, bf16[8,128,128]{2,1,0:T(8,128)(2,1)S(1)}, u32[]{:S(2)}, u32[]{:S(2)}) collective-permute-start(bf16[8,128,128]{2,1,0:T(8,128)(2,1)S(1)} %add_add_fusion.1), channel_id=1, source_target_pairs={{0,4},{4,0},{8,12},{12,8},{16,20},{20,16},{24,28},{28,24},{32,36},... | collective-permute-start | bytes 786440 | tf_op jit(solution)/shard_map/ppermute | solution.py:29
  124.8 8.6 %collective-permute-start.13 = (bf16[8,128,128]{2,1,0:T(8,128)(2,1)S(1)}, bf16[8,128,128]{2,1,0:T(8,128)(2,1)S(1)}, u32[]{:S(2)}, u32[]{:S(2)}) collective-permute-start(bf16[8,128,128]{2,1,0:T(8,128)(2,1)S(1)} %add_add_fusion), channel_id=1, source_target_pairs={{0,4},{4,0},{8,12},{12,8},{16,20},{20,16},{24,28},{28,24},{32,36},... | collective-permute-start | bytes 786440 | tf_op jit(solution)/shard_map/ppermute | solution.py:29
  133.5 7.3 %collective-permute-start.19 = (bf16[8,128,128]{2,1,0:T(8,128)(2,1)S(1)}, bf16[8,128,128]{2,1,0:T(8,128)(2,1)S(1)}, u32[]{:S(2)}, u32[]{:S(2)}) collective-permute-start(bf16[8,128,128]{2,1,0:T(8,128)(2,1)S(1)} %add.521.refs_0_), channel_id=1, source_target_pairs={{0,64},{4,68},{8,72},{12,76},{16,80},{20,84},{24,88},{28,92},{32,9... | collective-permute-start | bytes 786440 | tf_op jit(solution)/shard_map/ppermute | solution.py:20
  134.0 11.6 %collective-permute-start.18 = (bf16[8,128,128]{2,1,0:T(8,128)(2,1)S(1)}, bf16[8,128,128]{2,1,0:T(8,128)(2,1)S(1)}, u32[]{:S(2)}, u32[]{:S(2)}) collective-permute-start(bf16[8,128,128]{2,1,0:T(8,128)(2,1)S(1)} %add.521.refs_0_), channel_id=1, source_target_pairs={{0,96},{4,100},{8,104},{12,108},{16,112},{20,116},{24,120},{28,124... | collective-permute-start | bytes 786440 | tf_op jit(solution)/shard_map/ppermute | solution.py:20
  134.7 13.2 %collective-permute-start.17 = (bf16[8,128,128]{2,1,0:T(8,128)(2,1)S(1)}, bf16[8,128,128]{2,1,0:T(8,128)(2,1)S(1)}, u32[]{:S(2)}, u32[]{:S(2)}) collective-permute-start(bf16[8,128,128]{2,1,0:T(8,128)(2,1)S(1)} %add.521.refs_0_), channel_id=1, source_target_pairs={{0,32},{4,36},{8,40},{12,44},{16,48},{20,52},{24,56},{28,60},{32,6... | collective-permute-start | bytes 786440 | tf_op jit(solution)/shard_map/ppermute | solution.py:20
  135.6 12.3 %collective-permute-start.16 = (bf16[8,128,128]{2,1,0:T(8,128)(2,1)S(1)}, bf16[8,128,128]{2,1,0:T(8,128)(2,1)S(1)}, u32[]{:S(2)}, u32[]{:S(2)}) collective-permute-start(bf16[8,128,128]{2,1,0:T(8,128)(2,1)S(1)} %add.520.refs_0_), channel_id=1, source_target_pairs={{0,16},{4,20},{8,24},{12,28},{16,0},{20,4},{24,8},{28,12},{32,48},... | collective-permute-start | bytes 786440 | tf_op jit(solution)/shard_map/ppermute | solution.py:25
  139.6 8.4 %collective-permute-start.15 = (bf16[8,128,128]{2,1,0:T(8,128)(2,1)S(1)}, bf16[8,128,128]{2,1,0:T(8,128)(2,1)S(1)}, u32[]{:S(2)}, u32[]{:S(2)}) collective-permute-start(bf16[8,128,128]{2,1,0:T(8,128)(2,1)S(1)} %add.520.refs_0_), channel_id=1, source_target_pairs={{0,24},{4,28},{8,0},{12,4},{16,8},{20,12},{24,16},{28,20},{32,56},... | collective-permute-start | bytes 786440 | tf_op jit(solution)/shard_map/ppermute | solution.py:25
  140.9 8.4 %collective-permute-start.14 = (bf16[8,128,128]{2,1,0:T(8,128)(2,1)S(1)}, bf16[8,128,128]{2,1,0:T(8,128)(2,1)S(1)}, u32[]{:S(2)}, u32[]{:S(2)}) collective-permute-start(bf16[8,128,128]{2,1,0:T(8,128)(2,1)S(1)} %add.520.refs_0_), channel_id=1, source_target_pairs={{0,8},{4,12},{8,16},{12,20},{16,24},{20,28},{24,0},{28,4},{32,40},... | collective-permute-start | bytes 786440 | tf_op jit(solution)/shard_map/ppermute | solution.py:25
  149.3 19.9 %collective-permute-start.23 = (bf16[32,128,128]{2,1,0:T(8,128)(2,1)S(1)}, bf16[32,128,128]{2,1,0:T(8,128)(2,1)S(1)}, u32[]{:S(2)}, u32[]{:S(2)}) collective-permute-start(bf16[32,128,128]{2,1,0:T(8,128)(2,1)S(1)} %assemble.3.refs_1_), channel_id=1, source_target_pairs={{0,24},{4,28},{8,0},{12,4},{16,8},{20,12},{24,16},{28,20},{32,56},... | collective-permute-start | bytes 3145736 | tf_op jit(solution)/shard_map/ppermute | solution.py:25
  151.2 21.2 %collective-permute-start.22 = (bf16[32,128,128]{2,1,0:T(8,128)(2,1)S(1)}, bf16[32,128,128]{2,1,0:T(8,128)(2,1)S(1)}, u32[]{:S(2)}, u32[]{:S(2)}) collective-permute-start(bf16[32,128,128]{2,1,0:T(8,128)(2,1)S(1)} %assemble.3.refs_1_), channel_id=1, source_target_pairs={{0,8},{4,12},{8,16},{12,20},{16,24},{20,28},{24,0},{28,4},{32,40},... | collective-permute-start | bytes 3145736 | tf_op jit(solution)/shard_map/ppermute | solution.py:25
  151.6 20.7 %collective-permute-start.21 = (bf16[32,128,128]{2,1,0:T(8,128)(2,1)S(1)}, bf16[32,128,128]{2,1,0:T(8,128)(2,1)S(1)}, u32[]{:S(2)}, u32[]{:S(2)}) collective-permute-start(bf16[32,128,128]{2,1,0:T(8,128)(2,1)S(1)} %assemble.2.refs_0_), channel_id=1, source_target_pairs={{0,96},{4,100},{8,104},{12,108},{16,112},{20,116},{24,120},{28,124... | collective-permute-start | bytes 3145736 | tf_op jit(solution)/shard_map/ppermute | solution.py:20
  153.2 21.3 %collective-permute-start.20 = (bf16[32,128,128]{2,1,0:T(8,128)(2,1)S(1)}, bf16[32,128,128]{2,1,0:T(8,128)(2,1)S(1)}, u32[]{:S(2)}, u32[]{:S(2)}) collective-permute-start(bf16[32,128,128]{2,1,0:T(8,128)(2,1)S(1)} %assemble.2.refs_0_), channel_id=1, source_target_pairs={{0,32},{4,36},{8,40},{12,44},{16,48},{20,52},{24,56},{28,60},{32,6... | collective-permute-start | bytes 3145736 | tf_op jit(solution)/shard_map/ppermute | solution.py:20
  174.7 18.0 %collective-permute-start.25 = (bf16[16,128,128]{2,1,0:T(8,128)(2,1)S(1)}, bf16[16,128,128]{2,1,0:T(8,128)(2,1)S(1)}, u32[]{:S(2)}, u32[]{:S(2)}) collective-permute-start(bf16[16,128,128]{2,1,0:T(8,128)(2,1)S(1)} %slice.63), channel_id=1, source_target_pairs={{0,96},{4,100},{8,104},{12,108},{16,112},{20,116},{24,120},{28,124... | collective-permute-start | bytes 1572872 | tf_op jit(solution)/shard_map/ppermute | solution.py:20
  177.3 15.3 %collective-permute-start.24 = (bf16[16,128,128]{2,1,0:T(8,128)(2,1)S(1)}, bf16[16,128,128]{2,1,0:T(8,128)(2,1)S(1)}, u32[]{:S(2)}, u32[]{:S(2)}) collective-permute-start(bf16[16,128,128]{2,1,0:T(8,128)(2,1)S(1)} %slice.62), channel_id=1, source_target_pairs={{0,32},{4,36},{8,40},{12,44},{16,48},{20,52},{24,56},{28,60},{32,6... | collective-permute-start | bytes 1572872 | tf_op jit(solution)/shard_map/ppermute | solution.py:20
  177.3 15.3 %collective-permute-start.27 = (bf16[16,128,128]{2,1,0:T(8,128)(2,1)S(1)}, bf16[16,128,128]{2,1,0:T(8,128)(2,1)S(1)}, u32[]{:S(2)}, u32[]{:S(2)}) collective-permute-start(bf16[16,128,128]{2,1,0:T(8,128)(2,1)S(1)} %slice.65), channel_id=1, source_target_pairs={{0,24},{4,28},{8,0},{12,4},{16,8},{20,12},{24,16},{28,20},{32,56},... | collective-permute-start | bytes 1572872 | tf_op jit(solution)/shard_map/ppermute | solution.py:25
  179.7 12.9 %collective-permute-start.26 = (bf16[16,128,128]{2,1,0:T(8,128)(2,1)S(1)}, bf16[16,128,128]{2,1,0:T(8,128)(2,1)S(1)}, u32[]{:S(2)}, u32[]{:S(2)}) collective-permute-start(bf16[16,128,128]{2,1,0:T(8,128)(2,1)S(1)} %slice.64), channel_id=1, source_target_pairs={{0,8},{4,12},{8,16},{12,20},{16,24},{20,28},{24,0},{28,4},{32,40},... | collective-permute-start | bytes 1572872 | tf_op jit(solution)/shard_map/ppermute | solution.py:25
  207.2 8.6 %collective-permute-start.28 = (bf16[32,101,256]{2,0,1:T(8,128)(2,1)S(1)}, bf16[32,101,256]{2,0,1:T(8,128)(2,1)S(1)}, u32[]{:S(2)}, u32[]{:S(2)}) collective-permute-start(bf16[32,101,256]{2,0,1:T(8,128)(2,1)S(1)} %copy.21), channel_id=1, source_target_pairs={{0,1},{1,0},{2,3},{3,2},{4,5},{5,4},{6,7},{7,6},{8,9},{9,8},{10,11... | collective-permute-start | bytes 4964360 | tf_op jit(solution)/shard_map/ppermute | solution.py:33
  216.5 23.8 %collective-permute-start.29 = (bf16[16,101,256]{2,0,1:T(8,128)(2,1)S(1)}, bf16[16,101,256]{2,0,1:T(8,128)(2,1)S(1)}, u32[]{:S(2)}, u32[]{:S(2)}) collective-permute-start(bf16[16,101,256]{2,0,1:T(8,128)(2,1)S(1)} %copy.25), channel_id=1, source_target_pairs={{0,2},{1,3},{2,0},{3,1},{4,6},{5,7},{6,4},{7,5},{8,10},{9,11},{10,... | collective-permute-start | bytes 2482184 | tf_op jit(solution)/shard_map/ppermute | solution.py:37
  242.1 3.9 %collective-permute-start.30 = (bf16[32,101,256]{2,0,1:T(8,128)(2,1)S(1)}, bf16[32,101,256]{2,0,1:T(8,128)(2,1)S(1)}, u32[]{:S(2)}, u32[]{:S(2)}) collective-permute-start(bf16[32,101,256]{2,0,1:T(8,128)(2,1)S(1)} %copy.27), channel_id=1, source_target_pairs={{0,1},{1,0},{2,3},{3,2},{4,5},{5,4},{6,7},{7,6},{8,9},{9,8},{10,11... | collective-permute-start | bytes 4964360 | tf_op jit(solution)/shard_map/ppermute | solution.py:33
  246.7 21.2 %collective-permute-start.31 = (bf16[16,101,256]{2,0,1:T(8,128)(2,1)S(1)}, bf16[16,101,256]{2,0,1:T(8,128)(2,1)S(1)}, u32[]{:S(2)}, u32[]{:S(2)}) collective-permute-start(bf16[16,101,256]{2,0,1:T(8,128)(2,1)S(1)} %copy.30), channel_id=1, source_target_pairs={{0,2},{1,3},{2,0},{3,1},{4,6},{5,7},{6,4},{7,5},{8,10},{9,11},{10,... | collective-permute-start | bytes 2482184 | tf_op jit(solution)/shard_map/ppermute | solution.py:37
  (9 other events, 104.6 us)

commit v8 on v7

--- a/solution.py
+++ b/solution.py
@@ -254,7 +254,12 @@
     sign = jnp.where(jnp.arange(128) < 64, -1.0, 1.0).astype(jnp.bfloat16)[None, :]
 
     barrier = lax.optimization_barrier
-    own = {d: pick_rows(jnp.stack([2 * ((x + d) % 4), 8 + 2 * ((y + d) % 4)]), pick, mask, spec) for d in (1, 3, 2, 0)}
+    own = {}
+    for d, before in ((1, None), (2, 1), (3, 2), (0, 3)):
+        first = jnp.stack([2 * ((x + d) % 4), 8 + 2 * ((y + d) % 4)])
+        if before is not None:
+            first, own[before] = barrier((first, own[before]))
+        own[d] = pick_rows(first, pick, mask, spec)
     got = {d: (shift_x(own[d][0], d), shift_y(own[d][1], d)) for d in (1, 3, 2)}
     got = barrier(got)
 

time: 271 us -> 258 us (0.952)
  starting transfers between devices: 58.5 us -> 44.7 us
    ppermute x13, waiting for transfers between devices: 19.1 us -> 36.4 us  [shift_y(): return lax.ppermute(x, 'chan', pairs)]
    ppermute x13, waiting for transfers between devices: 58.7 us -> 41.8 us  [shift_x(): return lax.ppermute(x, 'chan', pairs)]
    ppermute x13, starting transfers between devices: 28.6 us -> 13.7 us  [shift_x(): return lax.ppermute(x, 'chan', pairs)]
  transfers between devices with their start and end apart: 32 -> 32, of which waited for: 17 -> 22; matrix products, arithmetic and copies ran while one was open for 2% -> 2% of each run, Pallas kernels for 17% -> 18%
where the time goes in v8:
time: 258 us; the launch traced here: 257 us
  waiting for transfers between devices  112 us (43%)
  Pallas kernels  62.4 us (24%)
  starting transfers between devices  44.7 us (17%)
  local copies, waits for them, and re-layouts  24.5 us (9%)
  other arithmetic  12.9 us (5%)
    pallas_call x3, Pallas kernels, correlate(): pl.pallas_call(kernel, grid_spec=pltpu.PrefetchScalarGridSpec(num_scalar_...  46.3 us
    ppermute x13, waiting for transfers between devices, shift_x(): return lax.ppermute(x, 'chan', pairs)  41.8 us
    ppermute x13, waiting for transfers between devices, shift_y(): return lax.ppermute(x, 'chan', pairs)  36.4 us
    ppermute x2, waiting for transfers between devices, swap_far(): return lax.ppermute(x, 'tm', [(a, a ^ 2) for a in range(4)])  19.5 us
    ppermute x13, starting transfers between devices, shift_y(): return lax.ppermute(x, 'chan', pairs)  19.2 us
    transpose x1, local copies, waits for them, and re-layouts, body(): spec = jnp.transpose(spectra, (2, 1, 0, 3)).reshape(BINS, 128, 256)  16.6 us
    pallas_call x4, Pallas kernels, pick_rows(): pl.pallas_call(pick_kernel, grid_spec=pltpu.PrefetchScalarGridSpec(num_sc...  15.9 us
    ppermute x13, starting transfers between devices, shift_x(): return lax.ppermute(x, 'chan', pairs)  13.7 us
  transfers between devices with their start and end apart: 32, of which 22 were waited for; matrix products, arithmetic and copies ran while one was open for 2% of the time, Pallas kernels for 18%

profile of v8, /device:TPU:1, one launch (start us, length us, event | category | flops | bytes accessed | tf_op | source)
XLA Modules:
  0.0 257.1 jit_solution(10037832833513953238)
XLA Ops:
  3.5 16.6 %copy.19 = bf16[250,2,64,256]{3,2,1,0:T(8,128)(2,1)} copy(bf16[250,2,64,256]{3,1,0,2:T(2,128)(2,1)} %bitcast.52) | data formatting | bytes 32768000 | tf_op jit(solution)/shard_map/transpose | solution.py:243
  20.2 3.6 %pick_rows.4 = (bf16[32,128,128]{2,1,0:T(8,128)(2,1)S(1)}, bf16[32,128,128]{2,1,0:T(8,128)(2,1)S(1)}) custom-call(s32[2]{0:T(128)S(1)} %get-tuple-element.124.first_ref, bf16[128,256]{1,0:T(8,128)(2,1)S(1)} %fusion.1.pick_ref, f32[1,128]{1,0:T(1,128)S(1)} %broadcast_in_dim_tile.3.mask_ref, bf16[250,128,256]{2,1,0:T(8,128)(2,1)} %bitcast.41, ...), custom_call_target="tpu_custom_call" | custom-call | flops 1048576 | bytes 65536 | tf_op jit(solution)/shard_map/pick_rows/pallas_call | solution.py:62
  27.1 4.4 %pick_rows.5 = (bf16[32,128,128]{2,1,0:T(8,128)(2,1)}, bf16[32,128,128]{2,1,0:T(8,128)(2,1)}) custom-call(s32[2]{0:T(128)S(1)} %get-tuple-element.56.first_ref, bf16[128,256]{1,0:T(8,128)(2,1)S(1)} %fusion.1.pick_ref, f32[1,128]{1,0:T(1,128)S(1)} %broadcast_in_dim_tile.3.mask_ref, bf16[250,128,256]{2,1,0:T(8,128)(2,1)} %bitcast.43, ...), custom_call_target="tpu_custom_call" | custom-call | flops 1048576 | bytes 65536 | tf_op jit(solution)/shard_map/pick_rows/pallas_call | solution.py:62
  31.6 2.5 collective-permute-start.2
  34.1 2.6 %collective-permute-start.3 = (bf16[32,128,128]{2,1,0:T(8,128)(2,1)}, bf16[32,128,128]{2,1,0:T(8,128)(2,1)}, u32[]{:S(2)}, u32[]{:S(2)}) collective-permute-start(bf16[32,128,128]{2,1,0:T(8,128)(2,1)} %get-tuple-element.67), channel_id=1, source_target_pairs={{0,16},{4,20},{8,24},{12,28},{16,0},{20,4},{24,8},{28,12},{32,48},... | collective-permute-start | bytes 3145736 | tf_op jit(solution)/shard_map/ppermute | solution.py:25
  36.7 4.4 %pick_rows.6 = (bf16[32,128,128]{2,1,0:T(8,128)(2,1)}, bf16[32,128,128]{2,1,0:T(8,128)(2,1)}) custom-call(s32[2]{0:T(128)S(1)} %get-tuple-element.59.first_ref, bf16[128,256]{1,0:T(8,128)(2,1)S(1)} %fusion.1.pick_ref, f32[1,128]{1,0:T(1,128)S(1)} %broadcast_in_dim_tile.3.mask_ref, bf16[250,128,256]{2,1,0:T(8,128)(2,1)} %bitcast.45, ...), custom_call_target="tpu_custom_call" | custom-call | flops 1048576 | bytes 65536 | tf_op jit(solution)/shard_map/pick_rows/pallas_call | solution.py:62
  42.3 7.4 %collective-permute-done = bf16[32,128,128]{2,1,0:T(8,128)(2,1)} collective-permute-done((bf16[32,128,128]{2,1,0:T(8,128)(2,1)S(1)}, bf16[32,128,128]{2,1,0:T(8,128)(2,1)}, u32[]{:S(2)}, u32[]{:S(2)}) %collective-permute-start) | collective-permute-done | bytes 1048608 | tf_op jit(solution)/shard_map/ppermute | solution.py:20
  49.7 3.1 %collective-permute-start.5 = (bf16[32,128,128]{2,1,0:T(8,128)(2,1)}, bf16[32,128,128]{2,1,0:T(8,128)(2,1)}, u32[]{:S(2)}, u32[]{:S(2)}) collective-permute-start(bf16[32,128,128]{2,1,0:T(8,128)(2,1)} %get-tuple-element.69), channel_id=1, source_target_pairs={{0,24},{4,28},{8,0},{12,4},{16,8},{20,12},{24,16},{28,20},{32,56},... | collective-permute-start | bytes 3145736 | tf_op jit(solution)/shard_map/ppermute | solution.py:25
  52.7 3.6 %pick_rows.7 = (bf16[32,128,128]{2,1,0:T(8,128)(2,1)S(1)}, bf16[32,128,128]{2,1,0:T(8,128)(2,1)S(1)}) custom-call(s32[2]{0:T(128)S(1)} %get-tuple-element.62.first_ref, bf16[128,256]{1,0:T(8,128)(2,1)S(1)} %fusion.1.pick_ref, f32[1,128]{1,0:T(1,128)S(1)} %broadcast_in_dim_tile.3.mask_ref, bf16[250,128,256]{2,1,0:T(8,128)(2,1)} %bitcast.47, ...), custom_call_target="tpu_custom_call" | custom-call | flops 1048576 | bytes 65536 | tf_op jit(solution)/shard_map/pick_rows/pallas_call | solution.py:62
  56.3 17.1 %collective-permute-done.2 = bf16[32,128,128]{2,1,0:T(8,128)(2,1)} collective-permute-done((bf16[32,128,128]{2,1,0:T(8,128)(2,1)}, bf16[32,128,128]{2,1,0:T(8,128)(2,1)}, u32[]{:S(2)}, u32[]{:S(2)}) %collective-permute-start.2) | collective-permute-done | bytes 1048608 | tf_op jit(solution)/shard_map/ppermute | solution.py:20
  74.6 4.5 %collective-permute-done.4 = bf16[32,128,128]{2,1,0:T(8,128)(2,1)} collective-permute-done((bf16[32,128,128]{2,1,0:T(8,128)(2,1)}, bf16[32,128,128]{2,1,0:T(8,128)(2,1)}, u32[]{:S(2)}, u32[]{:S(2)}) %collective-permute-start.4) | collective-permute-done | bytes 1048608 | tf_op jit(solution)/shard_map/ppermute | solution.py:20
  79.1 2.4 collective-permute-done.5
  83.9 3.4 %collective-permute-start.10 = (bf16[8,128,128]{2,1,0:T(8,128)(2,1)}, bf16[8,128,128]{2,1,0:T(8,128)(2,1)S(1)}, u32[]{:S(2)}, u32[]{:S(2)}) collective-permute-start(bf16[8,128,128]{2,1,0:T(8,128)(2,1)} %get-tuple-element.106), channel_id=1, source_target_pairs={{0,24},{4,28},{8,0},{12,4},{16,8},{20,12},{24,16},{28,20},{32,56},... | collective-permute-start | bytes 786440 | tf_op jit(solution)/shard_map/ppermute | solution.py:25
  89.0 2.5 add_add_fusion.2
  96.0 6.8 %collective-permute-done.6 = bf16[8,128,128]{2,1,0:T(8,128)(2,1)S(1)} collective-permute-done((bf16[8,128,128]{2,1,0:T(8,128)(2,1)S(1)}, bf16[8,128,128]{2,1,0:T(8,128)(2,1)S(1)}, u32[]{:S(2)}, u32[]{:S(2)}) %collective-permute-start.6) | collective-permute-done | bytes 262176 | tf_op jit(solution)/shard_map/ppermute | solution.py:25
  102.8 3.8 %collective-permute-done.7 = bf16[8,128,128]{2,1,0:T(8,128)(2,1)} collective-permute-done((bf16[8,128,128]{2,1,0:T(8,128)(2,1)}, bf16[8,128,128]{2,1,0:T(8,128)(2,1)}, u32[]{:S(2)}, u32[]{:S(2)}) %collective-permute-start.7) | collective-permute-done | bytes 262176 | tf_op jit(solution)/shard_map/ppermute | solution.py:20
  111.0 2.7 %collective-permute-done.12 = bf16[8,128,128]{2,1,0:T(8,128)(2,1)S(1)} collective-permute-done((bf16[8,128,128]{2,1,0:T(8,128)(2,1)S(1)}, bf16[8,128,128]{2,1,0:T(8,128)(2,1)S(1)}, u32[]{:S(2)}, u32[]{:S(2)}) %collective-permute-start.12) | collective-permute-done | bytes 262176 | tf_op jit(solution)/shard_map/ppermute | solution.py:29
  113.7 5.6 %collective-permute-done.13 = bf16[8,128,128]{2,1,0:T(8,128)(2,1)S(1)} collective-permute-done((bf16[8,128,128]{2,1,0:T(8,128)(2,1)S(1)}, bf16[8,128,128]{2,1,0:T(8,128)(2,1)S(1)}, u32[]{:S(2)}, u32[]{:S(2)}) %collective-permute-start.13) | collective-permute-done | bytes 262176 | tf_op jit(solution)/shard_map/ppermute | solution.py:29
  126.3 4.1 %collective-permute-done.18.refs_2_ = bf16[8,128,128]{2,1,0:T(8,128)(2,1)S(1)} collective-permute-done((bf16[8,128,128]{2,1,0:T(8,128)(2,1)S(1)}, bf16[8,128,128]{2,1,0:T(8,128)(2,1)S(1)}, u32[]{:S(2)}, u32[]{:S(2)}) %collective-permute-start.18) | collective-permute-done | bytes 262176 | tf_op jit(solution)/shard_map/ppermute | solution.py:20
  130.4 2.8 %collective-permute-done.17.refs_1_ = bf16[8,128,128]{2,1,0:T(8,128)(2,1)S(1)} collective-permute-done((bf16[8,128,128]{2,1,0:T(8,128)(2,1)S(1)}, bf16[8,128,128]{2,1,0:T(8,128)(2,1)S(1)}, u32[]{:S(2)}, u32[]{:S(2)}) %collective-permute-start.17) | collective-permute-done | bytes 262176 | tf_op jit(solution)/shard_map/ppermute | solution.py:20
  135.8 2.8 %collective-permute-start.23 = (bf16[32,128,128]{2,1,0:T(8,128)(2,1)S(1)}, bf16[32,128,128]{2,1,0:T(8,128)(2,1)S(1)}, u32[]{:S(2)}, u32[]{:S(2)}) collective-permute-start(bf16[32,128,128]{2,1,0:T(8,128)(2,1)S(1)} %assemble.3.refs_1_), channel_id=1, source_target_pairs={{0,24},{4,28},{8,0},{12,4},{16,8},{20,12},{24,16},{28,20},{32,56},... | collective-permute-start | bytes 3145736 | tf_op jit(solution)/shard_map/ppermute | solution.py:25
  141.0 17.4 %collective-permute-done.23.refs_1_.refs_5_ = bf16[32,128,128]{2,1,0:T(8,128)(2,1)S(1)} collective-permute-done((bf16[32,128,128]{2,1,0:T(8,128)(2,1)S(1)}, bf16[32,128,128]{2,1,0:T(8,128)(2,1)S(1)}, u32[]{:S(2)}, u32[]{:S(2)}) %collective-permute-start.23) | collective-permute-done | bytes 1048608 | tf_op jit(solution)/shard_map/ppermute | solution.py:25
  158.4 3.1 %collective-permute-done.22.refs_0_.refs_4_ = bf16[32,128,128]{2,1,0:T(8,128)(2,1)S(1)} collective-permute-done((bf16[32,128,128]{2,1,0:T(8,128)(2,1)S(1)}, bf16[32,128,128]{2,1,0:T(8,128)(2,1)S(1)}, u32[]{:S(2)}, u32[]{:S(2)}) %collective-permute-start.22) | collective-permute-done | bytes 1048608 | tf_op jit(solution)/shard_map/ppermute | solution.py:25
  164.1 2.8 %collective-permute-start.27 = (bf16[16,128,128]{2,1,0:T(8,128)(2,1)S(1)}, bf16[16,128,128]{2,1,0:T(8,128)(2,1)S(1)}, u32[]{:S(2)}, u32[]{:S(2)}) collective-permute-start(bf16[16,128,128]{2,1,0:T(8,128)(2,1)S(1)} %slice.65), channel_id=1, source_target_pairs={{0,24},{4,28},{8,0},{12,4},{16,8},{20,12},{24,16},{28,20},{32,56},... | collective-permute-start | bytes 1572872 | tf_op jit(solution)/shard_map/ppermute | solution.py:25
  166.9 12.9 %early_kernel.1.refs_6_ = f32[64,112,256]{2,1,0:T(8,128)} custom-call(s32[4]{0:T(128)S(1)} %pad_add_fusion.5.blocks_ref, bf16[1,112,256]{2,1,0:T(8,128)(2,1)S(1)} %bitcast.40, bf16[1,128]{1,0:T(2,128)(2,1)S(1)} %fusion.11.sign_ref, bf16[250,128,256]{2,1,0:T(8,128)(2,1)} %bitcast.49, bf16[32,128,128]{2,1,0:T(8,128)(2,1)S(1)} %assemble.2.refs_0_, ...), custom_call_target="tpu_custom_call" | custom-call | flops 12000000000 | bytes 16777216 | tf_op jit(solution)/shard_map/early_kernel/pallas_call | solution.py:215
  179.9 12.7 %late_kernel.1 = (bf16[32,101,256]{2,1,0:T(8,128)(2,1)}, bf16[32,101,256]{2,1,0:T(8,128)(2,1)}) custom-call(s32[4]{0:T(128)S(1)} %pad_add_fusion.blocks_ref, bf16[1,112,256]{2,1,0:T(8,128)(2,1)S(1)} %bitcast.39, bf16[1,128]{1,0:T(2,128)(2,1)S(1)} %fusion.11.sign_ref, bf16[250,128,256]{2,1,0:T(8,128)(2,1)} %bitcast.50, ...), custom_call_target="tpu_custom_call" | custom-call | flops 12000000000 | bytes 16777216 | tf_op jit(solution)/shard_map/late_kernel/pallas_call | solution.py:215
  194.4 5.1 %collective-permute-start.28 = (bf16[32,101,256]{2,0,1:T(8,128)(2,1)S(1)}, bf16[32,101,256]{2,0,1:T(8,128)(2,1)S(1)}, u32[]{:S(2)}, u32[]{:S(2)}) collective-permute-start(bf16[32,101,256]{2,0,1:T(8,128)(2,1)S(1)} %copy.21), channel_id=1, source_target_pairs={{0,1},{1,0},{2,3},{3,2},{4,5},{5,4},{6,7},{7,6},{8,9},{9,8},{10,11... | collective-permute-start | bytes 4964360 | tf_op jit(solution)/shard_map/ppermute | solution.py:33
  199.5 3.1 %collective-permute-done.28 = bf16[32,101,256]{2,0,1:T(8,128)(2,1)S(1)} collective-permute-done((bf16[32,101,256]{2,0,1:T(8,128)(2,1)S(1)}, bf16[32,101,256]{2,0,1:T(8,128)(2,1)S(1)}, u32[]{:S(2)}, u32[]{:S(2)}) %collective-permute-start.28) | collective-permute-done | bytes 1654816 | tf_op jit(solution)/shard_map/ppermute | solution.py:33
  203.3 3.0 %collective-permute-start.29 = (bf16[16,101,256]{2,0,1:T(8,128)(2,1)S(1)}, bf16[16,101,256]{2,0,1:T(8,128)(2,1)S(1)}, u32[]{:S(2)}, u32[]{:S(2)}) collective-permute-start(bf16[16,101,256]{2,0,1:T(8,128)(2,1)S(1)} %copy.25), channel_id=1, source_target_pairs={{0,2},{1,3},{2,0},{3,1},{4,6},{5,7},{6,4},{7,5},{8,10},{9,11},{10,... | collective-permute-start | bytes 2482184 | tf_op jit(solution)/shard_map/ppermute | solution.py:37
  206.4 20.7 %whole_kernel.1 = (bf16[32,101,256]{2,1,0:T(8,128)(2,1)}, bf16[32,101,256]{2,1,0:T(8,128)(2,1)}) custom-call(s32[8]{0:T(128)S(1)} %stack.81.blocks_ref, bf16[2,112,256]{2,1,0:T(8,128)(2,1)S(1)} %bitcast.38, bf16[1,128]{1,0:T(2,128)(2,1)S(1)} %fusion.11.sign_ref, bf16[250,128,256]{2,1,0:T(8,128)(2,1)} %bitcast.51, bf16[32,128,128]{2,1,0:T(8,128)(2,1)S(1)} %assemble.2.refs_0_, ...), custom_call_target="tpu_custom_call" | custom-call | flops 24000000000 | bytes 33554432 | tf_op jit(solution)/shard_map/whole_kernel/pallas_call | solution.py:215
  229.6 3.2 %collective-permute-done.30 = bf16[32,101,256]{2,0,1:T(8,128)(2,1)S(1)} collective-permute-done((bf16[32,101,256]{2,0,1:T(8,128)(2,1)S(1)}, bf16[32,101,256]{2,0,1:T(8,128)(2,1)S(1)}, u32[]{:S(2)}, u32[]{:S(2)}) %collective-permute-start.30) | collective-permute-done | bytes 1654816 | tf_op jit(solution)/shard_map/ppermute | solution.py:33
  235.2 19.5 %collective-permute-done.31 = bf16[16,101,256]{2,0,1:T(8,128)(2,1)S(1)} collective-permute-done((bf16[16,101,256]{2,0,1:T(8,128)(2,1)S(1)}, bf16[16,101,256]{2,0,1:T(8,128)(2,1)S(1)}, u32[]{:S(2)}, u32[]{:S(2)}) %collective-permute-start.31) | collective-permute-done | bytes 827424 | tf_op jit(solution)/shard_map/ppermute | solution.py:37
  (105 shorter events, 46.6 us)
Async XLA Ops:
  23.7 25.9 %collective-permute-start = (bf16[32,128,128]{2,1,0:T(8,128)(2,1)S(1)}, bf16[32,128,128]{2,1,0:T(8,128)(2,1)}, u32[]{:S(2)}, u32[]{:S(2)}) collective-permute-start(bf16[32,128,128]{2,1,0:T(8,128)(2,1)S(1)} %get-tuple-element.64), channel_id=1, source_target_pairs={{0,32},{4,36},{8,40},{12,44},{16,48},{20,52},{24,56},{28,60},{32,6... | collective-permute-start | bytes 3145736 | tf_op jit(solution)/shard_map/ppermute | solution.py:20
  25.9 30.4 %collective-permute-start.1 = (bf16[32,128,128]{2,1,0:T(8,128)(2,1)S(1)}, bf16[32,128,128]{2,1,0:T(8,128)(2,1)}, u32[]{:S(2)}, u32[]{:S(2)}) collective-permute-start(bf16[32,128,128]{2,1,0:T(8,128)(2,1)S(1)} %get-tuple-element.65), channel_id=1, source_target_pairs={{0,8},{4,12},{8,16},{12,20},{16,24},{20,28},{24,0},{28,4},{32,40},... | collective-permute-start | bytes 3145736 | tf_op jit(solution)/shard_map/ppermute | solution.py:25
  31.6 41.8 %collective-permute-start.2 = (bf16[32,128,128]{2,1,0:T(8,128)(2,1)}, bf16[32,128,128]{2,1,0:T(8,128)(2,1)}, u32[]{:S(2)}, u32[]{:S(2)}) collective-permute-start(bf16[32,128,128]{2,1,0:T(8,128)(2,1)} %get-tuple-element.66), channel_id=1, source_target_pairs={{0,64},{4,68},{8,72},{12,76},{16,80},{20,84},{24,88},{28,92},{32,9... | collective-permute-start | bytes 3145736 | tf_op jit(solution)/shard_map/ppermute | solution.py:20
  34.1 40.5 %collective-permute-start.3 = (bf16[32,128,128]{2,1,0:T(8,128)(2,1)}, bf16[32,128,128]{2,1,0:T(8,128)(2,1)}, u32[]{:S(2)}, u32[]{:S(2)}) collective-permute-start(bf16[32,128,128]{2,1,0:T(8,128)(2,1)} %get-tuple-element.67), channel_id=1, source_target_pairs={{0,16},{4,20},{8,24},{12,28},{16,0},{20,4},{24,8},{28,12},{32,48},... | collective-permute-start | bytes 3145736 | tf_op jit(solution)/shard_map/ppermute | solution.py:25
  41.1 38.0 %collective-permute-start.4 = (bf16[32,128,128]{2,1,0:T(8,128)(2,1)}, bf16[32,128,128]{2,1,0:T(8,128)(2,1)}, u32[]{:S(2)}, u32[]{:S(2)}) collective-permute-start(bf16[32,128,128]{2,1,0:T(8,128)(2,1)} %get-tuple-element.68), channel_id=1, source_target_pairs={{0,96},{4,100},{8,104},{12,108},{16,112},{20,116},{24,120},{28,124... | collective-permute-start | bytes 3145736 | tf_op jit(solution)/shard_map/ppermute | solution.py:20
  49.7 31.9 %collective-permute-start.5 = (bf16[32,128,128]{2,1,0:T(8,128)(2,1)}, bf16[32,128,128]{2,1,0:T(8,128)(2,1)}, u32[]{:S(2)}, u32[]{:S(2)}) collective-permute-start(bf16[32,128,128]{2,1,0:T(8,128)(2,1)} %get-tuple-element.69), channel_id=1, source_target_pairs={{0,24},{4,28},{8,0},{12,4},{16,8},{20,12},{24,16},{28,20},{32,56},... | collective-permute-start | bytes 3145736 | tf_op jit(solution)/shard_map/ppermute | solution.py:25
  83.9 9.7 %collective-permute-start.10 = (bf16[8,128,128]{2,1,0:T(8,128)(2,1)}, bf16[8,128,128]{2,1,0:T(8,128)(2,1)S(1)}, u32[]{:S(2)}, u32[]{:S(2)}) collective-permute-start(bf16[8,128,128]{2,1,0:T(8,128)(2,1)} %get-tuple-element.106), channel_id=1, source_target_pairs={{0,24},{4,28},{8,0},{12,4},{16,8},{20,12},{24,16},{28,20},{32,56},... | collective-permute-start | bytes 786440 | tf_op jit(solution)/shard_map/ppermute | solution.py:25
  87.4 8.6 %collective-permute-start.8 = (bf16[8,128,128]{2,1,0:T(8,128)(2,1)S(1)}, bf16[8,128,128]{2,1,0:T(8,128)(2,1)S(1)}, u32[]{:S(2)}, u32[]{:S(2)}) collective-permute-start(bf16[8,128,128]{2,1,0:T(8,128)(2,1)S(1)} %get-tuple-element.107), channel_id=1, source_target_pairs={{0,16},{4,20},{8,24},{12,28},{16,0},{20,4},{24,8},{28,12},{32,48},... | collective-permute-start | bytes 786440 | tf_op jit(solution)/shard_map/ppermute | solution.py:25
  89.0 13.8 %collective-permute-start.6 = (bf16[8,128,128]{2,1,0:T(8,128)(2,1)S(1)}, bf16[8,128,128]{2,1,0:T(8,128)(2,1)S(1)}, u32[]{:S(2)}, u32[]{:S(2)}) collective-permute-start(bf16[8,128,128]{2,1,0:T(8,128)(2,1)S(1)} %get-tuple-element.108), channel_id=1, source_target_pairs={{0,8},{4,12},{8,16},{12,20},{16,24},{20,28},{24,0},{28,4},{32,40},... | collective-permute-start | bytes 786440 | tf_op jit(solution)/shard_map/ppermute | solution.py:25
  91.5 11.3 %collective-permute-start.11 = (bf16[8,128,128]{2,1,0:T(8,128)(2,1)}, bf16[8,128,128]{2,1,0:T(8,128)(2,1)}, u32[]{:S(2)}, u32[]{:S(2)}) collective-permute-start(bf16[8,128,128]{2,1,0:T(8,128)(2,1)} %get-tuple-element.103), channel_id=1, source_target_pairs={{0,96},{4,100},{8,104},{12,108},{16,112},{20,116},{24,120},{28,124... | collective-permute-start | bytes 786440 | tf_op jit(solution)/shard_map/ppermute | solution.py:20
  92.7 10.1 %collective-permute-start.9 = (bf16[8,128,128]{2,1,0:T(8,128)(2,1)}, bf16[8,128,128]{2,1,0:T(8,128)(2,1)}, u32[]{:S(2)}, u32[]{:S(2)}) collective-permute-start(bf16[8,128,128]{2,1,0:T(8,128)(2,1)} %get-tuple-element.104), channel_id=1, source_target_pairs={{0,64},{4,68},{8,72},{12,76},{16,80},{20,84},{24,88},{28,92},{32,9... | collective-permute-start | bytes 786440 | tf_op jit(solution)/shard_map/ppermute | solution.py:20
  93.7 12.9 %collective-permute-start.7 = (bf16[8,128,128]{2,1,0:T(8,128)(2,1)}, bf16[8,128,128]{2,1,0:T(8,128)(2,1)}, u32[]{:S(2)}, u32[]{:S(2)}) collective-permute-start(bf16[8,128,128]{2,1,0:T(8,128)(2,1)} %get-tuple-element.105), channel_id=1, source_target_pairs={{0,32},{4,36},{8,40},{12,44},{16,48},{20,52},{24,56},{28,60},{32,6... | collective-permute-start | bytes 786440 | tf_op jit(solution)/shard_map/ppermute | solution.py:20
  107.8 6.0 %collective-permute-start.12 = (bf16[8,128,128]{2,1,0:T(8,128)(2,1)S(1)}, bf16[8,128,128]{2,1,0:T(8,128)(2,1)S(1)}, u32[]{:S(2)}, u32[]{:S(2)}) collective-permute-start(bf16[8,128,128]{2,1,0:T(8,128)(2,1)S(1)} %add_add_fusion.1), channel_id=1, source_target_pairs={{0,4},{4,0},{8,12},{12,8},{16,20},{20,16},{24,28},{28,24},{32,36},... | collective-permute-start | bytes 786440 | tf_op jit(solution)/shard_map/ppermute | solution.py:29
  110.9 8.4 %collective-permute-start.13 = (bf16[8,128,128]{2,1,0:T(8,128)(2,1)S(1)}, bf16[8,128,128]{2,1,0:T(8,128)(2,1)S(1)}, u32[]{:S(2)}, u32[]{:S(2)}) collective-permute-start(bf16[8,128,128]{2,1,0:T(8,128)(2,1)S(1)} %add_add_fusion), channel_id=1, source_target_pairs={{0,4},{4,0},{8,12},{12,8},{16,20},{20,16},{24,28},{28,24},{32,36},... | collective-permute-start | bytes 786440 | tf_op jit(solution)/shard_map/ppermute | solution.py:29
  119.4 6.9 %collective-permute-start.19 = (bf16[8,128,128]{2,1,0:T(8,128)(2,1)S(1)}, bf16[8,128,128]{2,1,0:T(8,128)(2,1)S(1)}, u32[]{:S(2)}, u32[]{:S(2)}) collective-permute-start(bf16[8,128,128]{2,1,0:T(8,128)(2,1)S(1)} %add.521.refs_0_), channel_id=1, source_target_pairs={{0,64},{4,68},{8,72},{12,76},{16,80},{20,84},{24,88},{28,92},{32,9... | collective-permute-start | bytes 786440 | tf_op jit(solution)/shard_map/ppermute | solution.py:20
  121.9 8.5 %collective-permute-start.18 = (bf16[8,128,128]{2,1,0:T(8,128)(2,1)S(1)}, bf16[8,128,128]{2,1,0:T(8,128)(2,1)S(1)}, u32[]{:S(2)}, u32[]{:S(2)}) collective-permute-start(bf16[8,128,128]{2,1,0:T(8,128)(2,1)S(1)} %add.521.refs_0_), channel_id=1, source_target_pairs={{0,96},{4,100},{8,104},{12,108},{16,112},{20,116},{24,120},{28,124... | collective-permute-start | bytes 786440 | tf_op jit(solution)/shard_map/ppermute | solution.py:20
  122.0 11.3 %collective-permute-start.17 = (bf16[8,128,128]{2,1,0:T(8,128)(2,1)S(1)}, bf16[8,128,128]{2,1,0:T(8,128)(2,1)S(1)}, u32[]{:S(2)}, u32[]{:S(2)}) collective-permute-start(bf16[8,128,128]{2,1,0:T(8,128)(2,1)S(1)} %add.521.refs_0_), channel_id=1, source_target_pairs={{0,32},{4,36},{8,40},{12,44},{16,48},{20,52},{24,56},{28,60},{32,6... | collective-permute-start | bytes 786440 | tf_op jit(solution)/shard_map/ppermute | solution.py:20
  123.5 9.8 %collective-permute-start.16 = (bf16[8,128,128]{2,1,0:T(8,128)(2,1)S(1)}, bf16[8,128,128]{2,1,0:T(8,128)(2,1)S(1)}, u32[]{:S(2)}, u32[]{:S(2)}) collective-permute-start(bf16[8,128,128]{2,1,0:T(8,128)(2,1)S(1)} %add.520.refs_0_), channel_id=1, source_target_pairs={{0,16},{4,20},{8,24},{12,28},{16,0},{20,4},{24,8},{28,12},{32,48},... | collective-permute-start | bytes 786440 | tf_op jit(solution)/shard_map/ppermute | solution.py:25
  124.7 10.2 %collective-permute-start.15 = (bf16[8,128,128]{2,1,0:T(8,128)(2,1)S(1)}, bf16[8,128,128]{2,1,0:T(8,128)(2,1)S(1)}, u32[]{:S(2)}, u32[]{:S(2)}) collective-permute-start(bf16[8,128,128]{2,1,0:T(8,128)(2,1)S(1)} %add.520.refs_0_), channel_id=1, source_target_pairs={{0,24},{4,28},{8,0},{12,4},{16,8},{20,12},{24,16},{28,20},{32,56},... | collective-permute-start | bytes 786440 | tf_op jit(solution)/shard_map/ppermute | solution.py:25
  126.3 9.4 %collective-permute-start.14 = (bf16[8,128,128]{2,1,0:T(8,128)(2,1)S(1)}, bf16[8,128,128]{2,1,0:T(8,128)(2,1)S(1)}, u32[]{:S(2)}, u32[]{:S(2)}) collective-permute-start(bf16[8,128,128]{2,1,0:T(8,128)(2,1)S(1)} %add.520.refs_0_), channel_id=1, source_target_pairs={{0,8},{4,12},{8,16},{12,20},{16,24},{20,28},{24,0},{28,4},{32,40},... | collective-permute-start | bytes 786440 | tf_op jit(solution)/shard_map/ppermute | solution.py:25
  135.8 22.6 %collective-permute-start.23 = (bf16[32,128,128]{2,1,0:T(8,128)(2,1)S(1)}, bf16[32,128,128]{2,1,0:T(8,128)(2,1)S(1)}, u32[]{:S(2)}, u32[]{:S(2)}) collective-permute-start(bf16[32,128,128]{2,1,0:T(8,128)(2,1)S(1)} %assemble.3.refs_1_), channel_id=1, source_target_pairs={{0,24},{4,28},{8,0},{12,4},{16,8},{20,12},{24,16},{28,20},{32,56},... | collective-permute-start | bytes 3145736 | tf_op jit(solution)/shard_map/ppermute | solution.py:25
  138.6 23.0 %collective-permute-start.22 = (bf16[32,128,128]{2,1,0:T(8,128)(2,1)S(1)}, bf16[32,128,128]{2,1,0:T(8,128)(2,1)S(1)}, u32[]{:S(2)}, u32[]{:S(2)}) collective-permute-start(bf16[32,128,128]{2,1,0:T(8,128)(2,1)S(1)} %assemble.3.refs_1_), channel_id=1, source_target_pairs={{0,8},{4,12},{8,16},{12,20},{16,24},{20,28},{24,0},{28,4},{32,40},... | collective-permute-start | bytes 3145736 | tf_op jit(solution)/shard_map/ppermute | solution.py:25
  138.6 22.9 %collective-permute-start.21 = (bf16[32,128,128]{2,1,0:T(8,128)(2,1)S(1)}, bf16[32,128,128]{2,1,0:T(8,128)(2,1)S(1)}, u32[]{:S(2)}, u32[]{:S(2)}) collective-permute-start(bf16[32,128,128]{2,1,0:T(8,128)(2,1)S(1)} %assemble.2.refs_0_), channel_id=1, source_target_pairs={{0,96},{4,100},{8,104},{12,108},{16,112},{20,116},{24,120},{28,124... | collective-permute-start | bytes 3145736 | tf_op jit(solution)/shard_map/ppermute | solution.py:20
  139.9 22.4 %collective-permute-start.20 = (bf16[32,128,128]{2,1,0:T(8,128)(2,1)S(1)}, bf16[32,128,128]{2,1,0:T(8,128)(2,1)S(1)}, u32[]{:S(2)}, u32[]{:S(2)}) collective-permute-start(bf16[32,128,128]{2,1,0:T(8,128)(2,1)S(1)} %assemble.2.refs_0_), channel_id=1, source_target_pairs={{0,32},{4,36},{8,40},{12,44},{16,48},{20,52},{24,56},{28,60},{32,6... | collective-permute-start | bytes 3145736 | tf_op jit(solution)/shard_map/ppermute | solution.py:20
  162.6 17.3 %collective-permute-start.25 = (bf16[16,128,128]{2,1,0:T(8,128)(2,1)S(1)}, bf16[16,128,128]{2,1,0:T(8,128)(2,1)S(1)}, u32[]{:S(2)}, u32[]{:S(2)}) collective-permute-start(bf16[16,128,128]{2,1,0:T(8,128)(2,1)S(1)} %slice.63), channel_id=1, source_target_pairs={{0,96},{4,100},{8,104},{12,108},{16,112},{20,116},{24,120},{28,124... | collective-permute-start | bytes 1572872 | tf_op jit(solution)/shard_map/ppermute | solution.py:20
  164.0 15.9 %collective-permute-start.24 = (bf16[16,128,128]{2,1,0:T(8,128)(2,1)S(1)}, bf16[16,128,128]{2,1,0:T(8,128)(2,1)S(1)}, u32[]{:S(2)}, u32[]{:S(2)}) collective-permute-start(bf16[16,128,128]{2,1,0:T(8,128)(2,1)S(1)} %slice.62), channel_id=1, source_target_pairs={{0,32},{4,36},{8,40},{12,44},{16,48},{20,52},{24,56},{28,60},{32,6... | collective-permute-start | bytes 1572872 | tf_op jit(solution)/shard_map/ppermute | solution.py:20
  164.1 15.8 %collective-permute-start.27 = (bf16[16,128,128]{2,1,0:T(8,128)(2,1)S(1)}, bf16[16,128,128]{2,1,0:T(8,128)(2,1)S(1)}, u32[]{:S(2)}, u32[]{:S(2)}) collective-permute-start(bf16[16,128,128]{2,1,0:T(8,128)(2,1)S(1)} %slice.65), channel_id=1, source_target_pairs={{0,24},{4,28},{8,0},{12,4},{16,8},{20,12},{24,16},{28,20},{32,56},... | collective-permute-start | bytes 1572872 | tf_op jit(solution)/shard_map/ppermute | solution.py:25
  166.9 13.0 %collective-permute-start.26 = (bf16[16,128,128]{2,1,0:T(8,128)(2,1)S(1)}, bf16[16,128,128]{2,1,0:T(8,128)(2,1)S(1)}, u32[]{:S(2)}, u32[]{:S(2)}) collective-permute-start(bf16[16,128,128]{2,1,0:T(8,128)(2,1)S(1)} %slice.64), channel_id=1, source_target_pairs={{0,8},{4,12},{8,16},{12,20},{16,24},{20,28},{24,0},{28,4},{32,40},... | collective-permute-start | bytes 1572872 | tf_op jit(solution)/shard_map/ppermute | solution.py:25
  194.4 8.3 %collective-permute-start.28 = (bf16[32,101,256]{2,0,1:T(8,128)(2,1)S(1)}, bf16[32,101,256]{2,0,1:T(8,128)(2,1)S(1)}, u32[]{:S(2)}, u32[]{:S(2)}) collective-permute-start(bf16[32,101,256]{2,0,1:T(8,128)(2,1)S(1)} %copy.21), channel_id=1, source_target_pairs={{0,1},{1,0},{2,3},{3,2},{4,5},{5,4},{6,7},{7,6},{8,9},{9,8},{10,11... | collective-permute-start | bytes 4964360 | tf_op jit(solution)/shard_map/ppermute | solution.py:33
  203.3 23.7 %collective-permute-start.29 = (bf16[16,101,256]{2,0,1:T(8,128)(2,1)S(1)}, bf16[16,101,256]{2,0,1:T(8,128)(2,1)S(1)}, u32[]{:S(2)}, u32[]{:S(2)}) collective-permute-start(bf16[16,101,256]{2,0,1:T(8,128)(2,1)S(1)} %copy.25), channel_id=1, source_target_pairs={{0,2},{1,3},{2,0},{3,1},{4,6},{5,7},{6,4},{7,5},{8,10},{9,11},{10,... | collective-permute-start | bytes 2482184 | tf_op jit(solution)/shard_map/ppermute | solution.py:37
  228.9 3.9 %collective-permute-start.30 = (bf16[32,101,256]{2,0,1:T(8,128)(2,1)S(1)}, bf16[32,101,256]{2,0,1:T(8,128)(2,1)S(1)}, u32[]{:S(2)}, u32[]{:S(2)}) collective-permute-start(bf16[32,101,256]{2,0,1:T(8,128)(2,1)S(1)} %copy.27), channel_id=1, source_target_pairs={{0,1},{1,0},{2,3},{3,2},{4,5},{5,4},{6,7},{7,6},{8,9},{9,8},{10,11... | collective-permute-start | bytes 4964360 | tf_op jit(solution)/shard_map/ppermute | solution.py:33
  233.5 21.2 %collective-permute-start.31 = (bf16[16,101,256]{2,0,1:T(8,128)(2,1)S(1)}, bf16[16,101,256]{2,0,1:T(8,128)(2,1)S(1)}, u32[]{:S(2)}, u32[]{:S(2)}) collective-permute-start(bf16[16,101,256]{2,0,1:T(8,128)(2,1)S(1)} %copy.30), channel_id=1, source_target_pairs={{0,2},{1,3},{2,0},{3,1},{4,6},{5,7},{6,4},{7,5},{8,10},{9,11},{10,... | collective-permute-start | bytes 2482184 | tf_op jit(solution)/shard_map/ppermute | solution.py:37
  (7 other events, 66.6 us)

commit v9 on v8

--- a/solution.py
+++ b/solution.py
@@ -271,7 +271,7 @@
     pieces = {d: (piece(0, y, d), piece(1, x, d)) for d in range(4)}
     more = barrier({d: (shift_y(pieces[d][0], d), shift_x(pieces[d][1], d)) for d in (1, 3, 2)})
     piece_a, piece_b = [(pieces[0][h] + more[1][h]) + (more[2][h] + more[3][h]) for h in range(2)]
-    far_a, far_b = barrier((swap_z(piece_a), swap_z(piece_b)))
+    far_a, far_b = swap_z(piece_a), swap_z(piece_b)
     piece_a, piece_b = piece_a + far_a, piece_b + far_b
 
     def gather(a, b, shift_a, shift_b):

time: 258 us -> 252 us (0.977)
  waiting for transfers between devices: 112 us -> 104 us
    ppermute x13, waiting for transfers between devices: 36.4 us -> 29.5 us  [shift_y(): return lax.ppermute(x, 'chan', pairs)]
    ppermute x2, waiting for transfers between devices: 8.33 us -> 4.46 us  [swap_z(): return lax.ppermute(x, 'chan', [(a, a ^ 1) for a in range(32)])]
where the time goes in v9:
time: 252 us; the launch traced here: 251 us
  waiting for transfers between devices  104 us (41%)
  Pallas kernels  62.3 us (25%)
  starting transfers between devices  47 us (19%)
  local copies, waits for them, and re-layouts  24.5 us (10%)
  other arithmetic  13.1 us (5%)
    pallas_call x3, Pallas kernels, correlate(): pl.pallas_call(kernel, grid_spec=pltpu.PrefetchScalarGridSpec(num_scalar_...  46.3 us
    ppermute x13, waiting for transfers between devices, shift_x(): return lax.ppermute(x, 'chan', pairs)  44.3 us
    ppermute x13, waiting for transfers between devices, shift_y(): return lax.ppermute(x, 'chan', pairs)  29.5 us
    ppermute x2, waiting for transfers between devices, swap_far(): return lax.ppermute(x, 'tm', [(a, a ^ 2) for a in range(4)])  19.4 us
    ppermute x13, starting transfers between devices, shift_y(): return lax.ppermute(x, 'chan', pairs)  18.6 us
    transpose x1, local copies, waits for them, and re-layouts, body(): spec = jnp.transpose(spectra, (2, 1, 0, 3)).reshape(BINS, 128, 256)  16.6 us
    pallas_call x4, Pallas kernels, pick_rows(): pl.pallas_call(pick_kernel, grid_spec=pltpu.PrefetchScalarGridSpec(num_sc...  15.9 us
    ppermute x13, starting transfers between devices, shift_x(): return lax.ppermute(x, 'chan', pairs)  15.8 us
  transfers between devices with their start and end apart: 32, of which 22 were waited for; matrix products, arithmetic and copies ran while one was open for 2% of the time, Pallas kernels for 18%

profile of v9, /device:TPU:1, one launch (start us, length us, event | category | flops | bytes accessed | tf_op | source)
XLA Modules:
  0.0 251.2 jit_solution(9009002040949772500)
XLA Ops:
  3.5 16.6 %copy.19 = bf16[250,2,64,256]{3,2,1,0:T(8,128)(2,1)} copy(bf16[250,2,64,256]{3,1,0,2:T(2,128)(2,1)} %bitcast.52) | data formatting | bytes 32768000 | tf_op jit(solution)/shard_map/transpose | solution.py:243
  20.2 3.6 %pick_rows.4 = (bf16[32,128,128]{2,1,0:T(8,128)(2,1)S(1)}, bf16[32,128,128]{2,1,0:T(8,128)(2,1)S(1)}) custom-call(s32[2]{0:T(128)S(1)} %get-tuple-element.120.first_ref, bf16[128,256]{1,0:T(8,128)(2,1)S(1)} %fusion.1.pick_ref, f32[1,128]{1,0:T(1,128)S(1)} %broadcast_in_dim_tile.3.mask_ref, bf16[250,128,256]{2,1,0:T(8,128)(2,1)} %bitcast.41, ...), custom_call_target="tpu_custom_call" | custom-call | flops 1048576 | bytes 65536 | tf_op jit(solution)/shard_map/pick_rows/pallas_call | solution.py:62
  27.1 4.4 %pick_rows.5 = (bf16[32,128,128]{2,1,0:T(8,128)(2,1)}, bf16[32,128,128]{2,1,0:T(8,128)(2,1)}) custom-call(s32[2]{0:T(128)S(1)} %get-tuple-element.54.first_ref, bf16[128,256]{1,0:T(8,128)(2,1)S(1)} %fusion.1.pick_ref, f32[1,128]{1,0:T(1,128)S(1)} %broadcast_in_dim_tile.3.mask_ref, bf16[250,128,256]{2,1,0:T(8,128)(2,1)} %bitcast.43, ...), custom_call_target="tpu_custom_call" | custom-call | flops 1048576 | bytes 65536 | tf_op jit(solution)/shard_map/pick_rows/pallas_call | solution.py:62
  31.6 2.5 collective-permute-start.2
  34.1 2.6 %collective-permute-start.3 = (bf16[32,128,128]{2,1,0:T(8,128)(2,1)}, bf16[32,128,128]{2,1,0:T(8,128)(2,1)}, u32[]{:S(2)}, u32[]{:S(2)}) collective-permute-start(bf16[32,128,128]{2,1,0:T(8,128)(2,1)} %get-tuple-element.65), channel_id=1, source_target_pairs={{0,16},{4,20},{8,24},{12,28},{16,0},{20,4},{24,8},{28,12},{32,48},... | collective-permute-start | bytes 3145736 | tf_op jit(solution)/shard_map/ppermute | solution.py:25
  36.7 4.4 %pick_rows.6 = (bf16[32,128,128]{2,1,0:T(8,128)(2,1)}, bf16[32,128,128]{2,1,0:T(8,128)(2,1)}) custom-call(s32[2]{0:T(128)S(1)} %get-tuple-element.57.first_ref, bf16[128,256]{1,0:T(8,128)(2,1)S(1)} %fusion.1.pick_ref, f32[1,128]{1,0:T(1,128)S(1)} %broadcast_in_dim_tile.3.mask_ref, bf16[250,128,256]{2,1,0:T(8,128)(2,1)} %bitcast.45, ...), custom_call_target="tpu_custom_call" | custom-call | flops 1048576 | bytes 65536 | tf_op jit(solution)/shard_map/pick_rows/pallas_call | solution.py:62
  42.3 7.4 %collective-permute-done = bf16[32,128,128]{2,1,0:T(8,128)(2,1)} collective-permute-done((bf16[32,128,128]{2,1,0:T(8,128)(2,1)S(1)}, bf16[32,128,128]{2,1,0:T(8,128)(2,1)}, u32[]{:S(2)}, u32[]{:S(2)}) %collective-permute-start) | collective-permute-done | bytes 1048608 | tf_op jit(solution)/shard_map/ppermute | solution.py:20
  49.7 3.1 %collective-permute-start.5 = (bf16[32,128,128]{2,1,0:T(8,128)(2,1)}, bf16[32,128,128]{2,1,0:T(8,128)(2,1)}, u32[]{:S(2)}, u32[]{:S(2)}) collective-permute-start(bf16[32,128,128]{2,1,0:T(8,128)(2,1)} %get-tuple-element.67), channel_id=1, source_target_pairs={{0,24},{4,28},{8,0},{12,4},{16,8},{20,12},{24,16},{28,20},{32,56},... | collective-permute-start | bytes 3145736 | tf_op jit(solution)/shard_map/ppermute | solution.py:25
  52.7 3.6 %pick_rows.7 = (bf16[32,128,128]{2,1,0:T(8,128)(2,1)S(1)}, bf16[32,128,128]{2,1,0:T(8,128)(2,1)S(1)}) custom-call(s32[2]{0:T(128)S(1)} %get-tuple-element.60.first_ref, bf16[128,256]{1,0:T(8,128)(2,1)S(1)} %fusion.1.pick_ref, f32[1,128]{1,0:T(1,128)S(1)} %broadcast_in_dim_tile.3.mask_ref, bf16[250,128,256]{2,1,0:T(8,128)(2,1)} %bitcast.47, ...), custom_call_target="tpu_custom_call" | custom-call | flops 1048576 | bytes 65536 | tf_op jit(solution)/shard_map/pick_rows/pallas_call | solution.py:62
  56.3 17.1 %collective-permute-done.2 = bf16[32,128,128]{2,1,0:T(8,128)(2,1)} collective-permute-done((bf16[32,128,128]{2,1,0:T(8,128)(2,1)}, bf16[32,128,128]{2,1,0:T(8,128)(2,1)}, u32[]{:S(2)}, u32[]{:S(2)}) %collective-permute-start.2) | collective-permute-done | bytes 1048608 | tf_op jit(solution)/shard_map/ppermute | solution.py:20
  74.6 4.5 %collective-permute-done.4 = bf16[32,128,128]{2,1,0:T(8,128)(2,1)} collective-permute-done((bf16[32,128,128]{2,1,0:T(8,128)(2,1)}, bf16[32,128,128]{2,1,0:T(8,128)(2,1)}, u32[]{:S(2)}, u32[]{:S(2)}) %collective-permute-start.4) | collective-permute-done | bytes 1048608 | tf_op jit(solution)/shard_map/ppermute | solution.py:20
  79.1 2.4 collective-permute-done.5
  81.5 2.4 add_add_fusion.3
  83.9 3.4 %collective-permute-start.10 = (bf16[8,128,128]{2,1,0:T(8,128)(2,1)}, bf16[8,128,128]{2,1,0:T(8,128)(2,1)S(1)}, u32[]{:S(2)}, u32[]{:S(2)}) collective-permute-start(bf16[8,128,128]{2,1,0:T(8,128)(2,1)} %get-tuple-element.102), channel_id=1, source_target_pairs={{0,24},{4,28},{8,0},{12,4},{16,8},{20,12},{24,16},{28,20},{32,56},... | collective-permute-start | bytes 786440 | tf_op jit(solution)/shard_map/ppermute | solution.py:25
  89.0 2.5 %add_add_fusion.2 = (bf16[8,128,128]{2,1,0:T(8,128)(2,1)}, bf16[8,128,128]{2,1,0:T(8,128)(2,1)}, bf16[8,128,128]{2,1,0:T(8,128)(2,1)}) fusion(bf16[32,128,128]{2,1,0:T(8,128)(2,1)} %collective-permute-done.5, s32[]{:T(128)S(6)} %select_n.323, bf16[32,128,128]{2,1,0:T(8,128)(2,1)} %collective-permute-done.3, bf16[32,128,128]{2,1,0:T(8,128)(2,1)} %collective-permute-done.1, ...), kind=kLoop, calls=%fused_computation.7 | loop fusion | flops 1179648 | bytes 3932172 | tf_op jit(solution)/shard_map/add | solution.py:269
  93.8 2.3 collective-permute-done.8
  96.1 6.7 %collective-permute-done.6 = bf16[8,128,128]{2,1,0:T(8,128)(2,1)} collective-permute-done((bf16[8,128,128]{2,1,0:T(8,128)(2,1)S(1)}, bf16[8,128,128]{2,1,0:T(8,128)(2,1)}, u32[]{:S(2)}, u32[]{:S(2)}) %collective-permute-start.6) | collective-permute-done | bytes 262176 | tf_op jit(solution)/shard_map/ppermute | solution.py:25
  102.8 3.8 %collective-permute-done.7 = bf16[8,128,128]{2,1,0:T(8,128)(2,1)} collective-permute-done((bf16[8,128,128]{2,1,0:T(8,128)(2,1)}, bf16[8,128,128]{2,1,0:T(8,128)(2,1)}, u32[]{:S(2)}, u32[]{:S(2)}) %collective-permute-start.7) | collective-permute-done | bytes 262176 | tf_op jit(solution)/shard_map/ppermute | solution.py:20
  111.0 2.9 %collective-permute-done.12 = bf16[8,128,128]{2,1,0:T(8,128)(2,1)S(1)} collective-permute-done((bf16[8,128,128]{2,1,0:T(8,128)(2,1)S(1)}, bf16[8,128,128]{2,1,0:T(8,128)(2,1)S(1)}, u32[]{:S(2)}, u32[]{:S(2)}) %collective-permute-start.12) | collective-permute-done | bytes 262176 | tf_op jit(solution)/shard_map/ppermute | solution.py:29
  123.6 3.1 %collective-permute-done.19.refs_3_ = bf16[8,128,128]{2,1,0:T(8,128)(2,1)S(1)} collective-permute-done((bf16[8,128,128]{2,1,0:T(8,128)(2,1)S(1)}, bf16[8,128,128]{2,1,0:T(8,128)(2,1)S(1)}, u32[]{:S(2)}, u32[]{:S(2)}) %collective-permute-start.19) | collective-permute-done | bytes 262176 | tf_op jit(solution)/shard_map/ppermute | solution.py:20
  127.9 2.2 collective-permute-done.17.refs_1_
  135.0 14.5 %collective-permute-done.23.refs_1_.refs_5_ = bf16[32,128,128]{2,1,0:T(8,128)(2,1)S(1)} collective-permute-done((bf16[32,128,128]{2,1,0:T(8,128)(2,1)S(1)}, bf16[32,128,128]{2,1,0:T(8,128)(2,1)S(1)}, u32[]{:S(2)}, u32[]{:S(2)}) %collective-permute-start.23) | collective-permute-done | bytes 1048608 | tf_op jit(solution)/shard_map/ppermute | solution.py:25
  151.7 3.9 %collective-permute-done.20.refs_2_ = bf16[32,128,128]{2,1,0:T(8,128)(2,1)S(1)} collective-permute-done((bf16[32,128,128]{2,1,0:T(8,128)(2,1)S(1)}, bf16[32,128,128]{2,1,0:T(8,128)(2,1)S(1)}, u32[]{:S(2)}, u32[]{:S(2)}) %collective-permute-start.20) | collective-permute-done | bytes 1048608 | tf_op jit(solution)/shard_map/ppermute | solution.py:20
  155.8 2.7 %collective-permute-start.25 = (bf16[16,128,128]{2,1,0:T(8,128)(2,1)S(1)}, bf16[16,128,128]{2,1,0:T(8,128)(2,1)S(1)}, u32[]{:S(2)}, u32[]{:S(2)}) collective-permute-start(bf16[16,128,128]{2,1,0:T(8,128)(2,1)S(1)} %slice.63), channel_id=1, source_target_pairs={{0,96},{4,100},{8,104},{12,108},{16,112},{20,116},{24,120},{28,124... | collective-permute-start | bytes 1572872 | tf_op jit(solution)/shard_map/ppermute | solution.py:20
  160.1 12.9 %early_kernel.1.refs_6_ = f32[64,112,256]{2,1,0:T(8,128)} custom-call(s32[4]{0:T(128)S(1)} %pad_add_fusion.5.blocks_ref, bf16[1,112,256]{2,1,0:T(8,128)(2,1)S(1)} %bitcast.40, bf16[1,128]{1,0:T(2,128)(2,1)S(1)} %fusion.11.sign_ref, bf16[250,128,256]{2,1,0:T(8,128)(2,1)} %bitcast.49, bf16[32,128,128]{2,1,0:T(8,128)(2,1)S(1)} %assemble.2.refs_0_, ...), custom_call_target="tpu_custom_call" | custom-call | flops 12000000000 | bytes 16777216 | tf_op jit(solution)/shard_map/early_kernel/pallas_call | solution.py:215
  173.0 12.7 %late_kernel.1 = (bf16[32,101,256]{2,1,0:T(8,128)(2,1)}, bf16[32,101,256]{2,1,0:T(8,128)(2,1)}) custom-call(s32[4]{0:T(128)S(1)} %pad_add_fusion.blocks_ref, bf16[1,112,256]{2,1,0:T(8,128)(2,1)S(1)} %bitcast.39, bf16[1,128]{1,0:T(2,128)(2,1)S(1)} %fusion.11.sign_ref, bf16[250,128,256]{2,1,0:T(8,128)(2,1)} %bitcast.50, ...), custom_call_target="tpu_custom_call" | custom-call | flops 12000000000 | bytes 16777216 | tf_op jit(solution)/shard_map/late_kernel/pallas_call | solution.py:215
  187.5 5.7 %collective-permute-start.28 = (bf16[32,101,256]{2,0,1:T(8,128)(2,1)S(1)}, bf16[32,101,256]{2,0,1:T(8,128)(2,1)S(1)}, u32[]{:S(2)}, u32[]{:S(2)}) collective-permute-start(bf16[32,101,256]{2,0,1:T(8,128)(2,1)S(1)} %copy.21), channel_id=1, source_target_pairs={{0,1},{1,0},{2,3},{3,2},{4,5},{5,4},{6,7},{7,6},{8,9},{9,8},{10,11... | collective-permute-start | bytes 4964360 | tf_op jit(solution)/shard_map/ppermute | solution.py:33
  193.3 3.1 %collective-permute-done.28 = bf16[32,101,256]{2,0,1:T(8,128)(2,1)S(1)} collective-permute-done((bf16[32,101,256]{2,0,1:T(8,128)(2,1)S(1)}, bf16[32,101,256]{2,0,1:T(8,128)(2,1)S(1)}, u32[]{:S(2)}, u32[]{:S(2)}) %collective-permute-start.28) | collective-permute-done | bytes 1654816 | tf_op jit(solution)/shard_map/ppermute | solution.py:33
  197.1 3.3 %collective-permute-start.29 = (bf16[16,101,256]{2,0,1:T(8,128)(2,1)S(1)}, bf16[16,101,256]{2,0,1:T(8,128)(2,1)S(1)}, u32[]{:S(2)}, u32[]{:S(2)}) collective-permute-start(bf16[16,101,256]{2,0,1:T(8,128)(2,1)S(1)} %copy.25), channel_id=1, source_target_pairs={{0,2},{1,3},{2,0},{3,1},{4,6},{5,7},{6,4},{7,5},{8,10},{9,11},{10,... | collective-permute-start | bytes 2482184 | tf_op jit(solution)/shard_map/ppermute | solution.py:37
  200.4 20.7 %whole_kernel.1 = (bf16[32,101,256]{2,1,0:T(8,128)(2,1)}, bf16[32,101,256]{2,1,0:T(8,128)(2,1)}) custom-call(s32[8]{0:T(128)S(1)} %stack.81.blocks_ref, bf16[2,112,256]{2,1,0:T(8,128)(2,1)S(1)} %bitcast.38, bf16[1,128]{1,0:T(2,128)(2,1)S(1)} %fusion.11.sign_ref, bf16[250,128,256]{2,1,0:T(8,128)(2,1)} %bitcast.51, bf16[32,128,128]{2,1,0:T(8,128)(2,1)S(1)} %assemble.2.refs_0_, ...), custom_call_target="tpu_custom_call" | custom-call | flops 24000000000 | bytes 33554432 | tf_op jit(solution)/shard_map/whole_kernel/pallas_call | solution.py:215
  223.7 3.2 %collective-permute-done.30 = bf16[32,101,256]{2,0,1:T(8,128)(2,1)S(1)} collective-permute-done((bf16[32,101,256]{2,0,1:T(8,128)(2,1)S(1)}, bf16[32,101,256]{2,0,1:T(8,128)(2,1)S(1)}, u32[]{:S(2)}, u32[]{:S(2)}) %collective-permute-start.30) | collective-permute-done | bytes 1654816 | tf_op jit(solution)/shard_map/ppermute | solution.py:33
  229.3 19.4 %collective-permute-done.31 = bf16[16,101,256]{2,0,1:T(8,128)(2,1)S(1)} collective-permute-done((bf16[16,101,256]{2,0,1:T(8,128)(2,1)S(1)}, bf16[16,101,256]{2,0,1:T(8,128)(2,1)S(1)}, u32[]{:S(2)}, u32[]{:S(2)}) %collective-permute-start.31) | collective-permute-done | bytes 827424 | tf_op jit(solution)/shard_map/ppermute | solution.py:37
  (105 shorter events, 47.3 us)
Async XLA Ops:
  23.7 25.9 %collective-permute-start = (bf16[32,128,128]{2,1,0:T(8,128)(2,1)S(1)}, bf16[32,128,128]{2,1,0:T(8,128)(2,1)}, u32[]{:S(2)}, u32[]{:S(2)}) collective-permute-start(bf16[32,128,128]{2,1,0:T(8,128)(2,1)S(1)} %get-tuple-element.62), channel_id=1, source_target_pairs={{0,32},{4,36},{8,40},{12,44},{16,48},{20,52},{24,56},{28,60},{32,6... | collective-permute-start | bytes 3145736 | tf_op jit(solution)/shard_map/ppermute | solution.py:20
  25.9 30.4 %collective-permute-start.1 = (bf16[32,128,128]{2,1,0:T(8,128)(2,1)S(1)}, bf16[32,128,128]{2,1,0:T(8,128)(2,1)}, u32[]{:S(2)}, u32[]{:S(2)}) collective-permute-start(bf16[32,128,128]{2,1,0:T(8,128)(2,1)S(1)} %get-tuple-element.63), channel_id=1, source_target_pairs={{0,8},{4,12},{8,16},{12,20},{16,24},{20,28},{24,0},{28,4},{32,40},... | collective-permute-start | bytes 3145736 | tf_op jit(solution)/shard_map/ppermute | solution.py:25
  31.6 41.8 %collective-permute-start.2 = (bf16[32,128,128]{2,1,0:T(8,128)(2,1)}, bf16[32,128,128]{2,1,0:T(8,128)(2,1)}, u32[]{:S(2)}, u32[]{:S(2)}) collective-permute-start(bf16[32,128,128]{2,1,0:T(8,128)(2,1)} %get-tuple-element.64), channel_id=1, source_target_pairs={{0,64},{4,68},{8,72},{12,76},{16,80},{20,84},{24,88},{28,92},{32,9... | collective-permute-start | bytes 3145736 | tf_op jit(solution)/shard_map/ppermute | solution.py:20
  34.1 40.5 %collective-permute-start.3 = (bf16[32,128,128]{2,1,0:T(8,128)(2,1)}, bf16[32,128,128]{2,1,0:T(8,128)(2,1)}, u32[]{:S(2)}, u32[]{:S(2)}) collective-permute-start(bf16[32,128,128]{2,1,0:T(8,128)(2,1)} %get-tuple-element.65), channel_id=1, source_target_pairs={{0,16},{4,20},{8,24},{12,28},{16,0},{20,4},{24,8},{28,12},{32,48},... | collective-permute-start | bytes 3145736 | tf_op jit(solution)/shard_map/ppermute | solution.py:25
  41.1 38.0 %collective-permute-start.4 = (bf16[32,128,128]{2,1,0:T(8,128)(2,1)}, bf16[32,128,128]{2,1,0:T(8,128)(2,1)}, u32[]{:S(2)}, u32[]{:S(2)}) collective-permute-start(bf16[32,128,128]{2,1,0:T(8,128)(2,1)} %get-tuple-element.66), channel_id=1, source_target_pairs={{0,96},{4,100},{8,104},{12,108},{16,112},{20,116},{24,120},{28,124... | collective-permute-start | bytes 3145736 | tf_op jit(solution)/shard_map/ppermute | solution.py:20
  49.7 31.9 %collective-permute-start.5 = (bf16[32,128,128]{2,1,0:T(8,128)(2,1)}, bf16[32,128,128]{2,1,0:T(8,128)(2,1)}, u32[]{:S(2)}, u32[]{:S(2)}) collective-permute-start(bf16[32,128,128]{2,1,0:T(8,128)(2,1)} %get-tuple-element.67), channel_id=1, source_target_pairs={{0,24},{4,28},{8,0},{12,4},{16,8},{20,12},{24,16},{28,20},{32,56},... | collective-permute-start | bytes 3145736 | tf_op jit(solution)/shard_map/ppermute | solution.py:25
  83.9 9.8 %collective-permute-start.10 = (bf16[8,128,128]{2,1,0:T(8,128)(2,1)}, bf16[8,128,128]{2,1,0:T(8,128)(2,1)S(1)}, u32[]{:S(2)}, u32[]{:S(2)}) collective-permute-start(bf16[8,128,128]{2,1,0:T(8,128)(2,1)} %get-tuple-element.102), channel_id=1, source_target_pairs={{0,24},{4,28},{8,0},{12,4},{16,8},{20,12},{24,16},{28,20},{32,56},... | collective-permute-start | bytes 786440 | tf_op jit(solution)/shard_map/ppermute | solution.py:25
  87.4 8.7 %collective-permute-start.8 = (bf16[8,128,128]{2,1,0:T(8,128)(2,1)S(1)}, bf16[8,128,128]{2,1,0:T(8,128)(2,1)}, u32[]{:S(2)}, u32[]{:S(2)}) collective-permute-start(bf16[8,128,128]{2,1,0:T(8,128)(2,1)S(1)} %get-tuple-element.103), channel_id=1, source_target_pairs={{0,16},{4,20},{8,24},{12,28},{16,0},{20,4},{24,8},{28,12},{32,48},... | collective-permute-start | bytes 786440 | tf_op jit(solution)/shard_map/ppermute | solution.py:25
  89.0 13.8 %collective-permute-start.6 = (bf16[8,128,128]{2,1,0:T(8,128)(2,1)S(1)}, bf16[8,128,128]{2,1,0:T(8,128)(2,1)}, u32[]{:S(2)}, u32[]{:S(2)}) collective-permute-start(bf16[8,128,128]{2,1,0:T(8,128)(2,1)S(1)} %get-tuple-element.104), channel_id=1, source_target_pairs={{0,8},{4,12},{8,16},{12,20},{16,24},{20,28},{24,0},{28,4},{32,40},... | collective-permute-start | bytes 786440 | tf_op jit(solution)/shard_map/ppermute | solution.py:25
  91.5 11.3 %collective-permute-start.11 = (bf16[8,128,128]{2,1,0:T(8,128)(2,1)}, bf16[8,128,128]{2,1,0:T(8,128)(2,1)S(1)}, u32[]{:S(2)}, u32[]{:S(2)}) collective-permute-start(bf16[8,128,128]{2,1,0:T(8,128)(2,1)} %get-tuple-element.99), channel_id=1, source_target_pairs={{0,96},{4,100},{8,104},{12,108},{16,112},{20,116},{24,120},{28,124... | collective-permute-start | bytes 786440 | tf_op jit(solution)/shard_map/ppermute | solution.py:20
  92.7 10.1 %collective-permute-start.9 = (bf16[8,128,128]{2,1,0:T(8,128)(2,1)}, bf16[8,128,128]{2,1,0:T(8,128)(2,1)S(1)}, u32[]{:S(2)}, u32[]{:S(2)}) collective-permute-start(bf16[8,128,128]{2,1,0:T(8,128)(2,1)} %get-tuple-element.100), channel_id=1, source_target_pairs={{0,64},{4,68},{8,72},{12,76},{16,80},{20,84},{24,88},{28,92},{32,9... | collective-permute-start | bytes 786440 | tf_op jit(solution)/shard_map/ppermute | solution.py:20
  93.8 12.8 %collective-permute-start.7 = (bf16[8,128,128]{2,1,0:T(8,128)(2,1)}, bf16[8,128,128]{2,1,0:T(8,128)(2,1)}, u32[]{:S(2)}, u32[]{:S(2)}) collective-permute-start(bf16[8,128,128]{2,1,0:T(8,128)(2,1)} %get-tuple-element.101), channel_id=1, source_target_pairs={{0,32},{4,36},{8,40},{12,44},{16,48},{20,52},{24,56},{28,60},{32,6... | collective-permute-start | bytes 786440 | tf_op jit(solution)/shard_map/ppermute | solution.py:20
  107.9 6.0 %collective-permute-start.12 = (bf16[8,128,128]{2,1,0:T(8,128)(2,1)S(1)}, bf16[8,128,128]{2,1,0:T(8,128)(2,1)S(1)}, u32[]{:S(2)}, u32[]{:S(2)}) collective-permute-start(bf16[8,128,128]{2,1,0:T(8,128)(2,1)S(1)} %add_add_fusion.1), channel_id=1, source_target_pairs={{0,4},{4,0},{8,12},{12,8},{16,20},{20,16},{24,28},{28,24},{32,36},... | collective-permute-start | bytes 786440 | tf_op jit(solution)/shard_map/ppermute | solution.py:29
  110.9 8.6 %collective-permute-start.16 = (bf16[8,128,128]{2,1,0:T(8,128)(2,1)S(1)}, bf16[8,128,128]{2,1,0:T(8,128)(2,1)S(1)}, u32[]{:S(2)}, u32[]{:S(2)}) collective-permute-start(bf16[8,128,128]{2,1,0:T(8,128)(2,1)S(1)} %add_add_fusion), channel_id=1, source_target_pairs={{0,4},{4,0},{8,12},{12,8},{16,20},{20,16},{24,28},{28,24},{32,36},... | collective-permute-start | bytes 786440 | tf_op jit(solution)/shard_map/ppermute | solution.py:29
  114.0 7.7 %collective-permute-start.15 = (bf16[8,128,128]{2,1,0:T(8,128)(2,1)S(1)}, bf16[8,128,128]{2,1,0:T(8,128)(2,1)S(1)}, u32[]{:S(2)}, u32[]{:S(2)}) collective-permute-start(bf16[8,128,128]{2,1,0:T(8,128)(2,1)S(1)} %add.513.refs_0_), channel_id=1, source_target_pairs={{0,16},{4,20},{8,24},{12,28},{16,0},{20,4},{24,8},{28,12},{32,48},... | collective-permute-start | bytes 786440 | tf_op jit(solution)/shard_map/ppermute | solution.py:25
  116.4 6.7 %collective-permute-start.14 = (bf16[8,128,128]{2,1,0:T(8,128)(2,1)S(1)}, bf16[8,128,128]{2,1,0:T(8,128)(2,1)S(1)}, u32[]{:S(2)}, u32[]{:S(2)}) collective-permute-start(bf16[8,128,128]{2,1,0:T(8,128)(2,1)S(1)} %add.513.refs_0_), channel_id=1, source_target_pairs={{0,24},{4,28},{8,0},{12,4},{16,8},{20,12},{24,16},{28,20},{32,56},... | collective-permute-start | bytes 786440 | tf_op jit(solution)/shard_map/ppermute | solution.py:25
  116.6 7.0 %collective-permute-start.13 = (bf16[8,128,128]{2,1,0:T(8,128)(2,1)S(1)}, bf16[8,128,128]{2,1,0:T(8,128)(2,1)S(1)}, u32[]{:S(2)}, u32[]{:S(2)}) collective-permute-start(bf16[8,128,128]{2,1,0:T(8,128)(2,1)S(1)} %add.513.refs_0_), channel_id=1, source_target_pairs={{0,8},{4,12},{8,16},{12,20},{16,24},{20,28},{24,0},{28,4},{32,40},... | collective-permute-start | bytes 786440 | tf_op jit(solution)/shard_map/ppermute | solution.py:25
  119.6 7.1 %collective-permute-start.19 = (bf16[8,128,128]{2,1,0:T(8,128)(2,1)S(1)}, bf16[8,128,128]{2,1,0:T(8,128)(2,1)S(1)}, u32[]{:S(2)}, u32[]{:S(2)}) collective-permute-start(bf16[8,128,128]{2,1,0:T(8,128)(2,1)S(1)} %add.521.refs_0_), channel_id=1, source_target_pairs={{0,64},{4,68},{8,72},{12,76},{16,80},{20,84},{24,88},{28,92},{32,9... | collective-permute-start | bytes 786440 | tf_op jit(solution)/shard_map/ppermute | solution.py:20
  121.7 6.2 %collective-permute-start.18 = (bf16[8,128,128]{2,1,0:T(8,128)(2,1)S(1)}, bf16[8,128,128]{2,1,0:T(8,128)(2,1)S(1)}, u32[]{:S(2)}, u32[]{:S(2)}) collective-permute-start(bf16[8,128,128]{2,1,0:T(8,128)(2,1)S(1)} %add.521.refs_0_), channel_id=1, source_target_pairs={{0,96},{4,100},{8,104},{12,108},{16,112},{20,116},{24,120},{28,124... | collective-permute-start | bytes 786440 | tf_op jit(solution)/shard_map/ppermute | solution.py:20
  121.7 8.4 %collective-permute-start.17 = (bf16[8,128,128]{2,1,0:T(8,128)(2,1)S(1)}, bf16[8,128,128]{2,1,0:T(8,128)(2,1)S(1)}, u32[]{:S(2)}, u32[]{:S(2)}) collective-permute-start(bf16[8,128,128]{2,1,0:T(8,128)(2,1)S(1)} %add.521.refs_0_), channel_id=1, source_target_pairs={{0,32},{4,36},{8,40},{12,44},{16,48},{20,52},{24,56},{28,60},{32,6... | collective-permute-start | bytes 786440 | tf_op jit(solution)/shard_map/ppermute | solution.py:20
  130.2 19.3 %collective-permute-start.23 = (bf16[32,128,128]{2,1,0:T(8,128)(2,1)S(1)}, bf16[32,128,128]{2,1,0:T(8,128)(2,1)S(1)}, u32[]{:S(2)}, u32[]{:S(2)}) collective-permute-start(bf16[32,128,128]{2,1,0:T(8,128)(2,1)S(1)} %assemble.3.refs_1_), channel_id=1, source_target_pairs={{0,24},{4,28},{8,0},{12,4},{16,8},{20,12},{24,16},{28,20},{32,56},... | collective-permute-start | bytes 3145736 | tf_op jit(solution)/shard_map/ppermute | solution.py:25
  131.4 19.2 %collective-permute-start.22 = (bf16[32,128,128]{2,1,0:T(8,128)(2,1)S(1)}, bf16[32,128,128]{2,1,0:T(8,128)(2,1)S(1)}, u32[]{:S(2)}, u32[]{:S(2)}) collective-permute-start(bf16[32,128,128]{2,1,0:T(8,128)(2,1)S(1)} %assemble.3.refs_1_), channel_id=1, source_target_pairs={{0,8},{4,12},{8,16},{12,20},{16,24},{20,28},{24,0},{28,4},{32,40},... | collective-permute-start | bytes 3145736 | tf_op jit(solution)/shard_map/ppermute | solution.py:25
  131.8 19.9 %collective-permute-start.21 = (bf16[32,128,128]{2,1,0:T(8,128)(2,1)S(1)}, bf16[32,128,128]{2,1,0:T(8,128)(2,1)S(1)}, u32[]{:S(2)}, u32[]{:S(2)}) collective-permute-start(bf16[32,128,128]{2,1,0:T(8,128)(2,1)S(1)} %assemble.2.refs_0_), channel_id=1, source_target_pairs={{0,96},{4,100},{8,104},{12,108},{16,112},{20,116},{24,120},{28,124... | collective-permute-start | bytes 3145736 | tf_op jit(solution)/shard_map/ppermute | solution.py:20
  132.5 23.2 %collective-permute-start.20 = (bf16[32,128,128]{2,1,0:T(8,128)(2,1)S(1)}, bf16[32,128,128]{2,1,0:T(8,128)(2,1)S(1)}, u32[]{:S(2)}, u32[]{:S(2)}) collective-permute-start(bf16[32,128,128]{2,1,0:T(8,128)(2,1)S(1)} %assemble.2.refs_0_), channel_id=1, source_target_pairs={{0,32},{4,36},{8,40},{12,44},{16,48},{20,52},{24,56},{28,60},{32,6... | collective-permute-start | bytes 3145736 | tf_op jit(solution)/shard_map/ppermute | solution.py:20
  155.8 17.2 %collective-permute-start.25 = (bf16[16,128,128]{2,1,0:T(8,128)(2,1)S(1)}, bf16[16,128,128]{2,1,0:T(8,128)(2,1)S(1)}, u32[]{:S(2)}, u32[]{:S(2)}) collective-permute-start(bf16[16,128,128]{2,1,0:T(8,128)(2,1)S(1)} %slice.63), channel_id=1, source_target_pairs={{0,96},{4,100},{8,104},{12,108},{16,112},{20,116},{24,120},{28,124... | collective-permute-start | bytes 1572872 | tf_op jit(solution)/shard_map/ppermute | solution.py:20
  158.6 14.4 %collective-permute-start.24 = (bf16[16,128,128]{2,1,0:T(8,128)(2,1)S(1)}, bf16[16,128,128]{2,1,0:T(8,128)(2,1)S(1)}, u32[]{:S(2)}, u32[]{:S(2)}) collective-permute-start(bf16[16,128,128]{2,1,0:T(8,128)(2,1)S(1)} %slice.62), channel_id=1, source_target_pairs={{0,32},{4,36},{8,40},{12,44},{16,48},{20,52},{24,56},{28,60},{32,6... | collective-permute-start | bytes 1572872 | tf_op jit(solution)/shard_map/ppermute | solution.py:20
  158.6 14.4 %collective-permute-start.27 = (bf16[16,128,128]{2,1,0:T(8,128)(2,1)S(1)}, bf16[16,128,128]{2,1,0:T(8,128)(2,1)S(1)}, u32[]{:S(2)}, u32[]{:S(2)}) collective-permute-start(bf16[16,128,128]{2,1,0:T(8,128)(2,1)S(1)} %slice.65), channel_id=1, source_target_pairs={{0,24},{4,28},{8,0},{12,4},{16,8},{20,12},{24,16},{28,20},{32,56},... | collective-permute-start | bytes 1572872 | tf_op jit(solution)/shard_map/ppermute | solution.py:25
  158.8 14.2 %collective-permute-start.26 = (bf16[16,128,128]{2,1,0:T(8,128)(2,1)S(1)}, bf16[16,128,128]{2,1,0:T(8,128)(2,1)S(1)}, u32[]{:S(2)}, u32[]{:S(2)}) collective-permute-start(bf16[16,128,128]{2,1,0:T(8,128)(2,1)S(1)} %slice.64), channel_id=1, source_target_pairs={{0,8},{4,12},{8,16},{12,20},{16,24},{20,28},{24,0},{28,4},{32,40},... | collective-permute-start | bytes 1572872 | tf_op jit(solution)/shard_map/ppermute | solution.py:25
  187.5 8.8 %collective-permute-start.28 = (bf16[32,101,256]{2,0,1:T(8,128)(2,1)S(1)}, bf16[32,101,256]{2,0,1:T(8,128)(2,1)S(1)}, u32[]{:S(2)}, u32[]{:S(2)}) collective-permute-start(bf16[32,101,256]{2,0,1:T(8,128)(2,1)S(1)} %copy.21), channel_id=1, source_target_pairs={{0,1},{1,0},{2,3},{3,2},{4,5},{5,4},{6,7},{7,6},{8,9},{9,8},{10,11... | collective-permute-start | bytes 4964360 | tf_op jit(solution)/shard_map/ppermute | solution.py:33
  197.1 24.0 %collective-permute-start.29 = (bf16[16,101,256]{2,0,1:T(8,128)(2,1)S(1)}, bf16[16,101,256]{2,0,1:T(8,128)(2,1)S(1)}, u32[]{:S(2)}, u32[]{:S(2)}) collective-permute-start(bf16[16,101,256]{2,0,1:T(8,128)(2,1)S(1)} %copy.25), channel_id=1, source_target_pairs={{0,2},{1,3},{2,0},{3,1},{4,6},{5,7},{6,4},{7,5},{8,10},{9,11},{10,... | collective-permute-start | bytes 2482184 | tf_op jit(solution)/shard_map/ppermute | solution.py:37
  222.9 3.9 %collective-permute-start.30 = (bf16[32,101,256]{2,0,1:T(8,128)(2,1)S(1)}, bf16[32,101,256]{2,0,1:T(8,128)(2,1)S(1)}, u32[]{:S(2)}, u32[]{:S(2)}) collective-permute-start(bf16[32,101,256]{2,0,1:T(8,128)(2,1)S(1)} %copy.27), channel_id=1, source_target_pairs={{0,1},{1,0},{2,3},{3,2},{4,5},{5,4},{6,7},{7,6},{8,9},{9,8},{10,11... | collective-permute-start | bytes 4964360 | tf_op jit(solution)/shard_map/ppermute | solution.py:33
  227.5 21.2 %collective-permute-start.31 = (bf16[16,101,256]{2,0,1:T(8,128)(2,1)S(1)}, bf16[16,101,256]{2,0,1:T(8,128)(2,1)S(1)}, u32[]{:S(2)}, u32[]{:S(2)}) collective-permute-start(bf16[16,101,256]{2,0,1:T(8,128)(2,1)S(1)} %copy.30), channel_id=1, source_target_pairs={{0,2},{1,3},{2,0},{3,1},{4,6},{5,7},{6,4},{7,5},{8,10},{9,11},{10,... | collective-permute-start | bytes 2482184 | tf_op jit(solution)/shard_map/ppermute | solution.py:37
  (7 other events, 74.5 us)
